TPU v7x, 256 devices: a whole 4x4x8 slice. The times are simulated.
256 devices in a mesh: seq: 16 (over z, x_hi), mp: 16 (over y, x_lo, core).
Axes of the slice: x: 4 (x_hi: 2, x_lo: 2; x = x_hi * 2 + x_lo), y: 4, z: 8, core: 2. Of those that a mesh axis runs over, the one named last changes fastest.
Arguments:
- tokens: bfloat16 [8192, 4608], P('seq', 'mp')
- pre_gain: bfloat16 [4608], P('mp'), may hold values from -2.5 to 2.5
- post_gain: bfloat16 [4608], P('mp'), may hold values from -2.5 to 2.5
- w_query: bfloat16 [4608, 4096], P('seq', 'mp')
- w_key: bfloat16 [4608, 2048], P('seq', 'mp')
- w_value: bfloat16 [4608, 2048], P('seq', 'mp'), may hold values from -0.09375 to 0.09375
- w_out: bfloat16 [4096, 4608], P('mp', 'seq')
- segment_ids: int32 [8192], P('seq'), may hold values from 0 to 3, never falling along the last dimension, each value on 1 to 6553 neighbouring positions
- page_table: int32 [64], P('seq'), may hold values from 0 to 63, as said below
Outputs:
- layer_output: bfloat16 [8192, 4608], P('seq', 'mp')
- key_cache: bfloat16 [64, 128, 2048], P('seq', None, 'mp')
- value_cache: bfloat16 [64, 128, 2048], P('seq', None, 'mp')
Inputs may be any that keep to these rules, and one draw needn't show every extreme that they name: segment_ids never fall along the stream, every tenant of 0 to 3 is present, each has at least 1 and at most 6553 tokens and one has exactly 6553. page_table is a permutation; the slot of page p lies in the same block of 4 slots as p, that is page_table[p] // 4 = p // 4.
All inputs are finite; a program needn't handle non-finite values.
Results may differ from a plain program's by a relative error of at most 0.019.
Values may be sent and summed in bfloat16 or wider, within the bound.
No kernel may reach another device: no remote copies, remote signals or barrier semaphores. Data moves between devices by JAX's collectives and lax.ppermute only.
A program may use at most 64 MiB of HBM per device.

v0:
```python
import math

import jax
import jax.numpy as jnp
from jax import lax
from jax.sharding import PartitionSpec as P

D = 4608
HQ = 32
HD = 128
WINDOW = 4096
PAGE = 128
SEGS = 4


EPSILON = 1e-06
SOFT_CAP = 50.0
LARGE_INDEX = 1 << 30


def from_behind(block, axis, distance):
    devices = range(lax.axis_size(axis))
    route = [(i - distance, i) for i in devices if i - distance in devices]
    return lax.ppermute(block, axis, route)


def rotate(values, positions):
    half = values.shape[-1] // 2
    freqs = jnp.exp(
        -math.log(10000.0) * jnp.arange(half, dtype=jnp.float32) * (2.0 / values.shape[-1])
    )
    angles = positions.astype(jnp.float32)[:, None] * freqs[None, :]
    cosine = jnp.cos(angles)[:, None, :]
    sine = jnp.sin(angles)[:, None, :]
    first = values[..., :half]
    second = values[..., half:]
    return jnp.concatenate(
        [first * cosine - second * sine, second * cosine + first * sine], axis=-1
    )


def add_product(normed, piece):
    return jnp.dot(normed, piece, preferred_element_type=jnp.float32)


def shards(tokens, pre_gain, post_gain, w_query, w_key, w_value, w_out, segment_ids, page_table):
    rows_here = tokens.shape[0]
    whole, gain_full = (
        lax.all_gather(tokens, "mp", axis=1, tiled=True),
        lax.all_gather(pre_gain, "mp", axis=0, tiled=True),
    )
    x_whole = whole.astype(jnp.float32)
    pre_scale = lax.rsqrt(jnp.mean(x_whole * x_whole, axis=1, keepdims=True) + EPSILON)
    normed = (x_whole * pre_scale * (1.0 + gain_full.astype(jnp.float32))[None, :]).astype(
        jnp.bfloat16
    )
    query_raw = add_product(normed, lax.all_gather(w_query, "seq", axis=0, tiled=True))
    key_raw = add_product(normed, lax.all_gather(w_key, "seq", axis=0, tiled=True))
    value_raw = add_product(normed, lax.all_gather(w_value, "seq", axis=0, tiled=True))
    heads_query = w_query.shape[1] // HD
    heads_kv = w_key.shape[1] // HD
    seq_index = lax.axis_index("seq")
    base = seq_index * rows_here
    global_index = base + jnp.arange(rows_here, dtype=jnp.int32)
    local_first = jnp.stack(
        [jnp.min(jnp.where(segment_ids == s, global_index, LARGE_INDEX)) for s in range(SEGS)]
    )
    starts = lax.pmin(local_first, "seq")
    offsets = jnp.zeros((rows_here,), jnp.int32)
    for s in range(SEGS):
        offsets = offsets + jnp.where(segment_ids == s, starts[s], 0)
    within = global_index - offsets
    query_scale = float(D // HQ) ** (-0.5)
    queries = (rotate(query_raw.reshape(rows_here, heads_query, HD), within) * query_scale).astype(
        jnp.bfloat16
    )
    keys_here = rotate(key_raw.reshape(rows_here, heads_kv, HD), within).astype(jnp.bfloat16)
    values_here = value_raw.reshape(rows_here, heads_kv, HD).astype(jnp.bfloat16)
    reach = WINDOW // rows_here
    earlier = []
    current = (keys_here, values_here)
    for distance in range(reach):
        current = from_behind((current[0], current[1]), "seq", 1)
        earlier.append(current)
    earlier = earlier[::-1]
    keys_all = jnp.concatenate([pair[0] for pair in earlier] + [keys_here], axis=0)
    values_all = jnp.concatenate([pair[1] for pair in earlier] + [values_here], axis=0)
    block = math.gcd(rows_here, 512)
    grouped = queries.reshape(rows_here, heads_kv, heads_query // heads_kv, HD)

    def attend(start):
        query_pos = base + start + jnp.arange(block, dtype=jnp.int32)
        key_pos = base - WINDOW + start + jnp.arange(WINDOW + block, dtype=jnp.int32)
        key_segment = jnp.zeros((WINDOW + block,), jnp.int32)
        for s in range(1, SEGS):
            key_segment = key_segment + (key_pos >= starts[s]).astype(jnp.int32)
        distance = query_pos[:, None] - key_pos[None, :]
        allowed = (
            (key_pos >= 0)[None, :]
            & (distance >= 0)
            & (distance < WINDOW)
            & (segment_ids[:, None] == key_segment[None, :])
        )
        scores = jnp.einsum("qgrd,kgd->grqk", grouped, keys_all, preferred_element_type=jnp.float32)
        capped = SOFT_CAP * jnp.tanh(scores / SOFT_CAP)
        weights = jnp.where(allowed[None, None], jnp.exp(capped), 0.0)
        denominator = jnp.sum(weights, axis=-1)
        rounded = weights.astype(jnp.bfloat16)
        summed = jnp.einsum(
            "grqk,kgd->qgrd", rounded, values_all, preferred_element_type=jnp.float32
        )
        result = summed / jnp.transpose(denominator, (2, 0, 1))[..., None]
        return result.astype(jnp.bfloat16).reshape(block, heads_query * HD)

    block_starts = jnp.arange(rows_here // block, dtype=jnp.int32) * block
    attended = lax.map(attend, block_starts).reshape(rows_here, heads_query * HD)
    group_terms = jnp.dot(
        attended,
        lax.all_gather(w_out, "seq", axis=1, tiled=True),
        preferred_element_type=jnp.float32,
    )
    attention_share = lax.psum_scatter(
        group_terms.astype(jnp.bfloat16), "mp", scatter_dimension=1, tiled=True
    ).astype(jnp.float32)
    squares = jnp.sum(attention_share * attention_share, axis=1)
    square_total = lax.psum(squares, "mp")
    post_scale = lax.rsqrt(square_total / D + EPSILON)
    post = attention_share * post_scale[:, None] * (1.0 + post_gain.astype(jnp.float32))[None, :]
    layer_output = (tokens.astype(jnp.float32) + post).astype(jnp.bfloat16)
    pages_here = page_table.shape[0]
    local_slot = page_table - seq_index * pages_here
    one_hot = (local_slot[None, :] == jnp.arange(pages_here, dtype=jnp.int32)[:, None]).astype(
        jnp.bfloat16
    )
    stacked = jnp.stack(
        [
            keys_here.reshape(pages_here, PAGE, heads_kv * HD),
            values_here.reshape(pages_here, PAGE, heads_kv * HD),
        ]
    )
    placed = jnp.einsum(
        "sp,tpce->tsce", one_hot, stacked, preferred_element_type=jnp.float32
    ).astype(jnp.bfloat16)
    return (layer_output, placed[0], placed[1])


def solution(mesh):
    return jax.shard_map(
        shards,
        mesh=mesh,
        in_specs=(
            P("seq", "mp"),
            P("mp"),
            P("mp"),
            P("seq", "mp"),
            P("seq", "mp"),
            P("seq", "mp"),
            P("mp", "seq"),
            P("seq"),
            P("seq"),
        ),
        out_specs=(P("seq", "mp"), P("seq", None, "mp"), P("seq", None, "mp")),
        check_vma=False,
    )
```

profile of v0, /device:TPU:1, one launch (start us, length us, event | category | flops | bytes accessed | tf_op | source)
XLA Modules:
  0.0 505.8 jit_solution(7526832199181364429)
XLA Ops:
  14.0 17.3 %pmin.7 = s32[4]{0:T(128)S(1)} all-reduce(s32[4]{0:T(128)S(1)} %pad_add_fusion), channel_id=1, replica_groups=mesh['seq'=16,'mp'=16] {'seq'}, use_global_device_ids=true, to_apply=%region_5.6 | all-reduce | flops 4 | bytes 32 | tf_op jit(solution)/shard_map/pmin | solution.py:68
  34.1 53.2 %all-reduce = bf16[4608]{0:T(1024)(128)(2,1)S(1)} all-reduce(bf16[4608]{0:T(1024)(128)(2,1)S(1)} %dynamic-update-slice), channel_id=1, replica_groups=mesh['seq'=16,'mp'=16] {'mp'}, use_global_device_ids=true, to_apply=%add | all-reduce | flops 4608 | bytes 18432
  90.6 3.4 fusion.2
  94.0 39.3 %all-gather.10.cloned.1.call-done = bf16[4608,128]{1,0:T(8,128)(2,1)} async-done(((bf16[288,128]{1,0:T(8,128)(2,1)}), bf16[4608,128]{1,0:T(8,128)(2,1)}) %all-gather.10.cloned.1.call-update) | async-done | bytes 1179664 | tf_op jit(solution)/shard_map/all_gather | solution.py:58
  133.3 4.4 convolution_bitcast_fusion
  140.5 71.9 %all-gather.8.cloned.1.call-done = bf16[4608,128]{1,0:T(8,128)(2,1)} async-done(((bf16[288,128]{1,0:T(8,128)(2,1)}), bf16[4608,128]{1,0:T(8,128)(2,1)}) %all-gather.8.cloned.1.call-update) | async-done | bytes 1179664 | tf_op jit(solution)/shard_map/all_gather | solution.py:59
  212.4 4.8 convolution_convert_fusion.2
  219.5 5.2 %collective-permute-start.9 = (bf16[512,1,128]{0,2,1:T(8,128)(2,1)S(1)}, bf16[512,1,128]{0,2,1:T(8,128)(2,1)S(1)}, u32[]{:S(2)}, u32[]{:S(2)}) collective-permute-start(bf16[512,1,128]{0,2,1:T(8,128)(2,1)S(1)} %collective-permute-done.8), channel_id=1, source_target_pairs={{0,16},{16,32},{32,48},{48,64},{64,80},{80,96},{96,112},{112,128},... | collective-permute-start | bytes 393224 | tf_op jit(solution)/shard_map/ppermute | solution.py:24
  227.7 5.3 %collective-permute-start.10 = (bf16[512,1,128]{0,2,1:T(8,128)(2,1)S(1)}, bf16[512,1,128]{0,2,1:T(8,128)(2,1)S(1)}, u32[]{:S(2)}, u32[]{:S(2)}) collective-permute-start(bf16[512,1,128]{0,2,1:T(8,128)(2,1)S(1)} %collective-permute-done.9), channel_id=1, source_target_pairs={{0,16},{16,32},{32,48},{48,64},{64,80},{80,96},{96,112},{112,128},... | collective-permute-start | bytes 393224 | tf_op jit(solution)/shard_map/ppermute | solution.py:24
  237.0 5.3 %collective-permute-start.11 = (bf16[512,1,128]{0,2,1:T(8,128)(2,1)S(1)}, bf16[512,1,128]{0,2,1:T(8,128)(2,1)S(1)}, u32[]{:S(2)}, u32[]{:S(2)}) collective-permute-start(bf16[512,1,128]{0,2,1:T(8,128)(2,1)S(1)} %collective-permute-done.10), channel_id=1, source_target_pairs={{0,16},{16,32},{32,48},{48,64},{64,80},{80,96},{96,112},{112,128},... | collective-permute-start | bytes 393224 | tf_op jit(solution)/shard_map/ppermute | solution.py:24
  242.3 5.2 %fusion.10 = pred[512,4608]{0,1:T(8,128)(4,1)S(1)} fusion(s32[512]{0:T(512)S(1)} %copy-done.21, s32[4608]{0:T(1024)S(1)} %get-tuple-element.61, s32[512]{0:T(512)S(1)} %iota_add_fusion.1, s32[4608]{0:T(1024)S(1)} %get-tuple-element.60, pred[4608]{0:T(1024)(128)(4,1)S(1)} %fusion.52), kind=kLoop, calls=%fused_computation.14 | loop fusion | flops 16515072 | bytes 2404864 | tf_op jit(solution)/shard_map/while/body/eval_jaxpr/and | solution.py:99
  249.7 5.8 %collective-permute-start.12 = (bf16[512,1,128]{0,2,1:T(8,128)(2,1)S(1)}, bf16[512,1,128]{0,2,1:T(8,128)(2,1)S(1)}, u32[]{:S(2)}, u32[]{:S(2)}) collective-permute-start(bf16[512,1,128]{0,2,1:T(8,128)(2,1)S(1)} %collective-permute-done.11), channel_id=1, source_target_pairs={{0,16},{16,32},{32,48},{48,64},{64,80},{80,96},{96,112},{112,128},... | collective-permute-start | bytes 393224 | tf_op jit(solution)/shard_map/ppermute | solution.py:24
  260.2 6.2 %collective-permute-start.13 = (bf16[512,1,128]{0,2,1:T(8,128)(2,1)S(1)}, bf16[512,1,128]{0,2,1:T(8,128)(2,1)}, u32[]{:S(2)}, u32[]{:S(2)}) collective-permute-start(bf16[512,1,128]{0,2,1:T(8,128)(2,1)S(1)} %collective-permute-done.12), channel_id=1, source_target_pairs={{0,16},{16,32},{32,48},{48,64},{64,80},{80,96},{96,112},{112,128},... | collective-permute-start | bytes 393224 | tf_op jit(solution)/shard_map/ppermute | solution.py:24
  266.4 36.1 %all-gather.12.cloned.1.call-done = bf16[4608,256]{1,0:T(8,128)(2,1)} async-done(((bf16[288,256]{1,0:T(8,128)(2,1)}), bf16[4608,256]{1,0:T(8,128)(2,1)}) %all-gather.12.cloned.1.call-update) | async-done | bytes 2359312 | tf_op jit(solution)/shard_map/all_gather | solution.py:57
  302.5 4.9 fusion.62
  310.1 4.9 collective-permute-start.14
  318.9 5.8 %collective-permute-start.15 = (bf16[512,1,128]{0,2,1:T(8,128)(2,1)}, bf16[512,1,128]{0,2,1:T(8,128)(2,1)S(1)}, u32[]{:S(2)}, u32[]{:S(2)}) collective-permute-start(bf16[512,1,128]{0,2,1:T(8,128)(2,1)} %collective-permute-done.14), channel_id=1, source_target_pairs={{0,16},{16,32},{32,48},{48,64},{64,80},{80,96},{96,112},{112,128},... | collective-permute-start | bytes 393224 | tf_op jit(solution)/shard_map/ppermute | solution.py:24
  326.0 3.0 collective-permute-start.7
  333.1 6.7 %fusion = (f32[2,512]{1,0:T(2,128)S(1)}, f32[4608,512,2]{1,0,2:T(8,128)S(1)}) fusion(pred[512,4608]{0,1:T(8,128)(4,1)S(1)} %fusion.10, f32[512,2,64]{2,0,1:T(8,128)S(1)} %get-tuple-element.39, f32[512,2,64]{2,0,1:T(8,128)S(1)} %get-tuple-element.38, bf16[4608,1,128]{0,2,1:T(8,128)(2,1)S(1)} %constant_dynamic-update-slice_fusion.9), kind=kOutput, calls=%fused_computation.3 | convolution fusion | flops 1227226112 | bytes 22941696 | tf_op jit(solution)/shard_map/while/body/eval_jaxpr/qgrd,kgd->grqk/dot_general | solution.py:104
  339.8 6.3 %fusion.24 = bf16[512,1,2,128]{0,3,2,1:T(8,128)(2,1)S(1)} fusion(f32[4608,512,2]{1,0,2:T(8,128)S(1)} %get-tuple-element.59, pred[512,4608]{0,1:T(8,128)(4,1)S(1)} %fusion.10, bf16[4608,1,128]{2,0,1:T(8,128)(2,1)S(1)} %constant_dynamic-update-slice_fusion, f32[512,2]{0,1:T(2,128)S(1)} %bitcast.95), kind=kOutput, calls=%fused_computation.26 | convolution fusion | flops 1227096064 | bytes 22679552 | tf_op jit(solution)/shard_map/while/body/eval_jaxpr/grqk,kgd->qgrd/dot_general | solution.py:109
  346.1 43.8 %all-gather.14.cloned.1.call-done = bf16[256,4608]{0,1:T(8,128)(2,1)} async-done(((bf16[256,288]{0,1:T(8,128)(2,1)}), bf16[256,4608]{0,1:T(8,128)(2,1)}) %all-gather.14.cloned.1.call-update) | async-done | bytes 2359312 | tf_op jit(solution)/shard_map/all_gather | solution.py:119
  389.9 5.2 %convolution_convert_fusion = bf16[512,4608]{0,1:T(8,128)(2,1)} fusion(bf16[256,4608]{0,1:T(8,128)(2,1)} %all-gather.14.cloned.1.call-done, bf16[512,256]{0,1:T(8,128)(2,1)S(1)} %bitcast.94), kind=kOutput, calls=%fused_computation.16 | convolution fusion | flops 1210318848 | bytes 7340032 | tf_op jit(solution)/shard_map/dot_general | solution.py:117
  398.1 68.9 %reduce-scatter.2.cloned.1.call-done = bf16[512,288]{0,1:T(8,128)(2,1)} async-done(((bf16[512,4608]{0,1:T(8,128)(2,1)}), bf16[512,288]{0,1:T(8,128)(2,1)}) %reduce-scatter.2.cloned.1.call-update) | async-done | bytes 294928 | tf_op jit(solution)/shard_map/reduce_scatter | solution.py:122
  468.0 29.2 %psum.7 = f32[512]{0:T(512)S(1)} all-reduce(f32[512]{0:T(512)S(1)} %fusion.29), channel_id=1, replica_groups=mesh['seq'=16,'mp'=16] {'mp'}, use_global_device_ids=true, to_apply=%region_9.10 | all-reduce | flops 512 | bytes 4096 | tf_op jit(solution)/shard_map/psum | solution.py:126
  (137 shorter events, 48.2 us)
Async XLA Ops:
  7.2 83.4 %all-gather.6.cloned.1.call-start = ((), (), s32[]{:S(2)}) async-start(), calls=%async_computation.1 | async-start | bytes 5013504 | tf_op jit(solution)/shard_map/all_gather | solution.py:49
  7.9 125.4 %all-gather.10.cloned.1.call-start = ((), (), s32[]{:S(2)}) async-start(), calls=%async_computation.3 | async-start | bytes 1253376 | tf_op jit(solution)/shard_map/all_gather | solution.py:58
  8.6 203.7 %all-gather.8.cloned.1.call-start = ((), (), s32[]{:S(2)}) async-start(), calls=%async_computation.2 | async-start | bytes 1253376 | tf_op jit(solution)/shard_map/all_gather | solution.py:59
  9.4 293.2 %all-gather.12.cloned.1.call-start = ((), (), s32[]{:S(2)}) async-start(), calls=%async_computation.4 | async-start | bytes 2506752 | tf_op jit(solution)/shard_map/all_gather | solution.py:57
  10.0 379.9 %all-gather.14.cloned.1.call-start = ((), (), s32[]{:S(2)}) async-start(), calls=%async_computation.5 | async-start | bytes 2506752 | tf_op jit(solution)/shard_map/all_gather | solution.py:119
  138.3 104.0 %copy-start.21 = (s32[512]{0:T(512)S(1)}, s32[512]{0:T(512)}, u32[]{:S(2)}) copy-start(s32[512]{0:T(512)} %param.16) | copy-start | bytes 6148
  138.3 81.1 %collective-permute-start.8 = (bf16[512,1,128]{0,2,1:T(8,128)(2,1)S(1)}, bf16[512,1,128]{0,2,1:T(8,128)(2,1)S(1)}, u32[]{:S(2)}, u32[]{:S(2)}) collective-permute-start(bf16[512,1,128]{0,2,1:T(8,128)(2,1)S(1)} %pad_maximum_fusion), channel_id=1, source_target_pairs={{0,16},{16,32},{32,48},{48,64},{64,80},{80,96},{96,112},{112,128},... | collective-permute-start | bytes 393224 | tf_op jit(solution)/shard_map/ppermute | solution.py:24
  217.2 7.5 %collective-permute-start = (bf16[512,1,128]{2,0,1:T(8,128)(2,1)S(1)}, bf16[512,1,128]{2,0,1:T(8,128)(2,1)S(1)}, u32[]{:S(2)}, u32[]{:S(2)}) collective-permute-start(bf16[512,1,128]{2,0,1:T(8,128)(2,1)S(1)} %bitcast.92), channel_id=1, source_target_pairs={{0,16},{16,32},{32,48},{48,64},{64,80},{80,96},{96,112},{112,128},... | collective-permute-start | bytes 393224 | tf_op jit(solution)/shard_map/ppermute | solution.py:24
  219.5 8.2 %collective-permute-start.9 = (bf16[512,1,128]{0,2,1:T(8,128)(2,1)S(1)}, bf16[512,1,128]{0,2,1:T(8,128)(2,1)S(1)}, u32[]{:S(2)}, u32[]{:S(2)}) collective-permute-start(bf16[512,1,128]{0,2,1:T(8,128)(2,1)S(1)} %collective-permute-done.8), channel_id=1, source_target_pairs={{0,16},{16,32},{32,48},{48,64},{64,80},{80,96},{96,112},{112,128},... | collective-permute-start | bytes 393224 | tf_op jit(solution)/shard_map/ppermute | solution.py:24
  224.7 242.3 %reduce-scatter.2.cloned.1.call-start = ((), (), s32[]{:S(2)}) async-start(), calls=%async_computation.6 | async-start | bytes 5013504 | tf_op jit(solution)/shard_map/reduce_scatter | solution.py:122
  224.7 10.3 %collective-permute-start.1 = (bf16[512,1,128]{2,0,1:T(8,128)(2,1)S(1)}, bf16[512,1,128]{2,0,1:T(8,128)(2,1)S(1)}, u32[]{:S(2)}, u32[]{:S(2)}) collective-permute-start(bf16[512,1,128]{2,0,1:T(8,128)(2,1)S(1)} %collective-permute-done), channel_id=1, source_target_pairs={{0,16},{16,32},{32,48},{48,64},{64,80},{80,96},{96,112},{112,128},... | collective-permute-start | bytes 393224 | tf_op jit(solution)/shard_map/ppermute | solution.py:24
  227.7 9.3 %collective-permute-start.10 = (bf16[512,1,128]{0,2,1:T(8,128)(2,1)S(1)}, bf16[512,1,128]{0,2,1:T(8,128)(2,1)S(1)}, u32[]{:S(2)}, u32[]{:S(2)}) collective-permute-start(bf16[512,1,128]{0,2,1:T(8,128)(2,1)S(1)} %collective-permute-done.9), channel_id=1, source_target_pairs={{0,16},{16,32},{32,48},{48,64},{64,80},{80,96},{96,112},{112,128},... | collective-permute-start | bytes 393224 | tf_op jit(solution)/shard_map/ppermute | solution.py:24
  235.0 12.4 %collective-permute-start.2 = (bf16[512,1,128]{2,0,1:T(8,128)(2,1)S(1)}, bf16[512,1,128]{2,0,1:T(8,128)(2,1)S(1)}, u32[]{:S(2)}, u32[]{:S(2)}) collective-permute-start(bf16[512,1,128]{2,0,1:T(8,128)(2,1)S(1)} %collective-permute-done.1), channel_id=1, source_target_pairs={{0,16},{16,32},{32,48},{48,64},{64,80},{80,96},{96,112},{112,128},... | collective-permute-start | bytes 393224 | tf_op jit(solution)/shard_map/ppermute | solution.py:24
  237.0 12.7 %collective-permute-start.11 = (bf16[512,1,128]{0,2,1:T(8,128)(2,1)S(1)}, bf16[512,1,128]{0,2,1:T(8,128)(2,1)S(1)}, u32[]{:S(2)}, u32[]{:S(2)}) collective-permute-start(bf16[512,1,128]{0,2,1:T(8,128)(2,1)S(1)} %collective-permute-done.10), channel_id=1, source_target_pairs={{0,16},{16,32},{32,48},{48,64},{64,80},{80,96},{96,112},{112,128},... | collective-permute-start | bytes 393224 | tf_op jit(solution)/shard_map/ppermute | solution.py:24
  247.5 9.8 %collective-permute-start.3 = (bf16[512,1,128]{2,0,1:T(8,128)(2,1)S(1)}, bf16[512,1,128]{2,0,1:T(8,128)(2,1)S(1)}, u32[]{:S(2)}, u32[]{:S(2)}) collective-permute-start(bf16[512,1,128]{2,0,1:T(8,128)(2,1)S(1)} %collective-permute-done.2), channel_id=1, source_target_pairs={{0,16},{16,32},{32,48},{48,64},{64,80},{80,96},{96,112},{112,128},... | collective-permute-start | bytes 393224 | tf_op jit(solution)/shard_map/ppermute | solution.py:24
  249.7 10.5 %collective-permute-start.12 = (bf16[512,1,128]{0,2,1:T(8,128)(2,1)S(1)}, bf16[512,1,128]{0,2,1:T(8,128)(2,1)S(1)}, u32[]{:S(2)}, u32[]{:S(2)}) collective-permute-start(bf16[512,1,128]{0,2,1:T(8,128)(2,1)S(1)} %collective-permute-done.11), channel_id=1, source_target_pairs={{0,16},{16,32},{32,48},{48,64},{64,80},{80,96},{96,112},{112,128},... | collective-permute-start | bytes 393224 | tf_op jit(solution)/shard_map/ppermute | solution.py:24
  257.3 50.1 %collective-permute-start.4 = (bf16[512,1,128]{2,0,1:T(8,128)(2,1)S(1)}, bf16[512,1,128]{2,0,1:T(8,128)(2,1)}, u32[]{:S(2)}, u32[]{:S(2)}) collective-permute-start(bf16[512,1,128]{2,0,1:T(8,128)(2,1)S(1)} %collective-permute-done.3), channel_id=1, source_target_pairs={{0,16},{16,32},{32,48},{48,64},{64,80},{80,96},{96,112},{112,128},... | collective-permute-start | bytes 393224 | tf_op jit(solution)/shard_map/ppermute | solution.py:24
  260.2 49.9 %collective-permute-start.13 = (bf16[512,1,128]{0,2,1:T(8,128)(2,1)S(1)}, bf16[512,1,128]{0,2,1:T(8,128)(2,1)}, u32[]{:S(2)}, u32[]{:S(2)}) collective-permute-start(bf16[512,1,128]{0,2,1:T(8,128)(2,1)S(1)} %collective-permute-done.12), channel_id=1, source_target_pairs={{0,16},{16,32},{32,48},{48,64},{64,80},{80,96},{96,112},{112,128},... | collective-permute-start | bytes 393224 | tf_op jit(solution)/shard_map/ppermute | solution.py:24
  307.5 9.7 %collective-permute-start.5 = (bf16[512,1,128]{2,0,1:T(8,128)(2,1)}, bf16[512,1,128]{2,0,1:T(8,128)(2,1)}, u32[]{:S(2)}, u32[]{:S(2)}) collective-permute-start(bf16[512,1,128]{2,0,1:T(8,128)(2,1)} %collective-permute-done.4), channel_id=1, source_target_pairs={{0,16},{16,32},{32,48},{48,64},{64,80},{80,96},{96,112},{112,128},... | collective-permute-start | bytes 393224 | tf_op jit(solution)/shard_map/ppermute | solution.py:24
  310.1 8.8 %collective-permute-start.14 = (bf16[512,1,128]{0,2,1:T(8,128)(2,1)}, bf16[512,1,128]{0,2,1:T(8,128)(2,1)}, u32[]{:S(2)}, u32[]{:S(2)}) collective-permute-start(bf16[512,1,128]{0,2,1:T(8,128)(2,1)} %collective-permute-done.13), channel_id=1, source_target_pairs={{0,16},{16,32},{32,48},{48,64},{64,80},{80,96},{96,112},{112,128},... | collective-permute-start | bytes 393224 | tf_op jit(solution)/shard_map/ppermute | solution.py:24
  317.2 8.7 %collective-permute-start.6 = (bf16[512,1,128]{2,0,1:T(8,128)(2,1)}, bf16[512,1,128]{2,0,1:T(8,128)(2,1)S(1)}, u32[]{:S(2)}, u32[]{:S(2)}) collective-permute-start(bf16[512,1,128]{2,0,1:T(8,128)(2,1)} %collective-permute-done.5), channel_id=1, source_target_pairs={{0,16},{16,32},{32,48},{48,64},{64,80},{80,96},{96,112},{112,128},... | collective-permute-start | bytes 393224 | tf_op jit(solution)/shard_map/ppermute | solution.py:24
  318.9 10.1 %collective-permute-start.15 = (bf16[512,1,128]{0,2,1:T(8,128)(2,1)}, bf16[512,1,128]{0,2,1:T(8,128)(2,1)S(1)}, u32[]{:S(2)}, u32[]{:S(2)}) collective-permute-start(bf16[512,1,128]{0,2,1:T(8,128)(2,1)} %collective-permute-done.14), channel_id=1, source_target_pairs={{0,16},{16,32},{32,48},{48,64},{64,80},{80,96},{96,112},{112,128},... | collective-permute-start | bytes 393224 | tf_op jit(solution)/shard_map/ppermute | solution.py:24
  326.0 5.1 collective-permute-start.7
  395.1 102.1 %copy-start = (bf16[512,288]{0,1:T(8,128)(2,1)S(1)}, bf16[512,288]{0,1:T(8,128)(2,1)}, u32[]{:S(2)}) copy-start(bf16[512,288]{0,1:T(8,128)(2,1)} %param.9) | copy-start | bytes 884740
  (22 other events, 444.4 us)
Sparse Core Ops, SparseCore 0:
  9.8 45.1 all-gather.5
  57.6 75.5 all-gather.9
  135.9 76.4 all-gather.7
  214.8 87.6 all-gather.11
  305.0 84.8 all-gather.13
  395.2 71.6 reduce-scatter.1
where the time goes:
time: 508 us; the launch traced here: 506 us
  waiting for transfers between devices  263 us (52%)
  blocking collectives  99.7 us (20%)
  starting transfers between devices  59.6 us (12%)
  matrix products  32.7 us (6%)
  other arithmetic  23.6 us (5%)
  between operations  15.6 us (3%)
  local copies, waits for them, and re-layouts  11.4 us (2%)
    all_gather x1, waiting for transfers between devices, shards(): lax.all_gather(w_value, 'seq', axis=0, tiled=True)  71.9 us
    reduce_scatter x1, waiting for transfers between devices, shards(): lax.psum_scatter(group_terms.astype(jnp.bfloat16), 'mp', scatter_dimensio...  68.9 us
    ppermute x16, starting transfers between devices, from_behind(): return lax.ppermute(block, axis, route)  59.4 us
    unnamed x1, blocking collectives  53.2 us
    all_gather x1, waiting for transfers between devices, shards(): lax.all_gather(w_out, 'seq', axis=1, tiled=True)  43.8 us
    all_gather x1, waiting for transfers between devices, shards(): lax.all_gather(w_key, 'seq', axis=0, tiled=True)  39.3 us
    all_gather x1, waiting for transfers between devices, shards(): lax.all_gather(w_query, 'seq', axis=0, tiled=True)  36.1 us
    psum x1, blocking collectives, shards(): square_total = lax.psum(squares, 'mp')  29.2 us
  transfers between devices with their start and end apart: 22, of which 6 were waited for; matrix products, arithmetic and copies ran while one was open for 12% of the time, Pallas kernels for 0%

commit v1 on v0

v1 whole, which is shorter than its diff:
```python
import functools
import math

import jax
import jax.numpy as jnp
from jax import lax
from jax.experimental import pallas as pl
from jax.experimental.pallas import tpu as pltpu
from jax.sharding import PartitionSpec as P

D = 4608
HQ = 32
HD = 128
WINDOW = 4096
PAGE = 128
SEGS = 4

EPSILON = 1e-06
SOFT_CAP = 50.0
LOG2E = 1.4426950408889634
EXTRA = 16
SEQ = 16
ROUNDS = 8

BF = jnp.bfloat16
F32 = jnp.float32

AHEAD = [(i, (i + 2) % SEQ) for i in range(SEQ)]
BEHIND = [((i + 2) % SEQ, i) for i in range(SEQ)]
LATER = [(i, i + 2) for i in range(SEQ - 2)]
ACROSS = [(i, i ^ 1) for i in range(SEQ)]
TURN = [(s * SEQ + m, m * SEQ + s) for s in range(SEQ) for m in range(SEQ)]


SIDE = [(i, i ^ 2) for i in range(SEQ)]
UP = [(i, (i + 4) % SEQ) for i in range(SEQ)]
DOWN = [((i + 4) % SEQ, i) for i in range(SEQ)]
SWAP = [(i, i ^ 1) for i in range(SEQ)]
PLACES = (((0, 0), (0, 1)), ((-1, 0), (-1, 1)), ((1, 0), (1, 1)), ((2, 0),), ((2, 1),))


def move(block, perm):
    return lax.ppermute(block, "seq", perm)


def shift(block, perm):
    return lax.ppermute(block, "mp", perm)


def tie(*values):
    return lax.optimization_barrier(values)


def start_loads(index_ref, x_refs, w_refs, pieces, x_ref, w_ref, x_sem, w_sem):
    w_copies, x_copies = [], []
    for slot in range(ROUNDS):
        place = index_ref[2 + ROUNDS + slot]
        for part in range(2):
            parity = index_ref[1] if part == 0 else 1 - index_ref[1]
            which, start, length = pieces[slot][part]
            w_copies.append(
                pltpu.make_async_copy(
                    w_refs[which].at[pl.ds(start, length)],
                    w_ref.at[place, parity],
                    w_sem.at[2 * slot + part],
                )
            )
    same, other = x_refs[: len(PLACES)], x_refs[len(PLACES) :]
    for k, places in enumerate(PLACES):
        for j in range(len(places)):
            for ref in (same[k], other[k]):
                n = len(x_copies)
                x_copies.append(
                    pltpu.make_async_copy(ref.at[j], x_ref.at[n // 2, n % 2], x_sem.at[n])
                )
    for copy in w_copies + x_copies:
        copy.start()
    for copy in w_copies:
        copy.wait()
    return x_copies


def project_kernel(pieces, rotated, factor, index_ref, cos_ref, sin_ref, *rest):
    n = 2 * len(PLACES)
    x_refs, w_refs = rest[:n], rest[n:-6]
    out_ref, x_ref, w_ref, acc_ref, x_sem, w_sem = rest[-6:]
    copies = start_loads(index_ref, x_refs, w_refs, pieces, x_ref, w_ref, x_sem, w_sem)
    depth = x_ref.shape[2]
    length = w_ref.shape[2]
    squares = jnp.zeros((1, x_ref.shape[3]), F32)
    for slot in range(ROUNDS):
        total = None
        place = index_ref[2 + slot]
        for part in range(2):
            copies[2 * slot + part].wait()
            parity = index_ref[0] if part == 0 else 1 - index_ref[0]
            side = x_ref[slot, part, depth - EXTRA :, :]
            squares = squares + jnp.sum(side.astype(F32), axis=0, keepdims=True)
            product = lax.dot_general(
                w_ref[place, parity],
                x_ref[slot, part, :length, :],
                (((0,), (0,)), ((), ())),
                preferred_element_type=F32,
            )
            total = product if total is None else total + product
        if slot == 0:
            acc_ref[...] = total
        else:
            acc_ref[...] += total
    scale = lax.rsqrt(squares * (1.0 / D) + EPSILON)
    half = HD // 2
    for head in range(2):
        start = head * HD
        if rotated[head]:
            first = acc_ref[start : start + half, :] * scale
            second = acc_ref[start + half : start + HD, :] * scale
            cos, sin = cos_ref[...], sin_ref[...]
            value = jnp.concatenate(
                [first * cos - second * sin, second * cos + first * sin], axis=0
            )
            if factor != 1.0:
                value = value * factor
        else:
            value = acc_ref[start : start + HD, :] * scale
        out_ref[:, start : start + HD] = jnp.transpose(value).astype(BF)


def project(chunks, weights, pieces, index, cos, sin, rotated, factor):
    _, depth, rows = chunks[0].shape
    vmem = pl.BlockSpec(memory_space=pltpu.VMEM)
    outside = pl.BlockSpec(memory_space=pltpu.HBM)
    return pl.pallas_call(
        functools.partial(project_kernel, pieces, rotated, factor),
        out_shape=jax.ShapeDtypeStruct((rows, 2 * HD), BF),
        in_specs=[pl.BlockSpec(memory_space=pltpu.SMEM), vmem, vmem]
        + [outside] * (len(chunks) + len(weights)),
        out_specs=vmem,
        scratch_shapes=[
            pltpu.VMEM((ROUNDS, 2, depth, rows), BF),
            pltpu.VMEM((ROUNDS, 2, pieces[0][0][2], 2 * HD), BF),
            pltpu.VMEM((2 * HD, rows), F32),
            pltpu.SemaphoreType.DMA((2 * ROUNDS,)),
            pltpu.SemaphoreType.DMA((2 * ROUNDS,)),
        ],
        compiler_params=pltpu.CompilerParams(vmem_limit_bytes=60 << 20),
        cost_estimate=pl.CostEstimate(
            flops=2 * rows * 2 * HD * D, bytes_accessed=8 << 20, transcendentals=0
        ),
    )(index, cos, sin, *chunks, *weights)


def attend_kernel(distances, first, last, low_ref, q_ref, *rest):
    n = len(distances)
    kv_refs = rest[:n]
    rest = rest[n:]
    if not first:
        sum_in, den_in = rest[:2]
        rest = rest[2:]
    rows = q_ref.shape[0]
    tile = 256

    def part(index, carry):
        here = pl.ds(pl.multiple_of((index // 2) * tile, tile), tile)
        columns = pl.ds(pl.multiple_of(lax.rem(index, 2) * HD, HD), HD)
        q = q_ref[here, columns]
        low = low_ref[here, :]
        if first:
            total = jnp.zeros((tile, HD), F32)
            den = jnp.zeros((tile, HD), F32)
        else:
            total = sum_in[here, columns]
            den = den_in[here, columns]
        for kv_ref, distance in zip(kv_refs, distances):
            score = lax.dot_general(
                q, kv_ref[:, :HD], (((1,), (1,)), ((), ())), preferred_element_type=F32
            )
            weight = jnp.exp2(jnp.tanh(score * (1.0 / SOFT_CAP)) * (SOFT_CAP * LOG2E))
            place = lax.broadcasted_iota(jnp.int32, (tile, rows), 1)
            allowed = place >= low + distance * rows
            if distance == 0:
                own = lax.broadcasted_iota(jnp.int32, (tile, rows), 0) + (index // 2) * tile
                allowed = allowed & (place <= own)
            weight = jnp.where(allowed, weight, 0.0)
            for c in range(rows // HD):
                den = den + weight[:, c * HD : (c + 1) * HD]
            total = total + jnp.dot(
                weight.astype(BF), kv_ref[:, HD:], preferred_element_type=F32
            )
        if last:
            whole = jnp.sum(den, axis=1, keepdims=True)
            rest[0][here, columns] = (total / whole).astype(BF)
        else:
            rest[0][here, columns] = total
            rest[1][here, columns] = den
        return carry

    lax.fori_loop(0, 2 * (rows // tile), part, 0)


def attend(low, queries, kvs, distances, state):
    first = state is None
    last = 8 in distances
    rows = queries.shape[0]
    vmem = pl.BlockSpec(memory_space=pltpu.VMEM)
    n_in = 2 + len(kvs) + (0 if first else 2)
    part = jax.ShapeDtypeStruct((rows, 2 * HD), F32)
    elements = 2 * rows * rows * len(kvs)
    return pl.pallas_call(
        functools.partial(attend_kernel, tuple(distances), first, last),
        out_shape=jax.ShapeDtypeStruct((rows, 2 * HD), BF) if last else (part, part),
        in_specs=[vmem] * n_in,
        out_specs=vmem if last else (vmem, vmem),
        input_output_aliases={} if (first or last) else {n_in - 2: 0, n_in - 1: 1},
        compiler_params=pltpu.CompilerParams(vmem_limit_bytes=8 << 20),
        cost_estimate=pl.CostEstimate(
            flops=elements * 512, bytes_accessed=4 << 20, transcendentals=2 * elements
        ),
    )(low, queries, *kvs, *(() if first else state))


def output_kernel(pieces, index_ref, *rest):
    n = 2 * len(PLACES)
    x_refs, w_refs = rest[:n], rest[n:-6]
    out_ref, square_ref, x_ref, w_ref, x_sem, w_sem = rest[-6:]
    copies = start_loads(index_ref, x_refs, w_refs, pieces, x_ref, w_ref, x_sem, w_sem)
    for slot in range(ROUNDS):
        total = None
        place = index_ref[2 + slot]
        for part in range(2):
            copies[2 * slot + part].wait()
            parity = index_ref[0] if part == 0 else 1 - index_ref[0]
            product = lax.dot_general(
                w_ref[place, parity],
                x_ref[slot, part],
                (((1,), (1,)), ((), ())),
                preferred_element_type=F32,
            )
            total = product if total is None else total + product
        if slot == 0:
            out_ref[...] = total
        elif slot < ROUNDS - 1:
            out_ref[...] += total
        else:
            total = out_ref[...] + total
            out_ref[...] = total
            square_ref[...] = jnp.sum(total * total, axis=0, keepdims=True)


def output(chunks, weights, index):
    _, rows, width = chunks[0].shape
    features = weights[0].shape[0] // 2
    vmem = pl.BlockSpec(memory_space=pltpu.VMEM)
    outside = pl.BlockSpec(memory_space=pltpu.HBM)
    pieces = tuple(((k, 0, features), (k, features, features)) for k in range(ROUNDS))
    return pl.pallas_call(
        functools.partial(output_kernel, pieces),
        out_shape=(
            jax.ShapeDtypeStruct((features, rows), F32),
            jax.ShapeDtypeStruct((1, rows), F32),
        ),
        in_specs=[pl.BlockSpec(memory_space=pltpu.SMEM)]
        + [outside] * (len(chunks) + len(weights)),
        out_specs=(vmem, vmem),
        scratch_shapes=[
            pltpu.VMEM((ROUNDS, 2, rows, width), BF),
            pltpu.VMEM((ROUNDS, 2, features, width), BF),
            pltpu.SemaphoreType.DMA((2 * ROUNDS,)),
            pltpu.SemaphoreType.DMA((2 * ROUNDS,)),
        ],
        compiler_params=pltpu.CompilerParams(vmem_limit_bytes=60 << 20),
        cost_estimate=pl.CostEstimate(
            flops=2 * rows * features * 4096, bytes_accessed=8 << 20, transcendentals=0
        ),
    )(index, *chunks, *weights)


def shards(tokens, pre_gain, post_gain, w_query, w_key, w_value, w_out, segment_ids, page_table):
    rows = tokens.shape[0]
    features = tokens.shape[1]
    seq_index = lax.axis_index("seq")
    z = seq_index // 2
    h = lax.rem(seq_index, 2)
    base = seq_index * rows

    x_own = tokens.T.astype(F32)
    gained = (x_own * (1.0 + pre_gain.astype(F32))[:, None]).astype(BF)
    squares = jnp.sum(x_own * x_own, axis=0, keepdims=True)
    upper = lax.reduce_precision(squares, 8, 7)
    lower = squares - upper
    side = jnp.concatenate(
        [upper.astype(BF), lower.astype(BF), jnp.zeros((EXTRA - 2, rows), BF)], axis=0
    )
    x_block = jnp.concatenate([gained, side], axis=0)[None]
    depth = features + EXTRA

    counts = jnp.stack([jnp.sum((segment_ids < s).astype(jnp.int32)) for s in range(1, SEGS)])
    digits = jnp.concatenate([counts // 16, lax.rem(counts, 16)]).astype(BF)
    digits = jnp.pad(digits[None, :], ((2, EXTRA - 3), (0, 2 * HD - 2 * (SEGS - 1))))
    own = jnp.concatenate(
        [jnp.concatenate([w_key, w_value], axis=1), digits, w_query], axis=0
    )
    facing = move(own, ACROSS)
    x_facing = shift(x_block, SIDE)
    q_from = 2 * depth
    start = jnp.concatenate([own[:depth], facing[:depth], w_query], axis=0)

    x_pair = jnp.concatenate([x_block, x_facing], axis=0)
    ring = {0: start, 1: move(start, AHEAD), -1: move(start, BEHIND)}
    x_up, x_down = shift(x_pair, UP), shift(x_pair, DOWN)
    x_swaps = [shift(x_pair, SWAP)]
    cross_near = move(jnp.concatenate([ring[1][q_from:], ring[-1][q_from:]], axis=0), ACROSS)
    ring[2] = move(ring[1], AHEAD)
    ring[-2] = move(ring[-1], BEHIND)
    ring[2], ring[-2], x_up, x_down, x_swaps[0] = tie(ring[2], ring[-2], x_up, x_down, x_swaps[0])
    x_swaps += [shift(x_up, SWAP), shift(x_down, SWAP)]
    x_far = [shift(x_up[:1], UP), shift(x_down[1:], DOWN)]
    cross_next = move(jnp.concatenate([ring[2][q_from:], ring[-2][q_from:]], axis=0), ACROSS)
    ring[3] = move(ring[2], AHEAD)
    ring[-3] = move(ring[-2], BEHIND)
    turned, _ = tie(w_out.T, ring[2])
    turned = lax.ppermute(turned, ("seq", "mp"), TURN)
    ring[3], ring[-3], cross_near, x_far[0], x_far[1], x_swaps[1], x_swaps[2] = tie(
        ring[3], ring[-3], cross_near, x_far[0], x_far[1], x_swaps[1], x_swaps[2]
    )
    x_swaps += [shift(x_far[0], SWAP), shift(x_far[1], SWAP)]
    ring[4] = move(ring[3][:q_from], AHEAD)
    ring[-4] = move(ring[-3][q_from:], BEHIND)
    x_chunks = [x_pair, x_up, x_down, *x_far, *x_swaps]

    mp_index = lax.axis_index("mp")
    y = mp_index // 4
    over = lax.rem(mp_index // 2, 2)
    placed = [
        2 * lax.rem(y + dy + 4, 4) + jnp.where(dx == 0, over, 1 - over)
        for places in PLACES
        for dy, dx in places
    ]

    def index_of(steps):
        places = [lax.rem(z - step + ROUNDS, ROUNDS) for step in steps]
        return jnp.stack([lax.rem(mp_index, 2), h, *placed, *places]).astype(jnp.int32)

    steps = [0, 1, -1, 2, -2, 3, -3, 4]
    index = index_of(steps)
    kv_weights = [ring[step] for step in steps]
    kv_pieces = tuple(((k, 0, depth), (k, depth, depth)) for k in range(ROUNDS))

    n_marks = 2 * (SEGS - 1)
    marks = jnp.zeros((n_marks,), F32)
    for block in kv_weights:
        for part in range(2):
            marks = marks + block[part * depth + features + 2, :n_marks].astype(F32)
    starts = (marks[: SEGS - 1] * 16.0 + marks[SEGS - 1 :]).astype(jnp.int32)
    global_index = base + jnp.arange(rows, dtype=jnp.int32)
    offsets = jnp.zeros((rows,), jnp.int32)
    for s in range(1, SEGS):
        offsets = jnp.where(segment_ids == s, starts[s - 1], offsets)
    within = (global_index - offsets).astype(F32)
    low = (jnp.maximum(offsets, global_index - (WINDOW - 1)) - base)[:, None]
    half = HD // 2
    freqs = jnp.exp(-math.log(10000.0) * jnp.arange(half, dtype=F32) * (2.0 / HD))
    angles = freqs[:, None] * within[None, :]
    cos = jnp.cos(angles)
    sin = jnp.sin(angles)

    kv = project(x_chunks, kv_weights, kv_pieces, index, cos, sin, (True, False), 1.0)

    q_last = jnp.concatenate([ring[3][q_from:], ring[-3][q_from:], ring[-4]], axis=0)
    cross_last = move(q_last, ACROSS)
    q_weights = kv_weights[:7] + [ring[-4], facing, cross_near, cross_next, cross_last]
    crossings = [(8, depth)] + [
        (9 + k // 2, (k % 2) * features) for k in range(6)
    ] + [(11, 2 * features)]
    q_pieces = tuple(
        (
            (k, q_from if k < 7 else 0, features),
            (*crossings[k], features),
        )
        for k in range(ROUNDS)
    )

    out_pair = jnp.concatenate([turned, move(turned, ACROSS)], axis=0)
    out_blocks = {0: out_pair}

    straight, crossed, current, crossing = [kv], [None], kv, None
    state = None
    for step in range(4):
        following = move(current, LATER)
        chosen = jnp.where(h == 0, current, following)
        extra = [] if crossing is None else [crossing]
        if step == 1:
            extra += [out_pair, cross_last]
        if step == 2:
            out_blocks[-1] = move(out_pair, BEHIND)
            extra += [out_blocks[-1], *state]
        if step == 3:
            out_blocks[-2] = move(out_blocks[-1], BEHIND)
            extra += [out_blocks[-2], *state]
        following, chosen, *extra = tie(following, chosen, *extra)
        if crossing is not None:
            crossed[-1] = extra[0]
        if step == 1:
            out_pair, cross_last = extra[1:]
            out_blocks[0] = out_pair
            q_weights[-1] = cross_last
            queries = project(
                x_chunks,
                q_weights,
                q_pieces,
                index,
                cos,
                sin,
                (True, True),
                float(D // HQ) ** (-0.5),
            )
            state = attend(low, queries, [kv], [0], None)
        if step > 1:
            out_blocks[1 - step], *state = extra[1:]
            k = step - 1
            state = attend(low, queries, [straight[k], crossed[k]], [2 * k, 2 * k - 1], state)
        crossing = move(chosen, ACROSS)
        straight.append(following)
        crossed.append(crossing)
        current = following
    for k in range(3, 5):
        state = attend(low, queries, [straight[k], crossed[k]], [2 * k, 2 * k - 1], state)

    a_block = state[None]
    a_pair = jnp.concatenate([a_block, shift(a_block, SIDE)], axis=0)
    a_up, a_down = shift(a_pair, UP), shift(a_pair, DOWN)
    a_swaps = [shift(a_pair, SWAP)]
    out_blocks[1] = move(out_blocks[0], AHEAD)
    out_blocks[-3] = move(out_blocks[-2], BEHIND)
    a_up, a_down, out_blocks[1], out_blocks[-3] = tie(a_up, a_down, out_blocks[1], out_blocks[-3])
    a_swaps += [shift(a_up, SWAP), shift(a_down, SWAP)]
    a_far = [shift(a_up[:1], UP), shift(a_down[1:], DOWN)]
    out_blocks[2] = move(out_blocks[1], AHEAD)
    out_blocks[-4] = move(out_blocks[-3], BEHIND)
    out_blocks[3] = move(out_blocks[2], AHEAD)
    a_far[0], a_far[1], out_blocks[2], out_blocks[-4] = tie(
        a_far[0], a_far[1], out_blocks[2], out_blocks[-4]
    )
    a_swaps += [shift(a_far[0], SWAP), shift(a_far[1], SWAP)]

    q_steps = steps[:7] + [-4]
    share, partial = output(
        [a_pair, a_up, a_down, *a_far, *a_swaps],
        [out_blocks[step] for step in q_steps],
        index,
    )
    everywhere = jnp.broadcast_to(partial, (lax.axis_size("mp"), rows))
    square_total = jnp.sum(lax.all_to_all(everywhere, "mp", 0, 0, tiled=True), axis=0)
    post_scale = lax.rsqrt(square_total / D + EPSILON)
    post = share * post_scale[None, :] * (1.0 + post_gain.astype(F32))[:, None]
    layer_output = (tokens.T.astype(F32) + post).astype(BF).T

    pages = page_table.shape[0]
    local_slot = page_table - seq_index * pages
    kv_pages = kv.reshape(pages, PAGE, 2 * HD)
    caches = []
    for slot in range(pages):
        chosen = kv_pages[0]
        for page in range(1, pages):
            chosen = jnp.where(local_slot[page] == slot, kv_pages[page], chosen)
        caches.append(chosen)
    caches = jnp.stack(caches)
    return (layer_output, caches[:, :, :HD], caches[:, :, HD:])


def solution(mesh):
    return jax.shard_map(
        shards,
        mesh=mesh,
        in_specs=(
            P("seq", "mp"),
            P("mp"),
            P("mp"),
            P("seq", "mp"),
            P("seq", "mp"),
            P("seq", "mp"),
            P("mp", "seq"),
            P("seq"),
            P("seq"),
        ),
        out_specs=(P("seq", "mp"), P("seq", None, "mp"), P("seq", None, "mp")),
        check_vma=False,
    )
```

time: 508 us -> 264 us (0.52)
  waiting for transfers between devices: 263 us -> 65.6 us
  blocking collectives: 99.7 us -> 0 us
  starting transfers between devices: 59.6 us -> 120 us
  Pallas kernels: 0 us -> 36.7 us
  matrix products: 32.7 us -> 0 us
  other arithmetic: 23.6 us -> 11 us
  between operations: 15.6 us -> 9.73 us
    all_gather x5 -> x0, waiting for transfers between devices: 191 us -> none  [the longest x1 71.9 us: shards(): lax.all_gather(w_value, 'seq', axis=0, tiled=True)]
    reduce_scatter x1 -> x0, waiting for transfers between devices: 68.9 us -> none  [shards(): lax.psum_scatter(group_terms.astype(jnp.bfloat16), 'mp', scatter_dimensio...]
    ppermute x16 -> x49, waiting for transfers between devices: 0.76 us -> 60.6 us  [the longest x28 38.8 us: move(): return lax.ppermute(block, 'seq', perm)]
    ppermute x16 -> x49, starting transfers between devices: 59.4 us -> 115 us  [the longest x28 65.4 us: move(): return lax.ppermute(block, 'seq', perm)]
    unnamed x1 -> x0, blocking collectives: 53.2 us -> none
    pallas_call x0 -> x8, Pallas kernels: none -> 36.7 us  [the longest x2 16.6 us: project(): pl.pallas_call(functools.partial(project_kernel, pieces, rotated, factor)...]
    dot_general x7 -> x0, matrix products: 32.7 us -> none  [the longest x3 14.1 us: add_product(): return jnp.dot(normed, piece, preferred_element_type=jnp.float32)]
    psum x1 -> x0, blocking collectives: 29.2 us -> none  [shards(): square_total = lax.psum(squares, 'mp')]
  transfers between devices with their start and end apart: 22 -> 50, of which waited for: 6 -> 19; matrix products, arithmetic and copies ran while one was open for 12% -> 4% of each run, Pallas kernels for 0% -> 7%
where the time goes in v1:
time: 264 us; the launch traced here: 259 us
  starting transfers between devices  120 us (45%)
  waiting for transfers between devices  65.6 us (25%)
  Pallas kernels  36.7 us (14%)
  local copies, waits for them, and re-layouts  16.2 us (6%)
  other arithmetic  11 us (4%)
  between operations  9.73 us (4%)
    ppermute x28, starting transfers between devices, move(): return lax.ppermute(block, 'seq', perm)  65.4 us
    ppermute x20, starting transfers between devices, shift(): return lax.ppermute(block, 'mp', perm)  40.7 us
    ppermute x28, waiting for transfers between devices, move(): return lax.ppermute(block, 'seq', perm)  38.8 us
    pallas_call x2, Pallas kernels, project(): pl.pallas_call(functools.partial(project_kernel, pieces, rotated, factor)...  16.6 us
    pallas_call x5, Pallas kernels, attend(): pl.pallas_call(functools.partial(attend_kernel, tuple(distances), first,...  13.4 us
    ppermute x20, waiting for transfers between devices, shift(): return lax.ppermute(block, 'mp', perm)  12.8 us
    unnamed x109, local copies, waits for them, and re-layouts  9.79 us
    ppermute x1, waiting for transfers between devices, shards(): turned = lax.ppermute(turned, ('seq', 'mp'), TURN)  8.97 us
  transfers between devices with their start and end apart: 50, of which 19 were waited for; matrix products, arithmetic and copies ran while one was open for 4% of the time, Pallas kernels for 7%

profile of v1, /device:TPU:1, one launch (start us, length us, event | category | flops | bytes accessed | tf_op | source)
XLA Modules:
  0.0 259.3 jit_solution(14433299447619476935)
XLA Ops:
  5.2 3.7 %collective-permute-start = (bf16[592,256]{1,0:T(8,128)(2,1)S(1)}, bf16[592,256]{1,0:T(8,128)(2,1)S(1)}, u32[]{:S(2)}, u32[]{:S(2)}) collective-permute-start(bf16[592,256]{1,0:T(8,128)(2,1)S(1)} %pad_maximum_fusion.4), channel_id=1, source_target_pairs={{0,16},{16,0},{32,48},{48,32},{64,80},{80,64},{96,112},{112,96},{1... | collective-permute-start | bytes 909320 | tf_op jit(solution)/shard_map/ppermute | solution.py:43
  9.6 5.1 %collective-permute-done.rest_18_ = bf16[592,256]{1,0:T(8,128)(2,1)S(1)} collective-permute-done((bf16[592,256]{1,0:T(8,128)(2,1)S(1)}, bf16[592,256]{1,0:T(8,128)(2,1)S(1)}, u32[]{:S(2)}, u32[]{:S(2)}) %collective-permute-start) | collective-permute-done | bytes 303136 | tf_op jit(solution)/shard_map/ppermute | solution.py:43
  18.1 4.0 %collective-permute-start.2 = (bf16[896,256]{1,0:T(8,128)(2,1)S(1)}, bf16[896,256]{1,0:T(8,128)(2,1)S(1)}, u32[]{:S(2)}, u32[]{:S(2)}) collective-permute-start(bf16[896,256]{1,0:T(8,128)(2,1)S(1)} %pad_maximum_fusion.2.rest_10_), channel_id=1, source_target_pairs={{32,0},{48,16},{64,32},{80,48},{96,64},{112,80},{128,96},{144,112}... | collective-permute-start | bytes 1376264 | tf_op jit(solution)/shard_map/ppermute | solution.py:43
  33.1 3.6 %collective-permute-done.6.rest_1_ = bf16[2,304,512]{2,1,0:T(8,128)(2,1)S(1)} collective-permute-done((bf16[2,304,512]{2,1,0:T(8,128)(2,1)S(1)}, bf16[2,304,512]{2,1,0:T(8,128)(2,1)S(1)}, u32[]{:S(2)}, u32[]{:S(2)}) %collective-permute-start.6) | collective-permute-done | bytes 622624 | tf_op jit(solution)/shard_map/ppermute | solution.py:47
  41.5 4.5 %collective-permute-start.14 = (bf16[2,304,512]{2,1,0:T(8,128)(2,1)S(1)}, bf16[2,304,512]{2,1,0:T(8,128)(2,1)S(1)}, u32[]{:S(2)}, u32[]{:S(2)}) collective-permute-start(bf16[2,304,512]{2,1,0:T(8,128)(2,1)S(1)} %collective-permute-done.6.rest_1_), channel_id=1, source_target_pairs={{0,1},{1,0},{2,3},{3,2},{4,5},{5,4},{6,7},{7,6},{8,9},{9,8},{10,11... | collective-permute-start | bytes 1867784 | tf_op jit(solution)/shard_map/ppermute | solution.py:47
  46.8 5.0 %collective-permute-start.10 = (bf16[896,256]{1,0:T(8,128)(2,1)S(1)}, bf16[896,256]{1,0:T(8,128)(2,1)S(1)}, u32[]{:S(2)}, u32[]{:S(2)}) collective-permute-start(bf16[896,256]{1,0:T(8,128)(2,1)S(1)} %collective-permute-done.4.rest_14_), channel_id=1, source_target_pairs={{32,0},{48,16},{64,32},{80,48},{96,64},{112,80},{128,96},{144,112}... | collective-permute-start | bytes 1376264 | tf_op jit(solution)/shard_map/ppermute | solution.py:43
  53.2 4.7 %collective-permute-done.13.rest_4_ = bf16[1,304,512]{2,1,0:T(8,128)(2,1)S(1)} collective-permute-done((bf16[1,304,512]{2,1,0:T(8,128)(2,1)S(1)}, bf16[1,304,512]{2,1,0:T(8,128)(2,1)S(1)}, u32[]{:S(2)}, u32[]{:S(2)}) %collective-permute-start.13) | collective-permute-done | bytes 311328 | tf_op jit(solution)/shard_map/ppermute | solution.py:47
  73.5 8.2 %shard_map.112.rest_0_ = bf16[512,256]{1,0:T(8,128)(2,1)} custom-call(s32[18]{0:T(128)} %stack.102.index_ref, f32[64,512]{1,0:T(8,128)} %get-tuple-element.118.cos_ref, f32[64,512]{1,0:T(8,128)} %get-tuple-element.117.sin_ref, bf16[2,304,512]{2,1,0:T(8,128)(2,1)} %copy-done.3, bf16[2,304,512]{2,1,0:T(8,128)(2,1)} %copy-done.6, ...), custom_call_target="tpu_custom_call" | custom-call | flops 1207959552 | bytes 8388608 | tf_op jit(solution)/shard_map/pallas_call | solution.py:132
  85.0 8.8 %collective-permute-start.24 = (bf16[288,256]{1,0:T(8,128)(2,1)S(1)}, bf16[288,256]{1,0:T(8,128)(2,1)S(1)}, u32[]{:S(2)}, u32[]{:S(2)}) collective-permute-start(bf16[288,256]{1,0:T(8,128)(2,1)S(1)} %bitcast.171), channel_id=1, source_target_pairs={{0,0},{1,16},{2,32},{3,48},{4,64},{5,80},{6,96},{7,112},{8,128},{9... | collective-permute-start | bytes 442376 | tf_op jit(solution)/shard_map/ppermute | solution.py:321
  95.7 9.0 %collective-permute-done.24 = bf16[288,256]{1,0:T(8,128)(2,1)S(1)} collective-permute-done((bf16[288,256]{1,0:T(8,128)(2,1)S(1)}, bf16[288,256]{1,0:T(8,128)(2,1)S(1)}, u32[]{:S(2)}, u32[]{:S(2)}) %collective-permute-start.24) | collective-permute-done | bytes 147488 | tf_op jit(solution)/shard_map/ppermute | solution.py:321
  105.6 5.1 %collective-permute-start.19 = (bf16[288,256]{1,0:T(8,128)(2,1)S(1)}, bf16[288,256]{1,0:T(8,128)(2,1)S(1)}, u32[]{:S(2)}, u32[]{:S(2)}) collective-permute-start(bf16[288,256]{1,0:T(8,128)(2,1)S(1)} %slice.181), channel_id=1, source_target_pairs={{32,0},{48,16},{64,32},{80,48},{96,64},{112,80},{128,96},{144,112}... | collective-permute-start | bytes 442376 | tf_op jit(solution)/shard_map/ppermute | solution.py:43
  123.4 11.9 %collective-permute-done.23.rest_1_ = bf16[512,256]{1,0:T(8,128)(2,1)S(1)} collective-permute-done((bf16[512,256]{1,0:T(8,128)(2,1)S(1)}, bf16[512,256]{1,0:T(8,128)(2,1)S(1)}, u32[]{:S(2)}, u32[]{:S(2)}) %collective-permute-start.23) | collective-permute-done | bytes 262176 | tf_op jit(solution)/shard_map/ppermute | solution.py:43
  139.4 3.7 %collective-permute-start.28 = (bf16[512,256]{1,0:T(8,128)(2,1)}, bf16[512,256]{1,0:T(8,128)(2,1)S(1)}, u32[]{:S(2)}, u32[]{:S(2)}) collective-permute-start(bf16[512,256]{1,0:T(8,128)(2,1)} %broadcast_select_fusion.2), channel_id=1, source_target_pairs={{0,16},{16,0},{32,48},{48,32},{64,80},{80,64},{96,112},{112,96},{1... | collective-permute-start | bytes 786440 | tf_op jit(solution)/shard_map/ppermute | solution.py:43
  143.8 8.4 %shard_map.113.q_ref = bf16[512,256]{1,0:T(8,128)(2,1)} custom-call(s32[18]{0:T(128)} %stack.102.index_ref, f32[64,512]{1,0:T(8,128)} %get-tuple-element.118.cos_ref, f32[64,512]{1,0:T(8,128)} %get-tuple-element.117.sin_ref, bf16[2,304,512]{2,1,0:T(8,128)(2,1)} %copy-done.3, bf16[2,304,512]{2,1,0:T(8,128)(2,1)} %copy-done.6, bf16[2,304,512]{2,1,0:T(8,128)(2,1)} %copy-done.7, ...), custom_call_target="tpu_custom_call" | custom-call | flops 1207959552 | bytes 8388608 | tf_op jit(solution)/shard_map/pallas_call | solution.py:132
  156.5 10.9 %collective-permute-start.32 = (bf16[576,256]{1,0:T(8,128)(2,1)S(1)}, bf16[576,256]{1,0:T(8,128)(2,1)S(1)}, u32[]{:S(2)}, u32[]{:S(2)}) collective-permute-start(bf16[576,256]{1,0:T(8,128)(2,1)S(1)} %collective-permute-done.29.rest_12_), channel_id=1, source_target_pairs={{32,0},{48,16},{64,32},{80,48},{96,64},{112,80},{128,96},{144,112}... | collective-permute-start | bytes 884744 | tf_op jit(solution)/shard_map/ppermute | solution.py:43
  170.4 3.8 %collective-permute-done.31.rest_1_ = bf16[512,256]{1,0:T(8,128)(2,1)S(1)} collective-permute-done((bf16[512,256]{1,0:T(8,128)(2,1)S(1)}, bf16[512,256]{1,0:T(8,128)(2,1)S(1)}, u32[]{:S(2)}, u32[]{:S(2)}) %collective-permute-start.31) | collective-permute-done | bytes 262176 | tf_op jit(solution)/shard_map/ppermute | solution.py:43
  185.5 6.1 %collective-permute-start.34 = (bf16[1,512,256]{2,1,0:T(8,128)(2,1)S(1)}, bf16[1,512,256]{2,1,0:T(8,128)(2,1)S(1)}, u32[]{:S(2)}, u32[]{:S(2)}) collective-permute-start(bf16[1,512,256]{2,1,0:T(8,128)(2,1)S(1)} %bitcast.165), channel_id=1, source_target_pairs={{0,2},{1,3},{2,0},{3,1},{4,6},{5,7},{6,4},{7,5},{8,10},{9,11},{10,... | collective-permute-start | bytes 786440 | tf_op jit(solution)/shard_map/ppermute | solution.py:47
  191.6 3.8 %collective-permute-done.34 = bf16[1,512,256]{2,1,0:T(8,128)(2,1)S(1)} collective-permute-done((bf16[1,512,256]{2,1,0:T(8,128)(2,1)S(1)}, bf16[1,512,256]{2,1,0:T(8,128)(2,1)S(1)}, u32[]{:S(2)}, u32[]{:S(2)}) %collective-permute-start.34) | collective-permute-done | bytes 262176 | tf_op jit(solution)/shard_map/ppermute | solution.py:47
  200.9 5.2 %collective-permute-start.43 = (bf16[2,512,256]{2,1,0:T(8,128)(2,1)S(1)}, bf16[2,512,256]{2,1,0:T(8,128)(2,1)S(1)}, u32[]{:S(2)}, u32[]{:S(2)}) collective-permute-start(bf16[2,512,256]{2,1,0:T(8,128)(2,1)S(1)} %pad_maximum_fusion.1.rest_0_), channel_id=1, source_target_pairs={{0,1},{1,0},{2,3},{3,2},{4,5},{5,4},{6,7},{7,6},{8,9},{9,8},{10,11... | collective-permute-start | bytes 1572872 | tf_op jit(solution)/shard_map/ppermute | solution.py:47
  220.5 6.5 %collective-permute-start.44 = (bf16[2,512,256]{2,1,0:T(8,128)(2,1)S(1)}, bf16[2,512,256]{2,1,0:T(8,128)(2,1)S(1)}, u32[]{:S(2)}, u32[]{:S(2)}) collective-permute-start(bf16[2,512,256]{2,1,0:T(8,128)(2,1)S(1)} %collective-permute-done.35.rest_1_), channel_id=1, source_target_pairs={{0,1},{1,0},{2,3},{3,2},{4,5},{5,4},{6,7},{7,6},{8,9},{9,8},{10,11... | collective-permute-start | bytes 1572872 | tf_op jit(solution)/shard_map/ppermute | solution.py:47
  231.1 6.2 %collective-permute-done.48.rest_15_ = bf16[576,256]{1,0:T(8,128)(2,1)S(1)} collective-permute-done((bf16[576,256]{1,0:T(8,128)(2,1)S(1)}, bf16[576,256]{1,0:T(8,128)(2,1)S(1)}, u32[]{:S(2)}, u32[]{:S(2)}) %collective-permute-start.48) | collective-permute-done | bytes 294944 | tf_op jit(solution)/shard_map/ppermute | solution.py:43
  238.1 6.7 %shard_map.119 = (f32[288,512]{1,0:T(8,128)}, f32[1,512]{1,0:T(1,128)}) custom-call(s32[18]{0:T(128)} %stack.102.index_ref, bf16[2,512,256]{2,1,0:T(8,128)(2,1)} %copy-done.16, bf16[2,512,256]{2,1,0:T(8,128)(2,1)} %copy-done.24, bf16[2,512,256]{2,1,0:T(8,128)(2,1)} %copy-done.25, bf16[1,512,256]{2,1,0:T(8,128)(2,1)} %copy-done.43, ...), custom_call_target="tpu_custom_call" | custom-call | flops 1207959552 | bytes 8388608 | tf_op jit(solution)/shard_map/pallas_call | solution.py:255
  246.1 5.2 %all-to-all-start = ((f32[16,1,512]{2,1,0:T(1,128)}), f32[16,1,512]{2,1,0:T(1,128)S(1)}, u32[]{:S(2)}, u32[]{:S(2)}) async-start(f32[16,1,512]{2,1,0:T(1,128)} %broadcast_in_dim.45), calls=%async_computation | async-start | bytes 65536 | tf_op jit(solution)/shard_map/all_to_all | solution.py:452
  252.1 5.0 %all-to-all-done = f32[16,1,512]{2,1,0:T(1,128)S(1)} async-done(((f32[16,1,512]{2,1,0:T(1,128)}), f32[16,1,512]{2,1,0:T(1,128)S(1)}, u32[]{:S(2)}, u32[]{:S(2)}) %all-to-all-start) | async-done | bytes 32800 | tf_op jit(solution)/shard_map/all_to_all | solution.py:452
  (248 shorter events, 104.4 us)
Async XLA Ops:
  9.2 13.2 %collective-permute-start.5 = (bf16[1,304,512]{2,1,0:T(8,128)(2,1)S(1)}, bf16[1,304,512]{2,1,0:T(8,128)(2,1)S(1)}, u32[]{:S(2)}, u32[]{:S(2)}) collective-permute-start(bf16[1,304,512]{2,1,0:T(8,128)(2,1)S(1)} %maximum_bitcast_fusion), channel_id=1, source_target_pairs={{0,2},{1,3},{2,0},{3,1},{4,6},{5,7},{6,4},{7,5},{8,10},{9,11},{10,... | collective-permute-start | bytes 933896 | tf_op jit(solution)/shard_map/ppermute | solution.py:47
  15.5 14.8 %collective-permute-start.1 = (bf16[896,256]{1,0:T(8,128)(2,1)S(1)}, bf16[896,256]{1,0:T(8,128)(2,1)S(1)}, u32[]{:S(2)}, u32[]{:S(2)}) collective-permute-start(bf16[896,256]{1,0:T(8,128)(2,1)S(1)} %pad_maximum_fusion.2.rest_10_), channel_id=1, source_target_pairs={{0,32},{16,48},{32,64},{48,80},{64,96},{80,112},{96,128},{112,144}... | collective-permute-start | bytes 1376264 | tf_op jit(solution)/shard_map/ppermute | solution.py:43
  18.1 12.1 %collective-permute-start.2 = (bf16[896,256]{1,0:T(8,128)(2,1)S(1)}, bf16[896,256]{1,0:T(8,128)(2,1)S(1)}, u32[]{:S(2)}, u32[]{:S(2)}) collective-permute-start(bf16[896,256]{1,0:T(8,128)(2,1)S(1)} %pad_maximum_fusion.2.rest_10_), channel_id=1, source_target_pairs={{32,0},{48,16},{64,32},{80,48},{96,64},{112,80},{128,96},{144,112}... | collective-permute-start | bytes 1376264 | tf_op jit(solution)/shard_map/ppermute | solution.py:43
  22.5 14.2 %collective-permute-start.6 = (bf16[2,304,512]{2,1,0:T(8,128)(2,1)S(1)}, bf16[2,304,512]{2,1,0:T(8,128)(2,1)S(1)}, u32[]{:S(2)}, u32[]{:S(2)}) collective-permute-start(bf16[2,304,512]{2,1,0:T(8,128)(2,1)S(1)} %pad_maximum_fusion.rest_0_), channel_id=1, source_target_pairs={{0,4},{1,5},{2,6},{3,7},{4,8},{5,9},{6,10},{7,11},{8,12},{9,13},{1... | collective-permute-start | bytes 1867784 | tf_op jit(solution)/shard_map/ppermute | solution.py:47
  23.9 15.1 %collective-permute-start.7 = (bf16[2,304,512]{2,1,0:T(8,128)(2,1)S(1)}, bf16[2,304,512]{2,1,0:T(8,128)(2,1)S(1)}, u32[]{:S(2)}, u32[]{:S(2)}) collective-permute-start(bf16[2,304,512]{2,1,0:T(8,128)(2,1)S(1)} %pad_maximum_fusion.rest_0_), channel_id=1, source_target_pairs={{4,0},{5,1},{6,2},{7,3},{8,4},{9,5},{10,6},{11,7},{12,8},{13,9},{1... | collective-permute-start | bytes 1867784 | tf_op jit(solution)/shard_map/ppermute | solution.py:47
  25.4 13.6 %collective-permute-start.8 = (bf16[2,304,512]{2,1,0:T(8,128)(2,1)S(1)}, bf16[2,304,512]{2,1,0:T(8,128)(2,1)S(1)}, u32[]{:S(2)}, u32[]{:S(2)}) collective-permute-start(bf16[2,304,512]{2,1,0:T(8,128)(2,1)S(1)} %pad_maximum_fusion.rest_0_), channel_id=1, source_target_pairs={{0,1},{1,0},{2,3},{3,2},{4,5},{5,4},{6,7},{7,6},{8,9},{9,8},{10,11... | collective-permute-start | bytes 1867784 | tf_op jit(solution)/shard_map/ppermute | solution.py:47
  41.5 17.3 %collective-permute-start.14 = (bf16[2,304,512]{2,1,0:T(8,128)(2,1)S(1)}, bf16[2,304,512]{2,1,0:T(8,128)(2,1)S(1)}, u32[]{:S(2)}, u32[]{:S(2)}) collective-permute-start(bf16[2,304,512]{2,1,0:T(8,128)(2,1)S(1)} %collective-permute-done.6.rest_1_), channel_id=1, source_target_pairs={{0,1},{1,0},{2,3},{3,2},{4,5},{5,4},{6,7},{7,6},{8,9},{9,8},{10,11... | collective-permute-start | bytes 1867784 | tf_op jit(solution)/shard_map/ppermute | solution.py:47
  46.1 12.8 %collective-permute-start.15 = (bf16[2,304,512]{2,1,0:T(8,128)(2,1)S(1)}, bf16[2,304,512]{2,1,0:T(8,128)(2,1)S(1)}, u32[]{:S(2)}, u32[]{:S(2)}) collective-permute-start(bf16[2,304,512]{2,1,0:T(8,128)(2,1)S(1)} %collective-permute-done.7.rest_2_), channel_id=1, source_target_pairs={{0,1},{1,0},{2,3},{3,2},{4,5},{5,4},{6,7},{7,6},{8,9},{9,8},{10,11... | collective-permute-start | bytes 1867784 | tf_op jit(solution)/shard_map/ppermute | solution.py:47
  46.1 12.8 %collective-permute-start.9 = (bf16[896,256]{1,0:T(8,128)(2,1)S(1)}, bf16[896,256]{1,0:T(8,128)(2,1)S(1)}, u32[]{:S(2)}, u32[]{:S(2)}) collective-permute-start(bf16[896,256]{1,0:T(8,128)(2,1)S(1)} %collective-permute-done.3.rest_13_), channel_id=1, source_target_pairs={{0,32},{16,48},{32,64},{48,80},{64,96},{80,112},{96,128},{112,144}... | collective-permute-start | bytes 1376264 | tf_op jit(solution)/shard_map/ppermute | solution.py:43
  81.7 29.0 %collective-permute-start.21 = (bf16[512,256]{1,0:T(8,128)(2,1)}, bf16[512,256]{1,0:T(8,128)(2,1)S(1)}, u32[]{:S(2)}, u32[]{:S(2)}) collective-permute-start(bf16[512,256]{1,0:T(8,128)(2,1)} %shard_map.112.rest_0_), channel_id=1, source_target_pairs={{0,32},{16,48},{32,64},{48,80},{64,96},{80,112},{96,128},{112,144}... | collective-permute-start | bytes 786440 | tf_op jit(solution)/shard_map/ppermute | solution.py:43
  85.0 19.6 %collective-permute-start.24 = (bf16[288,256]{1,0:T(8,128)(2,1)S(1)}, bf16[288,256]{1,0:T(8,128)(2,1)S(1)}, u32[]{:S(2)}, u32[]{:S(2)}) collective-permute-start(bf16[288,256]{1,0:T(8,128)(2,1)S(1)} %bitcast.171), channel_id=1, source_target_pairs={{0,0},{1,16},{2,32},{3,48},{4,64},{5,80},{6,96},{7,112},{8,128},{9... | collective-permute-start | bytes 442376 | tf_op jit(solution)/shard_map/ppermute | solution.py:321
  104.6 15.1 %collective-permute-start.25 = (bf16[288,256]{1,0:T(8,128)(2,1)S(1)}, bf16[288,256]{1,0:T(8,128)(2,1)S(1)}, u32[]{:S(2)}, u32[]{:S(2)}) collective-permute-start(bf16[288,256]{1,0:T(8,128)(2,1)S(1)} %collective-permute-done.24), channel_id=1, source_target_pairs={{0,16},{16,0},{32,48},{48,32},{64,80},{80,64},{96,112},{112,96},{1... | collective-permute-start | bytes 442376 | tf_op jit(solution)/shard_map/ppermute | solution.py:43
  116.7 26.4 %collective-permute-start.20 = (bf16[576,256]{1,0:T(8,128)(2,1)S(1)}, bf16[576,256]{1,0:T(8,128)(2,1)S(1)}, u32[]{:S(2)}, u32[]{:S(2)}) collective-permute-start(bf16[576,256]{1,0:T(8,128)(2,1)S(1)} %pad_maximum_fusion.6), channel_id=1, source_target_pairs={{0,16},{16,0},{32,48},{48,32},{64,80},{80,64},{96,112},{112,96},{1... | collective-permute-start | bytes 884744 | tf_op jit(solution)/shard_map/ppermute | solution.py:43
  116.8 18.5 %collective-permute-start.23 = (bf16[512,256]{1,0:T(8,128)(2,1)S(1)}, bf16[512,256]{1,0:T(8,128)(2,1)S(1)}, u32[]{:S(2)}, u32[]{:S(2)}) collective-permute-start(bf16[512,256]{1,0:T(8,128)(2,1)S(1)} %broadcast_select_fusion.3), channel_id=1, source_target_pairs={{0,16},{16,0},{32,48},{48,32},{64,80},{80,64},{96,112},{112,96},{1... | collective-permute-start | bytes 786440 | tf_op jit(solution)/shard_map/ppermute | solution.py:43
  135.3 19.8 %collective-permute-start.27 = (bf16[512,256]{1,0:T(8,128)(2,1)S(1)}, bf16[512,256]{1,0:T(8,128)(2,1)S(1)}, u32[]{:S(2)}, u32[]{:S(2)}) collective-permute-start(bf16[512,256]{1,0:T(8,128)(2,1)S(1)} %collective-permute-done.22.rest_0_), channel_id=1, source_target_pairs={{0,32},{16,48},{32,64},{48,80},{64,96},{80,112},{96,128},{112,144}... | collective-permute-start | bytes 786440 | tf_op jit(solution)/shard_map/ppermute | solution.py:43
  138.8 16.4 %collective-permute-start.29 = (bf16[576,256]{1,0:T(8,128)(2,1)S(1)}, bf16[576,256]{1,0:T(8,128)(2,1)S(1)}, u32[]{:S(2)}, u32[]{:S(2)}) collective-permute-start(bf16[576,256]{1,0:T(8,128)(2,1)S(1)} %pad_maximum_fusion.7.rest_10_), channel_id=1, source_target_pairs={{32,0},{48,16},{64,32},{80,48},{96,64},{112,80},{128,96},{144,112}... | collective-permute-start | bytes 884744 | tf_op jit(solution)/shard_map/ppermute | solution.py:43
  139.4 15.7 %collective-permute-start.28 = (bf16[512,256]{1,0:T(8,128)(2,1)}, bf16[512,256]{1,0:T(8,128)(2,1)S(1)}, u32[]{:S(2)}, u32[]{:S(2)}) collective-permute-start(bf16[512,256]{1,0:T(8,128)(2,1)} %broadcast_select_fusion.2), channel_id=1, source_target_pairs={{0,16},{16,0},{32,48},{48,32},{64,80},{80,64},{96,112},{112,96},{1... | collective-permute-start | bytes 786440 | tf_op jit(solution)/shard_map/ppermute | solution.py:43
  155.2 15.2 %collective-permute-start.30 = (bf16[512,256]{1,0:T(8,128)(2,1)S(1)}, bf16[512,256]{1,0:T(8,128)(2,1)S(1)}, u32[]{:S(2)}, u32[]{:S(2)}) collective-permute-start(bf16[512,256]{1,0:T(8,128)(2,1)S(1)} %collective-permute-done.27.rest_0_), channel_id=1, source_target_pairs={{0,32},{16,48},{32,64},{48,80},{64,96},{80,112},{96,128},{112,144}... | collective-permute-start | bytes 786440 | tf_op jit(solution)/shard_map/ppermute | solution.py:43
  156.5 17.7 %collective-permute-start.32 = (bf16[576,256]{1,0:T(8,128)(2,1)S(1)}, bf16[576,256]{1,0:T(8,128)(2,1)S(1)}, u32[]{:S(2)}, u32[]{:S(2)}) collective-permute-start(bf16[576,256]{1,0:T(8,128)(2,1)S(1)} %collective-permute-done.29.rest_12_), channel_id=1, source_target_pairs={{32,0},{48,16},{64,32},{80,48},{96,64},{112,80},{128,96},{144,112}... | collective-permute-start | bytes 884744 | tf_op jit(solution)/shard_map/ppermute | solution.py:43
  200.9 27.0 %collective-permute-start.43 = (bf16[2,512,256]{2,1,0:T(8,128)(2,1)S(1)}, bf16[2,512,256]{2,1,0:T(8,128)(2,1)S(1)}, u32[]{:S(2)}, u32[]{:S(2)}) collective-permute-start(bf16[2,512,256]{2,1,0:T(8,128)(2,1)S(1)} %pad_maximum_fusion.1.rest_0_), channel_id=1, source_target_pairs={{0,1},{1,0},{2,3},{3,2},{4,5},{5,4},{6,7},{7,6},{8,9},{9,8},{10,11... | collective-permute-start | bytes 1572872 | tf_op jit(solution)/shard_map/ppermute | solution.py:47
  206.3 14.2 %collective-permute-start.39 = (bf16[1,512,256]{2,1,0:T(8,128)(2,1)S(1)}, bf16[1,512,256]{2,1,0:T(8,128)(2,1)S(1)}, u32[]{:S(2)}, u32[]{:S(2)}) collective-permute-start(bf16[1,512,256]{2,1,0:T(8,128)(2,1)S(1)} %slice.185), channel_id=1, source_target_pairs={{0,4},{1,5},{2,6},{3,7},{4,8},{5,9},{6,10},{7,11},{8,12},{9,13},{1... | collective-permute-start | bytes 786440 | tf_op jit(solution)/shard_map/ppermute | solution.py:47
  206.4 20.6 %collective-permute-start.40 = (bf16[1,512,256]{2,1,0:T(8,128)(2,1)S(1)}, bf16[1,512,256]{2,1,0:T(8,128)(2,1)S(1)}, u32[]{:S(2)}, u32[]{:S(2)}) collective-permute-start(bf16[1,512,256]{2,1,0:T(8,128)(2,1)S(1)} %slice.186), channel_id=1, source_target_pairs={{4,0},{5,1},{6,2},{7,3},{8,4},{9,5},{10,6},{11,7},{12,8},{13,9},{1... | collective-permute-start | bytes 786440 | tf_op jit(solution)/shard_map/ppermute | solution.py:47
  209.1 18.2 %collective-permute-start.41 = (bf16[576,256]{1,0:T(8,128)(2,1)S(1)}, bf16[576,256]{1,0:T(8,128)(2,1)S(1)}, u32[]{:S(2)}, u32[]{:S(2)}) collective-permute-start(bf16[576,256]{1,0:T(8,128)(2,1)S(1)} %collective-permute-done.37.rest_11_), channel_id=1, source_target_pairs={{0,32},{16,48},{32,64},{48,80},{64,96},{80,112},{96,128},{112,144}... | collective-permute-start | bytes 884744 | tf_op jit(solution)/shard_map/ppermute | solution.py:43
  209.3 18.0 %collective-permute-start.42 = (bf16[576,256]{1,0:T(8,128)(2,1)}, bf16[576,256]{1,0:T(8,128)(2,1)S(1)}, u32[]{:S(2)}, u32[]{:S(2)}) collective-permute-start(bf16[576,256]{1,0:T(8,128)(2,1)} %collective-permute-done.38.rest_16_), channel_id=1, source_target_pairs={{32,0},{48,16},{64,32},{80,48},{96,64},{112,80},{128,96},{144,112}... | collective-permute-start | bytes 884744 | tf_op jit(solution)/shard_map/ppermute | solution.py:43
  (81 other events, 783.3 us)

commit v2 on v1

v2 whole, which is shorter than its diff:
```python
import functools
import math

import jax
import jax.numpy as jnp
from jax import lax
from jax.experimental import pallas as pl
from jax.experimental.pallas import tpu as pltpu
from jax.sharding import PartitionSpec as P

D = 4608
HQ = 32
HD = 128
WINDOW = 4096
PAGE = 128
SEGS = 4

EPSILON = 1e-06
SOFT_CAP = 50.0
LOG2E = 1.4426950408889634
EXTRA = 16
SEQ = 16
ROUNDS = 8

BF = jnp.bfloat16
F32 = jnp.float32

AHEAD = [(i, (i + 2) % SEQ) for i in range(SEQ)]
BEHIND = [((i + 2) % SEQ, i) for i in range(SEQ)]
LATER = [(i, i + 2) for i in range(SEQ - 2)]
ACROSS = [(i, i ^ 1) for i in range(SEQ)]
TURN = [(s * SEQ + m, m * SEQ + s) for s in range(SEQ) for m in range(SEQ)]


SIDE = [(i, i ^ 2) for i in range(SEQ)]
UP = [(i, (i + 4) % SEQ) for i in range(SEQ)]
DOWN = [((i + 4) % SEQ, i) for i in range(SEQ)]
SWAP = [(i, i ^ 1) for i in range(SEQ)]
COLUMNS = [[2 * i + c for i in range(ROUNDS)] for c in range(2)]
PLACES = (((0, 0), (0, 1)), ((-1, 0), (-1, 1)), ((1, 0), (1, 1)), ((2, 0),), ((2, 1),))


def move(block, perm):
    return lax.ppermute(block, "seq", perm)


def shift(block, perm):
    return lax.ppermute(block, "mp", perm)


def tie(*values):
    return lax.optimization_barrier(values)


def project_kernel(pieces, rotated, factor, index_ref, cos_ref, sin_ref, x_hbm, *rest):
    w_refs = rest[:-6]
    out_ref, x_ref, w_ref, acc_ref, x_sem, w_sem = rest[-6:]
    chunks, depth, rows = x_ref.shape
    copies = []
    for slot in range(ROUNDS):
        place = index_ref[2 + ROUNDS + slot]
        for part in range(2):
            parity = index_ref[1] if part == 0 else 1 - index_ref[1]
            which, lead = pieces[slot]
            source = w_refs[which] if lead is None else w_refs[which].at[lead]
            copies.append(
                pltpu.make_async_copy(
                    source.at[pl.ds(part * depth, depth)],
                    w_ref.at[2 * place + parity],
                    w_sem.at[2 * slot + part],
                )
            )
    step = chunks // 4
    for k in range(4):
        copies.append(
            pltpu.make_async_copy(
                x_hbm.at[pl.ds(k * step, step)], x_ref.at[pl.ds(k * step, step)], x_sem.at[k]
            )
        )
    for copy in copies:
        copy.start()
    for copy in copies[:-4]:
        copy.wait()
    squares = jnp.zeros((1, rows), F32)
    for k in range(4):
        copies[k - 4].wait()
        here = slice(k * step, (k + 1) * step)
        side = x_ref[here, depth - EXTRA :, :].astype(F32)
        squares = squares + jnp.sum(jnp.sum(side, axis=0), axis=0, keepdims=True)
        product = lax.dot_general(
            w_ref[here].reshape(step * depth, 2 * HD),
            x_ref[here].reshape(step * depth, rows),
            (((0,), (0,)), ((), ())),
            preferred_element_type=F32,
        )
        if k == 0:
            acc_ref[...] = product
        else:
            acc_ref[...] += product
    scale = lax.rsqrt(squares * (1.0 / D) + EPSILON)
    half = HD // 2
    for head in range(2):
        start = head * HD
        if rotated[head]:
            first = acc_ref[start : start + half, :] * scale
            second = acc_ref[start + half : start + HD, :] * scale
            cos, sin = cos_ref[...], sin_ref[...]
            value = jnp.concatenate(
                [first * cos - second * sin, second * cos + first * sin], axis=0
            )
            if factor != 1.0:
                value = value * factor
        else:
            value = acc_ref[start : start + HD, :] * scale
        out_ref[:, start : start + HD] = jnp.transpose(value).astype(BF)


def project(x_all, weights, pieces, index, cos, sin, rotated, factor):
    chunks, depth, rows = x_all.shape
    vmem = pl.BlockSpec(memory_space=pltpu.VMEM)
    outside = pl.BlockSpec(memory_space=pl.ANY)
    return pl.pallas_call(
        functools.partial(project_kernel, pieces, rotated, factor),
        out_shape=jax.ShapeDtypeStruct((rows, 2 * HD), BF),
        in_specs=[pl.BlockSpec(memory_space=pltpu.SMEM), vmem, vmem]
        + [outside] * (1 + len(weights)),
        out_specs=vmem,
        scratch_shapes=[
            pltpu.VMEM((chunks, depth, rows), BF),
            pltpu.VMEM((chunks, depth, 2 * HD), BF),
            pltpu.VMEM((2 * HD, rows), F32),
            pltpu.SemaphoreType.DMA((4,)),
            pltpu.SemaphoreType.DMA((2 * ROUNDS,)),
        ],
        compiler_params=pltpu.CompilerParams(vmem_limit_bytes=60 << 20),
        cost_estimate=pl.CostEstimate(
            flops=2 * rows * 2 * HD * D, bytes_accessed=8 << 20, transcendentals=0
        ),
    )(index, cos, sin, x_all, *weights)


def attend_kernel(distances, first, last, low_ref, q_ref, *rest):
    n = len(distances)
    kv_refs = rest[:n]
    rest = rest[n:]
    if not first:
        sum_in, den_in = rest[:2]
        rest = rest[2:]
    rows = q_ref.shape[0]
    tile = 256

    def part(index, carry):
        here = pl.ds(pl.multiple_of((index // 2) * tile, tile), tile)
        columns = pl.ds(pl.multiple_of(lax.rem(index, 2) * HD, HD), HD)
        q = q_ref[here, columns]
        low = low_ref[here, :]
        if first:
            total = jnp.zeros((tile, HD), F32)
            den = jnp.zeros((tile, HD), F32)
        else:
            total = sum_in[here, columns]
            den = den_in[here, columns]
        for kv_ref, distance in zip(kv_refs, distances):
            score = lax.dot_general(
                q, kv_ref[:, :HD], (((1,), (1,)), ((), ())), preferred_element_type=F32
            )
            weight = jnp.exp2(jnp.tanh(score * (1.0 / SOFT_CAP)) * (SOFT_CAP * LOG2E))
            place = lax.broadcasted_iota(jnp.int32, (tile, rows), 1)
            allowed = place >= low + distance * rows
            if distance == 0:
                own = lax.broadcasted_iota(jnp.int32, (tile, rows), 0) + (index // 2) * tile
                allowed = allowed & (place <= own)
            weight = jnp.where(allowed, weight, 0.0)
            for c in range(rows // HD):
                den = den + weight[:, c * HD : (c + 1) * HD]
            total = total + jnp.dot(
                weight.astype(BF), kv_ref[:, HD:], preferred_element_type=F32
            )
        if last:
            whole = jnp.sum(den, axis=1, keepdims=True)
            rest[0][here, columns] = (total / whole).astype(BF)
        else:
            rest[0][here, columns] = total
            rest[1][here, columns] = den
        return carry

    lax.fori_loop(0, 2 * (rows // tile), part, 0)


def attend(low, queries, kvs, distances, state):
    first = state is None
    last = 8 in distances
    rows = queries.shape[0]
    vmem = pl.BlockSpec(memory_space=pltpu.VMEM)
    n_in = 2 + len(kvs) + (0 if first else 2)
    part = jax.ShapeDtypeStruct((rows, 2 * HD), F32)
    elements = 2 * rows * rows * len(kvs)
    return pl.pallas_call(
        functools.partial(attend_kernel, tuple(distances), first, last),
        out_shape=jax.ShapeDtypeStruct((rows, 2 * HD), BF) if last else (part, part),
        in_specs=[vmem] * n_in,
        out_specs=vmem if last else (vmem, vmem),
        input_output_aliases={} if (first or last) else {n_in - 2: 0, n_in - 1: 1},
        compiler_params=pltpu.CompilerParams(vmem_limit_bytes=8 << 20),
        cost_estimate=pl.CostEstimate(
            flops=elements * 512, bytes_accessed=4 << 20, transcendentals=2 * elements
        ),
    )(low, queries, *kvs, *(() if first else state))


def output_kernel(index_ref, *rest):
    n = len(PLACES)
    same, other = rest[:n], rest[n : 2 * n]
    w_ref, out_ref, square_ref = rest[2 * n :]
    features = out_ref.shape[0]
    slot = 0
    for k, places in enumerate(PLACES):
        for j in range(len(places)):
            total = None
            place = index_ref[2 + slot]
            for part, ref in enumerate((same[k], other[k])):
                parity = index_ref[0] if part == 0 else 1 - index_ref[0]
                swapped = jnp.where(parity == index_ref[1], 0, 1)
                product = lax.dot_general(
                    w_ref[2 * place + swapped],
                    ref[j],
                    (((1,), (1,)), ((), ())),
                    preferred_element_type=F32,
                )
                total = product if total is None else total + product
            if slot == 0:
                out_ref[...] = total
            elif slot < ROUNDS - 1:
                out_ref[...] += total
            else:
                total = out_ref[...] + total
                out_ref[...] = total
                square_ref[...] = jnp.sum(total * total, axis=0, keepdims=True)
            slot += 1


def output(chunks, weights, index):
    rows = chunks[0].shape[1]
    features = weights.shape[1]
    vmem = pl.BlockSpec(memory_space=pltpu.VMEM)
    return pl.pallas_call(
        output_kernel,
        out_shape=(
            jax.ShapeDtypeStruct((features, rows), F32),
            jax.ShapeDtypeStruct((1, rows), F32),
        ),
        in_specs=[pl.BlockSpec(memory_space=pltpu.SMEM)] + [vmem] * (len(chunks) + 1),
        out_specs=(vmem, vmem),
        compiler_params=pltpu.CompilerParams(vmem_limit_bytes=10 << 20),
        cost_estimate=pl.CostEstimate(
            flops=2 * rows * features * 4096, bytes_accessed=8 << 20, transcendentals=0
        ),
    )(index, *chunks, weights)


def shards(tokens, pre_gain, post_gain, w_query, w_key, w_value, w_out, segment_ids, page_table):
    rows = tokens.shape[0]
    features = tokens.shape[1]
    seq_index = lax.axis_index("seq")
    z = seq_index // 2
    h = lax.rem(seq_index, 2)
    base = seq_index * rows

    x_own = tokens.T.astype(F32)
    gained = (x_own * (1.0 + pre_gain.astype(F32))[:, None]).astype(BF)
    squares = jnp.sum(x_own * x_own, axis=0, keepdims=True)
    upper = lax.reduce_precision(squares, 8, 7)
    lower = squares - upper
    side = jnp.concatenate(
        [upper.astype(BF), lower.astype(BF), jnp.zeros((EXTRA - 2, rows), BF)], axis=0
    )
    x_all = lax.all_gather(jnp.concatenate([gained, side], axis=0), "mp", axis=0)
    depth = features + EXTRA

    counts = jnp.stack([jnp.sum((segment_ids < s).astype(jnp.int32)) for s in range(1, SEGS)])
    digits = jnp.concatenate([counts // 16, lax.rem(counts, 16)]).astype(BF)
    digits = jnp.pad(digits[None, :], ((2, EXTRA - 3), (0, 2 * HD - 2 * (SEGS - 1))))
    kv_own = jnp.concatenate([jnp.concatenate([w_key, w_value], axis=1), digits], axis=0)
    start = jnp.concatenate([kv_own, move(kv_own, ACROSS)], axis=0)
    turned = lax.ppermute(w_out.T, ("seq", "mp"), TURN)
    q_own = jnp.pad(w_query, ((0, EXTRA), (0, 0)))
    q_pair = jnp.concatenate([q_own, move(q_own, ACROSS)], axis=0)
    ring = {0: start, 1: move(start, AHEAD), -1: move(start, BEHIND)}
    ring[1], ring[-1], q_pair = tie(ring[1], ring[-1], q_pair)
    q_all = lax.all_gather(q_pair, "seq", axis=0, axis_index_groups=COLUMNS)
    ring[2] = move(ring[1], AHEAD)
    ring[-2] = move(ring[-1], BEHIND)
    ring[2], ring[-2], turned = tie(ring[2], ring[-2], turned)
    out_pair = jnp.concatenate([turned, move(turned, ACROSS)], axis=0)
    ring[3] = move(ring[2], AHEAD)
    ring[-3] = move(ring[-2], BEHIND)
    ring[3], ring[-3], out_pair = tie(ring[3], ring[-3], out_pair)
    out_all = lax.all_gather(out_pair, "seq", axis=0, axis_index_groups=COLUMNS)
    last = move(ring[3][:, :HD], AHEAD)
    ring[4] = jnp.concatenate([last, move(ring[-3][:, HD:], BEHIND)], axis=1)

    mp_index = lax.axis_index("mp")
    y = mp_index // 4
    over = lax.rem(mp_index // 2, 2)
    placed = [
        2 * lax.rem(y + dy + 4, 4) + jnp.where(dx == 0, over, 1 - over)
        for places in PLACES
        for dy, dx in places
    ]

    def index_of(steps, origin):
        places = [lax.rem(jnp.int32(origin - step + ROUNDS), ROUNDS) for step in steps]
        return jnp.stack([lax.rem(mp_index, 2), h, *placed, *places]).astype(jnp.int32)

    steps = [0, 1, -1, 2, -2, 3, -3, 4]
    index = index_of(steps, z)
    kv_weights = [ring[step] for step in steps]
    kv_pieces = tuple((k, None) for k in range(ROUNDS))
    q_pieces = tuple((0, k) for k in range(ROUNDS))

    n_marks = 2 * (SEGS - 1)
    marks = jnp.zeros((n_marks,), F32)
    for block in kv_weights:
        for part in range(2):
            marks = marks + block[part * depth + features + 2, :n_marks].astype(F32)
    starts = (marks[: SEGS - 1] * 16.0 + marks[SEGS - 1 :]).astype(jnp.int32)
    global_index = base + jnp.arange(rows, dtype=jnp.int32)
    offsets = jnp.zeros((rows,), jnp.int32)
    for s in range(1, SEGS):
        offsets = jnp.where(segment_ids == s, starts[s - 1], offsets)
    within = (global_index - offsets).astype(F32)
    low = (jnp.maximum(offsets, global_index - (WINDOW - 1)) - base)[:, None]
    half = HD // 2
    freqs = jnp.exp(-math.log(10000.0) * jnp.arange(half, dtype=F32) * (2.0 / HD))
    angles = freqs[:, None] * within[None, :]
    cos = jnp.cos(angles)
    sin = jnp.sin(angles)

    kv = project(x_all, kv_weights, kv_pieces, index, cos, sin, (True, False), 1.0)

    straight, crossed, current, crossing = [kv], [None], kv, None
    for step in range(4):
        following = move(current, LATER)
        chosen = jnp.where(h == 0, current, following)
        if crossing is None:
            following, chosen = tie(following, chosen)
        else:
            following, chosen, crossed[-1] = tie(following, chosen, crossing)
        crossing = move(chosen, ACROSS)
        straight.append(following)
        crossed.append(crossing)
        current = following
    q_all, straight[-1] = tie(q_all, straight[-1])
    queries = project(
        x_all,
        [q_all],
        q_pieces,
        index_of([-k for k in range(ROUNDS)], 0),
        cos,
        sin,
        (True, True),
        float(D // HQ) ** (-0.5),
    )
    state = attend(low, queries, [kv], [0], None)
    for k in range(1, 5):
        state = attend(low, queries, [straight[k], crossed[k]], [2 * k, 2 * k - 1], state)

    a_block = state[None]
    a_pair = jnp.concatenate([a_block, shift(a_block, SIDE)], axis=0)
    a_up, a_down = shift(a_pair, UP), shift(a_pair, DOWN)
    a_far = [shift(a_up[:1], UP), shift(a_down[1:], DOWN)]
    a_swaps = [shift(block, SWAP) for block in (a_pair, a_up, a_down, *a_far)]
    share, partial = output(
        [a_pair, a_up, a_down, *a_far, *a_swaps],
        out_all.reshape(2 * ROUNDS, features, 2 * HD),
        index,
    )
    everywhere = jnp.broadcast_to(partial, (lax.axis_size("mp"), rows))
    square_total = jnp.sum(lax.all_to_all(everywhere, "mp", 0, 0, tiled=True), axis=0)
    post_scale = lax.rsqrt(square_total / D + EPSILON)
    post = share * post_scale[None, :] * (1.0 + post_gain.astype(F32))[:, None]
    layer_output = (tokens.T.astype(F32) + post).astype(BF).T

    pages = page_table.shape[0]
    local_slot = page_table - seq_index * pages
    kv_pages = kv.reshape(pages, PAGE, 2 * HD)
    caches = []
    for slot in range(pages):
        chosen = kv_pages[0]
        for page in range(1, pages):
            chosen = jnp.where(local_slot[page] == slot, kv_pages[page], chosen)
        caches.append(chosen)
    caches = jnp.stack(caches)
    return (layer_output, caches[:, :, :HD], caches[:, :, HD:])


def solution(mesh):
    return jax.shard_map(
        shards,
        mesh=mesh,
        in_specs=(
            P("seq", "mp"),
            P("mp"),
            P("mp"),
            P("seq", "mp"),
            P("seq", "mp"),
            P("seq", "mp"),
            P("mp", "seq"),
            P("seq"),
            P("seq"),
        ),
        out_specs=(P("seq", "mp"), P("seq", None, "mp"), P("seq", None, "mp")),
        check_vma=False,
    )
```

time: 264 us -> 231 us (0.88); the launches traced: 259 us -> 230 us
  starting transfers between devices: 120 us -> 59.7 us
  waiting for transfers between devices: 65.6 us -> 92 us
  between operations: 9.73 us -> 22.1 us
  Pallas kernels: 36.7 us -> 29.3 us
  local copies, waits for them, and re-layouts: 16.2 us -> 11.5 us
  other arithmetic: 11 us -> 15.5 us
    ppermute x28 -> x19, starting transfers between devices: 65.4 us -> 34.8 us  [move(): return lax.ppermute(block, 'seq', perm)]
    ppermute x20 -> x10, starting transfers between devices: 40.7 us -> 13.1 us  [shift(): return lax.ppermute(block, 'mp', perm)]
    ppermute x28 -> x19, waiting for transfers between devices: 38.8 us -> 56.5 us  [move(): return lax.ppermute(block, 'seq', perm)]
    ppermute x1, waiting for transfers between devices: 8.97 us -> 16.1 us  [shards(): turned = lax.ppermute(w_out.T, ('seq', 'mp'), TURN)]
    unnamed x109 -> x37, local copies, waits for them, and re-layouts: 9.79 us -> 5.43 us
    pallas_call x1, Pallas kernels: 6.7 us -> 2.61 us  [output(): pl.pallas_call(output_kernel, out_shape=(jax.ShapeDtypeStruct((features,...]
    pallas_call x2, Pallas kernels: 16.6 us -> 13.3 us  [project(): pl.pallas_call(functools.partial(project_kernel, pieces, rotated, factor)...]
    slice x11 -> x2, local copies, waits for them, and re-layouts: 2.86 us -> 0.02 us  [the longest x1 0.01 us: shards(): last = move(ring[3][:, :HD], AHEAD)]
  transfers between devices with their start and end apart: 50 -> 34, of which waited for: 19 -> 16; matrix products, arithmetic and copies ran while one was open for 4% -> 7% of each run, Pallas kernels for 7% -> 12%
where the time goes in v2:
time: 231 us; the launch traced here: 230 us
  waiting for transfers between devices  92 us (40%)
  starting transfers between devices  59.7 us (26%)
  Pallas kernels  29.3 us (13%)
  between operations  22.1 us (10%)
  other arithmetic  15.5 us (7%)
  local copies, waits for them, and re-layouts  11.5 us (5%)
    ppermute x19, waiting for transfers between devices, move(): return lax.ppermute(block, 'seq', perm)  56.5 us
    ppermute x19, starting transfers between devices, move(): return lax.ppermute(block, 'seq', perm)  34.8 us
    ppermute x1, waiting for transfers between devices, shards(): turned = lax.ppermute(w_out.T, ('seq', 'mp'), TURN)  16.1 us
    ppermute x10, waiting for transfers between devices, shift(): return lax.ppermute(block, 'mp', perm)  15.1 us
    pallas_call x5, Pallas kernels, attend(): pl.pallas_call(functools.partial(attend_kernel, tuple(distances), first,...  13.4 us
    pallas_call x2, Pallas kernels, project(): pl.pallas_call(functools.partial(project_kernel, pieces, rotated, factor)...  13.3 us
    ppermute x10, starting transfers between devices, shift(): return lax.ppermute(block, 'mp', perm)  13.1 us
    ppermute x1, starting transfers between devices, shards(): turned = lax.ppermute(w_out.T, ('seq', 'mp'), TURN)  8.2 us
  transfers between devices with their start and end apart: 34, of which 16 were waited for; matrix products, arithmetic and copies ran while one was open for 7% of the time, Pallas kernels for 12%

profile of v2, /device:TPU:1, one launch (start us, length us, event | category | flops | bytes accessed | tf_op | source)
XLA Modules:
  0.0 230.1 jit_solution(12881628931603615031)
XLA Ops:
  15.4 3.7 %collective-permute-start = (bf16[304,256]{1,0:T(8,128)(2,1)S(1)}, bf16[304,256]{1,0:T(8,128)(2,1)S(1)}, u32[]{:S(2)}, u32[]{:S(2)}) collective-permute-start(bf16[304,256]{1,0:T(8,128)(2,1)S(1)} %pad_maximum_fusion.6), channel_id=1, source_target_pairs={{0,16},{16,0},{32,48},{48,32},{64,80},{80,64},{96,112},{112,96},{1... | collective-permute-start | bytes 466952 | tf_op jit(solution)/shard_map/ppermute | solution.py:44
  24.5 4.0 %collective-permute-start.2 = (bf16[608,256]{1,0:T(8,128)(2,1)S(1)}, bf16[608,256]{1,0:T(8,128)(2,1)S(1)}, u32[]{:S(2)}, u32[]{:S(2)}) collective-permute-start(bf16[608,256]{1,0:T(8,128)(2,1)S(1)} %pad_maximum_fusion.1.rest_0_), channel_id=1, source_target_pairs={{32,0},{48,16},{64,32},{80,48},{96,64},{112,80},{128,96},{144,112}... | collective-permute-start | bytes 933896 | tf_op jit(solution)/shard_map/ppermute | solution.py:44
  31.4 6.8 %collective-permute-done.3 = bf16[304,256]{1,0:T(8,128)(2,1)S(1)} collective-permute-done((bf16[304,256]{1,0:T(8,128)(2,1)S(1)}, bf16[304,256]{1,0:T(8,128)(2,1)S(1)}, u32[]{:S(2)}, u32[]{:S(2)}) %collective-permute-start.3) | collective-permute-done | bytes 155680 | tf_op jit(solution)/shard_map/ppermute | solution.py:44
  41.8 8.2 %collective-permute-start.6 = (bf16[288,256]{1,0:T(8,128)(2,1)S(1)}, bf16[288,256]{1,0:T(8,128)(2,1)S(1)}, u32[]{:S(2)}, u32[]{:S(2)}) collective-permute-start(bf16[288,256]{1,0:T(8,128)(2,1)S(1)} %bitcast.144), channel_id=1, source_target_pairs={{0,0},{1,16},{2,32},{3,48},{4,64},{5,80},{6,96},{7,112},{8,128},{9... | collective-permute-start | bytes 442376 | tf_op jit(solution)/shard_map/ppermute | solution.py:285
  50.0 16.1 %collective-permute-done.6 = bf16[288,256]{1,0:T(8,128)(2,1)S(1)} collective-permute-done((bf16[288,256]{1,0:T(8,128)(2,1)S(1)}, bf16[288,256]{1,0:T(8,128)(2,1)S(1)}, u32[]{:S(2)}, u32[]{:S(2)}) %collective-permute-start.6) | collective-permute-done | bytes 147488 | tf_op jit(solution)/shard_map/ppermute | solution.py:285
  66.2 5.4 %collective-permute-start.8 = (bf16[608,256]{1,0:T(8,128)(2,1)S(1)}, bf16[608,256]{1,0:T(8,128)(2,1)S(1)}, u32[]{:S(2)}, u32[]{:S(2)}) collective-permute-start(bf16[608,256]{1,0:T(8,128)(2,1)S(1)} %collective-permute-done.5.rest_4_), channel_id=1, source_target_pairs={{32,0},{48,16},{64,32},{80,48},{96,64},{112,80},{128,96},{144,112}... | collective-permute-start | bytes 933896 | tf_op jit(solution)/shard_map/ppermute | solution.py:44
  71.5 5.9 %collective-permute-done.9 = bf16[288,256]{1,0:T(8,128)(2,1)S(1)} collective-permute-done((bf16[288,256]{1,0:T(8,128)(2,1)S(1)}, bf16[288,256]{1,0:T(8,128)(2,1)S(1)}, u32[]{:S(2)}, u32[]{:S(2)}) %collective-permute-start.9) | collective-permute-done | bytes 147488 | tf_op jit(solution)/shard_map/ppermute | solution.py:44
  81.8 3.8 %collective-permute-done.10 = bf16[608,128]{1,0:T(8,128)(2,1)S(1)} collective-permute-done((bf16[608,128]{1,0:T(8,128)(2,1)S(1)}, bf16[608,128]{1,0:T(8,128)(2,1)S(1)}, u32[]{:S(2)}, u32[]{:S(2)}) %collective-permute-start.10) | collective-permute-done | bytes 155680 | tf_op jit(solution)/shard_map/ppermute | solution.py:44
  90.3 6.7 %shard_map.112.rest_0_ = bf16[512,256]{1,0:T(8,128)(2,1)} custom-call(s32[18]{0:T(128)} %stack.115.index_ref, f32[64,512]{1,0:T(8,128)} %get-tuple-element.82.cos_ref, f32[64,512]{1,0:T(8,128)} %get-tuple-element.81.sin_ref, bf16[16,304,512]{2,1,0:T(8,128)(2,1)} %bitcast.138, bf16[608,256]{1,0:T(8,128)(2,1)} %copy-done.6, bf16[608,256]{1,0:T(8,128)(2,1)} %copy-done.9, ...), custom_call_target="tpu_custom_call" | custom-call | flops 1207959552 | bytes 8388608 | tf_op jit(solution)/shard_map/pallas_call | solution.py:122
  98.2 12.0 %collective-permute-done.12.rest_0_ = bf16[512,256]{1,0:T(8,128)(2,1)S(1)} collective-permute-done((bf16[512,256]{1,0:T(8,128)(2,1)}, bf16[512,256]{1,0:T(8,128)(2,1)S(1)}, u32[]{:S(2)}, u32[]{:S(2)}) %collective-permute-start.12) | collective-permute-done | bytes 262176 | tf_op jit(solution)/shard_map/ppermute | solution.py:44
  111.2 4.1 %collective-permute-start.13 = (bf16[512,256]{1,0:T(8,128)(2,1)S(1)}, bf16[512,256]{1,0:T(8,128)(2,1)S(1)}, u32[]{:S(2)}, u32[]{:S(2)}) collective-permute-start(bf16[512,256]{1,0:T(8,128)(2,1)S(1)} %collective-permute-done.12.rest_0_), channel_id=1, source_target_pairs={{0,32},{16,48},{32,64},{48,80},{64,96},{80,112},{96,128},{112,144}... | collective-permute-start | bytes 786440 | tf_op jit(solution)/shard_map/ppermute | solution.py:44
  115.5 5.5 %collective-permute-done.13.rest_0_ = bf16[512,256]{1,0:T(8,128)(2,1)S(1)} collective-permute-done((bf16[512,256]{1,0:T(8,128)(2,1)S(1)}, bf16[512,256]{1,0:T(8,128)(2,1)S(1)}, u32[]{:S(2)}, u32[]{:S(2)}) %collective-permute-start.13) | collective-permute-done | bytes 262176 | tf_op jit(solution)/shard_map/ppermute | solution.py:44
  121.0 3.2 %collective-permute-done.14.rest_1_ = bf16[512,256]{1,0:T(8,128)(2,1)S(1)} collective-permute-done((bf16[512,256]{1,0:T(8,128)(2,1)S(1)}, bf16[512,256]{1,0:T(8,128)(2,1)S(1)}, u32[]{:S(2)}, u32[]{:S(2)}) %collective-permute-start.14) | collective-permute-done | bytes 262176 | tf_op jit(solution)/shard_map/ppermute | solution.py:44
  127.1 3.9 %collective-permute-done.15.rest_0_ = bf16[512,256]{1,0:T(8,128)(2,1)S(1)} collective-permute-done((bf16[512,256]{1,0:T(8,128)(2,1)S(1)}, bf16[512,256]{1,0:T(8,128)(2,1)S(1)}, u32[]{:S(2)}, u32[]{:S(2)}) %collective-permute-start.15) | collective-permute-done | bytes 262176 | tf_op jit(solution)/shard_map/ppermute | solution.py:44
  131.0 3.7 %collective-permute-done.16.rest_1_ = bf16[512,256]{1,0:T(8,128)(2,1)S(1)} collective-permute-done((bf16[512,256]{1,0:T(8,128)(2,1)S(1)}, bf16[512,256]{1,0:T(8,128)(2,1)S(1)}, u32[]{:S(2)}, u32[]{:S(2)}) %collective-permute-start.16) | collective-permute-done | bytes 262176 | tf_op jit(solution)/shard_map/ppermute | solution.py:44
  137.8 9.0 %collective-permute-done.17.rest_0_ = bf16[512,256]{1,0:T(8,128)(2,1)S(1)} collective-permute-done((bf16[512,256]{1,0:T(8,128)(2,1)S(1)}, bf16[512,256]{1,0:T(8,128)(2,1)S(1)}, u32[]{:S(2)}, u32[]{:S(2)}) %collective-permute-start.17) | collective-permute-done | bytes 262176 | tf_op jit(solution)/shard_map/ppermute | solution.py:44
  147.0 6.7 %shard_map.113.q_ref = bf16[512,256]{1,0:T(8,128)(2,1)} custom-call(s32[18]{0:T(128)} %stack.120.index_ref, f32[64,512]{1,0:T(8,128)} %get-tuple-element.82.cos_ref, f32[64,512]{1,0:T(8,128)} %get-tuple-element.81.sin_ref, bf16[16,304,512]{2,1,0:T(8,128)(2,1)} %bitcast.139, bf16[8,608,256]{2,1,0:T(8,128)(2,1)} %bitcast.140), custom_call_target="tpu_custom_call" | custom-call | flops 1207959552 | bytes 8388608 | tf_op jit(solution)/shard_map/pallas_call | solution.py:122
  159.4 2.9 %shard_map.116 = (f32[512,256]{1,0:T(8,128)S(1)}, f32[512,256]{1,0:T(8,128)S(1)}) custom-call(s32[512,1]{1,0:T(8,128)S(1)} %copy.32.low_ref, bf16[512,256]{1,0:T(8,128)(2,1)S(1)} %copy-done.4, bf16[512,256]{1,0:T(8,128)(2,1)S(1)} %collective-permute-done.13.rest_0_, ...), custom_call_target="tpu_custom_call", output_to_operand_aliasing={{0}: (4, {}), {1}: (5, {})} | custom-call | flops 536870912 | bytes 4194304 | tf_op jit(solution)/shard_map/pallas_call | solution.py:198
  165.2 2.9 %shard_map.118 = bf16[512,256]{1,0:T(8,128)(2,1)S(1)} custom-call(s32[512,1]{1,0:T(8,128)S(1)} %copy.32.low_ref, bf16[512,256]{1,0:T(8,128)(2,1)S(1)} %copy-done.4, bf16[512,256]{1,0:T(8,128)(2,1)S(1)} %collective-permute-done.17.rest_0_, bf16[512,256]{1,0:T(8,128)(2,1)S(1)} %collective-permute-done.19.rest_1_, f32[512,256]{1,0:T(8,128)S(1)} %get-tuple-element.62.rest_2_, ...), custom_call_target="tpu_custom_call" | custom-call | flops 536870912 | bytes 4194304 | tf_op jit(solution)/shard_map/pallas_call | solution.py:198
  168.2 5.2 %collective-permute-done.20 = bf16[1,512,256]{2,1,0:T(8,128)(2,1)S(1)} collective-permute-done((bf16[1,512,256]{2,1,0:T(8,128)(2,1)S(1)}, bf16[1,512,256]{2,1,0:T(8,128)(2,1)S(1)}, u32[]{:S(2)}, u32[]{:S(2)}) %collective-permute-start.20) | collective-permute-done | bytes 262176 | tf_op jit(solution)/shard_map/ppermute | solution.py:48
  176.2 7.8 %collective-permute-done.21.rest_1_ = bf16[2,512,256]{2,1,0:T(8,128)(2,1)S(1)} collective-permute-done((bf16[2,512,256]{2,1,0:T(8,128)(2,1)S(1)}, bf16[2,512,256]{2,1,0:T(8,128)(2,1)S(1)}, u32[]{:S(2)}, u32[]{:S(2)}) %collective-permute-start.21) | collective-permute-done | bytes 524320 | tf_op jit(solution)/shard_map/ppermute | solution.py:48
  195.2 6.4 %collective-permute-start.25 = (bf16[2,512,256]{2,1,0:T(8,128)(2,1)S(1)}, bf16[2,512,256]{2,1,0:T(8,128)(2,1)S(1)}, u32[]{:S(2)}, u32[]{:S(2)}) collective-permute-start(bf16[2,512,256]{2,1,0:T(8,128)(2,1)S(1)} %pad_maximum_fusion.rest_0_), channel_id=1, source_target_pairs={{0,1},{1,0},{2,3},{3,2},{4,5},{5,4},{6,7},{7,6},{8,9},{9,8},{10,11... | collective-permute-start | bytes 1572872 | tf_op jit(solution)/shard_map/ppermute | solution.py:48
  212.4 3.4 %all-to-all-start = ((f32[16,1,512]{2,1,0:T(1,128)}), f32[16,1,512]{2,1,0:T(1,128)S(1)}, u32[]{:S(2)}, u32[]{:S(2)}) async-start(f32[16,1,512]{2,1,0:T(1,128)} %broadcast_in_dim.41), calls=%async_computation | async-start | bytes 65536 | tf_op jit(solution)/shard_map/all_to_all | solution.py:379
  217.5 4.2 %all-to-all-done = f32[16,1,512]{2,1,0:T(1,128)S(1)} async-done(((f32[16,1,512]{2,1,0:T(1,128)}), f32[16,1,512]{2,1,0:T(1,128)S(1)}, u32[]{:S(2)}, u32[]{:S(2)}) %all-to-all-start) | async-done | bytes 32800 | tf_op jit(solution)/shard_map/all_to_all | solution.py:379
  (138 shorter events, 66.7 us)
Async XLA Ops:
  7.2 83.0 %all-gather.7.cloned.1.call-start = ((), (), s32[]{:S(2)}) async-start(), calls=%async_computation.1 | async-start | bytes 5292032 | tf_op jit(solution)/shard_map/all_gather | solution.py:277
  10.1 136.8 %all-gather.9.cloned.1.call-start = ((), (), s32[]{:S(2)}) async-start(), calls=%async_computation.2 | async-start | bytes 2801664 | tf_op jit(solution)/shard_map/all_gather | solution.py:290
  21.8 17.1 %collective-permute-start.1 = (bf16[608,256]{1,0:T(8,128)(2,1)S(1)}, bf16[608,256]{1,0:T(8,128)(2,1)S(1)}, u32[]{:S(2)}, u32[]{:S(2)}) collective-permute-start(bf16[608,256]{1,0:T(8,128)(2,1)S(1)} %pad_maximum_fusion.1.rest_0_), channel_id=1, source_target_pairs={{0,32},{16,48},{32,64},{48,80},{64,96},{80,112},{96,128},{112,144}... | collective-permute-start | bytes 933896 | tf_op jit(solution)/shard_map/ppermute | solution.py:44
  24.5 14.4 %collective-permute-start.2 = (bf16[608,256]{1,0:T(8,128)(2,1)S(1)}, bf16[608,256]{1,0:T(8,128)(2,1)S(1)}, u32[]{:S(2)}, u32[]{:S(2)}) collective-permute-start(bf16[608,256]{1,0:T(8,128)(2,1)S(1)} %pad_maximum_fusion.1.rest_0_), channel_id=1, source_target_pairs={{32,0},{48,16},{64,32},{80,48},{96,64},{112,80},{128,96},{144,112}... | collective-permute-start | bytes 933896 | tf_op jit(solution)/shard_map/ppermute | solution.py:44
  28.5 9.6 %collective-permute-start.3 = (bf16[304,256]{1,0:T(8,128)(2,1)S(1)}, bf16[304,256]{1,0:T(8,128)(2,1)S(1)}, u32[]{:S(2)}, u32[]{:S(2)}) collective-permute-start(bf16[304,256]{1,0:T(8,128)(2,1)S(1)} %pad.9), channel_id=1, source_target_pairs={{0,16},{16,0},{32,48},{48,32},{64,80},{80,64},{96,112},{112,96},{1... | collective-permute-start | bytes 466952 | tf_op jit(solution)/shard_map/ppermute | solution.py:44
  39.0 164.5 %all-gather.11.cloned.1.call-start = ((), (), s32[]{:S(2)}) async-start(), calls=%async_computation.3 | async-start | bytes 2654208 | tf_op jit(solution)/shard_map/all_gather | solution.py:298
  39.0 27.1 %collective-permute-start.4 = (bf16[608,256]{1,0:T(8,128)(2,1)S(1)}, bf16[608,256]{1,0:T(8,128)(2,1)S(1)}, u32[]{:S(2)}, u32[]{:S(2)}) collective-permute-start(bf16[608,256]{1,0:T(8,128)(2,1)S(1)} %collective-permute-done.1.rest_1_), channel_id=1, source_target_pairs={{0,32},{16,48},{32,64},{48,80},{64,96},{80,112},{96,128},{112,144}... | collective-permute-start | bytes 933896 | tf_op jit(solution)/shard_map/ppermute | solution.py:44
  39.1 27.0 %collective-permute-start.5 = (bf16[608,256]{1,0:T(8,128)(2,1)S(1)}, bf16[608,256]{1,0:T(8,128)(2,1)S(1)}, u32[]{:S(2)}, u32[]{:S(2)}) collective-permute-start(bf16[608,256]{1,0:T(8,128)(2,1)S(1)} %collective-permute-done.2.rest_2_), channel_id=1, source_target_pairs={{32,0},{48,16},{64,32},{80,48},{96,64},{112,80},{128,96},{144,112}... | collective-permute-start | bytes 933896 | tf_op jit(solution)/shard_map/ppermute | solution.py:44
  41.8 24.3 %collective-permute-start.6 = (bf16[288,256]{1,0:T(8,128)(2,1)S(1)}, bf16[288,256]{1,0:T(8,128)(2,1)S(1)}, u32[]{:S(2)}, u32[]{:S(2)}) collective-permute-start(bf16[288,256]{1,0:T(8,128)(2,1)S(1)} %bitcast.144), channel_id=1, source_target_pairs={{0,0},{1,16},{2,32},{3,48},{4,64},{5,80},{6,96},{7,112},{8,128},{9... | collective-permute-start | bytes 442376 | tf_op jit(solution)/shard_map/ppermute | solution.py:285
  66.1 12.1 %collective-permute-start.7 = (bf16[608,256]{1,0:T(8,128)(2,1)S(1)}, bf16[608,256]{1,0:T(8,128)(2,1)S(1)}, u32[]{:S(2)}, u32[]{:S(2)}) collective-permute-start(bf16[608,256]{1,0:T(8,128)(2,1)S(1)} %collective-permute-done.4.rest_3_), channel_id=1, source_target_pairs={{0,32},{16,48},{32,64},{48,80},{64,96},{80,112},{96,128},{112,144}... | collective-permute-start | bytes 933896 | tf_op jit(solution)/shard_map/ppermute | solution.py:44
  66.2 12.0 %collective-permute-start.8 = (bf16[608,256]{1,0:T(8,128)(2,1)S(1)}, bf16[608,256]{1,0:T(8,128)(2,1)S(1)}, u32[]{:S(2)}, u32[]{:S(2)}) collective-permute-start(bf16[608,256]{1,0:T(8,128)(2,1)S(1)} %collective-permute-done.5.rest_4_), channel_id=1, source_target_pairs={{32,0},{48,16},{64,32},{80,48},{96,64},{112,80},{128,96},{144,112}... | collective-permute-start | bytes 933896 | tf_op jit(solution)/shard_map/ppermute | solution.py:44
  79.2 10.3 %collective-permute-start.11 = (bf16[608,128]{1,0:T(8,128)(2,1)S(1)}, bf16[608,128]{1,0:T(8,128)(2,1)S(1)}, u32[]{:S(2)}, u32[]{:S(2)}) collective-permute-start(bf16[608,128]{1,0:T(8,128)(2,1)S(1)} %slice.146), channel_id=1, source_target_pairs={{32,0},{48,16},{64,32},{80,48},{96,64},{112,80},{128,96},{144,112}... | collective-permute-start | bytes 466952 | tf_op jit(solution)/shard_map/ppermute | solution.py:44
  96.9 13.3 %collective-permute-start.12 = (bf16[512,256]{1,0:T(8,128)(2,1)}, bf16[512,256]{1,0:T(8,128)(2,1)S(1)}, u32[]{:S(2)}, u32[]{:S(2)}) collective-permute-start(bf16[512,256]{1,0:T(8,128)(2,1)} %shard_map.112.rest_0_), channel_id=1, source_target_pairs={{0,32},{16,48},{32,64},{48,80},{64,96},{80,112},{96,128},{112,144}... | collective-permute-start | bytes 786440 | tf_op jit(solution)/shard_map/ppermute | solution.py:44
  111.2 9.8 %collective-permute-start.13 = (bf16[512,256]{1,0:T(8,128)(2,1)S(1)}, bf16[512,256]{1,0:T(8,128)(2,1)S(1)}, u32[]{:S(2)}, u32[]{:S(2)}) collective-permute-start(bf16[512,256]{1,0:T(8,128)(2,1)S(1)} %collective-permute-done.12.rest_0_), channel_id=1, source_target_pairs={{0,32},{16,48},{32,64},{48,80},{64,96},{80,112},{96,128},{112,144}... | collective-permute-start | bytes 786440 | tf_op jit(solution)/shard_map/ppermute | solution.py:44
  115.4 8.9 %collective-permute-start.14 = (bf16[512,256]{1,0:T(8,128)(2,1)S(1)}, bf16[512,256]{1,0:T(8,128)(2,1)S(1)}, u32[]{:S(2)}, u32[]{:S(2)}) collective-permute-start(bf16[512,256]{1,0:T(8,128)(2,1)S(1)} %broadcast_select_fusion.3), channel_id=1, source_target_pairs={{0,16},{16,0},{32,48},{48,32},{64,80},{80,64},{96,112},{112,96},{1... | collective-permute-start | bytes 786440 | tf_op jit(solution)/shard_map/ppermute | solution.py:44
  134.6 12.1 %collective-permute-start.17 = (bf16[512,256]{1,0:T(8,128)(2,1)S(1)}, bf16[512,256]{1,0:T(8,128)(2,1)S(1)}, u32[]{:S(2)}, u32[]{:S(2)}) collective-permute-start(bf16[512,256]{1,0:T(8,128)(2,1)S(1)} %collective-permute-done.15.rest_0_), channel_id=1, source_target_pairs={{0,32},{16,48},{32,64},{48,80},{64,96},{80,112},{96,128},{112,144}... | collective-permute-start | bytes 786440 | tf_op jit(solution)/shard_map/ppermute | solution.py:44
  136.9 9.9 %collective-permute-start.18 = (bf16[512,256]{1,0:T(8,128)(2,1)S(1)}, bf16[512,256]{1,0:T(8,128)(2,1)S(1)}, u32[]{:S(2)}, u32[]{:S(2)}) collective-permute-start(bf16[512,256]{1,0:T(8,128)(2,1)S(1)} %broadcast_select_fusion.1), channel_id=1, source_target_pairs={{0,16},{16,0},{32,48},{48,32},{64,80},{80,64},{96,112},{112,96},{1... | collective-permute-start | bytes 786440 | tf_op jit(solution)/shard_map/ppermute | solution.py:44
  146.9 18.3 %collective-permute-start.19 = (bf16[512,256]{1,0:T(8,128)(2,1)S(1)}, bf16[512,256]{1,0:T(8,128)(2,1)S(1)}, u32[]{:S(2)}, u32[]{:S(2)}) collective-permute-start(bf16[512,256]{1,0:T(8,128)(2,1)S(1)} %broadcast_select_fusion), channel_id=1, source_target_pairs={{0,16},{16,0},{32,48},{48,32},{64,80},{80,64},{96,112},{112,96},{1... | collective-permute-start | bytes 786440 | tf_op jit(solution)/shard_map/ppermute | solution.py:44
  173.4 10.5 %collective-permute-start.21 = (bf16[2,512,256]{2,1,0:T(8,128)(2,1)S(1)}, bf16[2,512,256]{2,1,0:T(8,128)(2,1)S(1)}, u32[]{:S(2)}, u32[]{:S(2)}) collective-permute-start(bf16[2,512,256]{2,1,0:T(8,128)(2,1)S(1)} %pad_maximum_fusion.rest_0_), channel_id=1, source_target_pairs={{0,4},{1,5},{2,6},{3,7},{4,8},{5,9},{6,10},{7,11},{8,12},{9,13},{1... | collective-permute-start | bytes 1572872 | tf_op jit(solution)/shard_map/ppermute | solution.py:48
  173.5 10.6 %collective-permute-start.22 = (bf16[2,512,256]{2,1,0:T(8,128)(2,1)S(1)}, bf16[2,512,256]{2,1,0:T(8,128)(2,1)S(1)}, u32[]{:S(2)}, u32[]{:S(2)}) collective-permute-start(bf16[2,512,256]{2,1,0:T(8,128)(2,1)S(1)} %pad_maximum_fusion.rest_0_), channel_id=1, source_target_pairs={{4,0},{5,1},{6,2},{7,3},{8,4},{9,5},{10,6},{11,7},{12,8},{13,9},{1... | collective-permute-start | bytes 1572872 | tf_op jit(solution)/shard_map/ppermute | solution.py:48
  184.0 18.1 %collective-permute-start.23 = (bf16[1,512,256]{2,1,0:T(8,128)(2,1)S(1)}, bf16[1,512,256]{2,1,0:T(8,128)(2,1)}, u32[]{:S(2)}, u32[]{:S(2)}) collective-permute-start(bf16[1,512,256]{2,1,0:T(8,128)(2,1)S(1)} %slice.161), channel_id=1, source_target_pairs={{0,4},{1,5},{2,6},{3,7},{4,8},{5,9},{6,10},{7,11},{8,12},{9,13},{1... | collective-permute-start | bytes 786440 | tf_op jit(solution)/shard_map/ppermute | solution.py:48
  184.1 18.2 %collective-permute-start.24 = (bf16[1,512,256]{2,1,0:T(8,128)(2,1)S(1)}, bf16[1,512,256]{2,1,0:T(8,128)(2,1)}, u32[]{:S(2)}, u32[]{:S(2)}) collective-permute-start(bf16[1,512,256]{2,1,0:T(8,128)(2,1)S(1)} %slice.162), channel_id=1, source_target_pairs={{4,0},{5,1},{6,2},{7,3},{8,4},{9,5},{10,6},{11,7},{12,8},{13,9},{1... | collective-permute-start | bytes 786440 | tf_op jit(solution)/shard_map/ppermute | solution.py:48
  195.2 8.3 %collective-permute-start.25 = (bf16[2,512,256]{2,1,0:T(8,128)(2,1)S(1)}, bf16[2,512,256]{2,1,0:T(8,128)(2,1)S(1)}, u32[]{:S(2)}, u32[]{:S(2)}) collective-permute-start(bf16[2,512,256]{2,1,0:T(8,128)(2,1)S(1)} %pad_maximum_fusion.rest_0_), channel_id=1, source_target_pairs={{0,1},{1,0},{2,3},{3,2},{4,5},{5,4},{6,7},{7,6},{8,9},{9,8},{10,11... | collective-permute-start | bytes 1572872 | tf_op jit(solution)/shard_map/ppermute | solution.py:48
  212.4 9.3 %all-to-all-start = ((f32[16,1,512]{2,1,0:T(1,128)}), f32[16,1,512]{2,1,0:T(1,128)S(1)}, u32[]{:S(2)}, u32[]{:S(2)}) async-start(f32[16,1,512]{2,1,0:T(1,128)} %broadcast_in_dim.41), calls=%async_computation | async-start | bytes 65536 | tf_op jit(solution)/shard_map/all_to_all | solution.py:379
  (28 other events, 500.9 us)
Sparse Core Ops, SparseCore 0:
  10.2 54.6 all-gather.6
  66.6 49.9 all-gather.8
  119.0 48.6 all-gather.10

commit v3 on v2

--- a/solution.py
+++ b/solution.py
@@ -29,7 +29,11 @@
 BEHIND = [((i + 2) % SEQ, i) for i in range(SEQ)]
 LATER = [(i, i + 2) for i in range(SEQ - 2)]
 ACROSS = [(i, i ^ 1) for i in range(SEQ)]
-TURN = [(s * SEQ + m, m * SEQ + s) for s in range(SEQ) for m in range(SEQ)]
+TURNS = (
+    [(s * SEQ + m, s * SEQ + (s + m) % SEQ) for s in range(SEQ) for m in range(SEQ)],
+    [(s * SEQ + c, ((c - s) % SEQ) * SEQ + c) for s in range(SEQ) for c in range(SEQ)],
+    [(m * SEQ + c, m * SEQ + (c - m) % SEQ) for m in range(SEQ) for c in range(SEQ)],
+)
 
 
 SIDE = [(i, i ^ 2) for i in range(SEQ)]
@@ -277,27 +281,33 @@
     x_all = lax.all_gather(jnp.concatenate([gained, side], axis=0), "mp", axis=0)
     depth = features + EXTRA
 
-    counts = jnp.stack([jnp.sum((segment_ids < s).astype(jnp.int32)) for s in range(1, SEGS)])
-    digits = jnp.concatenate([counts // 16, lax.rem(counts, 16)]).astype(BF)
-    digits = jnp.pad(digits[None, :], ((2, EXTRA - 3), (0, 2 * HD - 2 * (SEGS - 1))))
+    lane = jnp.arange(2 * HD, dtype=jnp.int32)
+    marked = 2 * (SEGS - 1)
+    limit = jnp.where(lane < marked, lax.rem(lane, SEGS - 1) + 1, 0)
+    counts = jnp.sum((segment_ids[:, None] < limit[None, :]).astype(F32), axis=0)
+    upper_digit = jnp.floor(counts * (1.0 / 16.0))
+    digits = jnp.where(lane < SEGS - 1, upper_digit, counts - 16.0 * upper_digit).astype(BF)
+    digits = jnp.pad(digits[None, :], ((2, EXTRA - 3), (0, 0)))
     kv_own = jnp.concatenate([jnp.concatenate([w_key, w_value], axis=1), digits], axis=0)
     start = jnp.concatenate([kv_own, move(kv_own, ACROSS)], axis=0)
-    turned = lax.ppermute(w_out.T, ("seq", "mp"), TURN)
-    q_own = jnp.pad(w_query, ((0, EXTRA), (0, 0)))
-    q_pair = jnp.concatenate([q_own, move(q_own, ACROSS)], axis=0)
     ring = {0: start, 1: move(start, AHEAD), -1: move(start, BEHIND)}
-    ring[1], ring[-1], q_pair = tie(ring[1], ring[-1], q_pair)
-    q_all = lax.all_gather(q_pair, "seq", axis=0, axis_index_groups=COLUMNS)
+    turned = lax.ppermute(w_out.T, ("seq", "mp"), TURNS[0])
     ring[2] = move(ring[1], AHEAD)
     ring[-2] = move(ring[-1], BEHIND)
     ring[2], ring[-2], turned = tie(ring[2], ring[-2], turned)
-    out_pair = jnp.concatenate([turned, move(turned, ACROSS)], axis=0)
+    q_own = jnp.pad(w_query, ((0, EXTRA), (0, 0)))
+    q_own, _ = tie(q_own, ring[1])
+    q_pair = jnp.concatenate([q_own, move(q_own, ACROSS)], axis=0)
+    turned = lax.ppermute(turned, ("seq", "mp"), TURNS[1])
     ring[3] = move(ring[2], AHEAD)
     ring[-3] = move(ring[-2], BEHIND)
-    ring[3], ring[-3], out_pair = tie(ring[3], ring[-3], out_pair)
-    out_all = lax.all_gather(out_pair, "seq", axis=0, axis_index_groups=COLUMNS)
+    ring[3], ring[-3], turned, q_pair = tie(ring[3], ring[-3], turned, q_pair)
+    q_all = lax.all_gather(q_pair, "seq", axis=0, axis_index_groups=COLUMNS)
+    turned = lax.ppermute(turned, ("seq", "mp"), TURNS[2])
     last = move(ring[3][:, :HD], AHEAD)
     ring[4] = jnp.concatenate([last, move(ring[-3][:, HD:], BEHIND)], axis=1)
+    ring[4], turned = tie(ring[4], turned)
+    facing_out = move(turned, ACROSS)
 
     mp_index = lax.axis_index("mp")
     y = mp_index // 4
@@ -338,17 +348,18 @@
 
     kv = project(x_all, kv_weights, kv_pieces, index, cos, sin, (True, False), 1.0)
 
-    straight, crossed, current, crossing = [kv], [None], kv, None
+    straight, crossed, current = [kv], [None], kv
     for step in range(4):
         following = move(current, LATER)
         chosen = jnp.where(h == 0, current, following)
-        if crossing is None:
-            following, chosen = tie(following, chosen)
+        if step == 0:
+            following, chosen, facing_out = tie(following, chosen, facing_out)
+            out_pair = jnp.concatenate([turned, facing_out], axis=0)
+            out_all = lax.all_gather(out_pair, "seq", axis=0, axis_index_groups=COLUMNS)
         else:
-            following, chosen, crossed[-1] = tie(following, chosen, crossing)
-        crossing = move(chosen, ACROSS)
+            following, chosen, crossed[step] = tie(following, chosen, crossed[step])
         straight.append(following)
-        crossed.append(crossing)
+        crossed.append(move(chosen, ACROSS))
         current = following
     q_all, straight[-1] = tie(q_all, straight[-1])
     queries = project(
@@ -368,6 +379,7 @@
     a_block = state[None]
     a_pair = jnp.concatenate([a_block, shift(a_block, SIDE)], axis=0)
     a_up, a_down = shift(a_pair, UP), shift(a_pair, DOWN)
+    a_up, a_down, out_all = tie(a_up, a_down, out_all)
     a_far = [shift(a_up[:1], UP), shift(a_down[1:], DOWN)]
     a_swaps = [shift(block, SWAP) for block in (a_pair, a_up, a_down, *a_far)]
     share, partial = output(

time: 231 us -> 226 us (0.978)
  the two profiles are of different devices: /device:TPU:1 before, /device:TPU:101 now
where the time goes in v3:
time: 226 us
  starting transfers between devices  81.3 us (36%)
  waiting for transfers between devices  77 us (34%)
  Pallas kernels  28.7 us (13%)
  between operations  22.2 us (10%)
  other arithmetic  9.59 us (4%)
  local copies, waits for them, and re-layouts  6.96 us (3%)
    ppermute x19, waiting for transfers between devices, move(): return lax.ppermute(block, 'seq', perm)  47 us
    ppermute x19, starting transfers between devices, move(): return lax.ppermute(block, 'seq', perm)  35.7 us
    ppermute x10, starting transfers between devices, shift(): return lax.ppermute(block, 'mp', perm)  20.4 us
    ppermute x10, waiting for transfers between devices, shift(): return lax.ppermute(block, 'mp', perm)  14.3 us
    pallas_call x5, Pallas kernels, attend(): pl.pallas_call(functools.partial(attend_kernel, tuple(distances), first,...  13.4 us
    pallas_call x2, Pallas kernels, project(): pl.pallas_call(functools.partial(project_kernel, pieces, rotated, factor)...  13.3 us
    ppermute x1, starting transfers between devices, shards(): turned = lax.ppermute(w_out.T, ('seq', 'mp'), TURNS[0])  7.46 us
    ppermute x1, starting transfers between devices, shards(): turned = lax.ppermute(turned, ('seq', 'mp'), TURNS[2])  6.59 us
  transfers between devices with their start and end apart: 36, of which 21 were waited for; matrix products, arithmetic and copies ran while one was open for 5% of the time, Pallas kernels for 12%

profile of v3, /device:TPU:101, one launch (start us, length us, event | category | flops | bytes accessed | tf_op | source)
XLA Modules:
  0.0 225.7 jit_solution(8225051337267186001)
XLA Ops:
  13.2 6.2 %collective-permute-done = bf16[304,256]{1,0:T(8,128)(2,1)S(1)} collective-permute-done((bf16[304,256]{1,0:T(8,128)(2,1)S(1)}, bf16[304,256]{1,0:T(8,128)(2,1)S(1)}, u32[]{:S(2)}, u32[]{:S(2)}) %collective-permute-start) | collective-permute-done | bytes 155680 | tf_op jit(solution)/shard_map/ppermute | solution.py:48
  19.4 2.9 %collective-permute-start.1 = (bf16[608,256]{1,0:T(8,128)(2,1)S(1)}, bf16[608,256]{1,0:T(8,128)(2,1)S(1)}, u32[]{:S(2)}, u32[]{:S(2)}) collective-permute-start(bf16[608,256]{1,0:T(8,128)(2,1)S(1)} %pad_maximum_fusion.1.rest_0_), channel_id=1, source_target_pairs={{0,32},{16,48},{32,64},{48,80},{64,96},{80,112},{96,128},{112,144}... | collective-permute-start | bytes 933896 | tf_op jit(solution)/shard_map/ppermute | solution.py:48
  22.3 5.1 %collective-permute-done.1.rest_1_ = bf16[608,256]{1,0:T(8,128)(2,1)S(1)} collective-permute-done((bf16[608,256]{1,0:T(8,128)(2,1)S(1)}, bf16[608,256]{1,0:T(8,128)(2,1)S(1)}, u32[]{:S(2)}, u32[]{:S(2)}) %collective-permute-start.1) | collective-permute-done | bytes 311328 | tf_op jit(solution)/shard_map/ppermute | solution.py:48
  27.4 3.4 %collective-permute-start.3 = (bf16[608,256]{1,0:T(8,128)(2,1)S(1)}, bf16[608,256]{1,0:T(8,128)(2,1)S(1)}, u32[]{:S(2)}, u32[]{:S(2)}) collective-permute-start(bf16[608,256]{1,0:T(8,128)(2,1)S(1)} %collective-permute-done.1.rest_1_), channel_id=1, source_target_pairs={{0,32},{16,48},{32,64},{48,80},{64,96},{80,112},{96,128},{112,144}... | collective-permute-start | bytes 933896 | tf_op jit(solution)/shard_map/ppermute | solution.py:48
  30.8 7.5 %collective-permute-start.5 = (bf16[288,256]{1,0:T(8,128)(2,1)S(1)}, bf16[288,256]{1,0:T(8,128)(2,1)S(1)}, u32[]{:S(2)}, u32[]{:S(2)}) collective-permute-start(bf16[288,256]{1,0:T(8,128)(2,1)S(1)} %bitcast.80), channel_id=1, source_target_pairs={{0,0},{1,1},{2,2},{3,3},{4,4},{5,5},{6,6},{7,7},{8,8},{9,9},{10,10... | collective-permute-start | bytes 442376 | tf_op jit(solution)/shard_map/ppermute | solution.py:294
  38.3 6.0 %collective-permute-done.5 = bf16[288,256]{1,0:T(8,128)(2,1)S(1)} collective-permute-done((bf16[288,256]{1,0:T(8,128)(2,1)S(1)}, bf16[288,256]{1,0:T(8,128)(2,1)S(1)}, u32[]{:S(2)}, u32[]{:S(2)}) %collective-permute-start.5) | collective-permute-done | bytes 147488 | tf_op jit(solution)/shard_map/ppermute | solution.py:294
  47.0 5.8 %collective-permute-start.8 = (bf16[288,256]{1,0:T(8,128)(2,1)S(1)}, bf16[288,256]{1,0:T(8,128)(2,1)S(1)}, u32[]{:S(2)}, u32[]{:S(2)}) collective-permute-start(bf16[288,256]{1,0:T(8,128)(2,1)S(1)} %collective-permute-done.5), channel_id=1, source_target_pairs={{0,0},{1,17},{2,34},{3,51},{4,68},{5,85},{6,102},{7,119},{8,136},{... | collective-permute-start | bytes 442376 | tf_op jit(solution)/shard_map/ppermute | solution.py:301
  56.4 3.4 %collective-permute-done.8 = bf16[288,256]{1,0:T(8,128)(2,1)S(1)} collective-permute-done((bf16[288,256]{1,0:T(8,128)(2,1)S(1)}, bf16[288,256]{1,0:T(8,128)(2,1)S(1)}, u32[]{:S(2)}, u32[]{:S(2)}) %collective-permute-start.8) | collective-permute-done | bytes 147488 | tf_op jit(solution)/shard_map/ppermute | solution.py:301
  63.6 6.6 %collective-permute-start.12 = (bf16[288,256]{1,0:T(8,128)(2,1)S(1)}, bf16[288,256]{1,0:T(8,128)(2,1)S(1)}, u32[]{:S(2)}, u32[]{:S(2)}) collective-permute-start(bf16[288,256]{1,0:T(8,128)(2,1)S(1)} %collective-permute-done.8), channel_id=1, source_target_pairs={{0,0},{1,1},{2,2},{3,3},{4,4},{5,5},{6,6},{7,7},{8,8},{9,9},{10,10... | collective-permute-start | bytes 442376 | tf_op jit(solution)/shard_map/ppermute | solution.py:306
  76.2 6.6 %shard_map.112.rest_0_ = bf16[512,256]{1,0:T(8,128)(2,1)} custom-call(s32[18]{0:T(128)} %stack.103.index_ref, f32[64,512]{1,0:T(8,128)} %get-tuple-element.86.cos_ref, f32[64,512]{1,0:T(8,128)} %get-tuple-element.85.sin_ref, bf16[16,304,512]{2,1,0:T(8,128)(2,1)} %bitcast.74, bf16[608,256]{1,0:T(8,128)(2,1)} %copy-done.5, bf16[608,256]{1,0:T(8,128)(2,1)} %copy-done.9, ...), custom_call_target="tpu_custom_call" | custom-call | flops 1207959552 | bytes 8388608 | tf_op jit(solution)/shard_map/pallas_call | solution.py:126
  82.9 4.4 %collective-permute-start.13 = (bf16[512,256]{1,0:T(8,128)(2,1)}, bf16[512,256]{1,0:T(8,128)(2,1)S(1)}, u32[]{:S(2)}, u32[]{:S(2)}) collective-permute-start(bf16[512,256]{1,0:T(8,128)(2,1)} %shard_map.112.rest_0_), channel_id=1, source_target_pairs={{0,32},{16,48},{32,64},{48,80},{64,96},{80,112},{96,128},{112,144}... | collective-permute-start | bytes 786440 | tf_op jit(solution)/shard_map/ppermute | solution.py:48
  89.0 9.8 %collective-permute-done.13.rest_0_ = bf16[512,256]{1,0:T(8,128)(2,1)S(1)} collective-permute-done((bf16[512,256]{1,0:T(8,128)(2,1)}, bf16[512,256]{1,0:T(8,128)(2,1)S(1)}, u32[]{:S(2)}, u32[]{:S(2)}) %collective-permute-start.13) | collective-permute-done | bytes 262176 | tf_op jit(solution)/shard_map/ppermute | solution.py:48
  99.6 5.3 %collective-permute-start.15 = (bf16[512,256]{1,0:T(8,128)(2,1)S(1)}, bf16[512,256]{1,0:T(8,128)(2,1)S(1)}, u32[]{:S(2)}, u32[]{:S(2)}) collective-permute-start(bf16[512,256]{1,0:T(8,128)(2,1)S(1)} %collective-permute-done.13.rest_0_), channel_id=1, source_target_pairs={{0,32},{16,48},{32,64},{48,80},{64,96},{80,112},{96,128},{112,144}... | collective-permute-start | bytes 786440 | tf_op jit(solution)/shard_map/ppermute | solution.py:48
  107.6 3.0 %collective-permute-done.15.rest_0_ = bf16[512,256]{1,0:T(8,128)(2,1)S(1)} collective-permute-done((bf16[512,256]{1,0:T(8,128)(2,1)S(1)}, bf16[512,256]{1,0:T(8,128)(2,1)S(1)}, u32[]{:S(2)}, u32[]{:S(2)}) %collective-permute-start.15) | collective-permute-done | bytes 262176 | tf_op jit(solution)/shard_map/ppermute | solution.py:48
  110.7 3.0 %collective-permute-done.16.rest_1_ = bf16[512,256]{1,0:T(8,128)(2,1)S(1)} collective-permute-done((bf16[512,256]{1,0:T(8,128)(2,1)S(1)}, bf16[512,256]{1,0:T(8,128)(2,1)S(1)}, u32[]{:S(2)}, u32[]{:S(2)}) %collective-permute-start.16) | collective-permute-done | bytes 262176 | tf_op jit(solution)/shard_map/ppermute | solution.py:48
  118.2 3.7 %collective-permute-done.17.rest_0_ = bf16[512,256]{1,0:T(8,128)(2,1)S(1)} collective-permute-done((bf16[512,256]{1,0:T(8,128)(2,1)S(1)}, bf16[512,256]{1,0:T(8,128)(2,1)S(1)}, u32[]{:S(2)}, u32[]{:S(2)}) %collective-permute-start.17) | collective-permute-done | bytes 262176 | tf_op jit(solution)/shard_map/ppermute | solution.py:48
  128.9 10.3 %collective-permute-done.19.rest_0_ = bf16[512,256]{1,0:T(8,128)(2,1)S(1)} collective-permute-done((bf16[512,256]{1,0:T(8,128)(2,1)S(1)}, bf16[512,256]{1,0:T(8,128)(2,1)S(1)}, u32[]{:S(2)}, u32[]{:S(2)}) %collective-permute-start.19) | collective-permute-done | bytes 262176 | tf_op jit(solution)/shard_map/ppermute | solution.py:48
  140.2 6.7 %shard_map.113.q_ref = bf16[512,256]{1,0:T(8,128)(2,1)} custom-call(s32[18]{0:T(128)} %stack.104.index_ref, f32[64,512]{1,0:T(8,128)} %get-tuple-element.86.cos_ref, f32[64,512]{1,0:T(8,128)} %get-tuple-element.85.sin_ref, bf16[16,304,512]{2,1,0:T(8,128)(2,1)} %bitcast.75, bf16[8,608,256]{2,1,0:T(8,128)(2,1)} %bitcast.76), custom_call_target="tpu_custom_call" | custom-call | flops 1207959552 | bytes 8388608 | tf_op jit(solution)/shard_map/pallas_call | solution.py:126
  161.4 5.2 %collective-permute-done.22 = bf16[1,512,256]{2,1,0:T(8,128)(2,1)S(1)} collective-permute-done((bf16[1,512,256]{2,1,0:T(8,128)(2,1)S(1)}, bf16[1,512,256]{2,1,0:T(8,128)(2,1)S(1)}, u32[]{:S(2)}, u32[]{:S(2)}) %collective-permute-start.22) | collective-permute-done | bytes 262176 | tf_op jit(solution)/shard_map/ppermute | solution.py:52
  168.5 3.1 %collective-permute-start.24 = (bf16[2,512,256]{2,1,0:T(8,128)(2,1)S(1)}, bf16[2,512,256]{2,1,0:T(8,128)(2,1)S(1)}, u32[]{:S(2)}, u32[]{:S(2)}) collective-permute-start(bf16[2,512,256]{2,1,0:T(8,128)(2,1)S(1)} %pad_maximum_fusion.rest_0_), channel_id=1, source_target_pairs={{4,0},{5,1},{6,2},{7,3},{8,4},{9,5},{10,6},{11,7},{12,8},{13,9},{1... | collective-permute-start | bytes 1572872 | tf_op jit(solution)/shard_map/ppermute | solution.py:52
  171.6 6.5 %collective-permute-done.23.rest_1_ = bf16[2,512,256]{2,1,0:T(8,128)(2,1)S(1)} collective-permute-done((bf16[2,512,256]{2,1,0:T(8,128)(2,1)S(1)}, bf16[2,512,256]{2,1,0:T(8,128)(2,1)S(1)}, u32[]{:S(2)}, u32[]{:S(2)}) %collective-permute-start.23) | collective-permute-done | bytes 524320 | tf_op jit(solution)/shard_map/ppermute | solution.py:52
  189.4 11.4 %collective-permute-start.27 = (bf16[2,512,256]{2,1,0:T(8,128)(2,1)S(1)}, bf16[2,512,256]{2,1,0:T(8,128)(2,1)S(1)}, u32[]{:S(2)}, u32[]{:S(2)}) collective-permute-start(bf16[2,512,256]{2,1,0:T(8,128)(2,1)S(1)} %pad_maximum_fusion.rest_0_), channel_id=1, source_target_pairs={{0,1},{1,0},{2,3},{3,2},{4,5},{5,4},{6,7},{7,6},{8,9},{9,8},{10,11... | collective-permute-start | bytes 1572872 | tf_op jit(solution)/shard_map/ppermute | solution.py:52
  207.1 5.3 %all-to-all-start = ((f32[16,1,512]{2,1,0:T(1,128)}), f32[16,1,512]{2,1,0:T(1,128)S(1)}, u32[]{:S(2)}, u32[]{:S(2)}) async-start(f32[16,1,512]{2,1,0:T(1,128)} %broadcast_in_dim.48), calls=%async_computation | async-start | bytes 65536 | tf_op jit(solution)/shard_map/all_to_all | solution.py:391
  213.2 5.1 %all-to-all-done = f32[16,1,512]{2,1,0:T(1,128)S(1)} async-done(((f32[16,1,512]{2,1,0:T(1,128)}), f32[16,1,512]{2,1,0:T(1,128)S(1)}, u32[]{:S(2)}, u32[]{:S(2)}) %all-to-all-start) | async-done | bytes 32800 | tf_op jit(solution)/shard_map/all_to_all | solution.py:391
  (142 shorter events, 67.3 us)
Async XLA Ops:
  7.2 69.0 %all-gather.7.cloned.1.call-start = ((), (), s32[]{:S(2)}) async-start(), calls=%async_computation.1 | async-start | bytes 5292032 | tf_op jit(solution)/shard_map/all_gather | solution.py:281
  10.1 129.2 %all-gather.9.cloned.1.call-start = ((), (), s32[]{:S(2)}) async-start(), calls=%async_computation.2 | async-start | bytes 2801664 | tf_op jit(solution)/shard_map/all_gather | solution.py:305
  27.4 16.9 %collective-permute-start.3 = (bf16[608,256]{1,0:T(8,128)(2,1)S(1)}, bf16[608,256]{1,0:T(8,128)(2,1)S(1)}, u32[]{:S(2)}, u32[]{:S(2)}) collective-permute-start(bf16[608,256]{1,0:T(8,128)(2,1)S(1)} %collective-permute-done.1.rest_1_), channel_id=1, source_target_pairs={{0,32},{16,48},{32,64},{48,80},{64,96},{80,112},{96,128},{112,144}... | collective-permute-start | bytes 933896 | tf_op jit(solution)/shard_map/ppermute | solution.py:48
  30.8 13.4 %collective-permute-start.4 = (bf16[608,256]{1,0:T(8,128)(2,1)S(1)}, bf16[608,256]{1,0:T(8,128)(2,1)S(1)}, u32[]{:S(2)}, u32[]{:S(2)}) collective-permute-start(bf16[608,256]{1,0:T(8,128)(2,1)S(1)} %collective-permute-done.2.rest_2_), channel_id=1, source_target_pairs={{32,0},{48,16},{64,32},{80,48},{96,64},{112,80},{128,96},{144,112}... | collective-permute-start | bytes 933896 | tf_op jit(solution)/shard_map/ppermute | solution.py:48
  30.8 13.4 %collective-permute-start.5 = (bf16[288,256]{1,0:T(8,128)(2,1)S(1)}, bf16[288,256]{1,0:T(8,128)(2,1)S(1)}, u32[]{:S(2)}, u32[]{:S(2)}) collective-permute-start(bf16[288,256]{1,0:T(8,128)(2,1)S(1)} %bitcast.80), channel_id=1, source_target_pairs={{0,0},{1,1},{2,2},{3,3},{4,4},{5,5},{6,6},{7,7},{8,8},{9,9},{10,10... | collective-permute-start | bytes 442376 | tf_op jit(solution)/shard_map/ppermute | solution.py:294
  44.3 15.6 %collective-permute-start.6 = (bf16[608,256]{1,0:T(8,128)(2,1)S(1)}, bf16[608,256]{1,0:T(8,128)(2,1)S(1)}, u32[]{:S(2)}, u32[]{:S(2)}) collective-permute-start(bf16[608,256]{1,0:T(8,128)(2,1)S(1)} %collective-permute-done.3.rest_3_), channel_id=1, source_target_pairs={{0,32},{16,48},{32,64},{48,80},{64,96},{80,112},{96,128},{112,144}... | collective-permute-start | bytes 933896 | tf_op jit(solution)/shard_map/ppermute | solution.py:48
  46.9 13.7 %collective-permute-start.7 = (bf16[608,256]{1,0:T(8,128)(2,1)S(1)}, bf16[608,256]{1,0:T(8,128)(2,1)S(1)}, u32[]{:S(2)}, u32[]{:S(2)}) collective-permute-start(bf16[608,256]{1,0:T(8,128)(2,1)S(1)} %collective-permute-done.4.rest_4_), channel_id=1, source_target_pairs={{32,0},{48,16},{64,32},{80,48},{96,64},{112,80},{128,96},{144,112}... | collective-permute-start | bytes 933896 | tf_op jit(solution)/shard_map/ppermute | solution.py:48
  47.0 12.8 %collective-permute-start.8 = (bf16[288,256]{1,0:T(8,128)(2,1)S(1)}, bf16[288,256]{1,0:T(8,128)(2,1)S(1)}, u32[]{:S(2)}, u32[]{:S(2)}) collective-permute-start(bf16[288,256]{1,0:T(8,128)(2,1)S(1)} %collective-permute-done.5), channel_id=1, source_target_pairs={{0,0},{1,17},{2,34},{3,51},{4,68},{5,85},{6,102},{7,119},{8,136},{... | collective-permute-start | bytes 442376 | tf_op jit(solution)/shard_map/ppermute | solution.py:301
  60.7 117.3 %all-gather.11.cloned.1.call-start = ((), (), s32[]{:S(2)}) async-start(), calls=%async_computation.3 | async-start | bytes 2654208 | tf_op jit(solution)/shard_map/all_gather | solution.py:358
  60.8 10.2 %collective-permute-start.11 = (bf16[608,128]{1,0:T(8,128)(2,1)S(1)}, bf16[608,128]{1,0:T(8,128)(2,1)S(1)}, u32[]{:S(2)}, u32[]{:S(2)}) collective-permute-start(bf16[608,128]{1,0:T(8,128)(2,1)S(1)} %slice.143), channel_id=1, source_target_pairs={{32,0},{48,16},{64,32},{80,48},{96,64},{112,80},{128,96},{144,112}... | collective-permute-start | bytes 466952 | tf_op jit(solution)/shard_map/ppermute | solution.py:48
  60.9 10.1 %collective-permute-start.10 = (bf16[608,128]{1,0:T(8,128)(2,1)S(1)}, bf16[608,128]{1,0:T(8,128)(2,1)S(1)}, u32[]{:S(2)}, u32[]{:S(2)}) collective-permute-start(bf16[608,128]{1,0:T(8,128)(2,1)S(1)} %slice.142), channel_id=1, source_target_pairs={{0,32},{16,48},{32,64},{48,80},{64,96},{80,112},{96,128},{112,144}... | collective-permute-start | bytes 466952 | tf_op jit(solution)/shard_map/ppermute | solution.py:48
  82.9 15.9 %collective-permute-start.13 = (bf16[512,256]{1,0:T(8,128)(2,1)}, bf16[512,256]{1,0:T(8,128)(2,1)S(1)}, u32[]{:S(2)}, u32[]{:S(2)}) collective-permute-start(bf16[512,256]{1,0:T(8,128)(2,1)} %shard_map.112.rest_0_), channel_id=1, source_target_pairs={{0,32},{16,48},{32,64},{48,80},{64,96},{80,112},{96,128},{112,144}... | collective-permute-start | bytes 786440 | tf_op jit(solution)/shard_map/ppermute | solution.py:48
  87.3 11.5 %collective-permute-start.14 = (bf16[288,256]{1,0:T(8,128)(2,1)S(1)}, bf16[288,256]{1,0:T(8,128)(2,1)S(1)}, u32[]{:S(2)}, u32[]{:S(2)}) collective-permute-start(bf16[288,256]{1,0:T(8,128)(2,1)S(1)} %collective-permute-done.12), channel_id=1, source_target_pairs={{0,16},{16,0},{32,48},{48,32},{64,80},{80,64},{96,112},{112,96},{1... | collective-permute-start | bytes 442376 | tf_op jit(solution)/shard_map/ppermute | solution.py:48
  99.6 11.1 %collective-permute-start.15 = (bf16[512,256]{1,0:T(8,128)(2,1)S(1)}, bf16[512,256]{1,0:T(8,128)(2,1)S(1)}, u32[]{:S(2)}, u32[]{:S(2)}) collective-permute-start(bf16[512,256]{1,0:T(8,128)(2,1)S(1)} %collective-permute-done.13.rest_0_), channel_id=1, source_target_pairs={{0,32},{16,48},{32,64},{48,80},{64,96},{80,112},{96,128},{112,144}... | collective-permute-start | bytes 786440 | tf_op jit(solution)/shard_map/ppermute | solution.py:48
  104.9 8.8 %collective-permute-start.16 = (bf16[512,256]{1,0:T(8,128)(2,1)S(1)}, bf16[512,256]{1,0:T(8,128)(2,1)S(1)}, u32[]{:S(2)}, u32[]{:S(2)}) collective-permute-start(bf16[512,256]{1,0:T(8,128)(2,1)S(1)} %broadcast_select_fusion.3), channel_id=1, source_target_pairs={{0,16},{16,0},{32,48},{48,32},{64,80},{80,64},{96,112},{112,96},{1... | collective-permute-start | bytes 786440 | tf_op jit(solution)/shard_map/ppermute | solution.py:48
  124.2 15.0 %collective-permute-start.19 = (bf16[512,256]{1,0:T(8,128)(2,1)S(1)}, bf16[512,256]{1,0:T(8,128)(2,1)S(1)}, u32[]{:S(2)}, u32[]{:S(2)}) collective-permute-start(bf16[512,256]{1,0:T(8,128)(2,1)S(1)} %collective-permute-done.17.rest_0_), channel_id=1, source_target_pairs={{0,32},{16,48},{32,64},{48,80},{64,96},{80,112},{96,128},{112,144}... | collective-permute-start | bytes 786440 | tf_op jit(solution)/shard_map/ppermute | solution.py:48
  126.4 12.8 %collective-permute-start.20 = (bf16[512,256]{1,0:T(8,128)(2,1)S(1)}, bf16[512,256]{1,0:T(8,128)(2,1)S(1)}, u32[]{:S(2)}, u32[]{:S(2)}) collective-permute-start(bf16[512,256]{1,0:T(8,128)(2,1)S(1)} %broadcast_select_fusion.1), channel_id=1, source_target_pairs={{0,16},{16,0},{32,48},{48,32},{64,80},{80,64},{96,112},{112,96},{1... | collective-permute-start | bytes 786440 | tf_op jit(solution)/shard_map/ppermute | solution.py:48
  139.3 19.1 %collective-permute-start.21 = (bf16[512,256]{1,0:T(8,128)(2,1)S(1)}, bf16[512,256]{1,0:T(8,128)(2,1)S(1)}, u32[]{:S(2)}, u32[]{:S(2)}) collective-permute-start(bf16[512,256]{1,0:T(8,128)(2,1)S(1)} %broadcast_select_fusion), channel_id=1, source_target_pairs={{0,16},{16,0},{32,48},{48,32},{64,80},{80,64},{96,112},{112,96},{1... | collective-permute-start | bytes 786440 | tf_op jit(solution)/shard_map/ppermute | solution.py:48
  166.7 11.3 %collective-permute-start.23 = (bf16[2,512,256]{2,1,0:T(8,128)(2,1)S(1)}, bf16[2,512,256]{2,1,0:T(8,128)(2,1)S(1)}, u32[]{:S(2)}, u32[]{:S(2)}) collective-permute-start(bf16[2,512,256]{2,1,0:T(8,128)(2,1)S(1)} %pad_maximum_fusion.rest_0_), channel_id=1, source_target_pairs={{0,4},{1,5},{2,6},{3,7},{4,8},{5,9},{6,10},{7,11},{8,12},{9,13},{1... | collective-permute-start | bytes 1572872 | tf_op jit(solution)/shard_map/ppermute | solution.py:52
  168.5 9.5 %collective-permute-start.24 = (bf16[2,512,256]{2,1,0:T(8,128)(2,1)S(1)}, bf16[2,512,256]{2,1,0:T(8,128)(2,1)S(1)}, u32[]{:S(2)}, u32[]{:S(2)}) collective-permute-start(bf16[2,512,256]{2,1,0:T(8,128)(2,1)S(1)} %pad_maximum_fusion.rest_0_), channel_id=1, source_target_pairs={{4,0},{5,1},{6,2},{7,3},{8,4},{9,5},{10,6},{11,7},{12,8},{13,9},{1... | collective-permute-start | bytes 1572872 | tf_op jit(solution)/shard_map/ppermute | solution.py:52
  178.1 23.2 %collective-permute-start.25 = (bf16[1,512,256]{2,1,0:T(8,128)(2,1)S(1)}, bf16[1,512,256]{2,1,0:T(8,128)(2,1)S(1)}, u32[]{:S(2)}, u32[]{:S(2)}) collective-permute-start(bf16[1,512,256]{2,1,0:T(8,128)(2,1)S(1)} %slice.151), channel_id=1, source_target_pairs={{0,4},{1,5},{2,6},{3,7},{4,8},{5,9},{6,10},{7,11},{8,12},{9,13},{1... | collective-permute-start | bytes 786440 | tf_op jit(solution)/shard_map/ppermute | solution.py:52
  179.3 22.2 %collective-permute-start.26 = (bf16[1,512,256]{2,1,0:T(8,128)(2,1)S(1)}, bf16[1,512,256]{2,1,0:T(8,128)(2,1)S(1)}, u32[]{:S(2)}, u32[]{:S(2)}) collective-permute-start(bf16[1,512,256]{2,1,0:T(8,128)(2,1)S(1)} %slice.152), channel_id=1, source_target_pairs={{4,0},{5,1},{6,2},{7,3},{8,4},{9,5},{10,6},{11,7},{12,8},{13,9},{1... | collective-permute-start | bytes 786440 | tf_op jit(solution)/shard_map/ppermute | solution.py:52
  189.4 12.9 %collective-permute-start.27 = (bf16[2,512,256]{2,1,0:T(8,128)(2,1)S(1)}, bf16[2,512,256]{2,1,0:T(8,128)(2,1)S(1)}, u32[]{:S(2)}, u32[]{:S(2)}) collective-permute-start(bf16[2,512,256]{2,1,0:T(8,128)(2,1)S(1)} %pad_maximum_fusion.rest_0_), channel_id=1, source_target_pairs={{0,1},{1,0},{2,3},{3,2},{4,5},{5,4},{6,7},{7,6},{8,9},{9,8},{10,11... | collective-permute-start | bytes 1572872 | tf_op jit(solution)/shard_map/ppermute | solution.py:52
  207.1 11.1 %all-to-all-start = ((f32[16,1,512]{2,1,0:T(1,128)}), f32[16,1,512]{2,1,0:T(1,128)S(1)}, u32[]{:S(2)}, u32[]{:S(2)}) async-start(f32[16,1,512]{2,1,0:T(1,128)} %broadcast_in_dim.48), calls=%async_computation | async-start | bytes 65536 | tf_op jit(solution)/shard_map/all_to_all | solution.py:391
  (30 other events, 570.8 us)
Sparse Core Ops, SparseCore 0:
  10.2 47.9 all-gather.6
  60.8 45.0 all-gather.8
  108.3 46.7 all-gather.10

commit v4 on v3

--- a/solution.py
+++ b/solution.py
@@ -56,38 +56,46 @@
     return lax.optimization_barrier(values)
 
 
-def project_kernel(pieces, rotated, factor, index_ref, cos_ref, sin_ref, x_hbm, *rest):
-    w_refs = rest[:-6]
+def project_kernel(pieces, rotated, factor, index_ref, cos_ref, sin_ref, *rest):
+    n = len(PLACES)
+    same, other, w_refs = rest[:n], rest[n : 2 * n], rest[2 * n : -6]
     out_ref, x_ref, w_ref, acc_ref, x_sem, w_sem = rest[-6:]
     chunks, depth, rows = x_ref.shape
+    step = chunks // 4
+    length = pieces[0][0][2]
     copies = []
     for slot in range(ROUNDS):
         place = index_ref[2 + ROUNDS + slot]
         for part in range(2):
             parity = index_ref[1] if part == 0 else 1 - index_ref[1]
-            which, lead = pieces[slot]
-            source = w_refs[which] if lead is None else w_refs[which].at[lead]
+            which, start, _ = pieces[slot][part]
             copies.append(
                 pltpu.make_async_copy(
-                    source.at[pl.ds(part * depth, depth)],
-                    w_ref.at[2 * place + parity],
+                    w_refs[which].at[pl.ds(start, length)],
+                    w_ref.at[2 * place + parity, pl.ds(0, length)],
                     w_sem.at[2 * slot + part],
                 )
             )
-    step = chunks // 4
-    for k in range(4):
-        copies.append(
-            pltpu.make_async_copy(
-                x_hbm.at[pl.ds(k * step, step)], x_ref.at[pl.ds(k * step, step)], x_sem.at[k]
-            )
-        )
+    slot = 0
+    for k, places in enumerate(PLACES):
+        for j in range(len(places)):
+            place = index_ref[2 + slot]
+            for part, ref in enumerate((same[k], other[k])):
+                parity = index_ref[0] if part == 0 else 1 - index_ref[0]
+                copies.append(
+                    pltpu.make_async_copy(
+                        ref.at[j], x_ref.at[2 * place + parity], x_sem.at[2 * slot + part]
+                    )
+                )
+            slot += 1
     for copy in copies:
         copy.start()
-    for copy in copies[:-4]:
+    if length < depth:
+        w_ref[:, length:, :] = jnp.zeros((chunks, depth - length, 2 * HD), BF)
+    for copy in copies:
         copy.wait()
     squares = jnp.zeros((1, rows), F32)
     for k in range(4):
-        copies[k - 4].wait()
         here = slice(k * step, (k + 1) * step)
         side = x_ref[here, depth - EXTRA :, :].astype(F32)
         squares = squares + jnp.sum(jnp.sum(side, axis=0), axis=0, keepdims=True)
@@ -119,28 +127,28 @@
         out_ref[:, start : start + HD] = jnp.transpose(value).astype(BF)
 
 
-def project(x_all, weights, pieces, index, cos, sin, rotated, factor):
-    chunks, depth, rows = x_all.shape
+def project(chunks, weights, pieces, index, cos, sin, rotated, factor):
+    _, depth, rows = chunks[0].shape
     vmem = pl.BlockSpec(memory_space=pltpu.VMEM)
     outside = pl.BlockSpec(memory_space=pl.ANY)
     return pl.pallas_call(
         functools.partial(project_kernel, pieces, rotated, factor),
         out_shape=jax.ShapeDtypeStruct((rows, 2 * HD), BF),
         in_specs=[pl.BlockSpec(memory_space=pltpu.SMEM), vmem, vmem]
-        + [outside] * (1 + len(weights)),
+        + [outside] * (len(chunks) + len(weights)),
         out_specs=vmem,
         scratch_shapes=[
-            pltpu.VMEM((chunks, depth, rows), BF),
-            pltpu.VMEM((chunks, depth, 2 * HD), BF),
+            pltpu.VMEM((2 * ROUNDS, depth, rows), BF),
+            pltpu.VMEM((2 * ROUNDS, depth, 2 * HD), BF),
             pltpu.VMEM((2 * HD, rows), F32),
-            pltpu.SemaphoreType.DMA((4,)),
+            pltpu.SemaphoreType.DMA((2 * ROUNDS,)),
             pltpu.SemaphoreType.DMA((2 * ROUNDS,)),
         ],
         compiler_params=pltpu.CompilerParams(vmem_limit_bytes=60 << 20),
         cost_estimate=pl.CostEstimate(
             flops=2 * rows * 2 * HD * D, bytes_accessed=8 << 20, transcendentals=0
         ),
-    )(index, cos, sin, x_all, *weights)
+    )(index, cos, sin, *chunks, *weights)
 
 
 def attend_kernel(distances, first, last, low_ref, q_ref, *rest):
@@ -214,9 +222,17 @@
 
 def output_kernel(index_ref, *rest):
     n = len(PLACES)
-    same, other = rest[:n], rest[n : 2 * n]
-    w_ref, out_ref, square_ref = rest[2 * n :]
+    same, other, w_refs = rest[:n], rest[n : 2 * n], rest[2 * n : -4]
+    out_ref, square_ref, w_ref, sem = rest[-4:]
     features = out_ref.shape[0]
+    copies = []
+    for slot in range(ROUNDS):
+        place = index_ref[2 + ROUNDS + slot]
+        copies.append(pltpu.make_async_copy(w_refs[slot], w_ref.at[place], sem.at[slot]))
+    for copy in copies:
+        copy.start()
+    for copy in copies:
+        copy.wait()
     slot = 0
     for k, places in enumerate(PLACES):
         for j in range(len(places)):
@@ -224,9 +240,9 @@
             place = index_ref[2 + slot]
             for part, ref in enumerate((same[k], other[k])):
                 parity = index_ref[0] if part == 0 else 1 - index_ref[0]
-                swapped = jnp.where(parity == index_ref[1], 0, 1)
+                swapped = jnp.where(parity == index_ref[1], 0, features)
                 product = lax.dot_general(
-                    w_ref[2 * place + swapped],
+                    w_ref[place, pl.ds(pl.multiple_of(swapped, 16), features), :],
                     ref[j],
                     (((1,), (1,)), ((), ())),
                     preferred_element_type=F32,
@@ -245,21 +261,28 @@
 
 def output(chunks, weights, index):
     rows = chunks[0].shape[1]
-    features = weights.shape[1]
+    features = weights[0].shape[0] // 2
     vmem = pl.BlockSpec(memory_space=pltpu.VMEM)
+    outside = pl.BlockSpec(memory_space=pl.ANY)
     return pl.pallas_call(
         output_kernel,
         out_shape=(
             jax.ShapeDtypeStruct((features, rows), F32),
             jax.ShapeDtypeStruct((1, rows), F32),
         ),
-        in_specs=[pl.BlockSpec(memory_space=pltpu.SMEM)] + [vmem] * (len(chunks) + 1),
+        in_specs=[pl.BlockSpec(memory_space=pltpu.SMEM)]
+        + [vmem] * len(chunks)
+        + [outside] * len(weights),
         out_specs=(vmem, vmem),
-        compiler_params=pltpu.CompilerParams(vmem_limit_bytes=10 << 20),
+        scratch_shapes=[
+            pltpu.VMEM((ROUNDS, 2 * features, 2 * HD), BF),
+            pltpu.SemaphoreType.DMA((ROUNDS,)),
+        ],
+        compiler_params=pltpu.CompilerParams(vmem_limit_bytes=12 << 20),
         cost_estimate=pl.CostEstimate(
             flops=2 * rows * features * 4096, bytes_accessed=8 << 20, transcendentals=0
         ),
-    )(index, *chunks, weights)
+    )(index, *chunks, *weights)
 
 
 def shards(tokens, pre_gain, post_gain, w_query, w_key, w_value, w_out, segment_ids, page_table):
@@ -278,8 +301,9 @@
     side = jnp.concatenate(
         [upper.astype(BF), lower.astype(BF), jnp.zeros((EXTRA - 2, rows), BF)], axis=0
     )
-    x_all = lax.all_gather(jnp.concatenate([gained, side], axis=0), "mp", axis=0)
+    x_block = jnp.concatenate([gained, side], axis=0)[None]
     depth = features + EXTRA
+    q_from = 2 * depth
 
     lane = jnp.arange(2 * HD, dtype=jnp.int32)
     marked = 2 * (SEGS - 1)
@@ -289,25 +313,33 @@
     digits = jnp.where(lane < SEGS - 1, upper_digit, counts - 16.0 * upper_digit).astype(BF)
     digits = jnp.pad(digits[None, :], ((2, EXTRA - 3), (0, 0)))
     kv_own = jnp.concatenate([jnp.concatenate([w_key, w_value], axis=1), digits], axis=0)
-    start = jnp.concatenate([kv_own, move(kv_own, ACROSS)], axis=0)
+    start = jnp.concatenate([kv_own, move(kv_own, ACROSS), w_query], axis=0)
+    x_pair = jnp.concatenate([x_block, shift(x_block, SIDE)], axis=0)
+
     ring = {0: start, 1: move(start, AHEAD), -1: move(start, BEHIND)}
-    turned = lax.ppermute(w_out.T, ("seq", "mp"), TURNS[0])
+    x_up, x_down = shift(x_pair, UP), shift(x_pair, DOWN)
+    x_swaps = [shift(x_pair, SWAP)]
+    cross_near = move(
+        jnp.concatenate([w_query, ring[1][q_from:], ring[-1][q_from:]], axis=0), ACROSS
+    )
     ring[2] = move(ring[1], AHEAD)
     ring[-2] = move(ring[-1], BEHIND)
-    ring[2], ring[-2], turned = tie(ring[2], ring[-2], turned)
-    q_own = jnp.pad(w_query, ((0, EXTRA), (0, 0)))
-    q_own, _ = tie(q_own, ring[1])
-    q_pair = jnp.concatenate([q_own, move(q_own, ACROSS)], axis=0)
-    turned = lax.ppermute(turned, ("seq", "mp"), TURNS[1])
+    ring[2], ring[-2], x_up, x_down, x_swaps[0] = tie(ring[2], ring[-2], x_up, x_down, x_swaps[0])
+    x_swaps += [shift(x_up, SWAP), shift(x_down, SWAP)]
+    x_far = [shift(x_up[:1], UP), shift(x_down[1:], DOWN)]
+    cross_next = move(jnp.concatenate([ring[2][q_from:], ring[-2][q_from:]], axis=0), ACROSS)
     ring[3] = move(ring[2], AHEAD)
     ring[-3] = move(ring[-2], BEHIND)
-    ring[3], ring[-3], turned, q_pair = tie(ring[3], ring[-3], turned, q_pair)
-    q_all = lax.all_gather(q_pair, "seq", axis=0, axis_index_groups=COLUMNS)
-    turned = lax.ppermute(turned, ("seq", "mp"), TURNS[2])
-    last = move(ring[3][:, :HD], AHEAD)
-    ring[4] = jnp.concatenate([last, move(ring[-3][:, HD:], BEHIND)], axis=1)
-    ring[4], turned = tie(ring[4], turned)
-    facing_out = move(turned, ACROSS)
+    turned = lax.ppermute(w_out.T, ("seq", "mp"), TURNS[0])
+    (ring[3], ring[-3], cross_near, x_far[0], x_far[1], x_swaps[1], x_swaps[2], turned) = tie(
+        ring[3], ring[-3], cross_near, x_far[0], x_far[1], x_swaps[1], x_swaps[2], turned
+    )
+    x_swaps += [shift(x_far[0], SWAP), shift(x_far[1], SWAP)]
+    ring[4] = move(ring[3][:q_from], AHEAD)
+    ring[-4] = move(ring[-3][q_from:], BEHIND)
+    turned = lax.ppermute(turned, ("seq", "mp"), TURNS[1])
+    ring[4], ring[-4], cross_next, turned = tie(ring[4], ring[-4], cross_next, turned)
+    x_chunks = [x_pair, x_up, x_down, *x_far, *x_swaps]
 
     mp_index = lax.axis_index("mp")
     y = mp_index // 4
@@ -325,8 +357,15 @@
     steps = [0, 1, -1, 2, -2, 3, -3, 4]
     index = index_of(steps, z)
     kv_weights = [ring[step] for step in steps]
-    kv_pieces = tuple((k, None) for k in range(ROUNDS))
-    q_pieces = tuple((0, k) for k in range(ROUNDS))
+    kv_pieces = tuple(((k, 0, depth), (k, depth, depth)) for k in range(ROUNDS))
+    q_weights = kv_weights[:7] + [ring[-4], w_query, cross_near, cross_next]
+    crossings = [(9, k * features) for k in range(3)]
+    crossings += [(10, k * features) for k in range(2)]
+    crossings += [(11, k * features) for k in range(3)]
+    own_places = [(8, 0)] + [(k, q_from) for k in range(1, 7)] + [(7, 0)]
+    q_pieces = tuple(
+        ((*own_places[k], features), (*crossings[k], features)) for k in range(ROUNDS)
+    )
 
     n_marks = 2 * (SEGS - 1)
     marks = jnp.zeros((n_marks,), F32)
@@ -346,46 +385,67 @@
     cos = jnp.cos(angles)
     sin = jnp.sin(angles)
 
-    kv = project(x_all, kv_weights, kv_pieces, index, cos, sin, (True, False), 1.0)
-
-    straight, crossed, current = [kv], [None], kv
+    kv = project(x_chunks, kv_weights, kv_pieces, index, cos, sin, (True, False), 1.0)
+
+    cross_last = move(
+        jnp.concatenate([ring[3][q_from:], ring[-3][q_from:], ring[-4]], axis=0), ACROSS
+    )
+    turned = lax.ppermute(turned, ("seq", "mp"), TURNS[2])
+    straight, crossed, current, state = [kv], [None], kv, None
+    out_blocks = {}
     for step in range(4):
         following = move(current, LATER)
         chosen = jnp.where(h == 0, current, following)
         if step == 0:
-            following, chosen, facing_out = tie(following, chosen, facing_out)
-            out_pair = jnp.concatenate([turned, facing_out], axis=0)
-            out_all = lax.all_gather(out_pair, "seq", axis=0, axis_index_groups=COLUMNS)
+            following, chosen, turned = tie(following, chosen, turned)
+            out_blocks[0] = jnp.concatenate([turned, move(turned, ACROSS)], axis=0)
+        elif step == 1:
+            following, chosen, crossed[1], cross_last, out_blocks[0] = tie(
+                following, chosen, crossed[1], cross_last, out_blocks[0]
+            )
+            out_blocks[-1] = move(out_blocks[0], BEHIND)
+            queries = project(
+                x_chunks,
+                q_weights + [cross_last],
+                q_pieces,
+                index_of(steps[:7] + [-4], z),
+                cos,
+                sin,
+                (True, True),
+                float(D // HQ) ** (-0.5),
+            )
+            state = attend(low, queries, [kv], [0], None)
         else:
-            following, chosen, crossed[step] = tie(following, chosen, crossed[step])
+            following, chosen, crossed[step], out_blocks[1 - step], *state = tie(
+                following, chosen, crossed[step], out_blocks[1 - step], *state
+            )
+            k = step - 1
+            state = attend(low, queries, [straight[k], crossed[k]], [2 * k, 2 * k - 1], state)
+            if step == 2:
+                out_blocks[-2] = move(out_blocks[-1], BEHIND)
         straight.append(following)
         crossed.append(move(chosen, ACROSS))
         current = following
-    q_all, straight[-1] = tie(q_all, straight[-1])
-    queries = project(
-        x_all,
-        [q_all],
-        q_pieces,
-        index_of([-k for k in range(ROUNDS)], 0),
-        cos,
-        sin,
-        (True, True),
-        float(D // HQ) ** (-0.5),
-    )
-    state = attend(low, queries, [kv], [0], None)
-    for k in range(1, 5):
-        state = attend(low, queries, [straight[k], crossed[k]], [2 * k, 2 * k - 1], state)
+    out_blocks[1] = move(out_blocks[0], AHEAD)
+    out_blocks[-3] = move(out_blocks[-2], BEHIND)
+    state = attend(low, queries, [straight[3], crossed[3]], [6, 5], state)
+    crossed[4], out_blocks[1], out_blocks[-3] = tie(crossed[4], out_blocks[1], out_blocks[-3])
+    state = attend(low, queries, [straight[4], crossed[4]], [8, 7], state)
 
     a_block = state[None]
     a_pair = jnp.concatenate([a_block, shift(a_block, SIDE)], axis=0)
+    out_blocks[2] = move(out_blocks[1], AHEAD)
+    out_blocks[-4] = move(out_blocks[-3], BEHIND)
     a_up, a_down = shift(a_pair, UP), shift(a_pair, DOWN)
-    a_up, a_down, out_all = tie(a_up, a_down, out_all)
+    a_up, a_down, out_blocks[2], out_blocks[-4] = tie(a_up, a_down, out_blocks[2], out_blocks[-4])
+    out_blocks[3] = move(out_blocks[2], AHEAD)
     a_far = [shift(a_up[:1], UP), shift(a_down[1:], DOWN)]
     a_swaps = [shift(block, SWAP) for block in (a_pair, a_up, a_down, *a_far)]
+    out_steps = steps[:7] + [-4]
     share, partial = output(
         [a_pair, a_up, a_down, *a_far, *a_swaps],
-        out_all.reshape(2 * ROUNDS, features, 2 * HD),
-        index,
+        [out_blocks[step] for step in out_steps],
+        index_of(out_steps, z),
     )
     everywhere = jnp.broadcast_to(partial, (lax.axis_size("mp"), rows))
     square_total = jnp.sum(lax.all_to_all(everywhere, "mp", 0, 0, tiled=True), axis=0)

time: 226 us -> 253 us (1.12)
  the two profiles are of different devices: /device:TPU:101 before, /device:TPU:1 now
where the time goes in v4:
time: 253 us; the launch traced here: 248 us
  starting transfers between devices  123 us (49%)
  waiting for transfers between devices  66.7 us (26%)
  Pallas kernels  30.4 us (12%)
  between operations  9.54 us (4%)
  local copies, waits for them, and re-layouts  9.45 us (4%)
  other arithmetic  8.91 us (4%)
    ppermute x28, starting transfers between devices, move(): return lax.ppermute(block, 'seq', perm)  74 us
    ppermute x28, waiting for transfers between devices, move(): return lax.ppermute(block, 'seq', perm)  48.7 us
    ppermute x20, starting transfers between devices, shift(): return lax.ppermute(block, 'mp', perm)  39 us
    pallas_call x2, Pallas kernels, project(): pl.pallas_call(functools.partial(project_kernel, pieces, rotated, factor)...  13.6 us
    ppermute x20, waiting for transfers between devices, shift(): return lax.ppermute(block, 'mp', perm)  13.5 us
    pallas_call x5, Pallas kernels, attend(): pl.pallas_call(functools.partial(attend_kernel, tuple(distances), first,...  13.4 us
  transfers between devices with their start and end apart: 52, of which 17 were waited for; matrix products, arithmetic and copies ran while one was open for 4% of the time, Pallas kernels for 7%

profile of v4, /device:TPU:1, one launch (start us, length us, event | category | flops | bytes accessed | tf_op | source)
XLA Modules:
  0.0 248.2 jit_solution(15338042686410278004)
XLA Ops:
  8.4 8.9 %collective-permute-done = bf16[304,256]{1,0:T(8,128)(2,1)S(1)} collective-permute-done((bf16[304,256]{1,0:T(8,128)(2,1)S(1)}, bf16[304,256]{1,0:T(8,128)(2,1)S(1)}, u32[]{:S(2)}, u32[]{:S(2)}) %collective-permute-start) | collective-permute-done | bytes 155680 | tf_op jit(solution)/shard_map/ppermute | solution.py:48
  19.7 4.0 %collective-permute-start.2 = (bf16[896,256]{1,0:T(8,128)(2,1)S(1)}, bf16[896,256]{1,0:T(8,128)(2,1)S(1)}, u32[]{:S(2)}, u32[]{:S(2)}) collective-permute-start(bf16[896,256]{1,0:T(8,128)(2,1)S(1)} %pad_maximum_fusion.2.rest_10_), channel_id=1, source_target_pairs={{32,0},{48,16},{64,32},{80,48},{96,64},{112,80},{128,96},{144,112}... | collective-permute-start | bytes 1376264 | tf_op jit(solution)/shard_map/ppermute | solution.py:48
  29.0 4.0 %collective-permute-done.1.rest_11_ = bf16[896,256]{1,0:T(8,128)(2,1)S(1)} collective-permute-done((bf16[896,256]{1,0:T(8,128)(2,1)S(1)}, bf16[896,256]{1,0:T(8,128)(2,1)S(1)}, u32[]{:S(2)}, u32[]{:S(2)}) %collective-permute-start.1) | collective-permute-done | bytes 458784 | tf_op jit(solution)/shard_map/ppermute | solution.py:48
  39.5 4.5 %collective-permute-done.3.rest_13_ = bf16[896,256]{1,0:T(8,128)(2,1)S(1)} collective-permute-done((bf16[896,256]{1,0:T(8,128)(2,1)S(1)}, bf16[896,256]{1,0:T(8,128)(2,1)S(1)}, u32[]{:S(2)}, u32[]{:S(2)}) %collective-permute-start.3) | collective-permute-done | bytes 458784 | tf_op jit(solution)/shard_map/ppermute | solution.py:48
  50.1 8.3 %collective-permute-start.10 = (bf16[896,256]{1,0:T(8,128)(2,1)S(1)}, bf16[896,256]{1,0:T(8,128)(2,1)S(1)}, u32[]{:S(2)}, u32[]{:S(2)}) collective-permute-start(bf16[896,256]{1,0:T(8,128)(2,1)S(1)} %collective-permute-done.4.rest_14_), channel_id=1, source_target_pairs={{32,0},{48,16},{64,32},{80,48},{96,64},{112,80},{128,96},{144,112}... | collective-permute-start | bytes 1376264 | tf_op jit(solution)/shard_map/ppermute | solution.py:48
  59.9 5.8 %collective-permute-done.13.rest_4_ = bf16[1,304,512]{2,1,0:T(8,128)(2,1)S(1)} collective-permute-done((bf16[1,304,512]{2,1,0:T(8,128)(2,1)S(1)}, bf16[1,304,512]{2,1,0:T(8,128)(2,1)S(1)}, u32[]{:S(2)}, u32[]{:S(2)}) %collective-permute-start.13) | collective-permute-done | bytes 311328 | tf_op jit(solution)/shard_map/ppermute | solution.py:52
  75.8 3.6 %collective-permute-start.20 = (bf16[288,256]{1,0:T(8,128)(2,1)}, bf16[288,256]{1,0:T(8,128)(2,1)S(1)}, u32[]{:S(2)}, u32[]{:S(2)}) collective-permute-start(bf16[288,256]{1,0:T(8,128)(2,1)} %collective-permute-done.16), channel_id=1, source_target_pairs={{0,0},{1,17},{2,34},{3,51},{4,68},{5,85},{6,102},{7,119},{8,136},{... | collective-permute-start | bytes 442376 | tf_op jit(solution)/shard_map/ppermute | solution.py:340
  89.3 6.8 %shard_map.112.rest_0_ = bf16[512,256]{1,0:T(8,128)(2,1)} custom-call(s32[18]{0:T(128)} %stack.134.index_ref, f32[64,512]{1,0:T(8,128)} %get-tuple-element.120.cos_ref, f32[64,512]{1,0:T(8,128)} %get-tuple-element.119.sin_ref, bf16[2,304,512]{2,1,0:T(8,128)(2,1)} %copy-done.8, bf16[2,304,512]{2,1,0:T(8,128)(2,1)} %copy-done.11, ...), custom_call_target="tpu_custom_call" | custom-call | flops 1207959552 | bytes 8388608 | tf_op jit(solution)/shard_map/pallas_call | solution.py:134
  96.1 5.0 %collective-permute-start.23 = (bf16[512,256]{1,0:T(8,128)(2,1)}, bf16[512,256]{1,0:T(8,128)(2,1)S(1)}, u32[]{:S(2)}, u32[]{:S(2)}) collective-permute-start(bf16[512,256]{1,0:T(8,128)(2,1)} %shard_map.112.rest_0_), channel_id=1, source_target_pairs={{0,32},{16,48},{32,64},{48,80},{64,96},{80,112},{96,128},{112,144}... | collective-permute-start | bytes 786440 | tf_op jit(solution)/shard_map/ppermute | solution.py:48
  104.8 5.3 %collective-permute-start.28 = (bf16[288,256]{1,0:T(8,128)(2,1)S(1)}, bf16[288,256]{1,0:T(8,128)(2,1)S(1)}, u32[]{:S(2)}, u32[]{:S(2)}) collective-permute-start(bf16[288,256]{1,0:T(8,128)(2,1)S(1)} %collective-permute-done.24), channel_id=1, source_target_pairs={{0,16},{16,0},{32,48},{48,32},{64,80},{80,64},{96,112},{112,96},{1... | collective-permute-start | bytes 442376 | tf_op jit(solution)/shard_map/ppermute | solution.py:48
  110.1 7.6 %collective-permute-start.25 = (bf16[512,256]{1,0:T(8,128)(2,1)S(1)}, bf16[512,256]{1,0:T(8,128)(2,1)S(1)}, u32[]{:S(2)}, u32[]{:S(2)}) collective-permute-start(bf16[512,256]{1,0:T(8,128)(2,1)S(1)} %collective-permute-done.23.rest_0_), channel_id=1, source_target_pairs={{0,32},{16,48},{32,64},{48,80},{64,96},{80,112},{96,128},{112,144}... | collective-permute-start | bytes 786440 | tf_op jit(solution)/shard_map/ppermute | solution.py:48
  123.5 7.5 %collective-permute-done.27.rest_21_ = bf16[864,256]{1,0:T(8,128)(2,1)S(1)} collective-permute-done((bf16[864,256]{1,0:T(8,128)(2,1)S(1)}, bf16[864,256]{1,0:T(8,128)(2,1)S(1)}, u32[]{:S(2)}, u32[]{:S(2)}) %collective-permute-start.27) | collective-permute-done | bytes 442400 | tf_op jit(solution)/shard_map/ppermute | solution.py:48
  130.9 5.6 %collective-permute-done.26.rest_1_ = bf16[512,256]{1,0:T(8,128)(2,1)S(1)} collective-permute-done((bf16[512,256]{1,0:T(8,128)(2,1)S(1)}, bf16[512,256]{1,0:T(8,128)(2,1)S(1)}, u32[]{:S(2)}, u32[]{:S(2)}) %collective-permute-start.26) | collective-permute-done | bytes 262176 | tf_op jit(solution)/shard_map/ppermute | solution.py:48
  138.8 6.8 %shard_map.113.q_ref = bf16[512,256]{1,0:T(8,128)(2,1)} custom-call(s32[18]{0:T(128)} %stack.132.index_ref, f32[64,512]{1,0:T(8,128)} %get-tuple-element.120.cos_ref, f32[64,512]{1,0:T(8,128)} %get-tuple-element.119.sin_ref, bf16[2,304,512]{2,1,0:T(8,128)(2,1)} %copy-done.8, bf16[2,304,512]{2,1,0:T(8,128)(2,1)} %copy-done.11, ...), custom_call_target="tpu_custom_call" | custom-call | flops 1207959552 | bytes 8388608 | tf_op jit(solution)/shard_map/pallas_call | solution.py:134
  148.6 5.2 %collective-permute-start.32 = (bf16[512,256]{1,0:T(8,128)(2,1)S(1)}, bf16[512,256]{1,0:T(8,128)(2,1)S(1)}, u32[]{:S(2)}, u32[]{:S(2)}) collective-permute-start(bf16[512,256]{1,0:T(8,128)(2,1)S(1)} %collective-permute-done.29.rest_0_), channel_id=1, source_target_pairs={{0,32},{16,48},{32,64},{48,80},{64,96},{80,112},{96,128},{112,144}... | collective-permute-start | bytes 786440 | tf_op jit(solution)/shard_map/ppermute | solution.py:48
  156.6 12.9 %collective-permute-start.33 = (bf16[512,256]{1,0:T(8,128)(2,1)S(1)}, bf16[512,256]{1,0:T(8,128)(2,1)S(1)}, u32[]{:S(2)}, u32[]{:S(2)}) collective-permute-start(bf16[512,256]{1,0:T(8,128)(2,1)S(1)} %broadcast_select_fusion.1), channel_id=1, source_target_pairs={{0,16},{16,0},{32,48},{48,32},{64,80},{80,64},{96,112},{112,96},{1... | collective-permute-start | bytes 786440 | tf_op jit(solution)/shard_map/ppermute | solution.py:48
  173.4 3.6 %collective-permute-start.35 = (bf16[512,256]{1,0:T(8,128)(2,1)S(1)}, bf16[512,256]{1,0:T(8,128)(2,1)S(1)}, u32[]{:S(2)}, u32[]{:S(2)}) collective-permute-start(bf16[512,256]{1,0:T(8,128)(2,1)S(1)} %broadcast_select_fusion), channel_id=1, source_target_pairs={{0,16},{16,0},{32,48},{48,32},{64,80},{80,64},{96,112},{112,96},{1... | collective-permute-start | bytes 786440 | tf_op jit(solution)/shard_map/ppermute | solution.py:48
  188.3 3.8 %collective-permute-done.38 = bf16[1,512,256]{2,1,0:T(8,128)(2,1)S(1)} collective-permute-done((bf16[1,512,256]{2,1,0:T(8,128)(2,1)S(1)}, bf16[1,512,256]{2,1,0:T(8,128)(2,1)S(1)}, u32[]{:S(2)}, u32[]{:S(2)}) %collective-permute-start.38) | collective-permute-done | bytes 262176 | tf_op jit(solution)/shard_map/ppermute | solution.py:52
  197.8 5.7 %collective-permute-start.45 = (bf16[2,512,256]{2,1,0:T(8,128)(2,1)S(1)}, bf16[2,512,256]{2,1,0:T(8,128)(2,1)S(1)}, u32[]{:S(2)}, u32[]{:S(2)}) collective-permute-start(bf16[2,512,256]{2,1,0:T(8,128)(2,1)S(1)} %pad_maximum_fusion.1.rest_0_), channel_id=1, source_target_pairs={{0,1},{1,0},{2,3},{3,2},{4,5},{5,4},{6,7},{7,6},{8,9},{9,8},{10,11... | collective-permute-start | bytes 1572872 | tf_op jit(solution)/shard_map/ppermute | solution.py:52
  215.4 7.4 %collective-permute-start.46 = (bf16[2,512,256]{2,1,0:T(8,128)(2,1)S(1)}, bf16[2,512,256]{2,1,0:T(8,128)(2,1)S(1)}, u32[]{:S(2)}, u32[]{:S(2)}) collective-permute-start(bf16[2,512,256]{2,1,0:T(8,128)(2,1)S(1)} %collective-permute-done.39.rest_1_), channel_id=1, source_target_pairs={{0,1},{1,0},{2,3},{3,2},{4,5},{5,4},{6,7},{7,6},{8,9},{9,8},{10,11... | collective-permute-start | bytes 1572872 | tf_op jit(solution)/shard_map/ppermute | solution.py:52
  224.9 7.7 %collective-permute-done.50.rest_15_ = bf16[576,256]{1,0:T(8,128)(2,1)S(1)} collective-permute-done((bf16[576,256]{1,0:T(8,128)(2,1)}, bf16[576,256]{1,0:T(8,128)(2,1)S(1)}, u32[]{:S(2)}, u32[]{:S(2)}) %collective-permute-start.50) | collective-permute-done | bytes 294944 | tf_op jit(solution)/shard_map/ppermute | solution.py:48
  232.7 3.4 %shard_map.119 = (f32[288,512]{1,0:T(8,128)S(1)}, f32[1,512]{1,0:T(1,128)S(1)}) custom-call(s32[18]{0:T(128)S(1)} %copy-done.7, bf16[2,512,256]{2,1,0:T(8,128)(2,1)S(1)} %pad_maximum_fusion.1.rest_0_, bf16[2,512,256]{2,1,0:T(8,128)(2,1)S(1)} %collective-permute-done.39.rest_1_, bf16[2,512,256]{2,1,0:T(8,128)(2,1)S(1)} %collective-permute-done.40.rest_2_, ...), custom_call_target="tpu_custom_call" | custom-call | flops 1207959552 | bytes 8388608 | tf_op jit(solution)/shard_map/pallas_call | solution.py:267
  236.7 4.5 %all-to-all-start = ((f32[16,1,512]{2,1,0:T(1,128)}), f32[16,1,512]{2,1,0:T(1,128)S(1)}, u32[]{:S(2)}, u32[]{:S(2)}) async-start(f32[16,1,512]{2,1,0:T(1,128)} %broadcast_in_dim.52), calls=%async_computation | async-start | bytes 65536 | tf_op jit(solution)/shard_map/all_to_all | solution.py:451
  243.0 4.1 %all-to-all-done = f32[16,1,512]{2,1,0:T(1,128)S(1)} async-done(((f32[16,1,512]{2,1,0:T(1,128)}), f32[16,1,512]{2,1,0:T(1,128)S(1)}, u32[]{:S(2)}, u32[]{:S(2)}) %all-to-all-start) | async-done | bytes 32800 | tf_op jit(solution)/shard_map/all_to_all | solution.py:451
  (224 shorter events, 96.9 us)
Async XLA Ops:
  2.6 21.1 %collective-permute-start.5 = (bf16[1,304,512]{2,1,0:T(8,128)(2,1)S(1)}, bf16[1,304,512]{2,1,0:T(8,128)(2,1)S(1)}, u32[]{:S(2)}, u32[]{:S(2)}) collective-permute-start(bf16[1,304,512]{2,1,0:T(8,128)(2,1)S(1)} %maximum_bitcast_fusion), channel_id=1, source_target_pairs={{0,2},{1,3},{2,0},{3,1},{4,6},{5,7},{6,4},{7,5},{8,10},{9,11},{10,... | collective-permute-start | bytes 933896 | tf_op jit(solution)/shard_map/ppermute | solution.py:52
  18.0 14.9 %collective-permute-start.1 = (bf16[896,256]{1,0:T(8,128)(2,1)S(1)}, bf16[896,256]{1,0:T(8,128)(2,1)S(1)}, u32[]{:S(2)}, u32[]{:S(2)}) collective-permute-start(bf16[896,256]{1,0:T(8,128)(2,1)S(1)} %pad_maximum_fusion.2.rest_10_), channel_id=1, source_target_pairs={{0,32},{16,48},{32,64},{48,80},{64,96},{80,112},{96,128},{112,144}... | collective-permute-start | bytes 1376264 | tf_op jit(solution)/shard_map/ppermute | solution.py:48
  19.7 13.2 %collective-permute-start.2 = (bf16[896,256]{1,0:T(8,128)(2,1)S(1)}, bf16[896,256]{1,0:T(8,128)(2,1)S(1)}, u32[]{:S(2)}, u32[]{:S(2)}) collective-permute-start(bf16[896,256]{1,0:T(8,128)(2,1)S(1)} %pad_maximum_fusion.2.rest_10_), channel_id=1, source_target_pairs={{32,0},{48,16},{64,32},{80,48},{96,64},{112,80},{128,96},{144,112}... | collective-permute-start | bytes 1376264 | tf_op jit(solution)/shard_map/ppermute | solution.py:48
  23.8 15.1 %collective-permute-start.6 = (bf16[2,304,512]{2,1,0:T(8,128)(2,1)S(1)}, bf16[2,304,512]{2,1,0:T(8,128)(2,1)S(1)}, u32[]{:S(2)}, u32[]{:S(2)}) collective-permute-start(bf16[2,304,512]{2,1,0:T(8,128)(2,1)S(1)} %pad_maximum_fusion.rest_0_), channel_id=1, source_target_pairs={{0,4},{1,5},{2,6},{3,7},{4,8},{5,9},{6,10},{7,11},{8,12},{9,13},{1... | collective-permute-start | bytes 1867784 | tf_op jit(solution)/shard_map/ppermute | solution.py:52
  25.2 14.3 %collective-permute-start.7 = (bf16[2,304,512]{2,1,0:T(8,128)(2,1)S(1)}, bf16[2,304,512]{2,1,0:T(8,128)(2,1)S(1)}, u32[]{:S(2)}, u32[]{:S(2)}) collective-permute-start(bf16[2,304,512]{2,1,0:T(8,128)(2,1)S(1)} %pad_maximum_fusion.rest_0_), channel_id=1, source_target_pairs={{4,0},{5,1},{6,2},{7,3},{8,4},{9,5},{10,6},{11,7},{12,8},{13,9},{1... | collective-permute-start | bytes 1867784 | tf_op jit(solution)/shard_map/ppermute | solution.py:52
  26.7 12.7 %collective-permute-start.8 = (bf16[2,304,512]{2,1,0:T(8,128)(2,1)S(1)}, bf16[2,304,512]{2,1,0:T(8,128)(2,1)S(1)}, u32[]{:S(2)}, u32[]{:S(2)}) collective-permute-start(bf16[2,304,512]{2,1,0:T(8,128)(2,1)S(1)} %pad_maximum_fusion.rest_0_), channel_id=1, source_target_pairs={{0,1},{1,0},{2,3},{3,2},{4,5},{5,4},{6,7},{7,6},{8,9},{9,8},{10,11... | collective-permute-start | bytes 1867784 | tf_op jit(solution)/shard_map/ppermute | solution.py:52
  39.0 19.4 %collective-permute-start.11 = (bf16[864,256]{1,0:T(8,128)(2,1)S(1)}, bf16[864,256]{1,0:T(8,128)(2,1)S(1)}, u32[]{:S(2)}, u32[]{:S(2)}) collective-permute-start(bf16[864,256]{1,0:T(8,128)(2,1)S(1)} %pad_maximum_fusion.3), channel_id=1, source_target_pairs={{0,16},{16,0},{32,48},{48,32},{64,80},{80,64},{96,112},{112,96},{1... | collective-permute-start | bytes 1327112 | tf_op jit(solution)/shard_map/ppermute | solution.py:48
  44.0 14.4 %collective-permute-start.12 = (bf16[1,304,512]{2,1,0:T(8,128)(2,1)S(1)}, bf16[1,304,512]{2,1,0:T(8,128)(2,1)S(1)}, u32[]{:S(2)}, u32[]{:S(2)}) collective-permute-start(bf16[1,304,512]{2,1,0:T(8,128)(2,1)S(1)} %slice.162), channel_id=1, source_target_pairs={{0,4},{1,5},{2,6},{3,7},{4,8},{5,9},{6,10},{7,11},{8,12},{9,13},{1... | collective-permute-start | bytes 933896 | tf_op jit(solution)/shard_map/ppermute | solution.py:52
  45.4 24.6 %collective-permute-start.14 = (bf16[2,304,512]{2,1,0:T(8,128)(2,1)S(1)}, bf16[2,304,512]{2,1,0:T(8,128)(2,1)S(1)}, u32[]{:S(2)}, u32[]{:S(2)}) collective-permute-start(bf16[2,304,512]{2,1,0:T(8,128)(2,1)S(1)} %collective-permute-done.6.rest_1_), channel_id=1, source_target_pairs={{0,1},{1,0},{2,3},{3,2},{4,5},{5,4},{6,7},{7,6},{8,9},{9,8},{10,11... | collective-permute-start | bytes 1867784 | tf_op jit(solution)/shard_map/ppermute | solution.py:52
  48.8 21.2 %collective-permute-start.15 = (bf16[2,304,512]{2,1,0:T(8,128)(2,1)S(1)}, bf16[2,304,512]{2,1,0:T(8,128)(2,1)S(1)}, u32[]{:S(2)}, u32[]{:S(2)}) collective-permute-start(bf16[2,304,512]{2,1,0:T(8,128)(2,1)S(1)} %collective-permute-done.7.rest_2_), channel_id=1, source_target_pairs={{0,1},{1,0},{2,3},{3,2},{4,5},{5,4},{6,7},{7,6},{8,9},{9,8},{10,11... | collective-permute-start | bytes 1867784 | tf_op jit(solution)/shard_map/ppermute | solution.py:52
  50.1 16.7 %collective-permute-start.10 = (bf16[896,256]{1,0:T(8,128)(2,1)S(1)}, bf16[896,256]{1,0:T(8,128)(2,1)S(1)}, u32[]{:S(2)}, u32[]{:S(2)}) collective-permute-start(bf16[896,256]{1,0:T(8,128)(2,1)S(1)} %collective-permute-done.4.rest_14_), channel_id=1, source_target_pairs={{32,0},{48,16},{64,32},{80,48},{96,64},{112,80},{128,96},{144,112}... | collective-permute-start | bytes 1376264 | tf_op jit(solution)/shard_map/ppermute | solution.py:48
  70.8 13.0 %collective-permute-start.17 = (bf16[608,256]{1,0:T(8,128)(2,1)}, bf16[608,256]{1,0:T(8,128)(2,1)S(1)}, u32[]{:S(2)}, u32[]{:S(2)}) collective-permute-start(bf16[608,256]{1,0:T(8,128)(2,1)} %slice.168), channel_id=1, source_target_pairs={{0,32},{16,48},{32,64},{48,80},{64,96},{80,112},{96,128},{112,144}... | collective-permute-start | bytes 933896 | tf_op jit(solution)/shard_map/ppermute | solution.py:48
  104.8 16.0 %collective-permute-start.28 = (bf16[288,256]{1,0:T(8,128)(2,1)S(1)}, bf16[288,256]{1,0:T(8,128)(2,1)S(1)}, u32[]{:S(2)}, u32[]{:S(2)}) collective-permute-start(bf16[288,256]{1,0:T(8,128)(2,1)S(1)} %collective-permute-done.24), channel_id=1, source_target_pairs={{0,16},{16,0},{32,48},{48,32},{64,80},{80,64},{96,112},{112,96},{1... | collective-permute-start | bytes 442376 | tf_op jit(solution)/shard_map/ppermute | solution.py:48
  110.1 13.4 %collective-permute-start.25 = (bf16[512,256]{1,0:T(8,128)(2,1)S(1)}, bf16[512,256]{1,0:T(8,128)(2,1)S(1)}, u32[]{:S(2)}, u32[]{:S(2)}) collective-permute-start(bf16[512,256]{1,0:T(8,128)(2,1)S(1)} %collective-permute-done.23.rest_0_), channel_id=1, source_target_pairs={{0,32},{16,48},{32,64},{48,80},{64,96},{80,112},{96,128},{112,144}... | collective-permute-start | bytes 786440 | tf_op jit(solution)/shard_map/ppermute | solution.py:48
  117.7 13.2 %collective-permute-start.27 = (bf16[864,256]{1,0:T(8,128)(2,1)S(1)}, bf16[864,256]{1,0:T(8,128)(2,1)S(1)}, u32[]{:S(2)}, u32[]{:S(2)}) collective-permute-start(bf16[864,256]{1,0:T(8,128)(2,1)S(1)} %pad_maximum_fusion.4), channel_id=1, source_target_pairs={{0,16},{16,0},{32,48},{48,32},{64,80},{80,64},{96,112},{112,96},{1... | collective-permute-start | bytes 1327112 | tf_op jit(solution)/shard_map/ppermute | solution.py:48
  117.8 18.7 %collective-permute-start.26 = (bf16[512,256]{1,0:T(8,128)(2,1)S(1)}, bf16[512,256]{1,0:T(8,128)(2,1)S(1)}, u32[]{:S(2)}, u32[]{:S(2)}) collective-permute-start(bf16[512,256]{1,0:T(8,128)(2,1)S(1)} %broadcast_select_fusion.3), channel_id=1, source_target_pairs={{0,16},{16,0},{32,48},{48,32},{64,80},{80,64},{96,112},{112,96},{1... | collective-permute-start | bytes 786440 | tf_op jit(solution)/shard_map/ppermute | solution.py:48
  148.6 23.8 %collective-permute-start.32 = (bf16[512,256]{1,0:T(8,128)(2,1)S(1)}, bf16[512,256]{1,0:T(8,128)(2,1)S(1)}, u32[]{:S(2)}, u32[]{:S(2)}) collective-permute-start(bf16[512,256]{1,0:T(8,128)(2,1)S(1)} %collective-permute-done.29.rest_0_), channel_id=1, source_target_pairs={{0,32},{16,48},{32,64},{48,80},{64,96},{80,112},{96,128},{112,144}... | collective-permute-start | bytes 786440 | tf_op jit(solution)/shard_map/ppermute | solution.py:48
  153.8 19.5 %collective-permute-start.34 = (bf16[576,256]{1,0:T(8,128)(2,1)S(1)}, bf16[576,256]{1,0:T(8,128)(2,1)S(1)}, u32[]{:S(2)}, u32[]{:S(2)}) collective-permute-start(bf16[576,256]{1,0:T(8,128)(2,1)S(1)} %collective-permute-done.31.rest_12_), channel_id=1, source_target_pairs={{32,0},{48,16},{64,32},{80,48},{96,64},{112,80},{128,96},{144,112}... | collective-permute-start | bytes 884744 | tf_op jit(solution)/shard_map/ppermute | solution.py:48
  153.9 28.9 %collective-permute-start.36 = (bf16[576,256]{1,0:T(8,128)(2,1)S(1)}, bf16[576,256]{1,0:T(8,128)(2,1)S(1)}, u32[]{:S(2)}, u32[]{:S(2)}) collective-permute-start(bf16[576,256]{1,0:T(8,128)(2,1)S(1)} %pad_maximum_fusion.6.rest_10_), channel_id=1, source_target_pairs={{0,32},{16,48},{32,64},{48,80},{64,96},{80,112},{96,128},{112,144}... | collective-permute-start | bytes 884744 | tf_op jit(solution)/shard_map/ppermute | solution.py:48
  156.6 16.7 %collective-permute-start.33 = (bf16[512,256]{1,0:T(8,128)(2,1)S(1)}, bf16[512,256]{1,0:T(8,128)(2,1)S(1)}, u32[]{:S(2)}, u32[]{:S(2)}) collective-permute-start(bf16[512,256]{1,0:T(8,128)(2,1)S(1)} %broadcast_select_fusion.1), channel_id=1, source_target_pairs={{0,16},{16,0},{32,48},{48,32},{64,80},{80,64},{96,112},{112,96},{1... | collective-permute-start | bytes 786440 | tf_op jit(solution)/shard_map/ppermute | solution.py:48
  197.8 25.1 %collective-permute-start.45 = (bf16[2,512,256]{2,1,0:T(8,128)(2,1)S(1)}, bf16[2,512,256]{2,1,0:T(8,128)(2,1)S(1)}, u32[]{:S(2)}, u32[]{:S(2)}) collective-permute-start(bf16[2,512,256]{2,1,0:T(8,128)(2,1)S(1)} %pad_maximum_fusion.1.rest_0_), channel_id=1, source_target_pairs={{0,1},{1,0},{2,3},{3,2},{4,5},{5,4},{6,7},{7,6},{8,9},{9,8},{10,11... | collective-permute-start | bytes 1572872 | tf_op jit(solution)/shard_map/ppermute | solution.py:52
  204.2 19.1 %collective-permute-start.43 = (bf16[1,512,256]{2,1,0:T(8,128)(2,1)S(1)}, bf16[1,512,256]{2,1,0:T(8,128)(2,1)S(1)}, u32[]{:S(2)}, u32[]{:S(2)}) collective-permute-start(bf16[1,512,256]{2,1,0:T(8,128)(2,1)S(1)} %slice.180), channel_id=1, source_target_pairs={{0,4},{1,5},{2,6},{3,7},{4,8},{5,9},{6,10},{7,11},{8,12},{9,13},{1... | collective-permute-start | bytes 786440 | tf_op jit(solution)/shard_map/ppermute | solution.py:52
  204.8 19.2 %collective-permute-start.44 = (bf16[1,512,256]{2,1,0:T(8,128)(2,1)S(1)}, bf16[1,512,256]{2,1,0:T(8,128)(2,1)S(1)}, u32[]{:S(2)}, u32[]{:S(2)}) collective-permute-start(bf16[1,512,256]{2,1,0:T(8,128)(2,1)S(1)} %slice.181), channel_id=1, source_target_pairs={{4,0},{5,1},{6,2},{7,3},{8,4},{9,5},{10,6},{11,7},{12,8},{13,9},{1... | collective-permute-start | bytes 786440 | tf_op jit(solution)/shard_map/ppermute | solution.py:52
  215.4 17.2 %collective-permute-start.46 = (bf16[2,512,256]{2,1,0:T(8,128)(2,1)S(1)}, bf16[2,512,256]{2,1,0:T(8,128)(2,1)S(1)}, u32[]{:S(2)}, u32[]{:S(2)}) collective-permute-start(bf16[2,512,256]{2,1,0:T(8,128)(2,1)S(1)} %collective-permute-done.39.rest_1_), channel_id=1, source_target_pairs={{0,1},{1,0},{2,3},{3,2},{4,5},{5,4},{6,7},{7,6},{8,9},{9,8},{10,11... | collective-permute-start | bytes 1572872 | tf_op jit(solution)/shard_map/ppermute | solution.py:52
  (69 other events, 740.2 us)

commit v5 on v3

v5 whole, which is shorter than its diff:
```python
import functools
import math

import jax
import jax.numpy as jnp
from jax import lax
from jax.experimental import pallas as pl
from jax.experimental.pallas import tpu as pltpu
from jax.sharding import PartitionSpec as P

D = 4608
HQ = 32
HD = 128
WINDOW = 4096
PAGE = 128
SEGS = 4

EPSILON = 1e-06
SOFT_CAP = 50.0
LOG2E = 1.4426950408889634
QUERY = float(D // HQ) ** (-0.5)
EXTRA = 16
SEQ = 16
ROUNDS = 8

BF = jnp.bfloat16
F32 = jnp.float32

AHEAD = [(i, (i + 2) % SEQ) for i in range(SEQ)]
BEHIND = [((i + 2) % SEQ, i) for i in range(SEQ)]
LATER = [(i, i + 2) for i in range(SEQ - 2)]
ACROSS = [(i, i ^ 1) for i in range(SEQ)]
SWAP = [(i, i ^ 1) for i in range(SEQ)]
COLUMNS = [[2 * i + c for i in range(ROUNDS)] for c in range(2)]

def move(block, perm):
    return lax.ppermute(block, "seq", perm)


def tie(*values):
    return lax.optimization_barrier(values)


def project_kernel(offsets, order_ref, cos_ref, sin_ref, x_hbm, *rest):
    w_refs = rest[:-7]
    kv_ref, q_ref, x_ref, w_ref, acc_ref, x_sem, w_sem = rest[-7:]
    chunks, depth, rows = x_ref.shape
    copies = []
    for k, (offset, source) in enumerate(zip(offsets, w_refs)):
        width = source.shape[1]
        for part in range(2):
            parity = order_ref[0] if part == 0 else 1 - order_ref[0]
            copies.append(
                pltpu.make_async_copy(
                    source.at[pl.ds(part * depth, depth)],
                    w_ref.at[2 * order_ref[1 + k] + parity, :, pl.ds(offset, width)],
                    w_sem.at[2 * k + part],
                )
            )
    step = chunks // 4
    for k in range(4):
        copies.append(
            pltpu.make_async_copy(
                x_hbm.at[pl.ds(k * step, step)], x_ref.at[pl.ds(k * step, step)], x_sem.at[k]
            )
        )
    for copy in copies:
        copy.start()
    for copy in copies[:-4]:
        copy.wait()
    squares = jnp.zeros((1, rows), F32)
    for k in range(4):
        copies[k - 4].wait()
        here = slice(k * step, (k + 1) * step)
        side = x_ref[here, depth - EXTRA :, :].astype(F32)
        squares = squares + jnp.sum(jnp.sum(side, axis=0), axis=0, keepdims=True)
        product = lax.dot_general(
            w_ref[here].reshape(step * depth, 4 * HD),
            x_ref[here].reshape(step * depth, rows),
            (((0,), (0,)), ((), ())),
            preferred_element_type=F32,
        )
        if k == 0:
            acc_ref[...] = product
        else:
            acc_ref[...] += product
    scale = lax.rsqrt(squares * (1.0 / D) + EPSILON)
    half = HD // 2
    cos, sin = cos_ref[...], sin_ref[...]
    for head, (ref, place, factor) in enumerate(
        ((kv_ref, 0, 1.0), (kv_ref, 1, None), (q_ref, 0, QUERY), (q_ref, 1, QUERY))
    ):
        start = head * HD
        if factor is None:
            value = acc_ref[start : start + HD, :] * scale
        else:
            first = acc_ref[start : start + half, :] * scale
            second = acc_ref[start + half : start + HD, :] * scale
            value = jnp.concatenate(
                [first * cos - second * sin, second * cos + first * sin], axis=0
            )
            if factor != 1.0:
                value = value * factor
        ref[:, place * HD : (place + 1) * HD] = jnp.transpose(value).astype(BF)


def project(x_all, blocks, order, cos, sin):
    chunks, depth, rows = x_all.shape
    vmem = pl.BlockSpec(memory_space=pltpu.VMEM)
    outside = pl.BlockSpec(memory_space=pl.ANY)
    out = jax.ShapeDtypeStruct((rows, 2 * HD), BF)
    return pl.pallas_call(
        functools.partial(project_kernel, tuple(offset for _, offset in blocks)),
        out_shape=(out, out),
        in_specs=[pl.BlockSpec(memory_space=pltpu.SMEM), vmem, vmem]
        + [outside] * (1 + len(blocks)),
        out_specs=(vmem, vmem),
        scratch_shapes=[
            pltpu.VMEM((chunks, depth, rows), BF),
            pltpu.VMEM((chunks, depth, 4 * HD), BF),
            pltpu.VMEM((4 * HD, rows), F32),
            pltpu.SemaphoreType.DMA((4,)),
            pltpu.SemaphoreType.DMA((2 * len(blocks),)),
        ],
        compiler_params=pltpu.CompilerParams(vmem_limit_bytes=60 << 20),
        cost_estimate=pl.CostEstimate(
            flops=2 * rows * 4 * HD * D, bytes_accessed=10 << 20, transcendentals=0
        ),
    )(order, cos, sin, x_all, *[block for block, _ in blocks])


def attend_kernel(distances, first, last, low_ref, q_ref, *rest):
    n = len(distances)
    kv_refs = rest[:n]
    rest = rest[n:]
    if not first:
        sum_in, den_in = rest[:2]
        rest = rest[2:]
    rows = q_ref.shape[0]
    tile = 256

    def part(index, carry):
        here = pl.ds(pl.multiple_of((index // 2) * tile, tile), tile)
        columns = pl.ds(pl.multiple_of(lax.rem(index, 2) * HD, HD), HD)
        q = q_ref[here, columns]
        low = low_ref[here, :]
        if first:
            total = jnp.zeros((tile, HD), F32)
            den = jnp.zeros((tile, HD), F32)
        else:
            total = sum_in[here, columns]
            den = den_in[here, columns]
        for kv_ref, distance in zip(kv_refs, distances):
            score = lax.dot_general(
                q, kv_ref[:, :HD], (((1,), (1,)), ((), ())), preferred_element_type=F32
            )
            weight = jnp.exp2(jnp.tanh(score * (1.0 / SOFT_CAP)) * (SOFT_CAP * LOG2E))
            place = lax.broadcasted_iota(jnp.int32, (tile, rows), 1)
            allowed = place >= low + distance * rows
            if distance == 0:
                own = lax.broadcasted_iota(jnp.int32, (tile, rows), 0) + (index // 2) * tile
                allowed = allowed & (place <= own)
            weight = jnp.where(allowed, weight, 0.0)
            for c in range(rows // HD):
                den = den + weight[:, c * HD : (c + 1) * HD]
            total = total + jnp.dot(
                weight.astype(BF), kv_ref[:, HD:], preferred_element_type=F32
            )
        if last:
            whole = jnp.sum(den, axis=1, keepdims=True)
            rest[0][here, columns] = (total / whole).astype(BF)
        else:
            rest[0][here, columns] = total
            rest[1][here, columns] = den
        return carry

    lax.fori_loop(0, 2 * (rows // tile), part, 0)


def attend(low, queries, kvs, distances, state):
    first = state is None
    last = 8 in distances
    rows = queries.shape[0]
    vmem = pl.BlockSpec(memory_space=pltpu.VMEM)
    n_in = 2 + len(kvs) + (0 if first else 2)
    part = jax.ShapeDtypeStruct((rows, 2 * HD), F32)
    elements = 2 * rows * rows * len(kvs)
    return pl.pallas_call(
        functools.partial(attend_kernel, tuple(distances), first, last),
        out_shape=jax.ShapeDtypeStruct((rows, 2 * HD), BF) if last else (part, part),
        in_specs=[vmem] * n_in,
        out_specs=vmem if last else (vmem, vmem),
        input_output_aliases={} if (first or last) else {n_in - 2: 0, n_in - 1: 1},
        compiler_params=pltpu.CompilerParams(vmem_limit_bytes=8 << 20),
        cost_estimate=pl.CostEstimate(
            flops=elements * 512, bytes_accessed=4 << 20, transcendentals=2 * elements
        ),
    )(low, queries, *kvs, *(() if first else state))


def terms_kernel(added, side_ref, a_ref, w_hbm, *rest):
    if added:
        in_ref, out_ref, w_ref, sem = rest
    else:
        out_ref, w_ref, sem = rest
    part = side_ref[0]
    copies = []
    for k in range(ROUNDS):
        copies.append(pltpu.make_async_copy(w_hbm.at[2 * k + part], w_ref.at[k], sem.at[k]))
    for copy in copies:
        copy.start()
    for k in range(ROUNDS):
        copies[k].wait()
        product = lax.dot_general(
            w_ref[k], a_ref[...], (((1,), (1,)), ((), ())), preferred_element_type=F32
        )
        if added:
            product = product + in_ref[k].astype(F32)
        out_ref[k] = product.astype(BF)


def terms(attended, weights, side, received):
    rows = attended.shape[0]
    _, features, width = weights.shape
    vmem = pl.BlockSpec(memory_space=pltpu.VMEM)
    added = received is not None
    return pl.pallas_call(
        functools.partial(terms_kernel, added),
        out_shape=jax.ShapeDtypeStruct((ROUNDS, features, rows), BF),
        in_specs=[
            pl.BlockSpec(memory_space=pltpu.SMEM),
            vmem,
            pl.BlockSpec(memory_space=pl.ANY),
        ]
        + [vmem] * added,
        out_specs=vmem,
        scratch_shapes=[
            pltpu.VMEM((ROUNDS, features, width), BF),
            pltpu.SemaphoreType.DMA((ROUNDS,)),
        ],
        compiler_params=pltpu.CompilerParams(vmem_limit_bytes=16 << 20),
        cost_estimate=pl.CostEstimate(
            flops=2 * rows * features * width * ROUNDS,
            bytes_accessed=6 << 20,
            transcendentals=0,
        ),
    )(side, attended, weights, *((received,) if added else ()))


def total_kernel(in_ref, out_ref, square_ref):
    total = in_ref[0].astype(F32)
    for k in range(1, ROUNDS):
        total = total + in_ref[k].astype(F32)
    out_ref[...] = total
    square_ref[...] = jnp.sum(total * total, axis=0, keepdims=True)


def total_of(parts):
    _, features, rows = parts.shape
    vmem = pl.BlockSpec(memory_space=pltpu.VMEM)
    return pl.pallas_call(
        total_kernel,
        out_shape=(
            jax.ShapeDtypeStruct((features, rows), F32),
            jax.ShapeDtypeStruct((1, rows), F32),
        ),
        in_specs=[vmem],
        out_specs=(vmem, vmem),
        compiler_params=pltpu.CompilerParams(vmem_limit_bytes=10 << 20),
        cost_estimate=pl.CostEstimate(flops=1 << 20, bytes_accessed=3 << 20, transcendentals=0),
    )(parts)


def shards(tokens, pre_gain, post_gain, w_query, w_key, w_value, w_out, segment_ids, page_table):
    rows = tokens.shape[0]
    features = tokens.shape[1]
    seq_index = lax.axis_index("seq")
    z = seq_index // 2
    h = lax.rem(seq_index, 2)
    base = seq_index * rows

    x_own = tokens.T.astype(F32)
    gained = (x_own * (1.0 + pre_gain.astype(F32))[:, None]).astype(BF)
    squares = jnp.sum(x_own * x_own, axis=0, keepdims=True)
    upper = lax.reduce_precision(squares, 8, 7)
    lower = squares - upper
    side = jnp.concatenate(
        [upper.astype(BF), lower.astype(BF), jnp.zeros((EXTRA - 2, rows), BF)], axis=0
    )
    x_all = lax.all_gather(jnp.concatenate([gained, side], axis=0), "mp", axis=0)
    depth = features + EXTRA

    lane = jnp.arange(4 * HD, dtype=jnp.int32)
    marked = 2 * (SEGS - 1)
    limit = jnp.where(lane < marked, lax.rem(lane, SEGS - 1) + 1, 0)
    counts = jnp.sum((segment_ids[:, None] < limit[None, :]).astype(F32), axis=0)
    upper_digit = jnp.floor(counts * (1.0 / 16.0))
    digits = jnp.where(lane < SEGS - 1, upper_digit, counts - 16.0 * upper_digit).astype(BF)
    digits = jnp.pad(digits[None, :], ((2, EXTRA - 3), (0, 0)))
    own = jnp.concatenate(
        [jnp.concatenate([w_key, w_value, w_query], axis=1), digits], axis=0
    )
    start = jnp.concatenate([own, move(own, ACROSS)], axis=0)
    ring = {0: start, 1: move(start, AHEAD), -1: move(start, BEHIND)}
    out_own = w_out.T
    out_facing = move(out_own, ACROSS)
    ring[2] = move(ring[1], AHEAD)
    ring[-2] = move(ring[-1], BEHIND)
    ring[2], ring[-2], out_facing = tie(ring[2], ring[-2], out_facing)
    out_all = lax.all_gather(
        jnp.concatenate([out_own, out_facing], axis=0)[None],
        "seq",
        axis=0,
        axis_index_groups=COLUMNS,
        tiled=True,
    )
    out_all = out_all.reshape(2 * ROUNDS, features, 2 * HD)
    ring[3] = move(ring[2], AHEAD)
    ring[-3] = move(ring[-2], BEHIND)
    last = move(ring[3][:, : 2 * HD], AHEAD)
    opposite = move(ring[-3][:, 2 * HD :], BEHIND)
    steps = [0, 1, -1, 2, -2, 3, -3, 4, 4]
    blocks = [(ring[step], 0) for step in steps[:7]] + [(last, 0), (opposite, 2 * HD)]
    places = [lax.rem(z - step + ROUNDS, ROUNDS) for step in steps]
    order = jnp.stack([h, *places]).astype(jnp.int32)
    parity = lax.rem(lax.axis_index("mp"), 2)

    n_marks = 2 * (SEGS - 1)
    marks = jnp.zeros((n_marks,), F32)
    for block, _ in blocks[:8]:
        for part in range(2):
            marks = marks + block[part * depth + features + 2, :n_marks].astype(F32)
    starts = (marks[: SEGS - 1] * 16.0 + marks[SEGS - 1 :]).astype(jnp.int32)
    global_index = base + jnp.arange(rows, dtype=jnp.int32)
    offsets = jnp.zeros((rows,), jnp.int32)
    for s in range(1, SEGS):
        offsets = jnp.where(segment_ids == s, starts[s - 1], offsets)
    within = (global_index - offsets).astype(F32)
    low = (jnp.maximum(offsets, global_index - (WINDOW - 1)) - base)[:, None]
    half = HD // 2
    freqs = jnp.exp(-math.log(10000.0) * jnp.arange(half, dtype=F32) * (2.0 / HD))
    angles = freqs[:, None] * within[None, :]
    cos = jnp.cos(angles)
    sin = jnp.sin(angles)

    kv, queries = project(x_all, blocks, order, cos, sin)

    straight, crossed, current = [kv], [None], kv
    state = attend(low, queries, [kv], [0], None)
    for step in range(4):
        following = move(current, LATER)
        chosen = jnp.where(h == 0, current, following)
        if step == 0:
            following, chosen = tie(following, chosen)
        else:
            following, chosen, crossed[step], *state = tie(
                following, chosen, crossed[step], *state
            )
            if step > 1:
                k = step - 1
                state = attend(low, queries, [straight[k], crossed[k]], [2 * k, 2 * k - 1], state)
        straight.append(following)
        crossed.append(move(chosen, ACROSS))
        current = following
    for k in range(3, 5):
        state = attend(low, queries, [straight[k], crossed[k]], [2 * k, 2 * k - 1], state)

    near = jnp.where(parity == h, 0, 1).astype(jnp.int32)[None]
    sent = lax.ppermute(terms(state, out_all, 1 - near, None), "mp", SWAP)
    mine = terms(state, out_all, near, sent)
    arrived = lax.all_to_all(mine, "mp", 0, 0, axis_index_groups=COLUMNS, tiled=True)
    share, partial = total_of(arrived)
    everywhere = jnp.broadcast_to(partial, (lax.axis_size("mp"), rows))
    square_total = jnp.sum(lax.all_to_all(everywhere, "mp", 0, 0, tiled=True), axis=0)
    post_scale = lax.rsqrt(square_total / D + EPSILON)
    post = share * post_scale[None, :] * (1.0 + post_gain.astype(F32))[:, None]
    layer_output = (tokens.T.astype(F32) + post).astype(BF).T

    pages = page_table.shape[0]
    local_slot = page_table - seq_index * pages
    kv_pages = kv.reshape(pages, PAGE, 2 * HD)
    caches = []
    for slot in range(pages):
        chosen = kv_pages[0]
        for page in range(1, pages):
            chosen = jnp.where(local_slot[page] == slot, kv_pages[page], chosen)
        caches.append(chosen)
    caches = jnp.stack(caches)
    return (layer_output, caches[:, :, :HD], caches[:, :, HD:])


def solution(mesh):
    return jax.shard_map(
        shards,
        mesh=mesh,
        in_specs=(
            P("seq", "mp"),
            P("mp"),
            P("mp"),
            P("seq", "mp"),
            P("seq", "mp"),
            P("seq", "mp"),
            P("mp", "seq"),
            P("seq"),
            P("seq"),
        ),
        out_specs=(P("seq", "mp"), P("seq", None, "mp"), P("seq", None, "mp")),
        check_vma=False,
    )
```

time: 226 us -> 232 us (1.027)
  the two profiles are of different devices: /device:TPU:101 before, /device:TPU:1 now
where the time goes in v5:
time: 232 us; the launch traced here: 229 us
  waiting for transfers between devices  88.7 us (38%)
  starting transfers between devices  64.9 us (28%)
  Pallas kernels  30.3 us (13%)
  between operations  22.3 us (10%)
  local copies, waits for them, and re-layouts  12 us (5%)
  other arithmetic  10.4 us (4%)
    ppermute x18, waiting for transfers between devices, move(): return lax.ppermute(block, 'seq', perm)  58.7 us
    ppermute x18, starting transfers between devices, move(): return lax.ppermute(block, 'seq', perm)  44 us
    all_to_all x1, waiting for transfers between devices, shards(): lax.all_to_all(mine, 'mp', 0, 0, axis_index_groups=COLUMNS, tiled=True)  20.7 us
    pallas_call x5, Pallas kernels, attend(): pl.pallas_call(functools.partial(attend_kernel, tuple(distances), first,...  13.4 us
    ppermute x1, starting transfers between devices, shards(): sent = lax.ppermute(terms(state, out_all, 1 - near, None), 'mp', SWAP)  10.3 us
    pallas_call x1, Pallas kernels, project(): pl.pallas_call(functools.partial(project_kernel, tuple((offset for _, off...  9.11 us
    pallas_call x2, Pallas kernels, terms(): pl.pallas_call(functools.partial(terms_kernel, added), out_shape=jax.Shap...  7.48 us
    unnamed x40, local copies, waits for them, and re-layouts  6.84 us
  transfers between devices with their start and end apart: 23, of which 15 were waited for; matrix products, arithmetic and copies ran while one was open for 6% of the time, Pallas kernels for 10%

profile of v5, /device:TPU:1, one launch (start us, length us, event | category | flops | bytes accessed | tf_op | source)
XLA Modules:
  0.0 228.7 jit_solution(15590940901119367778)
XLA Ops:
  13.8 3.7 %collective-permute-start = (bf16[304,512]{1,0:T(8,128)(2,1)S(1)}, bf16[304,512]{1,0:T(8,128)(2,1)S(1)}, u32[]{:S(2)}, u32[]{:S(2)}) collective-permute-start(bf16[304,512]{1,0:T(8,128)(2,1)S(1)} %pad_maximum_fusion.1), channel_id=1, source_target_pairs={{0,16},{16,0},{32,48},{48,32},{64,80},{80,64},{96,112},{112,96},{1... | collective-permute-start | bytes 933896 | tf_op jit(solution)/shard_map/ppermute | solution.py:37
  17.4 6.0 %collective-permute-done = bf16[304,512]{1,0:T(8,128)(2,1)S(1)} collective-permute-done((bf16[304,512]{1,0:T(8,128)(2,1)S(1)}, bf16[304,512]{1,0:T(8,128)(2,1)S(1)}, u32[]{:S(2)}, u32[]{:S(2)}) %collective-permute-start) | collective-permute-done | bytes 311328 | tf_op jit(solution)/shard_map/ppermute | solution.py:37
  26.2 4.0 %collective-permute-start.2 = (bf16[608,512]{1,0:T(8,128)(2,1)S(1)}, bf16[608,512]{1,0:T(8,128)(2,1)S(1)}, u32[]{:S(2)}, u32[]{:S(2)}) collective-permute-start(bf16[608,512]{1,0:T(8,128)(2,1)S(1)} %pad_maximum_fusion.rest_0_), channel_id=1, source_target_pairs={{32,0},{48,16},{64,32},{80,48},{96,64},{112,80},{128,96},{144,112}... | collective-permute-start | bytes 1867784 | tf_op jit(solution)/shard_map/ppermute | solution.py:37
  30.2 11.4 %collective-permute-done.1.rest_1_ = bf16[608,512]{1,0:T(8,128)(2,1)S(1)} collective-permute-done((bf16[608,512]{1,0:T(8,128)(2,1)S(1)}, bf16[608,512]{1,0:T(8,128)(2,1)S(1)}, u32[]{:S(2)}, u32[]{:S(2)}) %collective-permute-start.1) | collective-permute-done | bytes 622624 | tf_op jit(solution)/shard_map/ppermute | solution.py:37
  46.1 6.6 %collective-permute-done.5 = bf16[288,256]{1,0:T(8,128)(2,1)S(1)} collective-permute-done((bf16[288,256]{1,0:T(8,128)(2,1)S(1)}, bf16[288,256]{1,0:T(8,128)(2,1)S(1)}, u32[]{:S(2)}, u32[]{:S(2)}) %collective-permute-start.5) | collective-permute-done | bytes 147488 | tf_op jit(solution)/shard_map/ppermute | solution.py:37
  58.4 9.2 %collective-permute-done.6.rest_5_ = bf16[608,512]{1,0:T(8,128)(2,1)S(1)} collective-permute-done((bf16[608,512]{1,0:T(8,128)(2,1)}, bf16[608,512]{1,0:T(8,128)(2,1)S(1)}, u32[]{:S(2)}, u32[]{:S(2)}) %collective-permute-start.6) | collective-permute-done | bytes 622624 | tf_op jit(solution)/shard_map/ppermute | solution.py:37
  71.8 3.8 %collective-permute-done.8.rest_7_ = bf16[608,256]{1,0:T(8,128)(2,1)S(1)} collective-permute-done((bf16[608,256]{1,0:T(8,128)(2,1)}, bf16[608,256]{1,0:T(8,128)(2,1)S(1)}, u32[]{:S(2)}, u32[]{:S(2)}) %collective-permute-start.8) | collective-permute-done | bytes 311328 | tf_op jit(solution)/shard_map/ppermute | solution.py:37
  80.3 9.1 %shard_map.112 = (bf16[512,256]{1,0:T(8,128)(2,1)}, bf16[512,256]{1,0:T(8,128)(2,1)}) custom-call(s32[10]{0:T(128)} %stack.55.order_ref, f32[64,512]{1,0:T(8,128)} %get-tuple-element.76.cos_ref, f32[64,512]{1,0:T(8,128)} %get-tuple-element.75.sin_ref, bf16[16,304,512]{2,1,0:T(8,128)(2,1)} %bitcast.68, bf16[608,512]{1,0:T(8,128)(2,1)} %copy-done.7, ...), custom_call_target="tpu_custom_call" | custom-call | flops 2415919104 | bytes 10485760 | tf_op jit(solution)/shard_map/pallas_call | solution.py:112
  89.5 3.7 %collective-permute-start.10 = (bf16[512,256]{1,0:T(8,128)(2,1)}, bf16[512,256]{1,0:T(8,128)(2,1)S(1)}, u32[]{:S(2)}, u32[]{:S(2)}) collective-permute-start(bf16[512,256]{1,0:T(8,128)(2,1)} %get-tuple-element.38.rest_0_), channel_id=1, source_target_pairs={{0,32},{16,48},{32,64},{48,80},{64,96},{80,112},{96,128},{112,144}... | collective-permute-start | bytes 786440 | tf_op jit(solution)/shard_map/ppermute | solution.py:37
  93.2 8.8 %collective-permute-done.10.rest_0_ = bf16[512,256]{1,0:T(8,128)(2,1)S(1)} collective-permute-done((bf16[512,256]{1,0:T(8,128)(2,1)}, bf16[512,256]{1,0:T(8,128)(2,1)S(1)}, u32[]{:S(2)}, u32[]{:S(2)}) %collective-permute-start.10) | collective-permute-done | bytes 262176 | tf_op jit(solution)/shard_map/ppermute | solution.py:37
  103.0 6.5 %collective-permute-start.11 = (bf16[512,256]{1,0:T(8,128)(2,1)S(1)}, bf16[512,256]{1,0:T(8,128)(2,1)S(1)}, u32[]{:S(2)}, u32[]{:S(2)}) collective-permute-start(bf16[512,256]{1,0:T(8,128)(2,1)S(1)} %collective-permute-done.10.rest_0_), channel_id=1, source_target_pairs={{0,32},{16,48},{32,64},{48,80},{64,96},{80,112},{96,128},{112,144}... | collective-permute-start | bytes 786440 | tf_op jit(solution)/shard_map/ppermute | solution.py:37
  116.7 4.1 %collective-permute-start.13 = (bf16[512,256]{1,0:T(8,128)(2,1)S(1)}, bf16[512,256]{1,0:T(8,128)(2,1)S(1)}, u32[]{:S(2)}, u32[]{:S(2)}) collective-permute-start(bf16[512,256]{1,0:T(8,128)(2,1)S(1)} %collective-permute-done.11.rest_0_), channel_id=1, source_target_pairs={{0,32},{16,48},{32,64},{48,80},{64,96},{80,112},{96,128},{112,144}... | collective-permute-start | bytes 786440 | tf_op jit(solution)/shard_map/ppermute | solution.py:37
  124.1 3.5 %collective-permute-done.14.rest_1_ = bf16[512,256]{1,0:T(8,128)(2,1)S(1)} collective-permute-done((bf16[512,256]{1,0:T(8,128)(2,1)S(1)}, bf16[512,256]{1,0:T(8,128)(2,1)S(1)}, u32[]{:S(2)}, u32[]{:S(2)}) %collective-permute-start.14) | collective-permute-done | bytes 262176 | tf_op jit(solution)/shard_map/ppermute | solution.py:37
  127.6 4.1 %collective-permute-start.15 = (bf16[512,256]{1,0:T(8,128)(2,1)S(1)}, bf16[512,256]{1,0:T(8,128)(2,1)S(1)}, u32[]{:S(2)}, u32[]{:S(2)}) collective-permute-start(bf16[512,256]{1,0:T(8,128)(2,1)S(1)} %collective-permute-done.13.rest_0_), channel_id=1, source_target_pairs={{0,32},{16,48},{32,64},{48,80},{64,96},{80,112},{96,128},{112,144}... | collective-permute-start | bytes 786440 | tf_op jit(solution)/shard_map/ppermute | solution.py:37
  133.1 2.9 %shard_map.114 = (f32[512,256]{1,0:T(8,128)S(1)}, f32[512,256]{1,0:T(8,128)S(1)}) custom-call(s32[512,1]{1,0:T(8,128)S(1)} %copy.32.low_ref, bf16[512,256]{1,0:T(8,128)(2,1)S(1)} %copy-done.6, bf16[512,256]{1,0:T(8,128)(2,1)S(1)} %collective-permute-done.10.rest_0_, ...), custom_call_target="tpu_custom_call", output_to_operand_aliasing={{0}: (4, {}), {1}: (5, {})} | custom-call | flops 536870912 | bytes 4194304 | tf_op jit(solution)/shard_map/pallas_call | solution.py:188
  146.4 2.9 %shard_map.117.a_ref = bf16[512,256]{1,0:T(8,128)(2,1)S(1)} custom-call(s32[512,1]{1,0:T(8,128)S(1)} %copy.32.low_ref, bf16[512,256]{1,0:T(8,128)(2,1)S(1)} %copy-done.6, bf16[512,256]{1,0:T(8,128)(2,1)S(1)} %collective-permute-done.15.rest_0_, bf16[512,256]{1,0:T(8,128)(2,1)S(1)} %collective-permute-done.17.rest_1_, ...), custom_call_target="tpu_custom_call" | custom-call | flops 536870912 | bytes 4194304 | tf_op jit(solution)/shard_map/pallas_call | solution.py:188
  151.0 3.7 %shard_map.118 = bf16[8,288,512]{2,1,0:T(8,128)(2,1)S(1)} custom-call(s32[1]{0:T(128)S(6)} %sub.59.side_ref, bf16[512,256]{1,0:T(8,128)(2,1)S(1)} %shard_map.117.a_ref, bf16[16,288,256]{2,1,0:T(8,128)(2,1)S(1)} %bitcast.65), custom_call_target="tpu_custom_call" | custom-call | flops 603979776 | bytes 6291456 | tf_op jit(solution)/shard_map/pallas_call | solution.py:227
  154.7 10.3 %collective-permute-start.18 = (bf16[8,288,512]{2,1,0:T(8,128)(2,1)S(1)}, bf16[8,288,512]{2,1,0:T(8,128)(2,1)S(1)}, u32[]{:S(2)}, u32[]{:S(2)}) collective-permute-start(bf16[8,288,512]{2,1,0:T(8,128)(2,1)S(1)} %shard_map.118), channel_id=1, source_target_pairs={{0,1},{1,0},{2,3},{3,2},{4,5},{5,4},{6,7},{7,6},{8,9},{9,8},{10,11... | collective-permute-start | bytes 7077896 | tf_op jit(solution)/shard_map/ppermute | solution.py:369
  165.0 4.2 %collective-permute-done.18.rest_0_ = bf16[8,288,512]{2,1,0:T(8,128)(2,1)S(1)} collective-permute-done((bf16[8,288,512]{2,1,0:T(8,128)(2,1)S(1)}, bf16[8,288,512]{2,1,0:T(8,128)(2,1)S(1)}, u32[]{:S(2)}, u32[]{:S(2)}) %collective-permute-start.18) | collective-permute-done | bytes 2359328 | tf_op jit(solution)/shard_map/ppermute | solution.py:369
  169.1 3.8 %shard_map.119 = bf16[8,288,512]{2,1,0:T(8,128)(2,1)S(1)} custom-call(s32[1]{0:T(128)} %bitcast.1.side_ref, bf16[512,256]{1,0:T(8,128)(2,1)S(1)} %shard_map.117.a_ref, bf16[16,288,256]{2,1,0:T(8,128)(2,1)S(1)} %bitcast.66, bf16[8,288,512]{2,1,0:T(8,128)(2,1)S(1)} %collective-permute-done.18.rest_0_), custom_call_target="tpu_custom_call" | custom-call | flops 603979776 | bytes 6291456 | tf_op jit(solution)/shard_map/pallas_call | solution.py:227
  174.3 5.8 %all-to-all-start = ((bf16[8,288,512]{2,1,0:T(8,128)(2,1)}), bf16[8,288,512]{2,1,0:T(8,128)(2,1)S(1)}, u32[]{:S(2)}, u32[]{:S(2)}) async-start(bf16[8,288,512]{2,1,0:T(8,128)(2,1)} %copy-done.2), calls=%async_computation | async-start | bytes 4718592 | tf_op jit(solution)/shard_map/all_to_all | solution.py:371
  188.6 20.7 %all-to-all-done.in_ref = bf16[8,288,512]{2,1,0:T(8,128)(2,1)S(1)} async-done(((bf16[8,288,512]{2,1,0:T(8,128)(2,1)}), bf16[8,288,512]{2,1,0:T(8,128)(2,1)S(1)}, u32[]{:S(2)}, u32[]{:S(2)}) %all-to-all-start) | async-done | bytes 2359328 | tf_op jit(solution)/shard_map/all_to_all | solution.py:371
  210.3 4.8 %all-to-all-start.1 = ((f32[16,1,512]{2,1,0:T(1,128)}), f32[16,1,512]{2,1,0:T(1,128)S(1)}, u32[]{:S(2)}, u32[]{:S(2)}) async-start(f32[16,1,512]{2,1,0:T(1,128)} %broadcast_in_dim.49), calls=%async_computation.1 | async-start | bytes 65536 | tf_op jit(solution)/shard_map/all_to_all | solution.py:374
  215.8 5.1 %all-to-all-done.1 = f32[16,1,512]{2,1,0:T(1,128)S(1)} async-done(((f32[16,1,512]{2,1,0:T(1,128)}), f32[16,1,512]{2,1,0:T(1,128)S(1)}, u32[]{:S(2)}, u32[]{:S(2)}) %all-to-all-start.1) | async-done | bytes 32800 | tf_op jit(solution)/shard_map/all_to_all | solution.py:374
  (112 shorter events, 58.0 us)
Async XLA Ops:
  7.2 73.1 %all-gather.5.cloned.1.call-start = ((), (), s32[]{:S(2)}) async-start(), calls=%async_computation.2 | async-start | bytes 5292032 | tf_op jit(solution)/shard_map/all_gather | solution.py:290
  10.0 139.3 %all-gather.7.cloned.1.call-start = ((), (), s32[]{:S(2)}) async-start(), calls=%async_computation.3 | async-start | bytes 2654208 | tf_op jit(solution)/shard_map/all_gather | solution.py:310
  11.9 65.2 %copy-start.16 = (s32[512]{0:T(512)S(1)}, s32[512]{0:T(512)}, u32[]{:S(2)}) copy-start(s32[512]{0:T(512)} %param.16) | copy-start | bytes 6148
  13.8 9.7 %collective-permute-start = (bf16[304,512]{1,0:T(8,128)(2,1)S(1)}, bf16[304,512]{1,0:T(8,128)(2,1)S(1)}, u32[]{:S(2)}, u32[]{:S(2)}) collective-permute-start(bf16[304,512]{1,0:T(8,128)(2,1)S(1)} %pad_maximum_fusion.1), channel_id=1, source_target_pairs={{0,16},{16,0},{32,48},{48,32},{64,80},{80,64},{96,112},{112,96},{1... | collective-permute-start | bytes 933896 | tf_op jit(solution)/shard_map/ppermute | solution.py:37
  23.5 18.1 %collective-permute-start.1 = (bf16[608,512]{1,0:T(8,128)(2,1)S(1)}, bf16[608,512]{1,0:T(8,128)(2,1)S(1)}, u32[]{:S(2)}, u32[]{:S(2)}) collective-permute-start(bf16[608,512]{1,0:T(8,128)(2,1)S(1)} %pad_maximum_fusion.rest_0_), channel_id=1, source_target_pairs={{0,32},{16,48},{32,64},{48,80},{64,96},{80,112},{96,128},{112,144}... | collective-permute-start | bytes 1867784 | tf_op jit(solution)/shard_map/ppermute | solution.py:37
  26.2 15.5 %collective-permute-start.2 = (bf16[608,512]{1,0:T(8,128)(2,1)S(1)}, bf16[608,512]{1,0:T(8,128)(2,1)S(1)}, u32[]{:S(2)}, u32[]{:S(2)}) collective-permute-start(bf16[608,512]{1,0:T(8,128)(2,1)S(1)} %pad_maximum_fusion.rest_0_), channel_id=1, source_target_pairs={{32,0},{48,16},{64,32},{80,48},{96,64},{112,80},{128,96},{144,112}... | collective-permute-start | bytes 1867784 | tf_op jit(solution)/shard_map/ppermute | solution.py:37
  41.6 13.4 %collective-permute-start.3 = (bf16[608,512]{1,0:T(8,128)(2,1)S(1)}, bf16[608,512]{1,0:T(8,128)(2,1)}, u32[]{:S(2)}, u32[]{:S(2)}) collective-permute-start(bf16[608,512]{1,0:T(8,128)(2,1)S(1)} %collective-permute-done.1.rest_1_), channel_id=1, source_target_pairs={{0,32},{16,48},{32,64},{48,80},{64,96},{80,112},{96,128},{112,144}... | collective-permute-start | bytes 1867784 | tf_op jit(solution)/shard_map/ppermute | solution.py:37
  41.7 13.4 %collective-permute-start.4 = (bf16[608,512]{1,0:T(8,128)(2,1)S(1)}, bf16[608,512]{1,0:T(8,128)(2,1)}, u32[]{:S(2)}, u32[]{:S(2)}) collective-permute-start(bf16[608,512]{1,0:T(8,128)(2,1)S(1)} %collective-permute-done.2.rest_2_), channel_id=1, source_target_pairs={{32,0},{48,16},{64,32},{80,48},{96,64},{112,80},{128,96},{144,112}... | collective-permute-start | bytes 1867784 | tf_op jit(solution)/shard_map/ppermute | solution.py:37
  44.3 8.4 %collective-permute-start.5 = (bf16[288,256]{1,0:T(8,128)(2,1)S(1)}, bf16[288,256]{1,0:T(8,128)(2,1)S(1)}, u32[]{:S(2)}, u32[]{:S(2)}) collective-permute-start(bf16[288,256]{1,0:T(8,128)(2,1)S(1)} %bitcast.69), channel_id=1, source_target_pairs={{0,16},{16,0},{32,48},{48,32},{64,80},{80,64},{96,112},{112,96},{1... | collective-permute-start | bytes 442376 | tf_op jit(solution)/shard_map/ppermute | solution.py:37
  55.0 12.6 %collective-permute-start.6 = (bf16[608,512]{1,0:T(8,128)(2,1)}, bf16[608,512]{1,0:T(8,128)(2,1)S(1)}, u32[]{:S(2)}, u32[]{:S(2)}) collective-permute-start(bf16[608,512]{1,0:T(8,128)(2,1)} %collective-permute-done.3.rest_3_), channel_id=1, source_target_pairs={{0,32},{16,48},{32,64},{48,80},{64,96},{80,112},{96,128},{112,144}... | collective-permute-start | bytes 1867784 | tf_op jit(solution)/shard_map/ppermute | solution.py:37
  57.0 14.1 %collective-permute-start.7 = (bf16[608,512]{1,0:T(8,128)(2,1)}, bf16[608,512]{1,0:T(8,128)(2,1)S(1)}, u32[]{:S(2)}, u32[]{:S(2)}) collective-permute-start(bf16[608,512]{1,0:T(8,128)(2,1)} %collective-permute-done.4.rest_4_), channel_id=1, source_target_pairs={{32,0},{48,16},{64,32},{80,48},{96,64},{112,80},{128,96},{144,112}... | collective-permute-start | bytes 1867784 | tf_op jit(solution)/shard_map/ppermute | solution.py:37
  68.4 7.2 %collective-permute-start.8 = (bf16[608,256]{1,0:T(8,128)(2,1)}, bf16[608,256]{1,0:T(8,128)(2,1)S(1)}, u32[]{:S(2)}, u32[]{:S(2)}) collective-permute-start(bf16[608,256]{1,0:T(8,128)(2,1)} %slice.164), channel_id=1, source_target_pairs={{0,32},{16,48},{32,64},{48,80},{64,96},{80,112},{96,128},{112,144}... | collective-permute-start | bytes 933896 | tf_op jit(solution)/shard_map/ppermute | solution.py:37
  71.2 9.1 %collective-permute-start.9 = (bf16[608,256]{1,0:T(8,128)(2,1)S(1)}, bf16[608,256]{1,0:T(8,128)(2,1)}, u32[]{:S(2)}, u32[]{:S(2)}) collective-permute-start(bf16[608,256]{1,0:T(8,128)(2,1)S(1)} %slice.167), channel_id=1, source_target_pairs={{32,0},{48,16},{64,32},{80,48},{96,64},{112,80},{128,96},{144,112}... | collective-permute-start | bytes 933896 | tf_op jit(solution)/shard_map/ppermute | solution.py:37
  89.5 12.5 %collective-permute-start.10 = (bf16[512,256]{1,0:T(8,128)(2,1)}, bf16[512,256]{1,0:T(8,128)(2,1)S(1)}, u32[]{:S(2)}, u32[]{:S(2)}) collective-permute-start(bf16[512,256]{1,0:T(8,128)(2,1)} %get-tuple-element.38.rest_0_), channel_id=1, source_target_pairs={{0,32},{16,48},{32,64},{48,80},{64,96},{80,112},{96,128},{112,144}... | collective-permute-start | bytes 786440 | tf_op jit(solution)/shard_map/ppermute | solution.py:37
  103.0 11.8 %collective-permute-start.11 = (bf16[512,256]{1,0:T(8,128)(2,1)S(1)}, bf16[512,256]{1,0:T(8,128)(2,1)S(1)}, u32[]{:S(2)}, u32[]{:S(2)}) collective-permute-start(bf16[512,256]{1,0:T(8,128)(2,1)S(1)} %collective-permute-done.10.rest_0_), channel_id=1, source_target_pairs={{0,32},{16,48},{32,64},{48,80},{64,96},{80,112},{96,128},{112,144}... | collective-permute-start | bytes 786440 | tf_op jit(solution)/shard_map/ppermute | solution.py:37
  109.7 7.0 %collective-permute-start.12 = (bf16[512,256]{1,0:T(8,128)(2,1)S(1)}, bf16[512,256]{1,0:T(8,128)(2,1)S(1)}, u32[]{:S(2)}, u32[]{:S(2)}) collective-permute-start(bf16[512,256]{1,0:T(8,128)(2,1)S(1)} %broadcast_select_fusion.3), channel_id=1, source_target_pairs={{0,16},{16,0},{32,48},{48,32},{64,80},{80,64},{96,112},{112,96},{1... | collective-permute-start | bytes 786440 | tf_op jit(solution)/shard_map/ppermute | solution.py:37
  116.7 7.4 %collective-permute-start.13 = (bf16[512,256]{1,0:T(8,128)(2,1)S(1)}, bf16[512,256]{1,0:T(8,128)(2,1)S(1)}, u32[]{:S(2)}, u32[]{:S(2)}) collective-permute-start(bf16[512,256]{1,0:T(8,128)(2,1)S(1)} %collective-permute-done.11.rest_0_), channel_id=1, source_target_pairs={{0,32},{16,48},{32,64},{48,80},{64,96},{80,112},{96,128},{112,144}... | collective-permute-start | bytes 786440 | tf_op jit(solution)/shard_map/ppermute | solution.py:37
  120.8 6.8 %collective-permute-start.14 = (bf16[512,256]{1,0:T(8,128)(2,1)S(1)}, bf16[512,256]{1,0:T(8,128)(2,1)S(1)}, u32[]{:S(2)}, u32[]{:S(2)}) collective-permute-start(bf16[512,256]{1,0:T(8,128)(2,1)S(1)} %broadcast_select_fusion.2), channel_id=1, source_target_pairs={{0,16},{16,0},{32,48},{48,32},{64,80},{80,64},{96,112},{112,96},{1... | collective-permute-start | bytes 786440 | tf_op jit(solution)/shard_map/ppermute | solution.py:37
  127.6 8.4 %collective-permute-start.15 = (bf16[512,256]{1,0:T(8,128)(2,1)S(1)}, bf16[512,256]{1,0:T(8,128)(2,1)S(1)}, u32[]{:S(2)}, u32[]{:S(2)}) collective-permute-start(bf16[512,256]{1,0:T(8,128)(2,1)S(1)} %collective-permute-done.13.rest_0_), channel_id=1, source_target_pairs={{0,32},{16,48},{32,64},{48,80},{64,96},{80,112},{96,128},{112,144}... | collective-permute-start | bytes 786440 | tf_op jit(solution)/shard_map/ppermute | solution.py:37
  131.7 6.8 %collective-permute-start.16 = (bf16[512,256]{1,0:T(8,128)(2,1)S(1)}, bf16[512,256]{1,0:T(8,128)(2,1)S(1)}, u32[]{:S(2)}, u32[]{:S(2)}) collective-permute-start(bf16[512,256]{1,0:T(8,128)(2,1)S(1)} %broadcast_select_fusion.1), channel_id=1, source_target_pairs={{0,16},{16,0},{32,48},{48,32},{64,80},{80,64},{96,112},{112,96},{1... | collective-permute-start | bytes 786440 | tf_op jit(solution)/shard_map/ppermute | solution.py:37
  138.5 7.9 %collective-permute-start.17 = (bf16[512,256]{1,0:T(8,128)(2,1)S(1)}, bf16[512,256]{1,0:T(8,128)(2,1)S(1)}, u32[]{:S(2)}, u32[]{:S(2)}) collective-permute-start(bf16[512,256]{1,0:T(8,128)(2,1)S(1)} %broadcast_select_fusion), channel_id=1, source_target_pairs={{0,16},{16,0},{32,48},{48,32},{64,80},{80,64},{96,112},{112,96},{1... | collective-permute-start | bytes 786440 | tf_op jit(solution)/shard_map/ppermute | solution.py:37
  154.7 14.4 %collective-permute-start.18 = (bf16[8,288,512]{2,1,0:T(8,128)(2,1)S(1)}, bf16[8,288,512]{2,1,0:T(8,128)(2,1)S(1)}, u32[]{:S(2)}, u32[]{:S(2)}) collective-permute-start(bf16[8,288,512]{2,1,0:T(8,128)(2,1)S(1)} %shard_map.118), channel_id=1, source_target_pairs={{0,1},{1,0},{2,3},{3,2},{4,5},{5,4},{6,7},{7,6},{8,9},{9,8},{10,11... | collective-permute-start | bytes 7077896 | tf_op jit(solution)/shard_map/ppermute | solution.py:369
  174.3 35.0 %all-to-all-start = ((bf16[8,288,512]{2,1,0:T(8,128)(2,1)}), bf16[8,288,512]{2,1,0:T(8,128)(2,1)S(1)}, u32[]{:S(2)}, u32[]{:S(2)}) async-start(bf16[8,288,512]{2,1,0:T(8,128)(2,1)} %copy-done.2), calls=%async_computation | async-start | bytes 4718592 | tf_op jit(solution)/shard_map/all_to_all | solution.py:371
  210.3 10.7 %all-to-all-start.1 = ((f32[16,1,512]{2,1,0:T(1,128)}), f32[16,1,512]{2,1,0:T(1,128)S(1)}, u32[]{:S(2)}, u32[]{:S(2)}) async-start(f32[16,1,512]{2,1,0:T(1,128)} %broadcast_in_dim.49), calls=%async_computation.1 | async-start | bytes 65536 | tf_op jit(solution)/shard_map/all_to_all | solution.py:374
  (18 other events, 371.3 us)
Sparse Core Ops, SparseCore 0:
  10.1 47.0 all-gather.4
  59.6 48.3 all-gather.6

commit v6 on v3

--- a/solution.py
+++ b/solution.py
@@ -18,6 +18,7 @@
 EPSILON = 1e-06
 SOFT_CAP = 50.0
 LOG2E = 1.4426950408889634
+QUERY = float(D // HQ) ** (-0.5)
 EXTRA = 16
 SEQ = 16
 ROUNDS = 8
@@ -41,6 +42,7 @@
 DOWN = [((i + 4) % SEQ, i) for i in range(SEQ)]
 SWAP = [(i, i ^ 1) for i in range(SEQ)]
 COLUMNS = [[2 * i + c for i in range(ROUNDS)] for c in range(2)]
+
 PLACES = (((0, 0), (0, 1)), ((-1, 0), (-1, 1)), ((1, 0), (1, 1)), ((2, 0),), ((2, 1),))
 
 
@@ -56,24 +58,57 @@
     return lax.optimization_barrier(values)
 
 
-def project_kernel(pieces, rotated, factor, index_ref, cos_ref, sin_ref, x_hbm, *rest):
-    w_refs = rest[:-6]
-    out_ref, x_ref, w_ref, acc_ref, x_sem, w_sem = rest[-6:]
-    chunks, depth, rows = x_ref.shape
+def block_kernel(segment_ref, key_ref, value_ref, query_ref, out_ref):
+    features = key_ref.shape[0]
+    out_ref[:features, :HD] = key_ref[...]
+    out_ref[:features, HD : 2 * HD] = value_ref[...]
+    out_ref[:features, 2 * HD :] = query_ref[...]
+    shape = (EXTRA, 4 * HD)
+    lane = lax.broadcasted_iota(jnp.int32, shape, 1)
+    digits = jnp.zeros(shape, F32)
+    for s in range(1, SEGS):
+        count = jnp.sum((segment_ref[...] < s).astype(F32), axis=1, keepdims=True)
+        upper = jnp.floor(count * (1.0 / 16.0))
+        digits = jnp.where(lane == s - 1, upper, digits)
+        digits = jnp.where(lane == s + SEGS - 2, count - 16.0 * upper, digits)
+    third = lax.broadcasted_iota(jnp.int32, shape, 0) == 2
+    out_ref[features:, :] = jnp.where(third, digits, 0.0).astype(BF)
+
+
+def weight_block(segments, w_key, w_value, w_query):
+    vmem = pl.BlockSpec(memory_space=pltpu.VMEM)
+    return pl.pallas_call(
+        block_kernel,
+        out_shape=jax.ShapeDtypeStruct((w_key.shape[0] + EXTRA, 4 * HD), BF),
+        in_specs=[vmem] * 4,
+        out_specs=vmem,
+        compiler_params=pltpu.CompilerParams(vmem_limit_bytes=8 << 20),
+        cost_estimate=pl.CostEstimate(flops=1 << 18, bytes_accessed=1 << 19, transcendentals=0),
+    )(segments[None, :], w_key, w_value, w_query)
+
+
+def load_weights(order_ref, offsets, w_refs, w_ref, sem, compact):
     copies = []
-    for slot in range(ROUNDS):
-        place = index_ref[2 + ROUNDS + slot]
+    for k, (offset, source) in enumerate(zip(offsets, w_refs)):
+        depth = w_ref.shape[1]
         for part in range(2):
-            parity = index_ref[1] if part == 0 else 1 - index_ref[1]
-            which, lead = pieces[slot]
-            source = w_refs[which] if lead is None else w_refs[which].at[lead]
+            parity = order_ref[0] if part == 0 else 1 - order_ref[0]
+            place = 0 if compact else order_ref[1 + k]
             copies.append(
                 pltpu.make_async_copy(
                     source.at[pl.ds(part * depth, depth)],
-                    w_ref.at[2 * place + parity],
-                    w_sem.at[2 * slot + part],
+                    w_ref.at[2 * place + parity, :, pl.ds(offset, source.shape[1])],
+                    sem.at[2 * k + part],
                 )
             )
+    return copies
+
+
+def early_kernel(order_ref, x_hbm, *rest):
+    w_refs = rest[:-6]
+    acc_ref, square_ref, x_ref, w_ref, x_sem, w_sem = rest[-6:]
+    chunks, depth, rows = x_ref.shape
+    copies = load_weights(order_ref, (0,) * len(w_refs), w_refs, w_ref, w_sem, False)
     step = chunks // 4
     for k in range(4):
         copies.append(
@@ -83,6 +118,7 @@
         )
     for copy in copies:
         copy.start()
+    w_ref[pl.ds(2 * order_ref[1 + len(w_refs)], 2)] = jnp.zeros((2, depth, 4 * HD), BF)
     for copy in copies[:-4]:
         copy.wait()
     squares = jnp.zeros((1, rows), F32)
@@ -92,7 +128,7 @@
         side = x_ref[here, depth - EXTRA :, :].astype(F32)
         squares = squares + jnp.sum(jnp.sum(side, axis=0), axis=0, keepdims=True)
         product = lax.dot_general(
-            w_ref[here].reshape(step * depth, 2 * HD),
+            w_ref[here].reshape(step * depth, 4 * HD),
             x_ref[here].reshape(step * depth, rows),
             (((0,), (0,)), ((), ())),
             preferred_element_type=F32,
@@ -101,46 +137,94 @@
             acc_ref[...] = product
         else:
             acc_ref[...] += product
-    scale = lax.rsqrt(squares * (1.0 / D) + EPSILON)
+    square_ref[...] = squares
+
+
+def late_kernel(offsets, order_ref, acc_ref, square_ref, cos_ref, sin_ref, x_hbm, *rest):
+    w_refs = rest[:-6]
+    kv_ref, q_ref, x_ref, w_ref, x_sem, w_sem = rest[-6:]
+    _, depth, rows = x_ref.shape
+    copies = load_weights(order_ref, offsets, w_refs, w_ref, w_sem, True)
+    copies.append(
+        pltpu.make_async_copy(x_hbm.at[pl.ds(2 * order_ref[ROUNDS], 2)], x_ref, x_sem)
+    )
+    for copy in copies:
+        copy.start()
+    for copy in copies:
+        copy.wait()
+    scale = lax.rsqrt(square_ref[...] * (1.0 / D) + EPSILON)
     half = HD // 2
-    for head in range(2):
-        start = head * HD
-        if rotated[head]:
-            first = acc_ref[start : start + half, :] * scale
-            second = acc_ref[start + half : start + HD, :] * scale
-            cos, sin = cos_ref[...], sin_ref[...]
+    cos, sin = cos_ref[...], sin_ref[...]
+    for head, (ref, place, factor) in enumerate(
+        ((kv_ref, 0, 1.0), (kv_ref, 1, None), (q_ref, 0, QUERY), (q_ref, 1, QUERY))
+    ):
+        if head % 2 == 0:
+            columns = slice(head * HD, (head + 2) * HD)
+            product = acc_ref[columns, :] + lax.dot_general(
+                w_ref[:, :, columns].reshape(2 * depth, 2 * HD),
+                x_ref[...].reshape(2 * depth, rows),
+                (((0,), (0,)), ((), ())),
+                preferred_element_type=F32,
+            )
+        value = product[place * HD : (place + 1) * HD] * scale
+        if factor is not None:
+            first, second = value[:half], value[half:]
             value = jnp.concatenate(
                 [first * cos - second * sin, second * cos + first * sin], axis=0
             )
             if factor != 1.0:
                 value = value * factor
-        else:
-            value = acc_ref[start : start + HD, :] * scale
-        out_ref[:, start : start + HD] = jnp.transpose(value).astype(BF)
-
-
-def project(x_all, weights, pieces, index, cos, sin, rotated, factor):
+        ref[:, place * HD : (place + 1) * HD] = jnp.transpose(value).astype(BF)
+
+
+def project_early(x_all, blocks, order):
     chunks, depth, rows = x_all.shape
     vmem = pl.BlockSpec(memory_space=pltpu.VMEM)
     outside = pl.BlockSpec(memory_space=pl.ANY)
     return pl.pallas_call(
-        functools.partial(project_kernel, pieces, rotated, factor),
-        out_shape=jax.ShapeDtypeStruct((rows, 2 * HD), BF),
-        in_specs=[pl.BlockSpec(memory_space=pltpu.SMEM), vmem, vmem]
-        + [outside] * (1 + len(weights)),
-        out_specs=vmem,
+        early_kernel,
+        out_shape=(
+            jax.ShapeDtypeStruct((4 * HD, rows), F32),
+            jax.ShapeDtypeStruct((1, rows), F32),
+        ),
+        in_specs=[pl.BlockSpec(memory_space=pltpu.SMEM)] + [outside] * (1 + len(blocks)),
+        out_specs=(vmem, vmem),
         scratch_shapes=[
             pltpu.VMEM((chunks, depth, rows), BF),
-            pltpu.VMEM((chunks, depth, 2 * HD), BF),
-            pltpu.VMEM((2 * HD, rows), F32),
+            pltpu.VMEM((chunks, depth, 4 * HD), BF),
             pltpu.SemaphoreType.DMA((4,)),
-            pltpu.SemaphoreType.DMA((2 * ROUNDS,)),
+            pltpu.SemaphoreType.DMA((2 * len(blocks),)),
         ],
         compiler_params=pltpu.CompilerParams(vmem_limit_bytes=60 << 20),
         cost_estimate=pl.CostEstimate(
-            flops=2 * rows * 2 * HD * D, bytes_accessed=8 << 20, transcendentals=0
-        ),
-    )(index, cos, sin, x_all, *weights)
+            flops=2 * rows * 4 * HD * D, bytes_accessed=10 << 20, transcendentals=0
+        ),
+    )(order, x_all, *blocks)
+
+
+def project_late(partial, x_all, blocks, order, cos, sin):
+    _, depth, rows = x_all.shape
+    vmem = pl.BlockSpec(memory_space=pltpu.VMEM)
+    outside = pl.BlockSpec(memory_space=pl.ANY)
+    out = jax.ShapeDtypeStruct((rows, 2 * HD), BF)
+    return pl.pallas_call(
+        functools.partial(late_kernel, tuple(offset for _, offset in blocks)),
+        out_shape=(out, out),
+        in_specs=[pl.BlockSpec(memory_space=pltpu.SMEM)]
+        + [vmem] * 4
+        + [outside] * (1 + len(blocks)),
+        out_specs=(vmem, vmem),
+        scratch_shapes=[
+            pltpu.VMEM((2, depth, rows), BF),
+            pltpu.VMEM((2, depth, 4 * HD), BF),
+            pltpu.SemaphoreType.DMA,
+            pltpu.SemaphoreType.DMA((2 * len(blocks),)),
+        ],
+        compiler_params=pltpu.CompilerParams(vmem_limit_bytes=60 << 20),
+        cost_estimate=pl.CostEstimate(
+            flops=2 * rows * 4 * HD * D // 8, bytes_accessed=4 << 20, transcendentals=0
+        ),
+    )(order, *partial, cos, sin, x_all, *[block for block, _ in blocks])
 
 
 def attend_kernel(distances, first, last, low_ref, q_ref, *rest):
@@ -270,7 +354,10 @@
     h = lax.rem(seq_index, 2)
     base = seq_index * rows
 
-    x_own = tokens.T.astype(F32)
+    own = weight_block(segment_ids, w_key, w_value, w_query)
+    facing = move(own, ACROSS)
+    x_own, own = tie(tokens.T, own)
+    x_own = x_own.astype(F32)
     gained = (x_own * (1.0 + pre_gain.astype(F32))[:, None]).astype(BF)
     squares = jnp.sum(x_own * x_own, axis=0, keepdims=True)
     upper = lax.reduce_precision(squares, 8, 7)
@@ -281,56 +368,48 @@
     x_all = lax.all_gather(jnp.concatenate([gained, side], axis=0), "mp", axis=0)
     depth = features + EXTRA
 
-    lane = jnp.arange(2 * HD, dtype=jnp.int32)
-    marked = 2 * (SEGS - 1)
-    limit = jnp.where(lane < marked, lax.rem(lane, SEGS - 1) + 1, 0)
-    counts = jnp.sum((segment_ids[:, None] < limit[None, :]).astype(F32), axis=0)
-    upper_digit = jnp.floor(counts * (1.0 / 16.0))
-    digits = jnp.where(lane < SEGS - 1, upper_digit, counts - 16.0 * upper_digit).astype(BF)
-    digits = jnp.pad(digits[None, :], ((2, EXTRA - 3), (0, 0)))
-    kv_own = jnp.concatenate([jnp.concatenate([w_key, w_value], axis=1), digits], axis=0)
-    start = jnp.concatenate([kv_own, move(kv_own, ACROSS)], axis=0)
+    start = jnp.concatenate([own, facing], axis=0)
     ring = {0: start, 1: move(start, AHEAD), -1: move(start, BEHIND)}
     turned = lax.ppermute(w_out.T, ("seq", "mp"), TURNS[0])
+    ring[1], ring[-1], turned = tie(ring[1], ring[-1], turned)
+    turned = lax.ppermute(turned, ("seq", "mp"), TURNS[1])
     ring[2] = move(ring[1], AHEAD)
     ring[-2] = move(ring[-1], BEHIND)
     ring[2], ring[-2], turned = tie(ring[2], ring[-2], turned)
-    q_own = jnp.pad(w_query, ((0, EXTRA), (0, 0)))
-    q_own, _ = tie(q_own, ring[1])
-    q_pair = jnp.concatenate([q_own, move(q_own, ACROSS)], axis=0)
-    turned = lax.ppermute(turned, ("seq", "mp"), TURNS[1])
+    turned = lax.ppermute(turned, ("seq", "mp"), TURNS[2])
     ring[3] = move(ring[2], AHEAD)
     ring[-3] = move(ring[-2], BEHIND)
-    ring[3], ring[-3], turned, q_pair = tie(ring[3], ring[-3], turned, q_pair)
-    q_all = lax.all_gather(q_pair, "seq", axis=0, axis_index_groups=COLUMNS)
-    turned = lax.ppermute(turned, ("seq", "mp"), TURNS[2])
-    last = move(ring[3][:, :HD], AHEAD)
-    ring[4] = jnp.concatenate([last, move(ring[-3][:, HD:], BEHIND)], axis=1)
-    ring[4], turned = tie(ring[4], turned)
-    facing_out = move(turned, ACROSS)
+    ring[3], ring[-3], turned = tie(ring[3], ring[-3], turned)
+    out_facing = move(turned, ACROSS)
+    last = move(ring[3][:, : 2 * HD], AHEAD)
+    opposite = move(ring[-3][:, 2 * HD :], BEHIND)
+    steps = [0, 1, -1, 2, -2, 3, -3, 4, 4]
+    blocks = [(ring[step], 0) for step in steps[:7]] + [(last, 0), (opposite, 2 * HD)]
+    places = [lax.rem(z - step + ROUNDS, ROUNDS) for step in steps]
+    order = jnp.stack([h, *places]).astype(jnp.int32)
+    partial = project_early(x_all, [block for block, _ in blocks[:7]], order)
+    last, opposite, out_facing, *partial = tie(last, opposite, out_facing, *partial)
+    blocks[7:] = [(last, 0), (opposite, 2 * HD)]
+    out_all = lax.all_gather(
+        jnp.concatenate([turned, out_facing], axis=0),
+        "seq",
+        axis=0,
+        axis_index_groups=COLUMNS,
+    )
 
     mp_index = lax.axis_index("mp")
     y = mp_index // 4
     over = lax.rem(mp_index // 2, 2)
     placed = [
         2 * lax.rem(y + dy + 4, 4) + jnp.where(dx == 0, over, 1 - over)
-        for places in PLACES
-        for dy, dx in places
+        for pairs in PLACES
+        for dy, dx in pairs
     ]
-
-    def index_of(steps, origin):
-        places = [lax.rem(jnp.int32(origin - step + ROUNDS), ROUNDS) for step in steps]
-        return jnp.stack([lax.rem(mp_index, 2), h, *placed, *places]).astype(jnp.int32)
-
-    steps = [0, 1, -1, 2, -2, 3, -3, 4]
-    index = index_of(steps, z)
-    kv_weights = [ring[step] for step in steps]
-    kv_pieces = tuple((k, None) for k in range(ROUNDS))
-    q_pieces = tuple((0, k) for k in range(ROUNDS))
+    index = jnp.stack([lax.rem(mp_index, 2), h, *placed]).astype(jnp.int32)
 
     n_marks = 2 * (SEGS - 1)
     marks = jnp.zeros((n_marks,), F32)
-    for block in kv_weights:
+    for block, _ in blocks[:8]:
         for part in range(2):
             marks = marks + block[part * depth + features + 2, :n_marks].astype(F32)
     starts = (marks[: SEGS - 1] * 16.0 + marks[SEGS - 1 :]).astype(jnp.int32)
@@ -346,42 +425,37 @@
     cos = jnp.cos(angles)
     sin = jnp.sin(angles)
 
-    kv = project(x_all, kv_weights, kv_pieces, index, cos, sin, (True, False), 1.0)
+    kv, queries = project_late(partial, x_all, blocks[7:], order, cos, sin)
 
     straight, crossed, current = [kv], [None], kv
+    state = attend(low, queries, [kv], [0], None)
     for step in range(4):
         following = move(current, LATER)
         chosen = jnp.where(h == 0, current, following)
         if step == 0:
-            following, chosen, facing_out = tie(following, chosen, facing_out)
-            out_pair = jnp.concatenate([turned, facing_out], axis=0)
-            out_all = lax.all_gather(out_pair, "seq", axis=0, axis_index_groups=COLUMNS)
+            following, chosen = tie(following, chosen)
         else:
-            following, chosen, crossed[step] = tie(following, chosen, crossed[step])
+            following, chosen, crossed[step], *state = tie(
+                following, chosen, crossed[step], *state
+            )
+            if step > 1:
+                k = step - 1
+                state = attend(low, queries, [straight[k], crossed[k]], [2 * k, 2 * k - 1], state)
         straight.append(following)
         crossed.append(move(chosen, ACROSS))
         current = following
-    q_all, straight[-1] = tie(q_all, straight[-1])
-    queries = project(
-        x_all,
-        [q_all],
-        q_pieces,
-        index_of([-k for k in range(ROUNDS)], 0),
-        cos,
-        sin,
-        (True, True),
-        float(D // HQ) ** (-0.5),
-    )
-    state = attend(low, queries, [kv], [0], None)
-    for k in range(1, 5):
+    for k in range(3, 5):
         state = attend(low, queries, [straight[k], crossed[k]], [2 * k, 2 * k - 1], state)
 
     a_block = state[None]
     a_pair = jnp.concatenate([a_block, shift(a_block, SIDE)], axis=0)
     a_up, a_down = shift(a_pair, UP), shift(a_pair, DOWN)
-    a_up, a_down, out_all = tie(a_up, a_down, out_all)
+    a_swaps = [shift(a_pair, SWAP)]
+    a_up, a_down, out_all, a_swaps[0] = tie(a_up, a_down, out_all, a_swaps[0])
     a_far = [shift(a_up[:1], UP), shift(a_down[1:], DOWN)]
-    a_swaps = [shift(block, SWAP) for block in (a_pair, a_up, a_down, *a_far)]
+    a_swaps += [shift(a_up, SWAP), shift(a_down, SWAP)]
+    a_far[0], a_far[1], a_swaps[1], a_swaps[2] = tie(*a_far, *a_swaps[1:])
+    a_swaps += [shift(block, SWAP) for block in a_far]
     share, partial = output(
         [a_pair, a_up, a_down, *a_far, *a_swaps],
         out_all.reshape(2 * ROUNDS, features, 2 * HD),

time: 226 us -> 236 us (1.044)
  the two profiles are of different devices: /device:TPU:101 before, /device:TPU:1 now
where the time goes in v6:
time: 236 us; the launch traced here: 234 us
  starting transfers between devices  84.3 us (36%)
  waiting for transfers between devices  72.3 us (31%)
  Pallas kernels  28.3 us (12%)
  between operations  22.1 us (9%)
  local copies, waits for them, and re-layouts  15.6 us (7%)
  other arithmetic  11.5 us (5%)
    ppermute x18, waiting for transfers between devices, move(): return lax.ppermute(block, 'seq', perm)  54.3 us
    ppermute x18, starting transfers between devices, move(): return lax.ppermute(block, 'seq', perm)  42.3 us
    ppermute x10, starting transfers between devices, shift(): return lax.ppermute(block, 'mp', perm)  31.4 us
    pallas_call x5, Pallas kernels, attend(): pl.pallas_call(functools.partial(attend_kernel, tuple(distances), first,...  13.4 us
    unnamed x45, local copies, waits for them, and re-layouts  8.98 us
    pallas_call x1, Pallas kernels, project_early(): pl.pallas_call(early_kernel, out_shape=(jax.ShapeDtypeStruct((4 * HD, row...  8.07 us
    ppermute x10, waiting for transfers between devices, shift(): return lax.ppermute(block, 'mp', perm)  7.17 us
    ppermute x1, waiting for transfers between devices, shards(): turned = lax.ppermute(turned, ('seq', 'mp'), TURNS[1])  5.73 us
  transfers between devices with their start and end apart: 34, of which 17 were waited for; matrix products, arithmetic and copies ran while one was open for 5% of the time, Pallas kernels for 11%

profile of v6, /device:TPU:1, one launch (start us, length us, event | category | flops | bytes accessed | tf_op | source)
XLA Modules:
  0.0 234.1 jit_solution(10650605042415351436)
XLA Ops:
  13.5 3.7 %collective-permute-start = (bf16[304,512]{1,0:T(8,128)(2,1)S(1)}, bf16[304,512]{1,0:T(8,128)(2,1)S(1)}, u32[]{:S(2)}, u32[]{:S(2)}) collective-permute-start(bf16[304,512]{1,0:T(8,128)(2,1)S(1)} %shard_map.112), channel_id=1, source_target_pairs={{0,16},{16,0},{32,48},{48,32},{64,80},{80,64},{96,112},{112,96},{1... | collective-permute-start | bytes 933896 | tf_op jit(solution)/shard_map/ppermute | solution.py:50
  17.2 6.0 %collective-permute-done = bf16[304,512]{1,0:T(8,128)(2,1)S(1)} collective-permute-done((bf16[304,512]{1,0:T(8,128)(2,1)S(1)}, bf16[304,512]{1,0:T(8,128)(2,1)S(1)}, u32[]{:S(2)}, u32[]{:S(2)}) %collective-permute-start) | collective-permute-done | bytes 311328 | tf_op jit(solution)/shard_map/ppermute | solution.py:50
  25.9 4.0 %collective-permute-start.2 = (bf16[608,512]{1,0:T(8,128)(2,1)S(1)}, bf16[608,512]{1,0:T(8,128)(2,1)}, u32[]{:S(2)}, u32[]{:S(2)}) collective-permute-start(bf16[608,512]{1,0:T(8,128)(2,1)S(1)} %constant_dynamic-update-slice_fusion.rest_0_), channel_id=1, source_target_pairs={{32,0},{48,16},{64,32},{80,48},{96,64},{112,80},{128,96},{144,112}... | collective-permute-start | bytes 1867784 | tf_op jit(solution)/shard_map/ppermute | solution.py:50
  31.5 11.1 %collective-permute-done.1.rest_1_ = bf16[608,512]{1,0:T(8,128)(2,1)S(1)} collective-permute-done((bf16[608,512]{1,0:T(8,128)(2,1)S(1)}, bf16[608,512]{1,0:T(8,128)(2,1)S(1)}, u32[]{:S(2)}, u32[]{:S(2)}) %collective-permute-start.1) | collective-permute-done | bytes 622624 | tf_op jit(solution)/shard_map/ppermute | solution.py:50
  45.3 4.6 %collective-permute-start.6 = (bf16[288,256]{1,0:T(8,128)(2,1)S(1)}, bf16[288,256]{1,0:T(8,128)(2,1)S(1)}, u32[]{:S(2)}, u32[]{:S(2)}) collective-permute-start(bf16[288,256]{1,0:T(8,128)(2,1)S(1)} %collective-permute-done.3), channel_id=1, source_target_pairs={{0,0},{1,17},{2,34},{3,51},{4,68},{5,85},{6,102},{7,119},{8,136},{... | collective-permute-start | bytes 442376 | tf_op jit(solution)/shard_map/ppermute | solution.py:375
  49.9 5.7 %collective-permute-done.6 = bf16[288,256]{1,0:T(8,128)(2,1)S(1)} collective-permute-done((bf16[288,256]{1,0:T(8,128)(2,1)S(1)}, bf16[288,256]{1,0:T(8,128)(2,1)S(1)}, u32[]{:S(2)}, u32[]{:S(2)}) %collective-permute-start.6) | collective-permute-done | bytes 147488 | tf_op jit(solution)/shard_map/ppermute | solution.py:375
  57.3 8.0 %collective-permute-start.7 = (bf16[608,512]{1,0:T(8,128)(2,1)}, bf16[608,512]{1,0:T(8,128)(2,1)S(1)}, u32[]{:S(2)}, u32[]{:S(2)}) collective-permute-start(bf16[608,512]{1,0:T(8,128)(2,1)} %collective-permute-done.4.rest_3_), channel_id=1, source_target_pairs={{0,32},{16,48},{32,64},{48,80},{64,96},{80,112},{96,128},{112,144}... | collective-permute-start | bytes 1867784 | tf_op jit(solution)/shard_map/ppermute | solution.py:50
  66.6 9.3 %collective-permute-done.7.rest_5_ = bf16[608,512]{1,0:T(8,128)(2,1)S(1)} collective-permute-done((bf16[608,512]{1,0:T(8,128)(2,1)}, bf16[608,512]{1,0:T(8,128)(2,1)S(1)}, u32[]{:S(2)}, u32[]{:S(2)}) %collective-permute-start.7) | collective-permute-done | bytes 622624 | tf_op jit(solution)/shard_map/ppermute | solution.py:50
  84.1 8.1 %shard_map.113 = (f32[512,512]{1,0:T(8,128)}, f32[1,512]{1,0:T(1,128)}) custom-call(s32[10]{0:T(128)} %stack.96.order_ref, bf16[16,304,512]{2,1,0:T(8,128)(2,1)} %bitcast.64, bf16[608,512]{1,0:T(8,128)(2,1)} %copy-done.15, bf16[608,512]{1,0:T(8,128)(2,1)} %copy-done.16, bf16[608,512]{1,0:T(8,128)(2,1)} %collective-permute-done.2.rest_2_, ...), custom_call_target="tpu_custom_call" | custom-call | flops 2415919104 | bytes 10485760 | tf_op jit(solution)/shard_map/pallas_call | solution.py:184
  98.7 4.2 %shard_map.114 = (bf16[512,256]{1,0:T(8,128)(2,1)}, bf16[512,256]{1,0:T(8,128)(2,1)}) custom-call(s32[10]{0:T(128)} %stack.96.order_ref, f32[512,512]{1,0:T(8,128)} %get-tuple-element.72.acc_ref, f32[1,512]{1,0:T(1,128)} %get-tuple-element.73.square_ref, f32[64,512]{1,0:T(8,128)} %get-tuple-element.122.cos_ref, f32[64,512]{1,0:T(8,128)} %get-tuple-element.121.sin_ref, ...), custom_call_target="tpu_custom_call" | custom-call | flops 301989888 | bytes 4194304 | tf_op jit(solution)/shard_map/pallas_call | solution.py:210
  103.0 3.4 %collective-permute-start.13 = (bf16[512,256]{1,0:T(8,128)(2,1)}, bf16[512,256]{1,0:T(8,128)(2,1)S(1)}, u32[]{:S(2)}, u32[]{:S(2)}) collective-permute-start(bf16[512,256]{1,0:T(8,128)(2,1)} %get-tuple-element.76.rest_0_), channel_id=1, source_target_pairs={{0,32},{16,48},{32,64},{48,80},{64,96},{80,112},{96,128},{112,144}... | collective-permute-start | bytes 786440 | tf_op jit(solution)/shard_map/ppermute | solution.py:50
  106.4 4.9 %collective-permute-done.13.rest_0_ = bf16[512,256]{1,0:T(8,128)(2,1)S(1)} collective-permute-done((bf16[512,256]{1,0:T(8,128)(2,1)}, bf16[512,256]{1,0:T(8,128)(2,1)S(1)}, u32[]{:S(2)}, u32[]{:S(2)}) %collective-permute-start.13) | collective-permute-done | bytes 262176 | tf_op jit(solution)/shard_map/ppermute | solution.py:50
  112.3 4.1 %collective-permute-start.14 = (bf16[512,256]{1,0:T(8,128)(2,1)S(1)}, bf16[512,256]{1,0:T(8,128)(2,1)S(1)}, u32[]{:S(2)}, u32[]{:S(2)}) collective-permute-start(bf16[512,256]{1,0:T(8,128)(2,1)S(1)} %collective-permute-done.13.rest_0_), channel_id=1, source_target_pairs={{0,32},{16,48},{32,64},{48,80},{64,96},{80,112},{96,128},{112,144}... | collective-permute-start | bytes 786440 | tf_op jit(solution)/shard_map/ppermute | solution.py:50
  120.7 4.8 %collective-permute-done.14.rest_0_ = bf16[512,256]{1,0:T(8,128)(2,1)S(1)} collective-permute-done((bf16[512,256]{1,0:T(8,128)(2,1)S(1)}, bf16[512,256]{1,0:T(8,128)(2,1)S(1)}, u32[]{:S(2)}, u32[]{:S(2)}) %collective-permute-start.14) | collective-permute-done | bytes 262176 | tf_op jit(solution)/shard_map/ppermute | solution.py:50
  125.5 4.2 %collective-permute-start.16 = (bf16[512,256]{1,0:T(8,128)(2,1)S(1)}, bf16[512,256]{1,0:T(8,128)(2,1)S(1)}, u32[]{:S(2)}, u32[]{:S(2)}) collective-permute-start(bf16[512,256]{1,0:T(8,128)(2,1)S(1)} %collective-permute-done.14.rest_0_), channel_id=1, source_target_pairs={{0,32},{16,48},{32,64},{48,80},{64,96},{80,112},{96,128},{112,144}... | collective-permute-start | bytes 786440 | tf_op jit(solution)/shard_map/ppermute | solution.py:50
  129.9 10.2 %collective-permute-done.16.rest_0_ = bf16[512,256]{1,0:T(8,128)(2,1)S(1)} collective-permute-done((bf16[512,256]{1,0:T(8,128)(2,1)S(1)}, bf16[512,256]{1,0:T(8,128)(2,1)S(1)}, u32[]{:S(2)}, u32[]{:S(2)}) %collective-permute-start.16) | collective-permute-done | bytes 262176 | tf_op jit(solution)/shard_map/ppermute | solution.py:50
  140.1 4.2 %collective-permute-start.18 = (bf16[512,256]{1,0:T(8,128)(2,1)S(1)}, bf16[512,256]{1,0:T(8,128)(2,1)S(1)}, u32[]{:S(2)}, u32[]{:S(2)}) collective-permute-start(bf16[512,256]{1,0:T(8,128)(2,1)S(1)} %collective-permute-done.16.rest_0_), channel_id=1, source_target_pairs={{0,32},{16,48},{32,64},{48,80},{64,96},{80,112},{96,128},{112,144}... | collective-permute-start | bytes 786440 | tf_op jit(solution)/shard_map/ppermute | solution.py:50
  158.7 2.9 %shard_map.119 = bf16[512,256]{1,0:T(8,128)(2,1)S(1)} custom-call(s32[512,1]{1,0:T(8,128)S(1)} %copy.32.low_ref, bf16[512,256]{1,0:T(8,128)(2,1)S(1)} %copy-done.12, bf16[512,256]{1,0:T(8,128)(2,1)S(1)} %collective-permute-done.18.rest_0_, bf16[512,256]{1,0:T(8,128)(2,1)S(1)} %collective-permute-done.20.rest_1_, f32[512,256]{1,0:T(8,128)S(1)} %get-tuple-element.100.rest_2_, ...), custom_call_target="tpu_custom_call" | custom-call | flops 536870912 | bytes 4194304 | tf_op jit(solution)/shard_map/pallas_call | solution.py:286
  161.6 8.4 %collective-permute-start.21 = (bf16[1,512,256]{2,1,0:T(8,128)(2,1)S(1)}, bf16[1,512,256]{2,1,0:T(8,128)(2,1)S(1)}, u32[]{:S(2)}, u32[]{:S(2)}) collective-permute-start(bf16[1,512,256]{2,1,0:T(8,128)(2,1)S(1)} %bitcast.60), channel_id=1, source_target_pairs={{0,2},{1,3},{2,0},{3,1},{4,6},{5,7},{6,4},{7,5},{8,10},{9,11},{10,... | collective-permute-start | bytes 786440 | tf_op jit(solution)/shard_map/ppermute | solution.py:54
  170.0 4.1 %collective-permute-done.21 = bf16[1,512,256]{2,1,0:T(8,128)(2,1)S(1)} collective-permute-done((bf16[1,512,256]{2,1,0:T(8,128)(2,1)S(1)}, bf16[1,512,256]{2,1,0:T(8,128)(2,1)S(1)}, u32[]{:S(2)}, u32[]{:S(2)}) %collective-permute-start.21) | collective-permute-done | bytes 262176 | tf_op jit(solution)/shard_map/ppermute | solution.py:54
  176.9 10.6 %collective-permute-start.24 = (bf16[2,512,256]{2,1,0:T(8,128)(2,1)S(1)}, bf16[2,512,256]{2,1,0:T(8,128)(2,1)S(1)}, u32[]{:S(2)}, u32[]{:S(2)}) collective-permute-start(bf16[2,512,256]{2,1,0:T(8,128)(2,1)S(1)} %pad_maximum_fusion.rest_0_), channel_id=1, source_target_pairs={{0,1},{1,0},{2,3},{3,2},{4,5},{5,4},{6,7},{7,6},{8,9},{9,8},{10,11... | collective-permute-start | bytes 1572872 | tf_op jit(solution)/shard_map/ppermute | solution.py:54
  189.0 5.7 %collective-permute-start.27 = (bf16[2,512,256]{2,1,0:T(8,128)(2,1)S(1)}, bf16[2,512,256]{2,1,0:T(8,128)(2,1)S(1)}, u32[]{:S(2)}, u32[]{:S(2)}) collective-permute-start(bf16[2,512,256]{2,1,0:T(8,128)(2,1)S(1)} %collective-permute-done.22.rest_1_), channel_id=1, source_target_pairs={{0,1},{1,0},{2,3},{3,2},{4,5},{5,4},{6,7},{7,6},{8,9},{9,8},{10,11... | collective-permute-start | bytes 1572872 | tf_op jit(solution)/shard_map/ppermute | solution.py:54
  215.9 3.7 %all-to-all-start = ((f32[16,1,512]{2,1,0:T(1,128)}), f32[16,1,512]{2,1,0:T(1,128)S(1)}, u32[]{:S(2)}, u32[]{:S(2)}) async-start(f32[16,1,512]{2,1,0:T(1,128)} %broadcast_in_dim.44), calls=%async_computation | async-start | bytes 65536 | tf_op jit(solution)/shard_map/all_to_all | solution.py:465
  220.3 5.1 %all-to-all-done = f32[16,1,512]{2,1,0:T(1,128)S(1)} async-done(((f32[16,1,512]{2,1,0:T(1,128)}), f32[16,1,512]{2,1,0:T(1,128)S(1)}, u32[]{:S(2)}, u32[]{:S(2)}) %all-to-all-start) | async-done | bytes 32800 | tf_op jit(solution)/shard_map/all_to_all | solution.py:465
  (137 shorter events, 70.9 us)
Async XLA Ops:
  7.2 76.9 %all-gather.5.cloned.1.call-start = ((), (), s32[]{:S(2)}) async-start(), calls=%async_computation.1 | async-start | bytes 5292032 | tf_op jit(solution)/shard_map/all_gather | solution.py:368
  13.4 175.6 %all-gather.7.cloned.1.call-start = ((), (), s32[]{:S(2)}) async-start(), calls=%async_computation.2 | async-start | bytes 2654208 | tf_op jit(solution)/shard_map/all_gather | solution.py:393
  13.5 9.7 %collective-permute-start = (bf16[304,512]{1,0:T(8,128)(2,1)S(1)}, bf16[304,512]{1,0:T(8,128)(2,1)S(1)}, u32[]{:S(2)}, u32[]{:S(2)}) collective-permute-start(bf16[304,512]{1,0:T(8,128)(2,1)S(1)} %shard_map.112), channel_id=1, source_target_pairs={{0,16},{16,0},{32,48},{48,32},{64,80},{80,64},{96,112},{112,96},{1... | collective-permute-start | bytes 933896 | tf_op jit(solution)/shard_map/ppermute | solution.py:50
  23.2 19.4 %collective-permute-start.1 = (bf16[608,512]{1,0:T(8,128)(2,1)S(1)}, bf16[608,512]{1,0:T(8,128)(2,1)S(1)}, u32[]{:S(2)}, u32[]{:S(2)}) collective-permute-start(bf16[608,512]{1,0:T(8,128)(2,1)S(1)} %constant_dynamic-update-slice_fusion.rest_0_), channel_id=1, source_target_pairs={{0,32},{16,48},{32,64},{48,80},{64,96},{80,112},{96,128},{112,144}... | collective-permute-start | bytes 1867784 | tf_op jit(solution)/shard_map/ppermute | solution.py:50
  25.9 16.7 %collective-permute-start.2 = (bf16[608,512]{1,0:T(8,128)(2,1)S(1)}, bf16[608,512]{1,0:T(8,128)(2,1)}, u32[]{:S(2)}, u32[]{:S(2)}) collective-permute-start(bf16[608,512]{1,0:T(8,128)(2,1)S(1)} %constant_dynamic-update-slice_fusion.rest_0_), channel_id=1, source_target_pairs={{32,0},{48,16},{64,32},{80,48},{96,64},{112,80},{128,96},{144,112}... | collective-permute-start | bytes 1867784 | tf_op jit(solution)/shard_map/ppermute | solution.py:50
  42.6 14.7 %collective-permute-start.4 = (bf16[608,512]{1,0:T(8,128)(2,1)S(1)}, bf16[608,512]{1,0:T(8,128)(2,1)}, u32[]{:S(2)}, u32[]{:S(2)}) collective-permute-start(bf16[608,512]{1,0:T(8,128)(2,1)S(1)} %collective-permute-done.1.rest_1_), channel_id=1, source_target_pairs={{0,32},{16,48},{32,64},{48,80},{64,96},{80,112},{96,128},{112,144}... | collective-permute-start | bytes 1867784 | tf_op jit(solution)/shard_map/ppermute | solution.py:50
  42.6 14.6 %collective-permute-start.5 = (bf16[608,512]{1,0:T(8,128)(2,1)}, bf16[608,512]{1,0:T(8,128)(2,1)}, u32[]{:S(2)}, u32[]{:S(2)}) collective-permute-start(bf16[608,512]{1,0:T(8,128)(2,1)} %collective-permute-done.2.rest_2_), channel_id=1, source_target_pairs={{32,0},{48,16},{64,32},{80,48},{96,64},{112,80},{128,96},{144,112}... | collective-permute-start | bytes 1867784 | tf_op jit(solution)/shard_map/ppermute | solution.py:50
  45.3 10.4 %collective-permute-start.6 = (bf16[288,256]{1,0:T(8,128)(2,1)S(1)}, bf16[288,256]{1,0:T(8,128)(2,1)S(1)}, u32[]{:S(2)}, u32[]{:S(2)}) collective-permute-start(bf16[288,256]{1,0:T(8,128)(2,1)S(1)} %collective-permute-done.3), channel_id=1, source_target_pairs={{0,0},{1,17},{2,34},{3,51},{4,68},{5,85},{6,102},{7,119},{8,136},{... | collective-permute-start | bytes 442376 | tf_op jit(solution)/shard_map/ppermute | solution.py:375
  57.3 18.7 %collective-permute-start.7 = (bf16[608,512]{1,0:T(8,128)(2,1)}, bf16[608,512]{1,0:T(8,128)(2,1)S(1)}, u32[]{:S(2)}, u32[]{:S(2)}) collective-permute-start(bf16[608,512]{1,0:T(8,128)(2,1)} %collective-permute-done.4.rest_3_), channel_id=1, source_target_pairs={{0,32},{16,48},{32,64},{48,80},{64,96},{80,112},{96,128},{112,144}... | collective-permute-start | bytes 1867784 | tf_op jit(solution)/shard_map/ppermute | solution.py:50
  65.3 12.4 %collective-permute-start.8 = (bf16[608,512]{1,0:T(8,128)(2,1)}, bf16[608,512]{1,0:T(8,128)(2,1)S(1)}, u32[]{:S(2)}, u32[]{:S(2)}) collective-permute-start(bf16[608,512]{1,0:T(8,128)(2,1)} %collective-permute-done.5.rest_4_), channel_id=1, source_target_pairs={{32,0},{48,16},{64,32},{80,48},{96,64},{112,80},{128,96},{144,112}... | collective-permute-start | bytes 1867784 | tf_op jit(solution)/shard_map/ppermute | solution.py:50
  78.5 13.7 %collective-permute-start.10 = (bf16[608,256]{1,0:T(8,128)(2,1)}, bf16[608,256]{1,0:T(8,128)(2,1)S(1)}, u32[]{:S(2)}, u32[]{:S(2)}) collective-permute-start(bf16[608,256]{1,0:T(8,128)(2,1)} %slice.141), channel_id=1, source_target_pairs={{0,32},{16,48},{32,64},{48,80},{64,96},{80,112},{96,128},{112,144}... | collective-permute-start | bytes 933896 | tf_op jit(solution)/shard_map/ppermute | solution.py:50
  80.2 12.0 %collective-permute-start.11 = (bf16[608,256]{1,0:T(8,128)(2,1)}, bf16[608,256]{1,0:T(8,128)(2,1)}, u32[]{:S(2)}, u32[]{:S(2)}) collective-permute-start(bf16[608,256]{1,0:T(8,128)(2,1)} %slice.142), channel_id=1, source_target_pairs={{32,0},{48,16},{64,32},{80,48},{96,64},{112,80},{128,96},{144,112}... | collective-permute-start | bytes 933896 | tf_op jit(solution)/shard_map/ppermute | solution.py:50
  81.9 10.3 %collective-permute-start.12 = (bf16[288,256]{1,0:T(8,128)(2,1)}, bf16[288,256]{1,0:T(8,128)(2,1)}, u32[]{:S(2)}, u32[]{:S(2)}) collective-permute-start(bf16[288,256]{1,0:T(8,128)(2,1)} %copy-done.18), channel_id=1, source_target_pairs={{0,16},{16,0},{32,48},{48,32},{64,80},{80,64},{96,112},{112,96},{1... | collective-permute-start | bytes 442376 | tf_op jit(solution)/shard_map/ppermute | solution.py:50
  112.3 13.2 %collective-permute-start.14 = (bf16[512,256]{1,0:T(8,128)(2,1)S(1)}, bf16[512,256]{1,0:T(8,128)(2,1)S(1)}, u32[]{:S(2)}, u32[]{:S(2)}) collective-permute-start(bf16[512,256]{1,0:T(8,128)(2,1)S(1)} %collective-permute-done.13.rest_0_), channel_id=1, source_target_pairs={{0,32},{16,48},{32,64},{48,80},{64,96},{80,112},{96,128},{112,144}... | collective-permute-start | bytes 786440 | tf_op jit(solution)/shard_map/ppermute | solution.py:50
  125.5 14.5 %collective-permute-start.16 = (bf16[512,256]{1,0:T(8,128)(2,1)S(1)}, bf16[512,256]{1,0:T(8,128)(2,1)S(1)}, u32[]{:S(2)}, u32[]{:S(2)}) collective-permute-start(bf16[512,256]{1,0:T(8,128)(2,1)S(1)} %collective-permute-done.14.rest_0_), channel_id=1, source_target_pairs={{0,32},{16,48},{32,64},{48,80},{64,96},{80,112},{96,128},{112,144}... | collective-permute-start | bytes 786440 | tf_op jit(solution)/shard_map/ppermute | solution.py:50
  129.8 10.3 %collective-permute-start.17 = (bf16[512,256]{1,0:T(8,128)(2,1)S(1)}, bf16[512,256]{1,0:T(8,128)(2,1)S(1)}, u32[]{:S(2)}, u32[]{:S(2)}) collective-permute-start(bf16[512,256]{1,0:T(8,128)(2,1)S(1)} %broadcast_select_fusion.2), channel_id=1, source_target_pairs={{0,16},{16,0},{32,48},{48,32},{64,80},{80,64},{96,112},{112,96},{1... | collective-permute-start | bytes 786440 | tf_op jit(solution)/shard_map/ppermute | solution.py:50
  161.6 12.4 %collective-permute-start.21 = (bf16[1,512,256]{2,1,0:T(8,128)(2,1)S(1)}, bf16[1,512,256]{2,1,0:T(8,128)(2,1)S(1)}, u32[]{:S(2)}, u32[]{:S(2)}) collective-permute-start(bf16[1,512,256]{2,1,0:T(8,128)(2,1)S(1)} %bitcast.60), channel_id=1, source_target_pairs={{0,2},{1,3},{2,0},{3,1},{4,6},{5,7},{6,4},{7,5},{8,10},{9,11},{10,... | collective-permute-start | bytes 786440 | tf_op jit(solution)/shard_map/ppermute | solution.py:54
  174.1 13.4 %collective-permute-start.22 = (bf16[2,512,256]{2,1,0:T(8,128)(2,1)S(1)}, bf16[2,512,256]{2,1,0:T(8,128)(2,1)S(1)}, u32[]{:S(2)}, u32[]{:S(2)}) collective-permute-start(bf16[2,512,256]{2,1,0:T(8,128)(2,1)S(1)} %pad_maximum_fusion.rest_0_), channel_id=1, source_target_pairs={{0,4},{1,5},{2,6},{3,7},{4,8},{5,9},{6,10},{7,11},{8,12},{9,13},{1... | collective-permute-start | bytes 1572872 | tf_op jit(solution)/shard_map/ppermute | solution.py:54
  174.2 13.3 %collective-permute-start.23 = (bf16[2,512,256]{2,1,0:T(8,128)(2,1)S(1)}, bf16[2,512,256]{2,1,0:T(8,128)(2,1)S(1)}, u32[]{:S(2)}, u32[]{:S(2)}) collective-permute-start(bf16[2,512,256]{2,1,0:T(8,128)(2,1)S(1)} %pad_maximum_fusion.rest_0_), channel_id=1, source_target_pairs={{4,0},{5,1},{6,2},{7,3},{8,4},{9,5},{10,6},{11,7},{12,8},{13,9},{1... | collective-permute-start | bytes 1572872 | tf_op jit(solution)/shard_map/ppermute | solution.py:54
  176.9 12.2 %collective-permute-start.24 = (bf16[2,512,256]{2,1,0:T(8,128)(2,1)S(1)}, bf16[2,512,256]{2,1,0:T(8,128)(2,1)S(1)}, u32[]{:S(2)}, u32[]{:S(2)}) collective-permute-start(bf16[2,512,256]{2,1,0:T(8,128)(2,1)S(1)} %pad_maximum_fusion.rest_0_), channel_id=1, source_target_pairs={{0,1},{1,0},{2,3},{3,2},{4,5},{5,4},{6,7},{7,6},{8,9},{9,8},{10,11... | collective-permute-start | bytes 1572872 | tf_op jit(solution)/shard_map/ppermute | solution.py:54
  189.0 18.3 %collective-permute-start.27 = (bf16[2,512,256]{2,1,0:T(8,128)(2,1)S(1)}, bf16[2,512,256]{2,1,0:T(8,128)(2,1)S(1)}, u32[]{:S(2)}, u32[]{:S(2)}) collective-permute-start(bf16[2,512,256]{2,1,0:T(8,128)(2,1)S(1)} %collective-permute-done.22.rest_1_), channel_id=1, source_target_pairs={{0,1},{1,0},{2,3},{3,2},{4,5},{5,4},{6,7},{7,6},{8,9},{9,8},{10,11... | collective-permute-start | bytes 1572872 | tf_op jit(solution)/shard_map/ppermute | solution.py:54
  194.8 12.6 %collective-permute-start.28 = (bf16[2,512,256]{2,1,0:T(8,128)(2,1)S(1)}, bf16[2,512,256]{2,1,0:T(8,128)(2,1)S(1)}, u32[]{:S(2)}, u32[]{:S(2)}) collective-permute-start(bf16[2,512,256]{2,1,0:T(8,128)(2,1)S(1)} %collective-permute-done.23.rest_2_), channel_id=1, source_target_pairs={{0,1},{1,0},{2,3},{3,2},{4,5},{5,4},{6,7},{7,6},{8,9},{9,8},{10,11... | collective-permute-start | bytes 1572872 | tf_op jit(solution)/shard_map/ppermute | solution.py:54
  196.3 11.0 %collective-permute-start.25 = (bf16[1,512,256]{2,1,0:T(8,128)(2,1)}, bf16[1,512,256]{2,1,0:T(8,128)(2,1)}, u32[]{:S(2)}, u32[]{:S(2)}) collective-permute-start(bf16[1,512,256]{2,1,0:T(8,128)(2,1)} %slice.150), channel_id=1, source_target_pairs={{0,4},{1,5},{2,6},{3,7},{4,8},{5,9},{6,10},{7,11},{8,12},{9,13},{1... | collective-permute-start | bytes 786440 | tf_op jit(solution)/shard_map/ppermute | solution.py:54
  196.3 11.1 %collective-permute-start.26 = (bf16[1,512,256]{2,1,0:T(8,128)(2,1)}, bf16[1,512,256]{2,1,0:T(8,128)(2,1)}, u32[]{:S(2)}, u32[]{:S(2)}) collective-permute-start(bf16[1,512,256]{2,1,0:T(8,128)(2,1)} %slice.151), channel_id=1, source_target_pairs={{4,0},{5,1},{6,2},{7,3},{8,4},{9,5},{10,6},{11,7},{12,8},{13,9},{1... | collective-permute-start | bytes 786440 | tf_op jit(solution)/shard_map/ppermute | solution.py:54
  (32 other events, 397.1 us)
Sparse Core Ops, SparseCore 0:
  13.6 46.9 all-gather.4
  94.1 52.7 all-gather.6

commit v7 on v3

--- a/solution.py
+++ b/solution.py
@@ -307,7 +307,6 @@
     last = move(ring[3][:, :HD], AHEAD)
     ring[4] = jnp.concatenate([last, move(ring[-3][:, HD:], BEHIND)], axis=1)
     ring[4], turned = tie(ring[4], turned)
-    facing_out = move(turned, ACROSS)
 
     mp_index = lax.axis_index("mp")
     y = mp_index // 4
@@ -348,40 +347,54 @@
 
     kv = project(x_all, kv_weights, kv_pieces, index, cos, sin, (True, False), 1.0)
 
-    straight, crossed, current = [kv], [None], kv
+    straight, crossed, current, state = [kv], [None], kv, None
     for step in range(4):
         following = move(current, LATER)
         chosen = jnp.where(h == 0, current, following)
         if step == 0:
-            following, chosen, facing_out = tie(following, chosen, facing_out)
-            out_pair = jnp.concatenate([turned, facing_out], axis=0)
-            out_all = lax.all_gather(out_pair, "seq", axis=0, axis_index_groups=COLUMNS)
+            following, chosen = tie(following, chosen)
+        elif step == 1:
+            following, chosen, crossed[1], q_all = tie(following, chosen, crossed[1], q_all)
+            queries = project(
+                x_all,
+                [q_all],
+                q_pieces,
+                index_of([-k for k in range(ROUNDS)], 0),
+                cos,
+                sin,
+                (True, True),
+                float(D // HQ) ** (-0.5),
+            )
+            state = attend(low, queries, [kv], [0], None)
         else:
-            following, chosen, crossed[step] = tie(following, chosen, crossed[step])
+            if step == 2:
+                facing_out = move(turned, ACROSS)
+                following, chosen, crossed[2], facing_out, *state = tie(
+                    following, chosen, crossed[2], facing_out, *state
+                )
+            else:
+                following, chosen, crossed[3], *state = tie(
+                    following, chosen, crossed[3], *state
+                )
+            k = step - 1
+            state = attend(low, queries, [straight[k], crossed[k]], [2 * k, 2 * k - 1], state)
         straight.append(following)
         crossed.append(move(chosen, ACROSS))
         current = following
-    q_all, straight[-1] = tie(q_all, straight[-1])
-    queries = project(
-        x_all,
-        [q_all],
-        q_pieces,
-        index_of([-k for k in range(ROUNDS)], 0),
-        cos,
-        sin,
-        (True, True),
-        float(D // HQ) ** (-0.5),
-    )
-    state = attend(low, queries, [kv], [0], None)
-    for k in range(1, 5):
+    out_pair, straight[4] = tie(jnp.concatenate([turned, facing_out], axis=0), straight[4])
+    out_all = lax.all_gather(out_pair, "seq", axis=0, axis_index_groups=COLUMNS)
+    for k in range(3, 5):
         state = attend(low, queries, [straight[k], crossed[k]], [2 * k, 2 * k - 1], state)
 
     a_block = state[None]
     a_pair = jnp.concatenate([a_block, shift(a_block, SIDE)], axis=0)
     a_up, a_down = shift(a_pair, UP), shift(a_pair, DOWN)
-    a_up, a_down, out_all = tie(a_up, a_down, out_all)
+    a_swaps = [shift(a_pair, SWAP)]
+    a_up, a_down, a_swaps[0] = tie(a_up, a_down, a_swaps[0])
     a_far = [shift(a_up[:1], UP), shift(a_down[1:], DOWN)]
-    a_swaps = [shift(block, SWAP) for block in (a_pair, a_up, a_down, *a_far)]
+    a_swaps += [shift(a_up, SWAP), shift(a_down, SWAP)]
+    a_far[0], a_far[1], a_swaps[1], a_swaps[2] = tie(*a_far, *a_swaps[1:])
+    a_swaps += [shift(block, SWAP) for block in a_far]
     share, partial = output(
         [a_pair, a_up, a_down, *a_far, *a_swaps],
         out_all.reshape(2 * ROUNDS, features, 2 * HD),

time: 226 us -> 223 us (0.987)
  the two profiles are of different devices: /device:TPU:101 before, /device:TPU:1 now
where the time goes in v7:
time: 223 us; the launch traced here: 221 us
  starting transfers between devices  84.2 us (38%)
  waiting for transfers between devices  52.5 us (24%)
  Pallas kernels  28.7 us (13%)
  between operations  21.8 us (10%)
  local copies, waits for them, and re-layouts  20.3 us (9%)
  other arithmetic  13.1 us (6%)
    ppermute x19, starting transfers between devices, move(): return lax.ppermute(block, 'seq', perm)  56.8 us
    ppermute x19, waiting for transfers between devices, move(): return lax.ppermute(block, 'seq', perm)  37.2 us
    ppermute x10, starting transfers between devices, shift(): return lax.ppermute(block, 'mp', perm)  18.8 us
    unnamed x65, local copies, waits for them, and re-layouts  14.3 us
    pallas_call x5, Pallas kernels, attend(): pl.pallas_call(functools.partial(attend_kernel, tuple(distances), first,...  13.4 us
    pallas_call x2, Pallas kernels, project(): pl.pallas_call(functools.partial(project_kernel, pieces, rotated, factor)...  13.3 us
    ppermute x10, waiting for transfers between devices, shift(): return lax.ppermute(block, 'mp', perm)  7.62 us
    all_to_all x1, starting transfers between devices, shards(): lax.all_to_all(everywhere, 'mp', 0, 0, tiled=True)  4.52 us
  transfers between devices with their start and end apart: 36, of which 13 were waited for; matrix products, arithmetic and copies ran while one was open for 7% of the time, Pallas kernels for 12%

profile of v7, /device:TPU:1, one launch (start us, length us, event | category | flops | bytes accessed | tf_op | source)
XLA Modules:
  0.0 220.5 jit_solution(8136636085246359959)
XLA Ops:
  12.8 3.7 %collective-permute-start = (bf16[304,256]{1,0:T(8,128)(2,1)S(1)}, bf16[304,256]{1,0:T(8,128)(2,1)S(1)}, u32[]{:S(2)}, u32[]{:S(2)}) collective-permute-start(bf16[304,256]{1,0:T(8,128)(2,1)S(1)} %pad_maximum_fusion.6), channel_id=1, source_target_pairs={{0,16},{16,0},{32,48},{48,32},{64,80},{80,64},{96,112},{112,96},{1... | collective-permute-start | bytes 466952 | tf_op jit(solution)/shard_map/ppermute | solution.py:48
  21.9 4.0 %collective-permute-start.2 = (bf16[608,256]{1,0:T(8,128)(2,1)S(1)}, bf16[608,256]{1,0:T(8,128)(2,1)S(1)}, u32[]{:S(2)}, u32[]{:S(2)}) collective-permute-start(bf16[608,256]{1,0:T(8,128)(2,1)S(1)} %pad_maximum_fusion.1.rest_0_), channel_id=1, source_target_pairs={{32,0},{48,16},{64,32},{80,48},{96,64},{112,80},{128,96},{144,112}... | collective-permute-start | bytes 933896 | tf_op jit(solution)/shard_map/ppermute | solution.py:48
  25.9 6.0 %collective-permute-done.1.rest_1_ = bf16[608,256]{1,0:T(8,128)(2,1)S(1)} collective-permute-done((bf16[608,256]{1,0:T(8,128)(2,1)S(1)}, bf16[608,256]{1,0:T(8,128)(2,1)S(1)}, u32[]{:S(2)}, u32[]{:S(2)}) %collective-permute-start.1) | collective-permute-done | bytes 311328 | tf_op jit(solution)/shard_map/ppermute | solution.py:48
  35.3 4.5 %collective-permute-done.3.rest_3_ = bf16[608,256]{1,0:T(8,128)(2,1)S(1)} collective-permute-done((bf16[608,256]{1,0:T(8,128)(2,1)S(1)}, bf16[608,256]{1,0:T(8,128)(2,1)S(1)}, u32[]{:S(2)}, u32[]{:S(2)}) %collective-permute-start.3) | collective-permute-done | bytes 311328 | tf_op jit(solution)/shard_map/ppermute | solution.py:48
  39.8 5.7 %collective-permute-start.6 = (bf16[608,256]{1,0:T(8,128)(2,1)S(1)}, bf16[608,256]{1,0:T(8,128)(2,1)S(1)}, u32[]{:S(2)}, u32[]{:S(2)}) collective-permute-start(bf16[608,256]{1,0:T(8,128)(2,1)S(1)} %collective-permute-done.3.rest_3_), channel_id=1, source_target_pairs={{0,32},{16,48},{32,64},{48,80},{64,96},{80,112},{96,128},{112,144}... | collective-permute-start | bytes 933896 | tf_op jit(solution)/shard_map/ppermute | solution.py:48
  45.8 4.8 %collective-permute-start.9 = (bf16[304,256]{1,0:T(8,128)(2,1)S(1)}, bf16[304,256]{1,0:T(8,128)(2,1)S(1)}, u32[]{:S(2)}, u32[]{:S(2)}) collective-permute-start(bf16[304,256]{1,0:T(8,128)(2,1)S(1)} %pad.9), channel_id=1, source_target_pairs={{0,16},{16,0},{32,48},{48,32},{64,80},{80,64},{96,112},{112,96},{1... | collective-permute-start | bytes 466952 | tf_op jit(solution)/shard_map/ppermute | solution.py:48
  52.5 3.5 %collective-permute-done.9 = bf16[304,256]{1,0:T(8,128)(2,1)S(1)} collective-permute-done((bf16[304,256]{1,0:T(8,128)(2,1)S(1)}, bf16[304,256]{1,0:T(8,128)(2,1)S(1)}, u32[]{:S(2)}, u32[]{:S(2)}) %collective-permute-start.9) | collective-permute-done | bytes 155680 | tf_op jit(solution)/shard_map/ppermute | solution.py:48
  56.8 3.5 %collective-permute-done.8 = bf16[288,256]{1,0:T(8,128)(2,1)S(1)} collective-permute-done((bf16[288,256]{1,0:T(8,128)(2,1)S(1)}, bf16[288,256]{1,0:T(8,128)(2,1)S(1)}, u32[]{:S(2)}, u32[]{:S(2)}) %collective-permute-start.8) | collective-permute-done | bytes 147488 | tf_op jit(solution)/shard_map/ppermute | solution.py:301
  65.3 3.2 %collective-permute-done.10 = bf16[608,128]{1,0:T(8,128)(2,1)S(1)} collective-permute-done((bf16[608,128]{1,0:T(8,128)(2,1)S(1)}, bf16[608,128]{1,0:T(8,128)(2,1)S(1)}, u32[]{:S(2)}, u32[]{:S(2)}) %collective-permute-start.10) | collective-permute-done | bytes 155680 | tf_op jit(solution)/shard_map/ppermute | solution.py:48
  72.6 6.7 %shard_map.112.rest_0_ = bf16[512,256]{1,0:T(8,128)(2,1)} custom-call(s32[18]{0:T(128)} %stack.103.index_ref, f32[64,512]{1,0:T(8,128)} %get-tuple-element.104.cos_ref, f32[64,512]{1,0:T(8,128)} %get-tuple-element.103.sin_ref, bf16[16,304,512]{2,1,0:T(8,128)(2,1)} %bitcast.73, bf16[608,256]{1,0:T(8,128)(2,1)} %copy-done.20, bf16[608,256]{1,0:T(8,128)(2,1)} %copy-done.23, ...), custom_call_target="tpu_custom_call" | custom-call | flops 1207959552 | bytes 8388608 | tf_op jit(solution)/shard_map/pallas_call | solution.py:126
  79.3 7.5 %collective-permute-start.13 = (bf16[512,256]{1,0:T(8,128)(2,1)}, bf16[512,256]{1,0:T(8,128)(2,1)S(1)}, u32[]{:S(2)}, u32[]{:S(2)}) collective-permute-start(bf16[512,256]{1,0:T(8,128)(2,1)} %shard_map.112.rest_0_), channel_id=1, source_target_pairs={{0,32},{16,48},{32,64},{48,80},{64,96},{80,112},{96,128},{112,144}... | collective-permute-start | bytes 786440 | tf_op jit(solution)/shard_map/ppermute | solution.py:48
  86.8 11.2 %collective-permute-done.13.rest_0_ = bf16[512,256]{1,0:T(8,128)(2,1)S(1)} collective-permute-done((bf16[512,256]{1,0:T(8,128)(2,1)}, bf16[512,256]{1,0:T(8,128)(2,1)S(1)}, u32[]{:S(2)}, u32[]{:S(2)}) %collective-permute-start.13) | collective-permute-done | bytes 262176 | tf_op jit(solution)/shard_map/ppermute | solution.py:48
  99.0 4.1 %collective-permute-start.14 = (bf16[512,256]{1,0:T(8,128)(2,1)S(1)}, bf16[512,256]{1,0:T(8,128)(2,1)S(1)}, u32[]{:S(2)}, u32[]{:S(2)}) collective-permute-start(bf16[512,256]{1,0:T(8,128)(2,1)S(1)} %collective-permute-done.13.rest_0_), channel_id=1, source_target_pairs={{0,32},{16,48},{32,64},{48,80},{64,96},{80,112},{96,128},{112,144}... | collective-permute-start | bytes 786440 | tf_op jit(solution)/shard_map/ppermute | solution.py:48
  103.1 4.3 %collective-permute-start.15 = (bf16[512,256]{1,0:T(8,128)(2,1)S(1)}, bf16[512,256]{1,0:T(8,128)(2,1)S(1)}, u32[]{:S(2)}, u32[]{:S(2)}) collective-permute-start(bf16[512,256]{1,0:T(8,128)(2,1)S(1)} %broadcast_select_fusion.3), channel_id=1, source_target_pairs={{0,16},{16,0},{32,48},{48,32},{64,80},{80,64},{96,112},{112,96},{1... | collective-permute-start | bytes 786440 | tf_op jit(solution)/shard_map/ppermute | solution.py:48
  107.4 4.9 %collective-permute-done.14.rest_0_ = bf16[512,256]{1,0:T(8,128)(2,1)S(1)} collective-permute-done((bf16[512,256]{1,0:T(8,128)(2,1)S(1)}, bf16[512,256]{1,0:T(8,128)(2,1)S(1)}, u32[]{:S(2)}, u32[]{:S(2)}) %collective-permute-start.14) | collective-permute-done | bytes 262176 | tf_op jit(solution)/shard_map/ppermute | solution.py:48
  113.4 3.1 %collective-permute-start.16 = (bf16[512,256]{1,0:T(8,128)(2,1)S(1)}, bf16[512,256]{1,0:T(8,128)(2,1)S(1)}, u32[]{:S(2)}, u32[]{:S(2)}) collective-permute-start(bf16[512,256]{1,0:T(8,128)(2,1)S(1)} %collective-permute-done.14.rest_0_), channel_id=1, source_target_pairs={{0,32},{16,48},{32,64},{48,80},{64,96},{80,112},{96,128},{112,144}... | collective-permute-start | bytes 786440 | tf_op jit(solution)/shard_map/ppermute | solution.py:48
  117.3 3.6 %collective-permute-start.18 = (bf16[288,256]{1,0:T(8,128)(2,1)}, bf16[288,256]{1,0:T(8,128)(2,1)S(1)}, u32[]{:S(2)}, u32[]{:S(2)}) collective-permute-start(bf16[288,256]{1,0:T(8,128)(2,1)} %collective-permute-done.12), channel_id=1, source_target_pairs={{0,16},{16,0},{32,48},{48,32},{64,80},{80,64},{96,112},{112,96},{1... | collective-permute-start | bytes 442376 | tf_op jit(solution)/shard_map/ppermute | solution.py:48
  121.2 6.6 %shard_map.113.q_ref = bf16[512,256]{1,0:T(8,128)(2,1)} custom-call(s32[18]{0:T(128)} %stack.104.index_ref, f32[64,512]{1,0:T(8,128)} %get-tuple-element.104.cos_ref, f32[64,512]{1,0:T(8,128)} %get-tuple-element.103.sin_ref, bf16[16,304,512]{2,1,0:T(8,128)(2,1)} %bitcast.74, bf16[8,608,256]{2,1,0:T(8,128)(2,1)} %bitcast.75), custom_call_target="tpu_custom_call" | custom-call | flops 1207959552 | bytes 8388608 | tf_op jit(solution)/shard_map/pallas_call | solution.py:126
  131.6 4.2 %collective-permute-start.19 = (bf16[512,256]{1,0:T(8,128)(2,1)S(1)}, bf16[512,256]{1,0:T(8,128)(2,1)S(1)}, u32[]{:S(2)}, u32[]{:S(2)}) collective-permute-start(bf16[512,256]{1,0:T(8,128)(2,1)S(1)} %collective-permute-done.16.rest_0_), channel_id=1, source_target_pairs={{0,32},{16,48},{32,64},{48,80},{64,96},{80,112},{96,128},{112,144}... | collective-permute-start | bytes 786440 | tf_op jit(solution)/shard_map/ppermute | solution.py:48
  155.5 5.3 %collective-permute-done.22 = bf16[1,512,256]{2,1,0:T(8,128)(2,1)S(1)} collective-permute-done((bf16[1,512,256]{2,1,0:T(8,128)(2,1)S(1)}, bf16[1,512,256]{2,1,0:T(8,128)(2,1)S(1)}, u32[]{:S(2)}, u32[]{:S(2)}) %collective-permute-start.22) | collective-permute-done | bytes 262176 | tf_op jit(solution)/shard_map/ppermute | solution.py:52
  164.5 5.1 %collective-permute-start.25 = (bf16[2,512,256]{2,1,0:T(8,128)(2,1)S(1)}, bf16[2,512,256]{2,1,0:T(8,128)(2,1)S(1)}, u32[]{:S(2)}, u32[]{:S(2)}) collective-permute-start(bf16[2,512,256]{2,1,0:T(8,128)(2,1)S(1)} %pad_maximum_fusion.rest_0_), channel_id=1, source_target_pairs={{0,1},{1,0},{2,3},{3,2},{4,5},{5,4},{6,7},{7,6},{8,9},{9,8},{10,11... | collective-permute-start | bytes 1572872 | tf_op jit(solution)/shard_map/ppermute | solution.py:52
  171.9 5.6 %collective-permute-start.28 = (bf16[2,512,256]{2,1,0:T(8,128)(2,1)S(1)}, bf16[2,512,256]{2,1,0:T(8,128)(2,1)S(1)}, u32[]{:S(2)}, u32[]{:S(2)}) collective-permute-start(bf16[2,512,256]{2,1,0:T(8,128)(2,1)S(1)} %collective-permute-done.23.rest_1_), channel_id=1, source_target_pairs={{0,1},{1,0},{2,3},{3,2},{4,5},{5,4},{6,7},{7,6},{8,9},{9,8},{10,11... | collective-permute-start | bytes 1572872 | tf_op jit(solution)/shard_map/ppermute | solution.py:52
  201.8 4.5 %all-to-all-start = ((f32[16,1,512]{2,1,0:T(1,128)}), f32[16,1,512]{2,1,0:T(1,128)S(1)}, u32[]{:S(2)}, u32[]{:S(2)}) async-start(f32[16,1,512]{2,1,0:T(1,128)} %broadcast_in_dim.48), calls=%async_computation | async-start | bytes 65536 | tf_op jit(solution)/shard_map/all_to_all | solution.py:404
  208.0 4.1 %all-to-all-done = f32[16,1,512]{2,1,0:T(1,128)S(1)} async-done(((f32[16,1,512]{2,1,0:T(1,128)}), f32[16,1,512]{2,1,0:T(1,128)S(1)}, u32[]{:S(2)}, u32[]{:S(2)}) %all-to-all-start) | async-done | bytes 32800 | tf_op jit(solution)/shard_map/all_to_all | solution.py:404
  (170 shorter events, 79.0 us)
Async XLA Ops:
  7.2 65.3 %all-gather.7.cloned.1.call-start = ((), (), s32[]{:S(2)}) async-start(), calls=%async_computation.1 | async-start | bytes 5292032 | tf_op jit(solution)/shard_map/all_gather | solution.py:281
  10.1 102.3 %all-gather.9.cloned.1.call-start = ((), (), s32[]{:S(2)}) async-start(), calls=%async_computation.2 | async-start | bytes 2801664 | tf_op jit(solution)/shard_map/all_gather | solution.py:305
  19.2 12.7 %collective-permute-start.1 = (bf16[608,256]{1,0:T(8,128)(2,1)S(1)}, bf16[608,256]{1,0:T(8,128)(2,1)S(1)}, u32[]{:S(2)}, u32[]{:S(2)}) collective-permute-start(bf16[608,256]{1,0:T(8,128)(2,1)S(1)} %pad_maximum_fusion.1.rest_0_), channel_id=1, source_target_pairs={{0,32},{16,48},{32,64},{48,80},{64,96},{80,112},{96,128},{112,144}... | collective-permute-start | bytes 933896 | tf_op jit(solution)/shard_map/ppermute | solution.py:48
  21.9 10.1 %collective-permute-start.2 = (bf16[608,256]{1,0:T(8,128)(2,1)S(1)}, bf16[608,256]{1,0:T(8,128)(2,1)S(1)}, u32[]{:S(2)}, u32[]{:S(2)}) collective-permute-start(bf16[608,256]{1,0:T(8,128)(2,1)S(1)} %pad_maximum_fusion.1.rest_0_), channel_id=1, source_target_pairs={{32,0},{48,16},{64,32},{80,48},{96,64},{112,80},{128,96},{144,112}... | collective-permute-start | bytes 933896 | tf_op jit(solution)/shard_map/ppermute | solution.py:48
  39.8 20.4 %collective-permute-start.6 = (bf16[608,256]{1,0:T(8,128)(2,1)S(1)}, bf16[608,256]{1,0:T(8,128)(2,1)S(1)}, u32[]{:S(2)}, u32[]{:S(2)}) collective-permute-start(bf16[608,256]{1,0:T(8,128)(2,1)S(1)} %collective-permute-done.3.rest_3_), channel_id=1, source_target_pairs={{0,32},{16,48},{32,64},{48,80},{64,96},{80,112},{96,128},{112,144}... | collective-permute-start | bytes 933896 | tf_op jit(solution)/shard_map/ppermute | solution.py:48
  45.5 14.7 %collective-permute-start.7 = (bf16[608,256]{1,0:T(8,128)(2,1)S(1)}, bf16[608,256]{1,0:T(8,128)(2,1)S(1)}, u32[]{:S(2)}, u32[]{:S(2)}) collective-permute-start(bf16[608,256]{1,0:T(8,128)(2,1)S(1)} %collective-permute-done.4.rest_4_), channel_id=1, source_target_pairs={{32,0},{48,16},{64,32},{80,48},{96,64},{112,80},{128,96},{144,112}... | collective-permute-start | bytes 933896 | tf_op jit(solution)/shard_map/ppermute | solution.py:48
  45.8 10.3 %collective-permute-start.9 = (bf16[304,256]{1,0:T(8,128)(2,1)S(1)}, bf16[304,256]{1,0:T(8,128)(2,1)S(1)}, u32[]{:S(2)}, u32[]{:S(2)}) collective-permute-start(bf16[304,256]{1,0:T(8,128)(2,1)S(1)} %pad.9), channel_id=1, source_target_pairs={{0,16},{16,0},{32,48},{48,32},{64,80},{80,64},{96,112},{112,96},{1... | collective-permute-start | bytes 466952 | tf_op jit(solution)/shard_map/ppermute | solution.py:48
  50.6 9.7 %collective-permute-start.8 = (bf16[288,256]{1,0:T(8,128)(2,1)S(1)}, bf16[288,256]{1,0:T(8,128)(2,1)S(1)}, u32[]{:S(2)}, u32[]{:S(2)}) collective-permute-start(bf16[288,256]{1,0:T(8,128)(2,1)S(1)} %collective-permute-done.5), channel_id=1, source_target_pairs={{0,0},{1,17},{2,34},{3,51},{4,68},{5,85},{6,102},{7,119},{8,136},{... | collective-permute-start | bytes 442376 | tf_op jit(solution)/shard_map/ppermute | solution.py:301
  60.3 132.4 %all-gather.11.cloned.1.call-start = ((), (), s32[]{:S(2)}) async-start(), calls=%async_computation.3 | async-start | bytes 2654208 | tf_op jit(solution)/shard_map/all_gather | solution.py:385
  79.3 18.7 %collective-permute-start.13 = (bf16[512,256]{1,0:T(8,128)(2,1)}, bf16[512,256]{1,0:T(8,128)(2,1)S(1)}, u32[]{:S(2)}, u32[]{:S(2)}) collective-permute-start(bf16[512,256]{1,0:T(8,128)(2,1)} %shard_map.112.rest_0_), channel_id=1, source_target_pairs={{0,32},{16,48},{32,64},{48,80},{64,96},{80,112},{96,128},{112,144}... | collective-permute-start | bytes 786440 | tf_op jit(solution)/shard_map/ppermute | solution.py:48
  99.0 13.4 %collective-permute-start.14 = (bf16[512,256]{1,0:T(8,128)(2,1)S(1)}, bf16[512,256]{1,0:T(8,128)(2,1)S(1)}, u32[]{:S(2)}, u32[]{:S(2)}) collective-permute-start(bf16[512,256]{1,0:T(8,128)(2,1)S(1)} %collective-permute-done.13.rest_0_), channel_id=1, source_target_pairs={{0,32},{16,48},{32,64},{48,80},{64,96},{80,112},{96,128},{112,144}... | collective-permute-start | bytes 786440 | tf_op jit(solution)/shard_map/ppermute | solution.py:48
  103.1 10.4 %collective-permute-start.15 = (bf16[512,256]{1,0:T(8,128)(2,1)S(1)}, bf16[512,256]{1,0:T(8,128)(2,1)S(1)}, u32[]{:S(2)}, u32[]{:S(2)}) collective-permute-start(bf16[512,256]{1,0:T(8,128)(2,1)S(1)} %broadcast_select_fusion.3), channel_id=1, source_target_pairs={{0,16},{16,0},{32,48},{48,32},{64,80},{80,64},{96,112},{112,96},{1... | collective-permute-start | bytes 786440 | tf_op jit(solution)/shard_map/ppermute | solution.py:48
  113.4 18.1 %collective-permute-start.16 = (bf16[512,256]{1,0:T(8,128)(2,1)S(1)}, bf16[512,256]{1,0:T(8,128)(2,1)S(1)}, u32[]{:S(2)}, u32[]{:S(2)}) collective-permute-start(bf16[512,256]{1,0:T(8,128)(2,1)S(1)} %collective-permute-done.14.rest_0_), channel_id=1, source_target_pairs={{0,32},{16,48},{32,64},{48,80},{64,96},{80,112},{96,128},{112,144}... | collective-permute-start | bytes 786440 | tf_op jit(solution)/shard_map/ppermute | solution.py:48
  117.3 14.3 %collective-permute-start.18 = (bf16[288,256]{1,0:T(8,128)(2,1)}, bf16[288,256]{1,0:T(8,128)(2,1)S(1)}, u32[]{:S(2)}, u32[]{:S(2)}) collective-permute-start(bf16[288,256]{1,0:T(8,128)(2,1)} %collective-permute-done.12), channel_id=1, source_target_pairs={{0,16},{16,0},{32,48},{48,32},{64,80},{80,64},{96,112},{112,96},{1... | collective-permute-start | bytes 442376 | tf_op jit(solution)/shard_map/ppermute | solution.py:48
  120.9 10.7 %collective-permute-start.17 = (bf16[512,256]{1,0:T(8,128)(2,1)S(1)}, bf16[512,256]{1,0:T(8,128)(2,1)S(1)}, u32[]{:S(2)}, u32[]{:S(2)}) collective-permute-start(bf16[512,256]{1,0:T(8,128)(2,1)S(1)} %broadcast_select_fusion.2), channel_id=1, source_target_pairs={{0,16},{16,0},{32,48},{48,32},{64,80},{80,64},{96,112},{112,96},{1... | collective-permute-start | bytes 786440 | tf_op jit(solution)/shard_map/ppermute | solution.py:48
  131.6 11.7 %collective-permute-start.19 = (bf16[512,256]{1,0:T(8,128)(2,1)S(1)}, bf16[512,256]{1,0:T(8,128)(2,1)S(1)}, u32[]{:S(2)}, u32[]{:S(2)}) collective-permute-start(bf16[512,256]{1,0:T(8,128)(2,1)S(1)} %collective-permute-done.16.rest_0_), channel_id=1, source_target_pairs={{0,32},{16,48},{32,64},{48,80},{64,96},{80,112},{96,128},{112,144}... | collective-permute-start | bytes 786440 | tf_op jit(solution)/shard_map/ppermute | solution.py:48
  143.3 8.8 %collective-permute-start.21 = (bf16[512,256]{1,0:T(8,128)(2,1)S(1)}, bf16[512,256]{1,0:T(8,128)(2,1)S(1)}, u32[]{:S(2)}, u32[]{:S(2)}) collective-permute-start(bf16[512,256]{1,0:T(8,128)(2,1)S(1)} %broadcast_select_fusion), channel_id=1, source_target_pairs={{0,16},{16,0},{32,48},{48,32},{64,80},{80,64},{96,112},{112,96},{1... | collective-permute-start | bytes 786440 | tf_op jit(solution)/shard_map/ppermute | solution.py:48
  160.8 11.1 %collective-permute-start.23 = (bf16[2,512,256]{2,1,0:T(8,128)(2,1)S(1)}, bf16[2,512,256]{2,1,0:T(8,128)(2,1)S(1)}, u32[]{:S(2)}, u32[]{:S(2)}) collective-permute-start(bf16[2,512,256]{2,1,0:T(8,128)(2,1)S(1)} %pad_maximum_fusion.rest_0_), channel_id=1, source_target_pairs={{0,4},{1,5},{2,6},{3,7},{4,8},{5,9},{6,10},{7,11},{8,12},{9,13},{1... | collective-permute-start | bytes 1572872 | tf_op jit(solution)/shard_map/ppermute | solution.py:52
  163.2 8.7 %collective-permute-start.24 = (bf16[2,512,256]{2,1,0:T(8,128)(2,1)S(1)}, bf16[2,512,256]{2,1,0:T(8,128)(2,1)S(1)}, u32[]{:S(2)}, u32[]{:S(2)}) collective-permute-start(bf16[2,512,256]{2,1,0:T(8,128)(2,1)S(1)} %pad_maximum_fusion.rest_0_), channel_id=1, source_target_pairs={{4,0},{5,1},{6,2},{7,3},{8,4},{9,5},{10,6},{11,7},{12,8},{13,9},{1... | collective-permute-start | bytes 1572872 | tf_op jit(solution)/shard_map/ppermute | solution.py:52
  171.9 16.6 %collective-permute-start.28 = (bf16[2,512,256]{2,1,0:T(8,128)(2,1)S(1)}, bf16[2,512,256]{2,1,0:T(8,128)(2,1)S(1)}, u32[]{:S(2)}, u32[]{:S(2)}) collective-permute-start(bf16[2,512,256]{2,1,0:T(8,128)(2,1)S(1)} %collective-permute-done.23.rest_1_), channel_id=1, source_target_pairs={{0,1},{1,0},{2,3},{3,2},{4,5},{5,4},{6,7},{7,6},{8,9},{9,8},{10,11... | collective-permute-start | bytes 1572872 | tf_op jit(solution)/shard_map/ppermute | solution.py:52
  177.6 11.0 %collective-permute-start.29 = (bf16[2,512,256]{2,1,0:T(8,128)(2,1)S(1)}, bf16[2,512,256]{2,1,0:T(8,128)(2,1)S(1)}, u32[]{:S(2)}, u32[]{:S(2)}) collective-permute-start(bf16[2,512,256]{2,1,0:T(8,128)(2,1)S(1)} %collective-permute-done.24.rest_2_), channel_id=1, source_target_pairs={{0,1},{1,0},{2,3},{3,2},{4,5},{5,4},{6,7},{7,6},{8,9},{9,8},{10,11... | collective-permute-start | bytes 1572872 | tf_op jit(solution)/shard_map/ppermute | solution.py:52
  177.6 10.9 %collective-permute-start.26 = (bf16[1,512,256]{2,1,0:T(8,128)(2,1)S(1)}, bf16[1,512,256]{2,1,0:T(8,128)(2,1)S(1)}, u32[]{:S(2)}, u32[]{:S(2)}) collective-permute-start(bf16[1,512,256]{2,1,0:T(8,128)(2,1)S(1)} %slice.151), channel_id=1, source_target_pairs={{0,4},{1,5},{2,6},{3,7},{4,8},{5,9},{6,10},{7,11},{8,12},{9,13},{1... | collective-permute-start | bytes 786440 | tf_op jit(solution)/shard_map/ppermute | solution.py:52
  178.3 10.2 %collective-permute-start.27 = (bf16[1,512,256]{2,1,0:T(8,128)(2,1)S(1)}, bf16[1,512,256]{2,1,0:T(8,128)(2,1)S(1)}, u32[]{:S(2)}, u32[]{:S(2)}) collective-permute-start(bf16[1,512,256]{2,1,0:T(8,128)(2,1)S(1)} %slice.152), channel_id=1, source_target_pairs={{4,0},{5,1},{6,2},{7,3},{8,4},{9,5},{10,6},{11,7},{12,8},{13,9},{1... | collective-permute-start | bytes 786440 | tf_op jit(solution)/shard_map/ppermute | solution.py:52
  201.8 10.3 %all-to-all-start = ((f32[16,1,512]{2,1,0:T(1,128)}), f32[16,1,512]{2,1,0:T(1,128)S(1)}, u32[]{:S(2)}, u32[]{:S(2)}) async-start(f32[16,1,512]{2,1,0:T(1,128)} %broadcast_in_dim.48), calls=%async_computation | async-start | bytes 65536 | tf_op jit(solution)/shard_map/all_to_all | solution.py:404
  (44 other events, 538.9 us)
Sparse Core Ops, SparseCore 0:
  10.2 46.0 all-gather.6
  60.4 48.8 all-gather.8
  143.5 41.2 all-gather.10

commit v8 on v7

--- a/solution.py
+++ b/solution.py
@@ -61,17 +61,17 @@
     out_ref, x_ref, w_ref, acc_ref, x_sem, w_sem = rest[-6:]
     chunks, depth, rows = x_ref.shape
     copies = []
-    for slot in range(ROUNDS):
+    for k, (which, lead, slot, offset) in enumerate(pieces):
         place = index_ref[2 + ROUNDS + slot]
+        source = w_refs[which] if lead is None else w_refs[which].at[lead]
+        width = source.shape[1]
         for part in range(2):
             parity = index_ref[1] if part == 0 else 1 - index_ref[1]
-            which, lead = pieces[slot]
-            source = w_refs[which] if lead is None else w_refs[which].at[lead]
             copies.append(
                 pltpu.make_async_copy(
                     source.at[pl.ds(part * depth, depth)],
-                    w_ref.at[2 * place + parity],
-                    w_sem.at[2 * slot + part],
+                    w_ref.at[2 * place + parity, :, pl.ds(offset, width)],
+                    w_sem.at[2 * k + part],
                 )
             )
     step = chunks // 4
@@ -134,7 +134,7 @@
             pltpu.VMEM((chunks, depth, 2 * HD), BF),
             pltpu.VMEM((2 * HD, rows), F32),
             pltpu.SemaphoreType.DMA((4,)),
-            pltpu.SemaphoreType.DMA((2 * ROUNDS,)),
+            pltpu.SemaphoreType.DMA((2 * len(pieces),)),
         ],
         compiler_params=pltpu.CompilerParams(vmem_limit_bytes=60 << 20),
         cost_estimate=pl.CostEstimate(
@@ -214,20 +214,40 @@
 
 def output_kernel(index_ref, *rest):
     n = len(PLACES)
-    same, other = rest[:n], rest[n : 2 * n]
-    w_ref, out_ref, square_ref = rest[2 * n :]
-    features = out_ref.shape[0]
+    sources, w_hbm = rest[: 2 * n], rest[2 * n]
+    out_ref, square_ref, x_ref, w_ref, x_sem, w_sem = rest[2 * n + 1 :]
+    load = pltpu.make_async_copy(w_hbm, w_ref, w_sem)
+    load.start()
+    copies = []
+    for k, places in enumerate(PLACES):
+        slot = sum(len(before) for before in PLACES[:k])
+        copies.append(
+            [
+                pltpu.make_async_copy(
+                    sources[part * n + k],
+                    x_ref.at[part, pl.ds(slot, len(places))],
+                    x_sem.at[part * n + k],
+                )
+                for part in range(2)
+            ]
+        )
+    for both in copies:
+        for copy in both:
+            copy.start()
+    load.wait()
     slot = 0
     for k, places in enumerate(PLACES):
-        for j in range(len(places)):
+        for copy in copies[k]:
+            copy.wait()
+        for _ in places:
             total = None
             place = index_ref[2 + slot]
-            for part, ref in enumerate((same[k], other[k])):
+            for part in range(2):
                 parity = index_ref[0] if part == 0 else 1 - index_ref[0]
                 swapped = jnp.where(parity == index_ref[1], 0, 1)
                 product = lax.dot_general(
                     w_ref[2 * place + swapped],
-                    ref[j],
+                    x_ref[part, slot],
                     (((1,), (1,)), ((), ())),
                     preferred_element_type=F32,
                 )
@@ -244,18 +264,25 @@
 
 
 def output(chunks, weights, index):
-    rows = chunks[0].shape[1]
+    _, rows, width = chunks[0].shape
     features = weights.shape[1]
     vmem = pl.BlockSpec(memory_space=pltpu.VMEM)
+    outside = pl.BlockSpec(memory_space=pl.ANY)
     return pl.pallas_call(
         output_kernel,
         out_shape=(
             jax.ShapeDtypeStruct((features, rows), F32),
             jax.ShapeDtypeStruct((1, rows), F32),
         ),
-        in_specs=[pl.BlockSpec(memory_space=pltpu.SMEM)] + [vmem] * (len(chunks) + 1),
+        in_specs=[pl.BlockSpec(memory_space=pltpu.SMEM)] + [outside] * (len(chunks) + 1),
         out_specs=(vmem, vmem),
-        compiler_params=pltpu.CompilerParams(vmem_limit_bytes=10 << 20),
+        scratch_shapes=[
+            pltpu.VMEM((2, ROUNDS, rows, width), BF),
+            pltpu.VMEM(weights.shape, BF),
+            pltpu.SemaphoreType.DMA((2 * len(PLACES),)),
+            pltpu.SemaphoreType.DMA,
+        ],
+        compiler_params=pltpu.CompilerParams(vmem_limit_bytes=60 << 20),
         cost_estimate=pl.CostEstimate(
             flops=2 * rows * features * 4096, bytes_accessed=8 << 20, transcendentals=0
         ),
@@ -270,7 +297,19 @@
     h = lax.rem(seq_index, 2)
     base = seq_index * rows
 
-    x_own = tokens.T.astype(F32)
+    depth = features + EXTRA
+    lane = jnp.arange(2 * HD, dtype=jnp.int32)
+    marked = 2 * (SEGS - 1)
+    limit = jnp.where(lane < marked, lax.rem(lane, SEGS - 1) + 1, 0)
+    counts = jnp.sum((segment_ids[:, None] < limit[None, :]).astype(F32), axis=0)
+    upper_digit = jnp.floor(counts * (1.0 / 16.0))
+    digits = jnp.where(lane < SEGS - 1, upper_digit, counts - 16.0 * upper_digit).astype(BF)
+    digits = jnp.pad(digits[None, :], ((2, EXTRA - 3), (0, 0)))
+    kv_own = jnp.concatenate([jnp.concatenate([w_key, w_value], axis=1), digits], axis=0)
+    q_own = jnp.pad(w_query, ((0, EXTRA), (0, 0)))
+    facing, q_facing = tie(move(kv_own, ACROSS), move(q_own, ACROSS))
+    x_own, kv_own = tie(tokens.T, kv_own)
+    x_own = x_own.astype(F32)
     gained = (x_own * (1.0 + pre_gain.astype(F32))[:, None]).astype(BF)
     squares = jnp.sum(x_own * x_own, axis=0, keepdims=True)
     upper = lax.reduce_precision(squares, 8, 7)
@@ -279,34 +318,22 @@
         [upper.astype(BF), lower.astype(BF), jnp.zeros((EXTRA - 2, rows), BF)], axis=0
     )
     x_all = lax.all_gather(jnp.concatenate([gained, side], axis=0), "mp", axis=0)
-    depth = features + EXTRA
-
-    lane = jnp.arange(2 * HD, dtype=jnp.int32)
-    marked = 2 * (SEGS - 1)
-    limit = jnp.where(lane < marked, lax.rem(lane, SEGS - 1) + 1, 0)
-    counts = jnp.sum((segment_ids[:, None] < limit[None, :]).astype(F32), axis=0)
-    upper_digit = jnp.floor(counts * (1.0 / 16.0))
-    digits = jnp.where(lane < SEGS - 1, upper_digit, counts - 16.0 * upper_digit).astype(BF)
-    digits = jnp.pad(digits[None, :], ((2, EXTRA - 3), (0, 0)))
-    kv_own = jnp.concatenate([jnp.concatenate([w_key, w_value], axis=1), digits], axis=0)
-    start = jnp.concatenate([kv_own, move(kv_own, ACROSS)], axis=0)
+    start = jnp.concatenate([kv_own, facing], axis=0)
     ring = {0: start, 1: move(start, AHEAD), -1: move(start, BEHIND)}
     turned = lax.ppermute(w_out.T, ("seq", "mp"), TURNS[0])
     ring[2] = move(ring[1], AHEAD)
     ring[-2] = move(ring[-1], BEHIND)
     ring[2], ring[-2], turned = tie(ring[2], ring[-2], turned)
-    q_own = jnp.pad(w_query, ((0, EXTRA), (0, 0)))
-    q_own, _ = tie(q_own, ring[1])
-    q_pair = jnp.concatenate([q_own, move(q_own, ACROSS)], axis=0)
+    q_pair = jnp.concatenate([q_own, q_facing], axis=0)
     turned = lax.ppermute(turned, ("seq", "mp"), TURNS[1])
     ring[3] = move(ring[2], AHEAD)
     ring[-3] = move(ring[-2], BEHIND)
-    ring[3], ring[-3], turned, q_pair = tie(ring[3], ring[-3], turned, q_pair)
+    ring[3], ring[-3], turned = tie(ring[3], ring[-3], turned)
     q_all = lax.all_gather(q_pair, "seq", axis=0, axis_index_groups=COLUMNS)
     turned = lax.ppermute(turned, ("seq", "mp"), TURNS[2])
     last = move(ring[3][:, :HD], AHEAD)
-    ring[4] = jnp.concatenate([last, move(ring[-3][:, HD:], BEHIND)], axis=1)
-    ring[4], turned = tie(ring[4], turned)
+    opposite = move(ring[-3][:, HD:], BEHIND)
+    last, opposite, turned = tie(last, opposite, turned)
 
     mp_index = lax.axis_index("mp")
     y = mp_index // 4
@@ -323,13 +350,13 @@
 
     steps = [0, 1, -1, 2, -2, 3, -3, 4]
     index = index_of(steps, z)
-    kv_weights = [ring[step] for step in steps]
-    kv_pieces = tuple((k, None) for k in range(ROUNDS))
-    q_pieces = tuple((0, k) for k in range(ROUNDS))
+    kv_weights = [ring[step] for step in steps[:7]] + [last, opposite]
+    kv_pieces = tuple((k, None, k, 0) for k in range(ROUNDS)) + ((8, None, 7, HD),)
+    q_pieces = tuple((0, k, k, 0) for k in range(ROUNDS))
 
     n_marks = 2 * (SEGS - 1)
     marks = jnp.zeros((n_marks,), F32)
-    for block in kv_weights:
+    for block in kv_weights[:8]:
         for part in range(2):
             marks = marks + block[part * depth + features + 2, :n_marks].astype(F32)
     starts = (marks[: SEGS - 1] * 16.0 + marks[SEGS - 1 :]).astype(jnp.int32)
@@ -369,8 +396,8 @@
         else:
             if step == 2:
                 facing_out = move(turned, ACROSS)
-                following, chosen, crossed[2], facing_out, *state = tie(
-                    following, chosen, crossed[2], facing_out, *state
+                following, chosen, crossed[2], facing_out = tie(
+                    following, chosen, crossed[2], facing_out
                 )
             else:
                 following, chosen, crossed[3], *state = tie(

time: 223 us -> 230 us (1.031)
  local copies, waits for them, and re-layouts: 20.3 us -> 7.58 us
  waiting for transfers between devices: 52.5 us -> 63.4 us
  Pallas kernels: 28.7 us -> 33.3 us
  starting transfers between devices: 84.2 us -> 88.4 us
    unnamed x65 -> x53, local copies, waits for them, and re-layouts: 14.3 us -> 1.78 us
    ppermute x19, waiting for transfers between devices: 37.2 us -> 48.1 us  [move(): return lax.ppermute(block, 'seq', perm)]
    pallas_call x1, Pallas kernels: 1.96 us -> 6.36 us  [output(): pl.pallas_call(output_kernel, out_shape=(jax.ShapeDtypeStruct((features,...]
    ppermute x1, starting transfers between devices: 1.92 us -> 5.75 us  [shards(): turned = lax.ppermute(turned, ('seq', 'mp'), TURNS[1])]
    ppermute x10, starting transfers between devices: 18.8 us -> 21.9 us  [shift(): return lax.ppermute(block, 'mp', perm)]
  transfers between devices with their start and end apart: 36 -> 36, of which waited for: 13 -> 16; matrix products, arithmetic and copies ran while one was open for 7% -> 5% of each run, Pallas kernels for 12% -> 12%
where the time goes in v8:
time: 230 us; the launch traced here: 228 us
  starting transfers between devices  88.4 us (38%)
  waiting for transfers between devices  63.4 us (28%)
  Pallas kernels  33.3 us (14%)
  between operations  22.4 us (10%)
  other arithmetic  13.1 us (6%)
  local copies, waits for them, and re-layouts  7.58 us (3%)
    ppermute x19, starting transfers between devices, move(): return lax.ppermute(block, 'seq', perm)  55 us
    ppermute x19, waiting for transfers between devices, move(): return lax.ppermute(block, 'seq', perm)  48.1 us
    ppermute x10, starting transfers between devices, shift(): return lax.ppermute(block, 'mp', perm)  21.9 us
    pallas_call x2, Pallas kernels, project(): pl.pallas_call(functools.partial(project_kernel, pieces, rotated, factor)...  13.6 us
    pallas_call x5, Pallas kernels, attend(): pl.pallas_call(functools.partial(attend_kernel, tuple(distances), first,...  13.4 us
    ppermute x10, waiting for transfers between devices, shift(): return lax.ppermute(block, 'mp', perm)  7.01 us
    pallas_call x1, Pallas kernels, output(): pl.pallas_call(output_kernel, out_shape=(jax.ShapeDtypeStruct((features,...  6.36 us
    ppermute x1, starting transfers between devices, shards(): turned = lax.ppermute(turned, ('seq', 'mp'), TURNS[1])  5.75 us
  transfers between devices with their start and end apart: 36, of which 16 were waited for; matrix products, arithmetic and copies ran while one was open for 5% of the time, Pallas kernels for 12%

profile of v8, /device:TPU:1, one launch (start us, length us, event | category | flops | bytes accessed | tf_op | source)
XLA Modules:
  0.0 228.3 jit_solution(14175143029453741723)
XLA Ops:
  11.9 3.7 %collective-permute-start = (bf16[304,256]{1,0:T(8,128)(2,1)S(1)}, bf16[304,256]{1,0:T(8,128)(2,1)S(1)}, u32[]{:S(2)}, u32[]{:S(2)}) collective-permute-start(bf16[304,256]{1,0:T(8,128)(2,1)S(1)} %fusion.4), channel_id=1, source_target_pairs={{0,16},{16,0},{32,48},{48,32},{64,80},{80,64},{96,112},{112,96},{1... | collective-permute-start | bytes 466952 | tf_op jit(solution)/shard_map/ppermute | solution.py:48
  18.2 5.8 %collective-permute-done.1 = bf16[304,256]{1,0:T(8,128)(2,1)S(1)} collective-permute-done((bf16[304,256]{1,0:T(8,128)(2,1)S(1)}, bf16[304,256]{1,0:T(8,128)(2,1)S(1)}, u32[]{:S(2)}, u32[]{:S(2)}) %collective-permute-start.1) | collective-permute-done | bytes 155680 | tf_op jit(solution)/shard_map/ppermute | solution.py:48
  25.2 4.0 %collective-permute-start.3 = (bf16[608,256]{1,0:T(8,128)(2,1)S(1)}, bf16[608,256]{1,0:T(8,128)(2,1)S(1)}, u32[]{:S(2)}, u32[]{:S(2)}) collective-permute-start(bf16[608,256]{1,0:T(8,128)(2,1)S(1)} %constant_dynamic-update-slice_fusion.rest_0_), channel_id=1, source_target_pairs={{32,0},{48,16},{64,32},{80,48},{96,64},{112,80},{128,96},{144,112}... | collective-permute-start | bytes 933896 | tf_op jit(solution)/shard_map/ppermute | solution.py:48
  29.3 5.7 %collective-permute-done.2.rest_1_ = bf16[608,256]{1,0:T(8,128)(2,1)S(1)} collective-permute-done((bf16[608,256]{1,0:T(8,128)(2,1)S(1)}, bf16[608,256]{1,0:T(8,128)(2,1)S(1)}, u32[]{:S(2)}, u32[]{:S(2)}) %collective-permute-start.2) | collective-permute-done | bytes 311328 | tf_op jit(solution)/shard_map/ppermute | solution.py:48
  38.3 4.2 %collective-permute-done.4.rest_3_ = bf16[608,256]{1,0:T(8,128)(2,1)S(1)} collective-permute-done((bf16[608,256]{1,0:T(8,128)(2,1)S(1)}, bf16[608,256]{1,0:T(8,128)(2,1)S(1)}, u32[]{:S(2)}, u32[]{:S(2)}) %collective-permute-start.4) | collective-permute-done | bytes 311328 | tf_op jit(solution)/shard_map/ppermute | solution.py:48
  42.5 6.5 %collective-permute-start.7 = (bf16[608,256]{1,0:T(8,128)(2,1)S(1)}, bf16[608,256]{1,0:T(8,128)(2,1)S(1)}, u32[]{:S(2)}, u32[]{:S(2)}) collective-permute-start(bf16[608,256]{1,0:T(8,128)(2,1)S(1)} %collective-permute-done.4.rest_3_), channel_id=1, source_target_pairs={{0,32},{16,48},{32,64},{48,80},{64,96},{80,112},{96,128},{112,144}... | collective-permute-start | bytes 933896 | tf_op jit(solution)/shard_map/ppermute | solution.py:48
  49.9 5.7 %collective-permute-start.9 = (bf16[288,256]{1,0:T(8,128)(2,1)S(1)}, bf16[288,256]{1,0:T(8,128)(2,1)S(1)}, u32[]{:S(2)}, u32[]{:S(2)}) collective-permute-start(bf16[288,256]{1,0:T(8,128)(2,1)S(1)} %collective-permute-done.6), channel_id=1, source_target_pairs={{0,0},{1,17},{2,34},{3,51},{4,68},{5,85},{6,102},{7,119},{8,136},{... | collective-permute-start | bytes 442376 | tf_op jit(solution)/shard_map/ppermute | solution.py:328
  62.1 3.4 %collective-permute-start.11 = (bf16[608,128]{1,0:T(8,128)(2,1)S(1)}, bf16[608,128]{1,0:T(8,128)(2,1)S(1)}, u32[]{:S(2)}, u32[]{:S(2)}) collective-permute-start(bf16[608,128]{1,0:T(8,128)(2,1)S(1)} %slice.142), channel_id=1, source_target_pairs={{32,0},{48,16},{64,32},{80,48},{96,64},{112,80},{128,96},{144,112}... | collective-permute-start | bytes 466952 | tf_op jit(solution)/shard_map/ppermute | solution.py:48
  73.1 7.0 %shard_map.112.rest_0_ = bf16[512,256]{1,0:T(8,128)(2,1)} custom-call(s32[18]{0:T(128)} %stack.103.index_ref, f32[64,512]{1,0:T(8,128)} %get-tuple-element.106.cos_ref, f32[64,512]{1,0:T(8,128)} %get-tuple-element.105.sin_ref, bf16[16,304,512]{2,1,0:T(8,128)(2,1)} %bitcast.61, bf16[608,256]{1,0:T(8,128)(2,1)} %copy-done.9, bf16[608,256]{1,0:T(8,128)(2,1)} %copy-done.13, ...), custom_call_target="tpu_custom_call" | custom-call | flops 1207959552 | bytes 8388608 | tf_op jit(solution)/shard_map/pallas_call | solution.py:126
  80.1 10.3 %collective-permute-start.13 = (bf16[512,256]{1,0:T(8,128)(2,1)}, bf16[512,256]{1,0:T(8,128)(2,1)S(1)}, u32[]{:S(2)}, u32[]{:S(2)}) collective-permute-start(bf16[512,256]{1,0:T(8,128)(2,1)} %shard_map.112.rest_0_), channel_id=1, source_target_pairs={{0,32},{16,48},{32,64},{48,80},{64,96},{80,112},{96,128},{112,144}... | collective-permute-start | bytes 786440 | tf_op jit(solution)/shard_map/ppermute | solution.py:48
  90.3 11.9 %collective-permute-done.13.rest_0_ = bf16[512,256]{1,0:T(8,128)(2,1)S(1)} collective-permute-done((bf16[512,256]{1,0:T(8,128)(2,1)}, bf16[512,256]{1,0:T(8,128)(2,1)S(1)}, u32[]{:S(2)}, u32[]{:S(2)}) %collective-permute-start.13) | collective-permute-done | bytes 262176 | tf_op jit(solution)/shard_map/ppermute | solution.py:48
  103.2 5.0 %collective-permute-start.14 = (bf16[512,256]{1,0:T(8,128)(2,1)S(1)}, bf16[512,256]{1,0:T(8,128)(2,1)S(1)}, u32[]{:S(2)}, u32[]{:S(2)}) collective-permute-start(bf16[512,256]{1,0:T(8,128)(2,1)S(1)} %collective-permute-done.13.rest_0_), channel_id=1, source_target_pairs={{0,32},{16,48},{32,64},{48,80},{64,96},{80,112},{96,128},{112,144}... | collective-permute-start | bytes 786440 | tf_op jit(solution)/shard_map/ppermute | solution.py:48
  113.0 3.5 %collective-permute-done.15.rest_1_ = bf16[512,256]{1,0:T(8,128)(2,1)S(1)} collective-permute-done((bf16[512,256]{1,0:T(8,128)(2,1)S(1)}, bf16[512,256]{1,0:T(8,128)(2,1)S(1)}, u32[]{:S(2)}, u32[]{:S(2)}) %collective-permute-start.15) | collective-permute-done | bytes 262176 | tf_op jit(solution)/shard_map/ppermute | solution.py:48
  116.4 4.2 %collective-permute-start.16 = (bf16[512,256]{1,0:T(8,128)(2,1)S(1)}, bf16[512,256]{1,0:T(8,128)(2,1)S(1)}, u32[]{:S(2)}, u32[]{:S(2)}) collective-permute-start(bf16[512,256]{1,0:T(8,128)(2,1)S(1)} %collective-permute-done.14.rest_0_), channel_id=1, source_target_pairs={{0,32},{16,48},{32,64},{48,80},{64,96},{80,112},{96,128},{112,144}... | collective-permute-start | bytes 786440 | tf_op jit(solution)/shard_map/ppermute | solution.py:48
  125.5 5.4 %collective-permute-done.18 = bf16[288,256]{1,0:T(8,128)(2,1)S(1)} collective-permute-done((bf16[288,256]{1,0:T(8,128)(2,1)S(1)}, bf16[288,256]{1,0:T(8,128)(2,1)S(1)}, u32[]{:S(2)}, u32[]{:S(2)}) %collective-permute-start.18) | collective-permute-done | bytes 147488 | tf_op jit(solution)/shard_map/ppermute | solution.py:48
  134.0 6.6 %shard_map.113.q_ref = bf16[512,256]{1,0:T(8,128)(2,1)} custom-call(s32[18]{0:T(128)} %stack.104.index_ref, f32[64,512]{1,0:T(8,128)} %get-tuple-element.106.cos_ref, f32[64,512]{1,0:T(8,128)} %get-tuple-element.105.sin_ref, bf16[16,304,512]{2,1,0:T(8,128)(2,1)} %bitcast.62, bf16[8,608,256]{2,1,0:T(8,128)(2,1)} %bitcast.63), custom_call_target="tpu_custom_call" | custom-call | flops 1207959552 | bytes 8388608 | tf_op jit(solution)/shard_map/pallas_call | solution.py:126
  148.4 5.0 %collective-permute-done.20.rest_1_ = bf16[512,256]{1,0:T(8,128)(2,1)S(1)} collective-permute-done((bf16[512,256]{1,0:T(8,128)(2,1)}, bf16[512,256]{1,0:T(8,128)(2,1)S(1)}, u32[]{:S(2)}, u32[]{:S(2)}) %collective-permute-start.20) | collective-permute-done | bytes 262176 | tf_op jit(solution)/shard_map/ppermute | solution.py:48
  164.9 4.2 %collective-permute-done.22 = bf16[1,512,256]{2,1,0:T(8,128)(2,1)S(1)} collective-permute-done((bf16[1,512,256]{2,1,0:T(8,128)(2,1)S(1)}, bf16[1,512,256]{2,1,0:T(8,128)(2,1)S(1)}, u32[]{:S(2)}, u32[]{:S(2)}) %collective-permute-start.22) | collective-permute-done | bytes 262176 | tf_op jit(solution)/shard_map/ppermute | solution.py:52
  169.2 3.3 %collective-permute-start.23 = (bf16[2,512,256]{2,1,0:T(8,128)(2,1)S(1)}, bf16[2,512,256]{2,1,0:T(8,128)(2,1)S(1)}, u32[]{:S(2)}, u32[]{:S(2)}) collective-permute-start(bf16[2,512,256]{2,1,0:T(8,128)(2,1)S(1)} %pad_maximum_fusion.rest_0_), channel_id=1, source_target_pairs={{0,4},{1,5},{2,6},{3,7},{4,8},{5,9},{6,10},{7,11},{8,12},{9,13},{1... | collective-permute-start | bytes 1572872 | tf_op jit(solution)/shard_map/ppermute | solution.py:52
  173.2 6.0 %collective-permute-start.25 = (bf16[2,512,256]{2,1,0:T(8,128)(2,1)S(1)}, bf16[2,512,256]{2,1,0:T(8,128)(2,1)S(1)}, u32[]{:S(2)}, u32[]{:S(2)}) collective-permute-start(bf16[2,512,256]{2,1,0:T(8,128)(2,1)S(1)} %pad_maximum_fusion.rest_0_), channel_id=1, source_target_pairs={{0,1},{1,0},{2,3},{3,2},{4,5},{5,4},{6,7},{7,6},{8,9},{9,8},{10,11... | collective-permute-start | bytes 1572872 | tf_op jit(solution)/shard_map/ppermute | solution.py:52
  180.9 6.5 %collective-permute-start.28 = (bf16[2,512,256]{2,1,0:T(8,128)(2,1)S(1)}, bf16[2,512,256]{2,1,0:T(8,128)(2,1)S(1)}, u32[]{:S(2)}, u32[]{:S(2)}) collective-permute-start(bf16[2,512,256]{2,1,0:T(8,128)(2,1)S(1)} %collective-permute-done.23.rest_1_), channel_id=1, source_target_pairs={{0,1},{1,0},{2,3},{3,2},{4,5},{5,4},{6,7},{7,6},{8,9},{9,8},{10,11... | collective-permute-start | bytes 1572872 | tf_op jit(solution)/shard_map/ppermute | solution.py:52
  202.1 6.4 %shard_map.119 = (f32[288,512]{1,0:T(8,128)}, f32[1,512]{1,0:T(1,128)}) custom-call(s32[18]{0:T(128)} %stack.103.index_ref, bf16[2,512,256]{2,1,0:T(8,128)(2,1)} %copy-done.3, bf16[2,512,256]{2,1,0:T(8,128)(2,1)} %copy-done.5, bf16[2,512,256]{2,1,0:T(8,128)(2,1)} %copy-done.6, bf16[1,512,256]{2,1,0:T(8,128)(2,1)} %copy-done.17, ...), custom_call_target="tpu_custom_call" | custom-call | flops 1207959552 | bytes 8388608 | tf_op jit(solution)/shard_map/pallas_call | solution.py:271
  209.7 4.2 %all-to-all-start = ((f32[16,1,512]{2,1,0:T(1,128)}), f32[16,1,512]{2,1,0:T(1,128)S(1)}, u32[]{:S(2)}, u32[]{:S(2)}) async-start(f32[16,1,512]{2,1,0:T(1,128)} %broadcast_in_dim.48), calls=%async_computation | async-start | bytes 65536 | tf_op jit(solution)/shard_map/all_to_all | solution.py:431
  214.7 5.1 %all-to-all-done = f32[16,1,512]{2,1,0:T(1,128)S(1)} async-done(((f32[16,1,512]{2,1,0:T(1,128)}), f32[16,1,512]{2,1,0:T(1,128)S(1)}, u32[]{:S(2)}, u32[]{:S(2)}) %all-to-all-start) | async-done | bytes 32800 | tf_op jit(solution)/shard_map/all_to_all | solution.py:431
  (155 shorter events, 72.3 us)
Async XLA Ops:
  7.2 65.8 %all-gather.7.cloned.1.call-start = ((), (), s32[]{:S(2)}) async-start(), calls=%async_computation.1 | async-start | bytes 5292032 | tf_op jit(solution)/shard_map/all_gather | solution.py:320
  11.8 101.1 %all-gather.9.cloned.1.call-start = ((), (), s32[]{:S(2)}) async-start(), calls=%async_computation.2 | async-start | bytes 2801664 | tf_op jit(solution)/shard_map/all_gather | solution.py:332
  24.9 177.1 %all-gather.11.cloned.1.call-start = ((), (), s32[]{:S(2)}) async-start(), calls=%async_computation.3 | async-start | bytes 2654208 | tf_op jit(solution)/shard_map/all_gather | solution.py:412
  25.0 10.0 %collective-permute-start.2 = (bf16[608,256]{1,0:T(8,128)(2,1)S(1)}, bf16[608,256]{1,0:T(8,128)(2,1)S(1)}, u32[]{:S(2)}, u32[]{:S(2)}) collective-permute-start(bf16[608,256]{1,0:T(8,128)(2,1)S(1)} %constant_dynamic-update-slice_fusion.rest_0_), channel_id=1, source_target_pairs={{0,32},{16,48},{32,64},{48,80},{64,96},{80,112},{96,128},{112,144}... | collective-permute-start | bytes 933896 | tf_op jit(solution)/shard_map/ppermute | solution.py:48
  25.2 9.8 %collective-permute-start.3 = (bf16[608,256]{1,0:T(8,128)(2,1)S(1)}, bf16[608,256]{1,0:T(8,128)(2,1)S(1)}, u32[]{:S(2)}, u32[]{:S(2)}) collective-permute-start(bf16[608,256]{1,0:T(8,128)(2,1)S(1)} %constant_dynamic-update-slice_fusion.rest_0_), channel_id=1, source_target_pairs={{32,0},{48,16},{64,32},{80,48},{96,64},{112,80},{128,96},{144,112}... | collective-permute-start | bytes 933896 | tf_op jit(solution)/shard_map/ppermute | solution.py:48
  42.5 16.2 %collective-permute-start.7 = (bf16[608,256]{1,0:T(8,128)(2,1)S(1)}, bf16[608,256]{1,0:T(8,128)(2,1)S(1)}, u32[]{:S(2)}, u32[]{:S(2)}) collective-permute-start(bf16[608,256]{1,0:T(8,128)(2,1)S(1)} %collective-permute-done.4.rest_3_), channel_id=1, source_target_pairs={{0,32},{16,48},{32,64},{48,80},{64,96},{80,112},{96,128},{112,144}... | collective-permute-start | bytes 933896 | tf_op jit(solution)/shard_map/ppermute | solution.py:48
  49.0 9.8 %collective-permute-start.8 = (bf16[608,256]{1,0:T(8,128)(2,1)S(1)}, bf16[608,256]{1,0:T(8,128)(2,1)S(1)}, u32[]{:S(2)}, u32[]{:S(2)}) collective-permute-start(bf16[608,256]{1,0:T(8,128)(2,1)S(1)} %collective-permute-done.5.rest_4_), channel_id=1, source_target_pairs={{32,0},{48,16},{64,32},{80,48},{96,64},{112,80},{128,96},{144,112}... | collective-permute-start | bytes 933896 | tf_op jit(solution)/shard_map/ppermute | solution.py:48
  49.9 8.9 %collective-permute-start.9 = (bf16[288,256]{1,0:T(8,128)(2,1)S(1)}, bf16[288,256]{1,0:T(8,128)(2,1)S(1)}, u32[]{:S(2)}, u32[]{:S(2)}) collective-permute-start(bf16[288,256]{1,0:T(8,128)(2,1)S(1)} %collective-permute-done.6), channel_id=1, source_target_pairs={{0,0},{1,17},{2,34},{3,51},{4,68},{5,85},{6,102},{7,119},{8,136},{... | collective-permute-start | bytes 442376 | tf_op jit(solution)/shard_map/ppermute | solution.py:328
  58.8 10.3 %collective-permute-start.10 = (bf16[608,128]{1,0:T(8,128)(2,1)S(1)}, bf16[608,128]{1,0:T(8,128)(2,1)S(1)}, u32[]{:S(2)}, u32[]{:S(2)}) collective-permute-start(bf16[608,128]{1,0:T(8,128)(2,1)S(1)} %slice.141), channel_id=1, source_target_pairs={{0,32},{16,48},{32,64},{48,80},{64,96},{80,112},{96,128},{112,144}... | collective-permute-start | bytes 466952 | tf_op jit(solution)/shard_map/ppermute | solution.py:48
  80.1 22.2 %collective-permute-start.13 = (bf16[512,256]{1,0:T(8,128)(2,1)}, bf16[512,256]{1,0:T(8,128)(2,1)S(1)}, u32[]{:S(2)}, u32[]{:S(2)}) collective-permute-start(bf16[512,256]{1,0:T(8,128)(2,1)} %shard_map.112.rest_0_), channel_id=1, source_target_pairs={{0,32},{16,48},{32,64},{48,80},{64,96},{80,112},{96,128},{112,144}... | collective-permute-start | bytes 786440 | tf_op jit(solution)/shard_map/ppermute | solution.py:48
  103.2 9.7 %collective-permute-start.14 = (bf16[512,256]{1,0:T(8,128)(2,1)S(1)}, bf16[512,256]{1,0:T(8,128)(2,1)S(1)}, u32[]{:S(2)}, u32[]{:S(2)}) collective-permute-start(bf16[512,256]{1,0:T(8,128)(2,1)S(1)} %collective-permute-done.13.rest_0_), channel_id=1, source_target_pairs={{0,32},{16,48},{32,64},{48,80},{64,96},{80,112},{96,128},{112,144}... | collective-permute-start | bytes 786440 | tf_op jit(solution)/shard_map/ppermute | solution.py:48
  108.2 8.2 %collective-permute-start.15 = (bf16[512,256]{1,0:T(8,128)(2,1)S(1)}, bf16[512,256]{1,0:T(8,128)(2,1)S(1)}, u32[]{:S(2)}, u32[]{:S(2)}) collective-permute-start(bf16[512,256]{1,0:T(8,128)(2,1)S(1)} %broadcast_select_fusion.3), channel_id=1, source_target_pairs={{0,16},{16,0},{32,48},{48,32},{64,80},{80,64},{96,112},{112,96},{1... | collective-permute-start | bytes 786440 | tf_op jit(solution)/shard_map/ppermute | solution.py:48
  116.4 8.3 %collective-permute-start.16 = (bf16[512,256]{1,0:T(8,128)(2,1)S(1)}, bf16[512,256]{1,0:T(8,128)(2,1)S(1)}, u32[]{:S(2)}, u32[]{:S(2)}) collective-permute-start(bf16[512,256]{1,0:T(8,128)(2,1)S(1)} %collective-permute-done.14.rest_0_), channel_id=1, source_target_pairs={{0,32},{16,48},{32,64},{48,80},{64,96},{80,112},{96,128},{112,144}... | collective-permute-start | bytes 786440 | tf_op jit(solution)/shard_map/ppermute | solution.py:48
  120.7 10.3 %collective-permute-start.17 = (bf16[512,256]{1,0:T(8,128)(2,1)S(1)}, bf16[512,256]{1,0:T(8,128)(2,1)S(1)}, u32[]{:S(2)}, u32[]{:S(2)}) collective-permute-start(bf16[512,256]{1,0:T(8,128)(2,1)S(1)} %broadcast_select_fusion.2), channel_id=1, source_target_pairs={{0,16},{16,0},{32,48},{48,32},{64,80},{80,64},{96,112},{112,96},{1... | collective-permute-start | bytes 786440 | tf_op jit(solution)/shard_map/ppermute | solution.py:48
  123.3 7.6 %collective-permute-start.18 = (bf16[288,256]{1,0:T(8,128)(2,1)S(1)}, bf16[288,256]{1,0:T(8,128)(2,1)S(1)}, u32[]{:S(2)}, u32[]{:S(2)}) collective-permute-start(bf16[288,256]{1,0:T(8,128)(2,1)S(1)} %collective-permute-done.12), channel_id=1, source_target_pairs={{0,16},{16,0},{32,48},{48,32},{64,80},{80,64},{96,112},{112,96},{1... | collective-permute-start | bytes 442376 | tf_op jit(solution)/shard_map/ppermute | solution.py:48
  130.9 17.5 %collective-permute-start.19 = (bf16[512,256]{1,0:T(8,128)(2,1)S(1)}, bf16[512,256]{1,0:T(8,128)(2,1)S(1)}, u32[]{:S(2)}, u32[]{:S(2)}) collective-permute-start(bf16[512,256]{1,0:T(8,128)(2,1)S(1)} %collective-permute-done.16.rest_0_), channel_id=1, source_target_pairs={{0,32},{16,48},{32,64},{48,80},{64,96},{80,112},{96,128},{112,144}... | collective-permute-start | bytes 786440 | tf_op jit(solution)/shard_map/ppermute | solution.py:48
  169.2 10.9 %collective-permute-start.23 = (bf16[2,512,256]{2,1,0:T(8,128)(2,1)S(1)}, bf16[2,512,256]{2,1,0:T(8,128)(2,1)S(1)}, u32[]{:S(2)}, u32[]{:S(2)}) collective-permute-start(bf16[2,512,256]{2,1,0:T(8,128)(2,1)S(1)} %pad_maximum_fusion.rest_0_), channel_id=1, source_target_pairs={{0,4},{1,5},{2,6},{3,7},{4,8},{5,9},{6,10},{7,11},{8,12},{9,13},{1... | collective-permute-start | bytes 1572872 | tf_op jit(solution)/shard_map/ppermute | solution.py:52
  172.5 8.4 %collective-permute-start.24 = (bf16[2,512,256]{2,1,0:T(8,128)(2,1)S(1)}, bf16[2,512,256]{2,1,0:T(8,128)(2,1)S(1)}, u32[]{:S(2)}, u32[]{:S(2)}) collective-permute-start(bf16[2,512,256]{2,1,0:T(8,128)(2,1)S(1)} %pad_maximum_fusion.rest_0_), channel_id=1, source_target_pairs={{4,0},{5,1},{6,2},{7,3},{8,4},{9,5},{10,6},{11,7},{12,8},{13,9},{1... | collective-permute-start | bytes 1572872 | tf_op jit(solution)/shard_map/ppermute | solution.py:52
  173.2 7.8 %collective-permute-start.25 = (bf16[2,512,256]{2,1,0:T(8,128)(2,1)S(1)}, bf16[2,512,256]{2,1,0:T(8,128)(2,1)S(1)}, u32[]{:S(2)}, u32[]{:S(2)}) collective-permute-start(bf16[2,512,256]{2,1,0:T(8,128)(2,1)S(1)} %pad_maximum_fusion.rest_0_), channel_id=1, source_target_pairs={{0,1},{1,0},{2,3},{3,2},{4,5},{5,4},{6,7},{7,6},{8,9},{9,8},{10,11... | collective-permute-start | bytes 1572872 | tf_op jit(solution)/shard_map/ppermute | solution.py:52
  180.9 18.1 %collective-permute-start.28 = (bf16[2,512,256]{2,1,0:T(8,128)(2,1)S(1)}, bf16[2,512,256]{2,1,0:T(8,128)(2,1)S(1)}, u32[]{:S(2)}, u32[]{:S(2)}) collective-permute-start(bf16[2,512,256]{2,1,0:T(8,128)(2,1)S(1)} %collective-permute-done.23.rest_1_), channel_id=1, source_target_pairs={{0,1},{1,0},{2,3},{3,2},{4,5},{5,4},{6,7},{7,6},{8,9},{9,8},{10,11... | collective-permute-start | bytes 1572872 | tf_op jit(solution)/shard_map/ppermute | solution.py:52
  187.4 11.6 %collective-permute-start.29 = (bf16[2,512,256]{2,1,0:T(8,128)(2,1)S(1)}, bf16[2,512,256]{2,1,0:T(8,128)(2,1)S(1)}, u32[]{:S(2)}, u32[]{:S(2)}) collective-permute-start(bf16[2,512,256]{2,1,0:T(8,128)(2,1)S(1)} %collective-permute-done.24.rest_2_), channel_id=1, source_target_pairs={{0,1},{1,0},{2,3},{3,2},{4,5},{5,4},{6,7},{7,6},{8,9},{9,8},{10,11... | collective-permute-start | bytes 1572872 | tf_op jit(solution)/shard_map/ppermute | solution.py:52
  187.6 11.4 %collective-permute-start.26 = (bf16[1,512,256]{2,1,0:T(8,128)(2,1)S(1)}, bf16[1,512,256]{2,1,0:T(8,128)(2,1)S(1)}, u32[]{:S(2)}, u32[]{:S(2)}) collective-permute-start(bf16[1,512,256]{2,1,0:T(8,128)(2,1)S(1)} %slice.150), channel_id=1, source_target_pairs={{0,4},{1,5},{2,6},{3,7},{4,8},{5,9},{6,10},{7,11},{8,12},{9,13},{1... | collective-permute-start | bytes 786440 | tf_op jit(solution)/shard_map/ppermute | solution.py:52
  188.4 10.6 %collective-permute-start.27 = (bf16[1,512,256]{2,1,0:T(8,128)(2,1)S(1)}, bf16[1,512,256]{2,1,0:T(8,128)(2,1)S(1)}, u32[]{:S(2)}, u32[]{:S(2)}) collective-permute-start(bf16[1,512,256]{2,1,0:T(8,128)(2,1)S(1)} %slice.151), channel_id=1, source_target_pairs={{4,0},{5,1},{6,2},{7,3},{8,4},{9,5},{10,6},{11,7},{12,8},{13,9},{1... | collective-permute-start | bytes 786440 | tf_op jit(solution)/shard_map/ppermute | solution.py:52
  209.7 10.0 %all-to-all-start = ((f32[16,1,512]{2,1,0:T(1,128)}), f32[16,1,512]{2,1,0:T(1,128)S(1)}, u32[]{:S(2)}, u32[]{:S(2)}) async-start(f32[16,1,512]{2,1,0:T(1,128)} %broadcast_in_dim.48), calls=%async_computation | async-start | bytes 65536 | tf_op jit(solution)/shard_map/all_to_all | solution.py:431
  (38 other events, 573.2 us)
Sparse Core Ops, SparseCore 0:
  12.0 45.6 all-gather.6
  59.5 44.6 all-gather.8
  153.6 39.4 all-gather.10

commit v9 on v8

--- a/solution.py
+++ b/solution.py
@@ -30,12 +30,9 @@
 LATER = [(i, i + 2) for i in range(SEQ - 2)]
 ACROSS = [(i, i ^ 1) for i in range(SEQ)]
 TURNS = (
-    [(s * SEQ + m, s * SEQ + (s + m) % SEQ) for s in range(SEQ) for m in range(SEQ)],
-    [(s * SEQ + c, ((c - s) % SEQ) * SEQ + c) for s in range(SEQ) for c in range(SEQ)],
-    [(m * SEQ + c, m * SEQ + (c - m) % SEQ) for m in range(SEQ) for c in range(SEQ)],
+    [(s * SEQ + m, (s + m) % SEQ * SEQ + m) for s in range(SEQ) for m in range(SEQ)],
+    [(a * SEQ + m, a * SEQ + (a - m) % SEQ) for a in range(SEQ) for m in range(SEQ)],
 )
-
-
 SIDE = [(i, i ^ 2) for i in range(SEQ)]
 UP = [(i, (i + 4) % SEQ) for i in range(SEQ)]
 DOWN = [((i + 4) % SEQ, i) for i in range(SEQ)]
@@ -244,9 +241,11 @@
             place = index_ref[2 + slot]
             for part in range(2):
                 parity = index_ref[0] if part == 0 else 1 - index_ref[0]
-                swapped = jnp.where(parity == index_ref[1], 0, 1)
+                holder = lax.rem(2 * place + parity + index_ref[2 + ROUNDS], 2 * ROUNDS)
+                side = lax.rem(holder, 2)
+                swapped = jnp.where(side == index_ref[1], 0, 1)
                 product = lax.dot_general(
-                    w_ref[2 * place + swapped],
+                    w_ref[holder - side + swapped],
                     x_ref[part, slot],
                     (((1,), (1,)), ((), ())),
                     preferred_element_type=F32,
@@ -297,7 +296,17 @@
     h = lax.rem(seq_index, 2)
     base = seq_index * rows
 
+    x_own = tokens.T.astype(F32)
+    gained = (x_own * (1.0 + pre_gain.astype(F32))[:, None]).astype(BF)
+    squares = jnp.sum(x_own * x_own, axis=0, keepdims=True)
+    upper = lax.reduce_precision(squares, 8, 7)
+    lower = squares - upper
+    side = jnp.concatenate(
+        [upper.astype(BF), lower.astype(BF), jnp.zeros((EXTRA - 2, rows), BF)], axis=0
+    )
+    x_all = lax.all_gather(jnp.concatenate([gained, side], axis=0), "mp", axis=0)
     depth = features + EXTRA
+
     lane = jnp.arange(2 * HD, dtype=jnp.int32)
     marked = 2 * (SEGS - 1)
     limit = jnp.where(lane < marked, lax.rem(lane, SEGS - 1) + 1, 0)
@@ -306,31 +315,20 @@
     digits = jnp.where(lane < SEGS - 1, upper_digit, counts - 16.0 * upper_digit).astype(BF)
     digits = jnp.pad(digits[None, :], ((2, EXTRA - 3), (0, 0)))
     kv_own = jnp.concatenate([jnp.concatenate([w_key, w_value], axis=1), digits], axis=0)
-    q_own = jnp.pad(w_query, ((0, EXTRA), (0, 0)))
-    facing, q_facing = tie(move(kv_own, ACROSS), move(q_own, ACROSS))
-    x_own, kv_own = tie(tokens.T, kv_own)
-    x_own = x_own.astype(F32)
-    gained = (x_own * (1.0 + pre_gain.astype(F32))[:, None]).astype(BF)
-    squares = jnp.sum(x_own * x_own, axis=0, keepdims=True)
-    upper = lax.reduce_precision(squares, 8, 7)
-    lower = squares - upper
-    side = jnp.concatenate(
-        [upper.astype(BF), lower.astype(BF), jnp.zeros((EXTRA - 2, rows), BF)], axis=0
-    )
-    x_all = lax.all_gather(jnp.concatenate([gained, side], axis=0), "mp", axis=0)
-    start = jnp.concatenate([kv_own, facing], axis=0)
+    start = jnp.concatenate([kv_own, move(kv_own, ACROSS)], axis=0)
     ring = {0: start, 1: move(start, AHEAD), -1: move(start, BEHIND)}
     turned = lax.ppermute(w_out.T, ("seq", "mp"), TURNS[0])
     ring[2] = move(ring[1], AHEAD)
     ring[-2] = move(ring[-1], BEHIND)
     ring[2], ring[-2], turned = tie(ring[2], ring[-2], turned)
-    q_pair = jnp.concatenate([q_own, q_facing], axis=0)
-    turned = lax.ppermute(turned, ("seq", "mp"), TURNS[1])
+    q_own = jnp.pad(w_query, ((0, EXTRA), (0, 0)))
+    q_own, _ = tie(q_own, ring[1])
+    q_pair = jnp.concatenate([q_own, move(q_own, ACROSS)], axis=0)
     ring[3] = move(ring[2], AHEAD)
     ring[-3] = move(ring[-2], BEHIND)
-    ring[3], ring[-3], turned = tie(ring[3], ring[-3], turned)
+    ring[3], ring[-3], q_pair = tie(ring[3], ring[-3], q_pair)
     q_all = lax.all_gather(q_pair, "seq", axis=0, axis_index_groups=COLUMNS)
-    turned = lax.ppermute(turned, ("seq", "mp"), TURNS[2])
+    turned = lax.ppermute(turned, ("seq", "mp"), TURNS[1])
     last = move(ring[3][:, :HD], AHEAD)
     opposite = move(ring[-3][:, HD:], BEHIND)
     last, opposite, turned = tie(last, opposite, turned)
@@ -396,8 +394,8 @@
         else:
             if step == 2:
                 facing_out = move(turned, ACROSS)
-                following, chosen, crossed[2], facing_out = tie(
-                    following, chosen, crossed[2], facing_out
+                following, chosen, crossed[2], facing_out, *state = tie(
+                    following, chosen, crossed[2], facing_out, *state
                 )
             else:
                 following, chosen, crossed[3], *state = tie(
@@ -425,7 +423,7 @@
     share, partial = output(
         [a_pair, a_up, a_down, *a_far, *a_swaps],
         out_all.reshape(2 * ROUNDS, features, 2 * HD),
-        index,
+        jnp.concatenate([index[: 2 + ROUNDS], mp_index[None].astype(jnp.int32)]),
     )
     everywhere = jnp.broadcast_to(partial, (lax.axis_size("mp"), rows))
     square_total = jnp.sum(lax.all_to_all(everywhere, "mp", 0, 0, tiled=True), axis=0)

time: 230 us -> 215 us (0.935)
  starting transfers between devices: 88.4 us -> 70.2 us
  local copies, waits for them, and re-layouts: 7.58 us -> 12 us
    ppermute x19, starting transfers between devices: 55 us -> 41.8 us  [move(): return lax.ppermute(block, 'seq', perm)]
    ppermute x19, waiting for transfers between devices: 48.1 us -> 36.8 us  [move(): return lax.ppermute(block, 'seq', perm)]
    ppermute x1, waiting for transfers between devices: 0.01 us -> 6.49 us  [shards(): turned = lax.ppermute(w_out.T, ('seq', 'mp'), TURNS[0])]
    ppermute x10, starting transfers between devices: 21.9 us -> 16.9 us  [shift(): return lax.ppermute(block, 'mp', perm)]
    ppermute x1, starting transfers between devices: 0.66 us -> 4.64 us  [shards(): turned = lax.ppermute(w_out.T, ('seq', 'mp'), TURNS[0])]
    unnamed x53 -> x55, local copies, waits for them, and re-layouts: 1.78 us -> 5.65 us
    ppermute x10, waiting for transfers between devices: 7.01 us -> 10.4 us  [shift(): return lax.ppermute(block, 'mp', perm)]
    ppermute x1, starting transfers between devices: 5.75 us -> 2.87 us  [shards(): turned = lax.ppermute(turned, ('seq', 'mp'), TURNS[1])]
  transfers between devices with their start and end apart: 36 -> 35, of which waited for: 16 -> 13; matrix products, arithmetic and copies ran while one was open for 5% -> 6% of each run, Pallas kernels for 12% -> 13%
where the time goes in v9:
time: 215 us; the launch traced here: 212 us
  starting transfers between devices  70.2 us (33%)
  waiting for transfers between devices  63 us (29%)
  Pallas kernels  33.3 us (15%)
  between operations  21.9 us (10%)
  local copies, waits for them, and re-layouts  12 us (6%)
  other arithmetic  11.6 us (5%)
    ppermute x19, starting transfers between devices, move(): return lax.ppermute(block, 'seq', perm)  41.8 us
    ppermute x19, waiting for transfers between devices, move(): return lax.ppermute(block, 'seq', perm)  36.8 us
    ppermute x10, starting transfers between devices, shift(): return lax.ppermute(block, 'mp', perm)  16.9 us
    pallas_call x2, Pallas kernels, project(): pl.pallas_call(functools.partial(project_kernel, pieces, rotated, factor)...  13.6 us
    pallas_call x5, Pallas kernels, attend(): pl.pallas_call(functools.partial(attend_kernel, tuple(distances), first,...  13.4 us
    ppermute x10, waiting for transfers between devices, shift(): return lax.ppermute(block, 'mp', perm)  10.4 us
    ppermute x1, waiting for transfers between devices, shards(): turned = lax.ppermute(w_out.T, ('seq', 'mp'), TURNS[0])  6.49 us
    pallas_call x1, Pallas kernels, output(): pl.pallas_call(output_kernel, out_shape=(jax.ShapeDtypeStruct((features,...  6.35 us
  transfers between devices with their start and end apart: 35, of which 13 were waited for; matrix products, arithmetic and copies ran while one was open for 6% of the time, Pallas kernels for 13%

profile of v9, /device:TPU:1, one launch (start us, length us, event | category | flops | bytes accessed | tf_op | source)
XLA Modules:
  0.0 212.1 jit_solution(1868283769605596623)
XLA Ops:
  12.8 3.7 %collective-permute-start = (bf16[304,256]{1,0:T(8,128)(2,1)S(1)}, bf16[304,256]{1,0:T(8,128)(2,1)S(1)}, u32[]{:S(2)}, u32[]{:S(2)}) collective-permute-start(bf16[304,256]{1,0:T(8,128)(2,1)S(1)} %pad_maximum_fusion.5), channel_id=1, source_target_pairs={{0,16},{16,0},{32,48},{48,32},{64,80},{80,64},{96,112},{112,96},{1... | collective-permute-start | bytes 466952 | tf_op jit(solution)/shard_map/ppermute | solution.py:45
  21.9 4.0 %collective-permute-start.2 = (bf16[608,256]{1,0:T(8,128)(2,1)S(1)}, bf16[608,256]{1,0:T(8,128)(2,1)S(1)}, u32[]{:S(2)}, u32[]{:S(2)}) collective-permute-start(bf16[608,256]{1,0:T(8,128)(2,1)S(1)} %pad_maximum_fusion.1.rest_0_), channel_id=1, source_target_pairs={{32,0},{48,16},{64,32},{80,48},{96,64},{112,80},{128,96},{144,112}... | collective-permute-start | bytes 933896 | tf_op jit(solution)/shard_map/ppermute | solution.py:45
  25.9 6.0 %collective-permute-done.1.rest_1_ = bf16[608,256]{1,0:T(8,128)(2,1)S(1)} collective-permute-done((bf16[608,256]{1,0:T(8,128)(2,1)S(1)}, bf16[608,256]{1,0:T(8,128)(2,1)S(1)}, u32[]{:S(2)}, u32[]{:S(2)}) %collective-permute-start.1) | collective-permute-done | bytes 311328 | tf_op jit(solution)/shard_map/ppermute | solution.py:45
  34.7 4.6 %collective-permute-start.5 = (bf16[288,256]{1,0:T(8,128)(2,1)S(1)}, bf16[288,256]{1,0:T(8,128)(2,1)S(1)}, u32[]{:S(2)}, u32[]{:S(2)}) collective-permute-start(bf16[288,256]{1,0:T(8,128)(2,1)S(1)} %bitcast.80), channel_id=1, source_target_pairs={{0,0},{1,17},{2,34},{3,51},{4,68},{5,85},{6,102},{7,119},{8,136},{... | collective-permute-start | bytes 442376 | tf_op jit(solution)/shard_map/ppermute | solution.py:320
  39.3 6.5 %collective-permute-done.5 = bf16[288,256]{1,0:T(8,128)(2,1)S(1)} collective-permute-done((bf16[288,256]{1,0:T(8,128)(2,1)S(1)}, bf16[288,256]{1,0:T(8,128)(2,1)S(1)}, u32[]{:S(2)}, u32[]{:S(2)}) %collective-permute-start.5) | collective-permute-done | bytes 147488 | tf_op jit(solution)/shard_map/ppermute | solution.py:320
  50.7 7.6 %collective-permute-done.8 = bf16[304,256]{1,0:T(8,128)(2,1)S(1)} collective-permute-done((bf16[304,256]{1,0:T(8,128)(2,1)S(1)}, bf16[304,256]{1,0:T(8,128)(2,1)S(1)}, u32[]{:S(2)}, u32[]{:S(2)}) %collective-permute-start.8) | collective-permute-done | bytes 155680 | tf_op jit(solution)/shard_map/ppermute | solution.py:45
  62.0 2.9 %collective-permute-start.11 = (bf16[288,256]{1,0:T(8,128)(2,1)S(1)}, bf16[288,256]{1,0:T(8,128)(2,1)S(1)}, u32[]{:S(2)}, u32[]{:S(2)}) collective-permute-start(bf16[288,256]{1,0:T(8,128)(2,1)S(1)} %collective-permute-done.5), channel_id=1, source_target_pairs={{0,0},{1,15},{2,14},{3,13},{4,12},{5,11},{6,10},{7,9},{8,8},{9,7},... | collective-permute-start | bytes 442376 | tf_op jit(solution)/shard_map/ppermute | solution.py:331
  65.7 4.3 %collective-permute-done.11 = bf16[288,256]{1,0:T(8,128)(2,1)S(1)} collective-permute-done((bf16[288,256]{1,0:T(8,128)(2,1)S(1)}, bf16[288,256]{1,0:T(8,128)(2,1)S(1)}, u32[]{:S(2)}, u32[]{:S(2)}) %collective-permute-start.11) | collective-permute-done | bytes 147488 | tf_op jit(solution)/shard_map/ppermute | solution.py:331
  73.9 7.0 %shard_map.112.rest_0_ = bf16[512,256]{1,0:T(8,128)(2,1)} custom-call(s32[18]{0:T(128)} %stack.105.index_ref, f32[64,512]{1,0:T(8,128)} %get-tuple-element.104.cos_ref, f32[64,512]{1,0:T(8,128)} %get-tuple-element.103.sin_ref, bf16[16,304,512]{2,1,0:T(8,128)(2,1)} %bitcast.72, bf16[608,256]{1,0:T(8,128)(2,1)} %copy-done.8, bf16[608,256]{1,0:T(8,128)(2,1)} %copy-done.16, ...), custom_call_target="tpu_custom_call" | custom-call | flops 1207959552 | bytes 8388608 | tf_op jit(solution)/shard_map/pallas_call | solution.py:123
  82.3 11.5 %collective-permute-done.12.rest_0_ = bf16[512,256]{1,0:T(8,128)(2,1)S(1)} collective-permute-done((bf16[512,256]{1,0:T(8,128)(2,1)}, bf16[512,256]{1,0:T(8,128)(2,1)S(1)}, u32[]{:S(2)}, u32[]{:S(2)}) %collective-permute-start.12) | collective-permute-done | bytes 262176 | tf_op jit(solution)/shard_map/ppermute | solution.py:45
  94.7 4.1 %collective-permute-start.13 = (bf16[512,256]{1,0:T(8,128)(2,1)S(1)}, bf16[512,256]{1,0:T(8,128)(2,1)S(1)}, u32[]{:S(2)}, u32[]{:S(2)}) collective-permute-start(bf16[512,256]{1,0:T(8,128)(2,1)S(1)} %collective-permute-done.12.rest_0_), channel_id=1, source_target_pairs={{0,32},{16,48},{32,64},{48,80},{64,96},{80,112},{96,128},{112,144}... | collective-permute-start | bytes 786440 | tf_op jit(solution)/shard_map/ppermute | solution.py:45
  100.1 8.9 %collective-permute-done.13.rest_0_ = bf16[512,256]{1,0:T(8,128)(2,1)S(1)} collective-permute-done((bf16[512,256]{1,0:T(8,128)(2,1)S(1)}, bf16[512,256]{1,0:T(8,128)(2,1)S(1)}, u32[]{:S(2)}, u32[]{:S(2)}) %collective-permute-start.13) | collective-permute-done | bytes 262176 | tf_op jit(solution)/shard_map/ppermute | solution.py:45
  109.1 4.1 %collective-permute-start.15 = (bf16[512,256]{1,0:T(8,128)(2,1)S(1)}, bf16[512,256]{1,0:T(8,128)(2,1)S(1)}, u32[]{:S(2)}, u32[]{:S(2)}) collective-permute-start(bf16[512,256]{1,0:T(8,128)(2,1)S(1)} %collective-permute-done.13.rest_0_), channel_id=1, source_target_pairs={{0,32},{16,48},{32,64},{48,80},{64,96},{80,112},{96,128},{112,144}... | collective-permute-start | bytes 786440 | tf_op jit(solution)/shard_map/ppermute | solution.py:45
  117.1 6.6 %shard_map.113.q_ref = bf16[512,256]{1,0:T(8,128)(2,1)} custom-call(s32[18]{0:T(128)} %stack.96.index_ref, f32[64,512]{1,0:T(8,128)} %get-tuple-element.104.cos_ref, f32[64,512]{1,0:T(8,128)} %get-tuple-element.103.sin_ref, bf16[16,304,512]{2,1,0:T(8,128)(2,1)} %bitcast.73, bf16[8,608,256]{2,1,0:T(8,128)(2,1)} %bitcast.74), custom_call_target="tpu_custom_call" | custom-call | flops 1207959552 | bytes 8388608 | tf_op jit(solution)/shard_map/pallas_call | solution.py:123
  127.5 3.2 %collective-permute-start.18 = (bf16[512,256]{1,0:T(8,128)(2,1)S(1)}, bf16[512,256]{1,0:T(8,128)(2,1)S(1)}, u32[]{:S(2)}, u32[]{:S(2)}) collective-permute-start(bf16[512,256]{1,0:T(8,128)(2,1)S(1)} %collective-permute-done.15.rest_0_), channel_id=1, source_target_pairs={{0,32},{16,48},{32,64},{48,80},{64,96},{80,112},{96,128},{112,144}... | collective-permute-start | bytes 786440 | tf_op jit(solution)/shard_map/ppermute | solution.py:45
  135.3 2.9 %shard_map.115 = (f32[512,256]{1,0:T(8,128)S(1)}, f32[512,256]{1,0:T(8,128)S(1)}) custom-call(s32[512,1]{1,0:T(8,128)S(1)} %copy.32.low_ref, bf16[512,256]{1,0:T(8,128)(2,1)S(1)} %copy-done.2, bf16[512,256]{1,0:T(8,128)(2,1)S(1)} %collective-permute-done.12.rest_0_, ...), custom_call_target="tpu_custom_call", output_to_operand_aliasing={{0}: (4, {}), {1}: (5, {})} | custom-call | flops 536870912 | bytes 4194304 | tf_op jit(solution)/shard_map/pallas_call | solution.py:199
  144.2 2.9 %shard_map.117 = (f32[512,256]{1,0:T(8,128)S(1)}, f32[512,256]{1,0:T(8,128)S(1)}) custom-call(s32[512,1]{1,0:T(8,128)S(1)} %copy.32.low_ref, bf16[512,256]{1,0:T(8,128)(2,1)S(1)} %copy-done.2, bf16[512,256]{1,0:T(8,128)(2,1)S(1)} %collective-permute-done.15.rest_0_, ...), custom_call_target="tpu_custom_call", output_to_operand_aliasing={{0}: (4, {}), {1}: (5, {})} | custom-call | flops 536870912 | bytes 4194304 | tf_op jit(solution)/shard_map/pallas_call | solution.py:199
  147.2 2.9 %shard_map.118 = bf16[512,256]{1,0:T(8,128)(2,1)S(1)} custom-call(s32[512,1]{1,0:T(8,128)S(1)} %copy.32.low_ref, bf16[512,256]{1,0:T(8,128)(2,1)S(1)} %copy-done.2, bf16[512,256]{1,0:T(8,128)(2,1)S(1)} %collective-permute-done.18.rest_0_, bf16[512,256]{1,0:T(8,128)(2,1)S(1)} %collective-permute-done.20.rest_1_, f32[512,256]{1,0:T(8,128)S(1)} %get-tuple-element.83.rest_2_, ...), custom_call_target="tpu_custom_call" | custom-call | flops 536870912 | bytes 4194304 | tf_op jit(solution)/shard_map/pallas_call | solution.py:199
  150.1 5.6 %collective-permute-done.21 = bf16[1,512,256]{2,1,0:T(8,128)(2,1)S(1)} collective-permute-done((bf16[1,512,256]{2,1,0:T(8,128)(2,1)S(1)}, bf16[1,512,256]{2,1,0:T(8,128)(2,1)S(1)}, u32[]{:S(2)}, u32[]{:S(2)}) %collective-permute-start.21) | collective-permute-done | bytes 262176 | tf_op jit(solution)/shard_map/ppermute | solution.py:49
  158.8 5.0 %collective-permute-start.24 = (bf16[2,512,256]{2,1,0:T(8,128)(2,1)S(1)}, bf16[2,512,256]{2,1,0:T(8,128)(2,1)S(1)}, u32[]{:S(2)}, u32[]{:S(2)}) collective-permute-start(bf16[2,512,256]{2,1,0:T(8,128)(2,1)S(1)} %pad_maximum_fusion.rest_0_), channel_id=1, source_target_pairs={{0,1},{1,0},{2,3},{3,2},{4,5},{5,4},{6,7},{7,6},{8,9},{9,8},{10,11... | collective-permute-start | bytes 1572872 | tf_op jit(solution)/shard_map/ppermute | solution.py:49
  166.9 4.8 %collective-permute-start.27 = (bf16[2,512,256]{2,1,0:T(8,128)(2,1)S(1)}, bf16[2,512,256]{2,1,0:T(8,128)(2,1)S(1)}, u32[]{:S(2)}, u32[]{:S(2)}) collective-permute-start(bf16[2,512,256]{2,1,0:T(8,128)(2,1)S(1)} %collective-permute-done.22.rest_1_), channel_id=1, source_target_pairs={{0,1},{1,0},{2,3},{3,2},{4,5},{5,4},{6,7},{7,6},{8,9},{9,8},{10,11... | collective-permute-start | bytes 1572872 | tf_op jit(solution)/shard_map/ppermute | solution.py:49
  186.3 6.4 %shard_map.119 = (f32[288,512]{1,0:T(8,128)}, f32[1,512]{1,0:T(1,128)}) custom-call(s32[11]{0:T(128)} %concatenate.28.index_ref, bf16[2,512,256]{2,1,0:T(8,128)(2,1)} %copy-done.7, bf16[2,512,256]{2,1,0:T(8,128)(2,1)} %copy-done.10, bf16[2,512,256]{2,1,0:T(8,128)(2,1)} %copy-done.11, bf16[1,512,256]{2,1,0:T(8,128)(2,1)} %collective-permute-done.25.rest_3_, ...), custom_call_target="tpu_custom_call" | custom-call | flops 1207959552 | bytes 8388608 | tf_op jit(solution)/shard_map/pallas_call | solution.py:270
  194.0 3.8 %all-to-all-start = ((f32[16,1,512]{2,1,0:T(1,128)}), f32[16,1,512]{2,1,0:T(1,128)S(1)}, u32[]{:S(2)}, u32[]{:S(2)}) async-start(f32[16,1,512]{2,1,0:T(1,128)} %broadcast_in_dim.52), calls=%async_computation | async-start | bytes 65536 | tf_op jit(solution)/shard_map/all_to_all | solution.py:429
  198.5 5.1 %all-to-all-done = f32[16,1,512]{2,1,0:T(1,128)S(1)} async-done(((f32[16,1,512]{2,1,0:T(1,128)}), f32[16,1,512]{2,1,0:T(1,128)S(1)}, u32[]{:S(2)}, u32[]{:S(2)}) %all-to-all-start) | async-done | bytes 32800 | tf_op jit(solution)/shard_map/all_to_all | solution.py:429
  (158 shorter events, 65.8 us)
Async XLA Ops:
  7.2 66.7 %all-gather.7.cloned.1.call-start = ((), (), s32[]{:S(2)}) async-start(), calls=%async_computation.1 | async-start | bytes 5292032 | tf_op jit(solution)/shard_map/all_gather | solution.py:307
  10.1 99.0 %all-gather.9.cloned.1.call-start = ((), (), s32[]{:S(2)}) async-start(), calls=%async_computation.2 | async-start | bytes 2801664 | tf_op jit(solution)/shard_map/all_gather | solution.py:330
  19.2 12.7 %collective-permute-start.1 = (bf16[608,256]{1,0:T(8,128)(2,1)S(1)}, bf16[608,256]{1,0:T(8,128)(2,1)S(1)}, u32[]{:S(2)}, u32[]{:S(2)}) collective-permute-start(bf16[608,256]{1,0:T(8,128)(2,1)S(1)} %pad_maximum_fusion.1.rest_0_), channel_id=1, source_target_pairs={{0,32},{16,48},{32,64},{48,80},{64,96},{80,112},{96,128},{112,144}... | collective-permute-start | bytes 933896 | tf_op jit(solution)/shard_map/ppermute | solution.py:45
  21.9 10.1 %collective-permute-start.2 = (bf16[608,256]{1,0:T(8,128)(2,1)S(1)}, bf16[608,256]{1,0:T(8,128)(2,1)S(1)}, u32[]{:S(2)}, u32[]{:S(2)}) collective-permute-start(bf16[608,256]{1,0:T(8,128)(2,1)S(1)} %pad_maximum_fusion.1.rest_0_), channel_id=1, source_target_pairs={{32,0},{48,16},{64,32},{80,48},{96,64},{112,80},{128,96},{144,112}... | collective-permute-start | bytes 933896 | tf_op jit(solution)/shard_map/ppermute | solution.py:45
  32.0 13.8 %collective-permute-start.3 = (bf16[608,256]{1,0:T(8,128)(2,1)S(1)}, bf16[608,256]{1,0:T(8,128)(2,1)S(1)}, u32[]{:S(2)}, u32[]{:S(2)}) collective-permute-start(bf16[608,256]{1,0:T(8,128)(2,1)S(1)} %collective-permute-done.1.rest_1_), channel_id=1, source_target_pairs={{0,32},{16,48},{32,64},{48,80},{64,96},{80,112},{96,128},{112,144}... | collective-permute-start | bytes 933896 | tf_op jit(solution)/shard_map/ppermute | solution.py:45
  32.0 13.8 %collective-permute-start.4 = (bf16[608,256]{1,0:T(8,128)(2,1)S(1)}, bf16[608,256]{1,0:T(8,128)(2,1)S(1)}, u32[]{:S(2)}, u32[]{:S(2)}) collective-permute-start(bf16[608,256]{1,0:T(8,128)(2,1)S(1)} %collective-permute-done.2.rest_2_), channel_id=1, source_target_pairs={{32,0},{48,16},{64,32},{80,48},{96,64},{112,80},{128,96},{144,112}... | collective-permute-start | bytes 933896 | tf_op jit(solution)/shard_map/ppermute | solution.py:45
  34.7 11.1 %collective-permute-start.5 = (bf16[288,256]{1,0:T(8,128)(2,1)S(1)}, bf16[288,256]{1,0:T(8,128)(2,1)S(1)}, u32[]{:S(2)}, u32[]{:S(2)}) collective-permute-start(bf16[288,256]{1,0:T(8,128)(2,1)S(1)} %bitcast.80), channel_id=1, source_target_pairs={{0,0},{1,17},{2,34},{3,51},{4,68},{5,85},{6,102},{7,119},{8,136},{... | collective-permute-start | bytes 442376 | tf_op jit(solution)/shard_map/ppermute | solution.py:320
  45.8 13.2 %collective-permute-start.6 = (bf16[608,256]{1,0:T(8,128)(2,1)S(1)}, bf16[608,256]{1,0:T(8,128)(2,1)S(1)}, u32[]{:S(2)}, u32[]{:S(2)}) collective-permute-start(bf16[608,256]{1,0:T(8,128)(2,1)S(1)} %collective-permute-done.3.rest_3_), channel_id=1, source_target_pairs={{0,32},{16,48},{32,64},{48,80},{64,96},{80,112},{96,128},{112,144}... | collective-permute-start | bytes 933896 | tf_op jit(solution)/shard_map/ppermute | solution.py:45
  45.9 13.1 %collective-permute-start.7 = (bf16[608,256]{1,0:T(8,128)(2,1)S(1)}, bf16[608,256]{1,0:T(8,128)(2,1)S(1)}, u32[]{:S(2)}, u32[]{:S(2)}) collective-permute-start(bf16[608,256]{1,0:T(8,128)(2,1)S(1)} %collective-permute-done.4.rest_4_), channel_id=1, source_target_pairs={{32,0},{48,16},{64,32},{80,48},{96,64},{112,80},{128,96},{144,112}... | collective-permute-start | bytes 933896 | tf_op jit(solution)/shard_map/ppermute | solution.py:45
  59.1 127.2 %all-gather.11.cloned.1.call-start = ((), (), s32[]{:S(2)}) async-start(), calls=%async_computation.3 | async-start | bytes 2654208 | tf_op jit(solution)/shard_map/all_gather | solution.py:410
  59.1 10.8 %collective-permute-start.9 = (bf16[608,128]{1,0:T(8,128)(2,1)S(1)}, bf16[608,128]{1,0:T(8,128)(2,1)S(1)}, u32[]{:S(2)}, u32[]{:S(2)}) collective-permute-start(bf16[608,128]{1,0:T(8,128)(2,1)S(1)} %slice.144), channel_id=1, source_target_pairs={{0,32},{16,48},{32,64},{48,80},{64,96},{80,112},{96,128},{112,144}... | collective-permute-start | bytes 466952 | tf_op jit(solution)/shard_map/ppermute | solution.py:45
  59.2 10.7 %collective-permute-start.10 = (bf16[608,128]{1,0:T(8,128)(2,1)S(1)}, bf16[608,128]{1,0:T(8,128)(2,1)S(1)}, u32[]{:S(2)}, u32[]{:S(2)}) collective-permute-start(bf16[608,128]{1,0:T(8,128)(2,1)S(1)} %slice.145), channel_id=1, source_target_pairs={{32,0},{48,16},{64,32},{80,48},{96,64},{112,80},{128,96},{144,112}... | collective-permute-start | bytes 466952 | tf_op jit(solution)/shard_map/ppermute | solution.py:45
  80.9 12.8 %collective-permute-start.12 = (bf16[512,256]{1,0:T(8,128)(2,1)}, bf16[512,256]{1,0:T(8,128)(2,1)S(1)}, u32[]{:S(2)}, u32[]{:S(2)}) collective-permute-start(bf16[512,256]{1,0:T(8,128)(2,1)} %shard_map.112.rest_0_), channel_id=1, source_target_pairs={{0,32},{16,48},{32,64},{48,80},{64,96},{80,112},{96,128},{112,144}... | collective-permute-start | bytes 786440 | tf_op jit(solution)/shard_map/ppermute | solution.py:45
  94.7 14.3 %collective-permute-start.13 = (bf16[512,256]{1,0:T(8,128)(2,1)S(1)}, bf16[512,256]{1,0:T(8,128)(2,1)S(1)}, u32[]{:S(2)}, u32[]{:S(2)}) collective-permute-start(bf16[512,256]{1,0:T(8,128)(2,1)S(1)} %collective-permute-done.12.rest_0_), channel_id=1, source_target_pairs={{0,32},{16,48},{32,64},{48,80},{64,96},{80,112},{96,128},{112,144}... | collective-permute-start | bytes 786440 | tf_op jit(solution)/shard_map/ppermute | solution.py:45
  98.8 10.3 %collective-permute-start.14 = (bf16[512,256]{1,0:T(8,128)(2,1)S(1)}, bf16[512,256]{1,0:T(8,128)(2,1)S(1)}, u32[]{:S(2)}, u32[]{:S(2)}) collective-permute-start(bf16[512,256]{1,0:T(8,128)(2,1)S(1)} %broadcast_select_fusion.3), channel_id=1, source_target_pairs={{0,16},{16,0},{32,48},{48,32},{64,80},{80,64},{96,112},{112,96},{1... | collective-permute-start | bytes 786440 | tf_op jit(solution)/shard_map/ppermute | solution.py:45
  109.1 18.3 %collective-permute-start.15 = (bf16[512,256]{1,0:T(8,128)(2,1)S(1)}, bf16[512,256]{1,0:T(8,128)(2,1)S(1)}, u32[]{:S(2)}, u32[]{:S(2)}) collective-permute-start(bf16[512,256]{1,0:T(8,128)(2,1)S(1)} %collective-permute-done.13.rest_0_), channel_id=1, source_target_pairs={{0,32},{16,48},{32,64},{48,80},{64,96},{80,112},{96,128},{112,144}... | collective-permute-start | bytes 786440 | tf_op jit(solution)/shard_map/ppermute | solution.py:45
  114.1 13.4 %collective-permute-start.17 = (bf16[288,256]{1,0:T(8,128)(2,1)S(1)}, bf16[288,256]{1,0:T(8,128)(2,1)S(1)}, u32[]{:S(2)}, u32[]{:S(2)}) collective-permute-start(bf16[288,256]{1,0:T(8,128)(2,1)S(1)} %collective-permute-done.11), channel_id=1, source_target_pairs={{0,16},{16,0},{32,48},{48,32},{64,80},{80,64},{96,112},{112,96},{1... | collective-permute-start | bytes 442376 | tf_op jit(solution)/shard_map/ppermute | solution.py:45
  116.6 10.9 %collective-permute-start.16 = (bf16[512,256]{1,0:T(8,128)(2,1)S(1)}, bf16[512,256]{1,0:T(8,128)(2,1)S(1)}, u32[]{:S(2)}, u32[]{:S(2)}) collective-permute-start(bf16[512,256]{1,0:T(8,128)(2,1)S(1)} %broadcast_select_fusion.2), channel_id=1, source_target_pairs={{0,16},{16,0},{32,48},{48,32},{64,80},{80,64},{96,112},{112,96},{1... | collective-permute-start | bytes 786440 | tf_op jit(solution)/shard_map/ppermute | solution.py:45
  127.5 11.4 %collective-permute-start.18 = (bf16[512,256]{1,0:T(8,128)(2,1)S(1)}, bf16[512,256]{1,0:T(8,128)(2,1)S(1)}, u32[]{:S(2)}, u32[]{:S(2)}) collective-permute-start(bf16[512,256]{1,0:T(8,128)(2,1)S(1)} %collective-permute-done.15.rest_0_), channel_id=1, source_target_pairs={{0,32},{16,48},{32,64},{48,80},{64,96},{80,112},{96,128},{112,144}... | collective-permute-start | bytes 786440 | tf_op jit(solution)/shard_map/ppermute | solution.py:45
  155.8 10.4 %collective-permute-start.22 = (bf16[2,512,256]{2,1,0:T(8,128)(2,1)S(1)}, bf16[2,512,256]{2,1,0:T(8,128)(2,1)S(1)}, u32[]{:S(2)}, u32[]{:S(2)}) collective-permute-start(bf16[2,512,256]{2,1,0:T(8,128)(2,1)S(1)} %pad_maximum_fusion.rest_0_), channel_id=1, source_target_pairs={{0,4},{1,5},{2,6},{3,7},{4,8},{5,9},{6,10},{7,11},{8,12},{9,13},{1... | collective-permute-start | bytes 1572872 | tf_op jit(solution)/shard_map/ppermute | solution.py:49
  166.9 16.6 %collective-permute-start.27 = (bf16[2,512,256]{2,1,0:T(8,128)(2,1)S(1)}, bf16[2,512,256]{2,1,0:T(8,128)(2,1)S(1)}, u32[]{:S(2)}, u32[]{:S(2)}) collective-permute-start(bf16[2,512,256]{2,1,0:T(8,128)(2,1)S(1)} %collective-permute-done.22.rest_1_), channel_id=1, source_target_pairs={{0,1},{1,0},{2,3},{3,2},{4,5},{5,4},{6,7},{7,6},{8,9},{9,8},{10,11... | collective-permute-start | bytes 1572872 | tf_op jit(solution)/shard_map/ppermute | solution.py:49
  171.7 11.7 %collective-permute-start.28 = (bf16[2,512,256]{2,1,0:T(8,128)(2,1)S(1)}, bf16[2,512,256]{2,1,0:T(8,128)(2,1)}, u32[]{:S(2)}, u32[]{:S(2)}) collective-permute-start(bf16[2,512,256]{2,1,0:T(8,128)(2,1)S(1)} %collective-permute-done.23.rest_2_), channel_id=1, source_target_pairs={{0,1},{1,0},{2,3},{3,2},{4,5},{5,4},{6,7},{7,6},{8,9},{9,8},{10,11... | collective-permute-start | bytes 1572872 | tf_op jit(solution)/shard_map/ppermute | solution.py:49
  171.8 11.5 %collective-permute-start.25 = (bf16[1,512,256]{2,1,0:T(8,128)(2,1)S(1)}, bf16[1,512,256]{2,1,0:T(8,128)(2,1)}, u32[]{:S(2)}, u32[]{:S(2)}) collective-permute-start(bf16[1,512,256]{2,1,0:T(8,128)(2,1)S(1)} %slice.153), channel_id=1, source_target_pairs={{0,4},{1,5},{2,6},{3,7},{4,8},{5,9},{6,10},{7,11},{8,12},{9,13},{1... | collective-permute-start | bytes 786440 | tf_op jit(solution)/shard_map/ppermute | solution.py:49
  173.4 10.0 %collective-permute-start.26 = (bf16[1,512,256]{2,1,0:T(8,128)(2,1)S(1)}, bf16[1,512,256]{2,1,0:T(8,128)(2,1)}, u32[]{:S(2)}, u32[]{:S(2)}) collective-permute-start(bf16[1,512,256]{2,1,0:T(8,128)(2,1)S(1)} %slice.154), channel_id=1, source_target_pairs={{4,0},{5,1},{6,2},{7,3},{8,4},{9,5},{10,6},{11,7},{12,8},{13,9},{1... | collective-permute-start | bytes 786440 | tf_op jit(solution)/shard_map/ppermute | solution.py:49
  (38 other events, 616.7 us)
Sparse Core Ops, SparseCore 0:
  10.2 46.4 all-gather.6
  59.2 47.2 all-gather.8
  139.1 39.7 all-gather.10

commit v10 on v9

--- a/solution.py
+++ b/solution.py
@@ -258,7 +258,8 @@
             else:
                 total = out_ref[...] + total
                 out_ref[...] = total
-                square_ref[...] = jnp.sum(total * total, axis=0, keepdims=True)
+                squares = jnp.sum(total * total, axis=0, keepdims=True)
+                square_ref[...] = jnp.broadcast_to(squares[None], square_ref.shape)
             slot += 1
 
 
@@ -271,7 +272,7 @@
         output_kernel,
         out_shape=(
             jax.ShapeDtypeStruct((features, rows), F32),
-            jax.ShapeDtypeStruct((1, rows), F32),
+            jax.ShapeDtypeStruct((SEQ, 1, rows), F32),
         ),
         in_specs=[pl.BlockSpec(memory_space=pltpu.SMEM)] + [outside] * (len(chunks) + 1),
         out_specs=(vmem, vmem),
@@ -318,15 +319,19 @@
     start = jnp.concatenate([kv_own, move(kv_own, ACROSS)], axis=0)
     ring = {0: start, 1: move(start, AHEAD), -1: move(start, BEHIND)}
     turned = lax.ppermute(w_out.T, ("seq", "mp"), TURNS[0])
+    ring[1], ring[-1], turned = tie(ring[1], ring[-1], turned)
+    q_own = jnp.pad(w_query, ((0, EXTRA), (0, 0)))
+    q_own, _ = tie(q_own, ring[1])
+    q_near = move(q_own[:, :HD], ACROSS)
     ring[2] = move(ring[1], AHEAD)
     ring[-2] = move(ring[-1], BEHIND)
-    ring[2], ring[-2], turned = tie(ring[2], ring[-2], turned)
-    q_own = jnp.pad(w_query, ((0, EXTRA), (0, 0)))
-    q_own, _ = tie(q_own, ring[1])
-    q_pair = jnp.concatenate([q_own, move(q_own, ACROSS)], axis=0)
+    ring[2], ring[-2], q_near = tie(ring[2], ring[-2], q_near)
+    q_far, _ = tie(q_own[:, HD:], q_near)
+    q_far = move(q_far, ACROSS)
     ring[3] = move(ring[2], AHEAD)
     ring[-3] = move(ring[-2], BEHIND)
-    ring[3], ring[-3], q_pair = tie(ring[3], ring[-3], q_pair)
+    ring[3], ring[-3], q_far = tie(ring[3], ring[-3], q_far)
+    q_pair = jnp.concatenate([q_own, jnp.concatenate([q_near, q_far], axis=1)], axis=0)
     q_all = lax.all_gather(q_pair, "seq", axis=0, axis_index_groups=COLUMNS)
     turned = lax.ppermute(turned, ("seq", "mp"), TURNS[1])
     last = move(ring[3][:, :HD], AHEAD)
@@ -425,8 +430,7 @@
         out_all.reshape(2 * ROUNDS, features, 2 * HD),
         jnp.concatenate([index[: 2 + ROUNDS], mp_index[None].astype(jnp.int32)]),
     )
-    everywhere = jnp.broadcast_to(partial, (lax.axis_size("mp"), rows))
-    square_total = jnp.sum(lax.all_to_all(everywhere, "mp", 0, 0, tiled=True), axis=0)
+    square_total = jnp.sum(lax.all_to_all(partial, "mp", 0, 0, tiled=True), axis=(0, 1))
     post_scale = lax.rsqrt(square_total / D + EPSILON)
     post = share * post_scale[None, :] * (1.0 + post_gain.astype(F32))[:, None]
     layer_output = (tokens.T.astype(F32) + post).astype(BF).T

time: 215 us -> 218 us (1.014)
  starting transfers between devices: 70.2 us -> 76.2 us
    ppermute x19 -> x20, waiting for transfers between devices: 36.8 us -> 29.2 us  [move(): return lax.ppermute(block, 'seq', perm)]
    all_gather x1, waiting for transfers between devices: 0.02 us -> 7.37 us  [shards(): q_all = lax.all_gather(q_pair, 'seq', axis=0, axis_index_groups=COLUMNS)]
    ppermute x19 -> x20, starting transfers between devices: 41.8 us -> 47.8 us  [move(): return lax.ppermute(block, 'seq', perm)]
  transfers between devices with their start and end apart: 35 -> 36, of which waited for: 13 -> 14; matrix products, arithmetic and copies ran while one was open for 6% -> 6% of each run, Pallas kernels for 13% -> 12%
where the time goes in v10:
time: 218 us; the launch traced here: 217 us
  starting transfers between devices  76.2 us (35%)
  waiting for transfers between devices  62.8 us (29%)
  Pallas kernels  33.3 us (15%)
  between operations  22.4 us (10%)
  other arithmetic  11.6 us (5%)
  local copies, waits for them, and re-layouts  10.7 us (5%)
    ppermute x20, starting transfers between devices, move(): return lax.ppermute(block, 'seq', perm)  47.8 us
    ppermute x20, waiting for transfers between devices, move(): return lax.ppermute(block, 'seq', perm)  29.2 us
    ppermute x10, starting transfers between devices, shift(): return lax.ppermute(block, 'mp', perm)  16.5 us
    pallas_call x2, Pallas kernels, project(): pl.pallas_call(functools.partial(project_kernel, pieces, rotated, factor)...  13.6 us
    pallas_call x5, Pallas kernels, attend(): pl.pallas_call(functools.partial(attend_kernel, tuple(distances), first,...  13.4 us
    ppermute x10, waiting for transfers between devices, shift(): return lax.ppermute(block, 'mp', perm)  10.7 us
    all_gather x1, waiting for transfers between devices, shards(): q_all = lax.all_gather(q_pair, 'seq', axis=0, axis_index_groups=COLUMNS)  7.37 us
    ppermute x1, waiting for transfers between devices, shards(): turned = lax.ppermute(w_out.T, ('seq', 'mp'), TURNS[0])  6.71 us
  transfers between devices with their start and end apart: 36, of which 14 were waited for; matrix products, arithmetic and copies ran while one was open for 6% of the time, Pallas kernels for 12%

profile of v10, /device:TPU:1, one launch (start us, length us, event | category | flops | bytes accessed | tf_op | source)
XLA Modules:
  0.0 217.2 jit_solution(11191627389981949915)
XLA Ops:
  12.8 3.7 %collective-permute-start = (bf16[304,256]{1,0:T(8,128)(2,1)S(1)}, bf16[304,256]{1,0:T(8,128)(2,1)S(1)}, u32[]{:S(2)}, u32[]{:S(2)}) collective-permute-start(bf16[304,256]{1,0:T(8,128)(2,1)S(1)} %pad_maximum_fusion.4), channel_id=1, source_target_pairs={{0,16},{16,0},{32,48},{48,32},{64,80},{80,64},{96,112},{112,96},{1... | collective-permute-start | bytes 466952 | tf_op jit(solution)/shard_map/ppermute | solution.py:45
  21.9 4.0 %collective-permute-start.2 = (bf16[608,256]{1,0:T(8,128)(2,1)S(1)}, bf16[608,256]{1,0:T(8,128)(2,1)S(1)}, u32[]{:S(2)}, u32[]{:S(2)}) collective-permute-start(bf16[608,256]{1,0:T(8,128)(2,1)S(1)} %pad_maximum_fusion.1.rest_0_), channel_id=1, source_target_pairs={{32,0},{48,16},{64,32},{80,48},{96,64},{112,80},{128,96},{144,112}... | collective-permute-start | bytes 933896 | tf_op jit(solution)/shard_map/ppermute | solution.py:45
  25.9 4.6 %collective-permute-start.3 = (bf16[288,256]{1,0:T(8,128)(2,1)S(1)}, bf16[288,256]{1,0:T(8,128)(2,1)S(1)}, u32[]{:S(2)}, u32[]{:S(2)}) collective-permute-start(bf16[288,256]{1,0:T(8,128)(2,1)S(1)} %bitcast.78), channel_id=1, source_target_pairs={{0,0},{1,17},{2,34},{3,51},{4,68},{5,85},{6,102},{7,119},{8,136},{... | collective-permute-start | bytes 442376 | tf_op jit(solution)/shard_map/ppermute | solution.py:321
  30.6 6.7 %collective-permute-done.3 = bf16[288,256]{1,0:T(8,128)(2,1)S(1)} collective-permute-done((bf16[288,256]{1,0:T(8,128)(2,1)S(1)}, bf16[288,256]{1,0:T(8,128)(2,1)S(1)}, u32[]{:S(2)}, u32[]{:S(2)}) %collective-permute-start.3) | collective-permute-done | bytes 147488 | tf_op jit(solution)/shard_map/ppermute | solution.py:321
  41.8 5.2 %collective-permute-done.6 = bf16[304,128]{1,0:T(8,128)(2,1)S(1)} collective-permute-done((bf16[304,128]{1,0:T(8,128)(2,1)S(1)}, bf16[304,128]{1,0:T(8,128)(2,1)S(1)}, u32[]{:S(2)}, u32[]{:S(2)}) %collective-permute-start.6) | collective-permute-done | bytes 77856 | tf_op jit(solution)/shard_map/ppermute | solution.py:45
  52.3 4.5 %collective-permute-done.9 = bf16[304,128]{1,0:T(8,128)(2,1)S(1)} collective-permute-done((bf16[304,128]{1,0:T(8,128)(2,1)S(1)}, bf16[304,128]{1,0:T(8,128)(2,1)S(1)}, u32[]{:S(2)}, u32[]{:S(2)}) %collective-permute-start.9) | collective-permute-done | bytes 77856 | tf_op jit(solution)/shard_map/ppermute | solution.py:45
  61.4 3.4 %collective-permute-start.12 = (bf16[288,256]{1,0:T(8,128)(2,1)S(1)}, bf16[288,256]{1,0:T(8,128)(2,1)S(1)}, u32[]{:S(2)}, u32[]{:S(2)}) collective-permute-start(bf16[288,256]{1,0:T(8,128)(2,1)S(1)} %collective-permute-done.3), channel_id=1, source_target_pairs={{0,0},{1,15},{2,14},{3,13},{4,12},{5,11},{6,10},{7,9},{8,8},{9,7},... | collective-permute-start | bytes 442376 | tf_op jit(solution)/shard_map/ppermute | solution.py:336
  65.7 3.7 %collective-permute-done.12 = bf16[288,256]{1,0:T(8,128)(2,1)S(1)} collective-permute-done((bf16[288,256]{1,0:T(8,128)(2,1)S(1)}, bf16[288,256]{1,0:T(8,128)(2,1)S(1)}, u32[]{:S(2)}, u32[]{:S(2)}) %collective-permute-start.12) | collective-permute-done | bytes 147488 | tf_op jit(solution)/shard_map/ppermute | solution.py:336
  73.4 7.0 %shard_map.112.rest_0_ = bf16[512,256]{1,0:T(8,128)(2,1)} custom-call(s32[18]{0:T(128)} %stack.105.index_ref, f32[64,512]{1,0:T(8,128)} %get-tuple-element.114.cos_ref, f32[64,512]{1,0:T(8,128)} %get-tuple-element.113.sin_ref, bf16[16,304,512]{2,1,0:T(8,128)(2,1)} %bitcast.71, bf16[608,256]{1,0:T(8,128)(2,1)} %copy-done.8, bf16[608,256]{1,0:T(8,128)(2,1)} %copy-done.16, ...), custom_call_target="tpu_custom_call" | custom-call | flops 1207959552 | bytes 8388608 | tf_op jit(solution)/shard_map/pallas_call | solution.py:123
  81.7 9.5 %collective-permute-done.13.rest_0_ = bf16[512,256]{1,0:T(8,128)(2,1)S(1)} collective-permute-done((bf16[512,256]{1,0:T(8,128)(2,1)}, bf16[512,256]{1,0:T(8,128)(2,1)S(1)}, u32[]{:S(2)}, u32[]{:S(2)}) %collective-permute-start.13) | collective-permute-done | bytes 262176 | tf_op jit(solution)/shard_map/ppermute | solution.py:45
  92.1 4.1 %collective-permute-start.14 = (bf16[512,256]{1,0:T(8,128)(2,1)S(1)}, bf16[512,256]{1,0:T(8,128)(2,1)S(1)}, u32[]{:S(2)}, u32[]{:S(2)}) collective-permute-start(bf16[512,256]{1,0:T(8,128)(2,1)S(1)} %collective-permute-done.13.rest_0_), channel_id=1, source_target_pairs={{0,32},{16,48},{32,64},{48,80},{64,96},{80,112},{96,128},{112,144}... | collective-permute-start | bytes 786440 | tf_op jit(solution)/shard_map/ppermute | solution.py:45
  96.3 3.6 %collective-permute-start.15 = (bf16[512,256]{1,0:T(8,128)(2,1)S(1)}, bf16[512,256]{1,0:T(8,128)(2,1)S(1)}, u32[]{:S(2)}, u32[]{:S(2)}) collective-permute-start(bf16[512,256]{1,0:T(8,128)(2,1)S(1)} %broadcast_select_fusion.3), channel_id=1, source_target_pairs={{0,16},{16,0},{32,48},{48,32},{64,80},{80,64},{96,112},{112,96},{1... | collective-permute-start | bytes 786440 | tf_op jit(solution)/shard_map/ppermute | solution.py:45
  99.8 6.5 %collective-permute-done.14.rest_0_ = bf16[512,256]{1,0:T(8,128)(2,1)S(1)} collective-permute-done((bf16[512,256]{1,0:T(8,128)(2,1)S(1)}, bf16[512,256]{1,0:T(8,128)(2,1)S(1)}, u32[]{:S(2)}, u32[]{:S(2)}) %collective-permute-start.14) | collective-permute-done | bytes 262176 | tf_op jit(solution)/shard_map/ppermute | solution.py:45
  106.4 7.4 %all-gather.9.cloned.1.call-done = bf16[4864,256]{1,0:T(8,128)(2,1)} async-done(((bf16[608,256]{1,0:T(8,128)(2,1)}), bf16[4864,256]{1,0:T(8,128)(2,1)}) %all-gather.9.cloned.1.call-update) | async-done | bytes 2490384 | tf_op jit(solution)/shard_map/all_gather | solution.py:335
  113.7 4.1 %collective-permute-start.16 = (bf16[512,256]{1,0:T(8,128)(2,1)S(1)}, bf16[512,256]{1,0:T(8,128)(2,1)S(1)}, u32[]{:S(2)}, u32[]{:S(2)}) collective-permute-start(bf16[512,256]{1,0:T(8,128)(2,1)S(1)} %collective-permute-done.14.rest_0_), channel_id=1, source_target_pairs={{0,32},{16,48},{32,64},{48,80},{64,96},{80,112},{96,128},{112,144}... | collective-permute-start | bytes 786440 | tf_op jit(solution)/shard_map/ppermute | solution.py:45
  122.0 6.6 %shard_map.113.q_ref = bf16[512,256]{1,0:T(8,128)(2,1)} custom-call(s32[18]{0:T(128)} %stack.96.index_ref, f32[64,512]{1,0:T(8,128)} %get-tuple-element.114.cos_ref, f32[64,512]{1,0:T(8,128)} %get-tuple-element.113.sin_ref, bf16[16,304,512]{2,1,0:T(8,128)(2,1)} %bitcast.72, bf16[8,608,256]{2,1,0:T(8,128)(2,1)} %bitcast.73), custom_call_target="tpu_custom_call" | custom-call | flops 1207959552 | bytes 8388608 | tf_op jit(solution)/shard_map/pallas_call | solution.py:123
  132.3 3.8 %collective-permute-start.19 = (bf16[512,256]{1,0:T(8,128)(2,1)S(1)}, bf16[512,256]{1,0:T(8,128)(2,1)S(1)}, u32[]{:S(2)}, u32[]{:S(2)}) collective-permute-start(bf16[512,256]{1,0:T(8,128)(2,1)S(1)} %collective-permute-done.16.rest_0_), channel_id=1, source_target_pairs={{0,32},{16,48},{32,64},{48,80},{64,96},{80,112},{96,128},{112,144}... | collective-permute-start | bytes 786440 | tf_op jit(solution)/shard_map/ppermute | solution.py:45
  156.2 5.6 %collective-permute-done.22 = bf16[1,512,256]{2,1,0:T(8,128)(2,1)S(1)} collective-permute-done((bf16[1,512,256]{2,1,0:T(8,128)(2,1)S(1)}, bf16[1,512,256]{2,1,0:T(8,128)(2,1)S(1)}, u32[]{:S(2)}, u32[]{:S(2)}) %collective-permute-start.22) | collective-permute-done | bytes 262176 | tf_op jit(solution)/shard_map/ppermute | solution.py:49
  164.6 4.6 %collective-permute-start.25 = (bf16[2,512,256]{2,1,0:T(8,128)(2,1)S(1)}, bf16[2,512,256]{2,1,0:T(8,128)(2,1)S(1)}, u32[]{:S(2)}, u32[]{:S(2)}) collective-permute-start(bf16[2,512,256]{2,1,0:T(8,128)(2,1)S(1)} %pad_maximum_fusion.rest_0_), channel_id=1, source_target_pairs={{0,1},{1,0},{2,3},{3,2},{4,5},{5,4},{6,7},{7,6},{8,9},{9,8},{10,11... | collective-permute-start | bytes 1572872 | tf_op jit(solution)/shard_map/ppermute | solution.py:49
  169.2 3.3 %collective-permute-done.23.rest_1_ = bf16[2,512,256]{2,1,0:T(8,128)(2,1)S(1)} collective-permute-done((bf16[2,512,256]{2,1,0:T(8,128)(2,1)S(1)}, bf16[2,512,256]{2,1,0:T(8,128)(2,1)S(1)}, u32[]{:S(2)}, u32[]{:S(2)}) %collective-permute-start.23) | collective-permute-done | bytes 524320 | tf_op jit(solution)/shard_map/ppermute | solution.py:49
  172.6 5.0 %collective-permute-start.28 = (bf16[2,512,256]{2,1,0:T(8,128)(2,1)S(1)}, bf16[2,512,256]{2,1,0:T(8,128)(2,1)S(1)}, u32[]{:S(2)}, u32[]{:S(2)}) collective-permute-start(bf16[2,512,256]{2,1,0:T(8,128)(2,1)S(1)} %collective-permute-done.23.rest_1_), channel_id=1, source_target_pairs={{0,1},{1,0},{2,3},{3,2},{4,5},{5,4},{6,7},{7,6},{8,9},{9,8},{10,11... | collective-permute-start | bytes 1572872 | tf_op jit(solution)/shard_map/ppermute | solution.py:49
  192.8 6.3 %shard_map.119 = (f32[288,512]{1,0:T(8,128)}, f32[16,1,512]{2,1,0:T(1,128)}) custom-call(s32[11]{0:T(128)} %concatenate.31.index_ref, bf16[2,512,256]{2,1,0:T(8,128)(2,1)} %copy-done.7, bf16[2,512,256]{2,1,0:T(8,128)(2,1)} %copy-done.10, bf16[2,512,256]{2,1,0:T(8,128)(2,1)} %copy-done.11, bf16[1,512,256]{2,1,0:T(8,128)(2,1)} %collective-permute-done.26.rest_3_, ...), custom_call_target="tpu_custom_call" | custom-call | flops 1207959552 | bytes 8388608 | tf_op jit(solution)/shard_map/pallas_call | solution.py:271
  199.1 3.7 %all-to-all-start = ((f32[16,1,512]{2,1,0:T(1,128)}), f32[16,1,512]{2,1,0:T(1,128)S(1)}, u32[]{:S(2)}, u32[]{:S(2)}) async-start(f32[16,1,512]{2,1,0:T(1,128)} %get-tuple-element.102), calls=%async_computation | async-start | bytes 65536 | tf_op jit(solution)/shard_map/all_to_all | solution.py:433
  203.5 5.1 %all-to-all-done = f32[16,1,512]{2,1,0:T(1,128)S(1)} async-done(((f32[16,1,512]{2,1,0:T(1,128)}), f32[16,1,512]{2,1,0:T(1,128)S(1)}, u32[]{:S(2)}, u32[]{:S(2)}) %all-to-all-start) | async-done | bytes 32800 | tf_op jit(solution)/shard_map/all_to_all | solution.py:433
  (160 shorter events, 72.7 us)
Async XLA Ops:
  7.2 66.1 %all-gather.7.cloned.1.call-start = ((), (), s32[]{:S(2)}) async-start(), calls=%async_computation.1 | async-start | bytes 5292032 | tf_op jit(solution)/shard_map/all_gather | solution.py:308
  10.1 103.7 %all-gather.9.cloned.1.call-start = ((), (), s32[]{:S(2)}) async-start(), calls=%async_computation.2 | async-start | bytes 2801664 | tf_op jit(solution)/shard_map/all_gather | solution.py:335
  19.2 18.1 %collective-permute-start.1 = (bf16[608,256]{1,0:T(8,128)(2,1)S(1)}, bf16[608,256]{1,0:T(8,128)(2,1)S(1)}, u32[]{:S(2)}, u32[]{:S(2)}) collective-permute-start(bf16[608,256]{1,0:T(8,128)(2,1)S(1)} %pad_maximum_fusion.1.rest_0_), channel_id=1, source_target_pairs={{0,32},{16,48},{32,64},{48,80},{64,96},{80,112},{96,128},{112,144}... | collective-permute-start | bytes 933896 | tf_op jit(solution)/shard_map/ppermute | solution.py:45
  21.9 15.4 %collective-permute-start.2 = (bf16[608,256]{1,0:T(8,128)(2,1)S(1)}, bf16[608,256]{1,0:T(8,128)(2,1)S(1)}, u32[]{:S(2)}, u32[]{:S(2)}) collective-permute-start(bf16[608,256]{1,0:T(8,128)(2,1)S(1)} %pad_maximum_fusion.1.rest_0_), channel_id=1, source_target_pairs={{32,0},{48,16},{64,32},{80,48},{96,64},{112,80},{128,96},{144,112}... | collective-permute-start | bytes 933896 | tf_op jit(solution)/shard_map/ppermute | solution.py:45
  25.9 11.4 %collective-permute-start.3 = (bf16[288,256]{1,0:T(8,128)(2,1)S(1)}, bf16[288,256]{1,0:T(8,128)(2,1)S(1)}, u32[]{:S(2)}, u32[]{:S(2)}) collective-permute-start(bf16[288,256]{1,0:T(8,128)(2,1)S(1)} %bitcast.78), channel_id=1, source_target_pairs={{0,0},{1,17},{2,34},{3,51},{4,68},{5,85},{6,102},{7,119},{8,136},{... | collective-permute-start | bytes 442376 | tf_op jit(solution)/shard_map/ppermute | solution.py:321
  37.3 9.7 %collective-permute-start.4 = (bf16[608,256]{1,0:T(8,128)(2,1)S(1)}, bf16[608,256]{1,0:T(8,128)(2,1)S(1)}, u32[]{:S(2)}, u32[]{:S(2)}) collective-permute-start(bf16[608,256]{1,0:T(8,128)(2,1)S(1)} %collective-permute-done.1.rest_1_), channel_id=1, source_target_pairs={{0,32},{16,48},{32,64},{48,80},{64,96},{80,112},{96,128},{112,144}... | collective-permute-start | bytes 933896 | tf_op jit(solution)/shard_map/ppermute | solution.py:45
  47.1 10.6 %collective-permute-start.7 = (bf16[608,256]{1,0:T(8,128)(2,1)S(1)}, bf16[608,256]{1,0:T(8,128)(2,1)S(1)}, u32[]{:S(2)}, u32[]{:S(2)}) collective-permute-start(bf16[608,256]{1,0:T(8,128)(2,1)S(1)} %collective-permute-done.4.rest_3_), channel_id=1, source_target_pairs={{0,32},{16,48},{32,64},{48,80},{64,96},{80,112},{96,128},{112,144}... | collective-permute-start | bytes 933896 | tf_op jit(solution)/shard_map/ppermute | solution.py:45
  47.2 10.5 %collective-permute-start.8 = (bf16[608,256]{1,0:T(8,128)(2,1)S(1)}, bf16[608,256]{1,0:T(8,128)(2,1)S(1)}, u32[]{:S(2)}, u32[]{:S(2)}) collective-permute-start(bf16[608,256]{1,0:T(8,128)(2,1)S(1)} %collective-permute-done.5.rest_4_), channel_id=1, source_target_pairs={{32,0},{48,16},{64,32},{80,48},{96,64},{112,80},{128,96},{144,112}... | collective-permute-start | bytes 933896 | tf_op jit(solution)/shard_map/ppermute | solution.py:45
  58.5 134.2 %all-gather.11.cloned.1.call-start = ((), (), s32[]{:S(2)}) async-start(), calls=%async_computation.3 | async-start | bytes 2654208 | tf_op jit(solution)/shard_map/all_gather | solution.py:415
  58.6 10.8 %collective-permute-start.10 = (bf16[608,128]{1,0:T(8,128)(2,1)S(1)}, bf16[608,128]{1,0:T(8,128)(2,1)S(1)}, u32[]{:S(2)}, u32[]{:S(2)}) collective-permute-start(bf16[608,128]{1,0:T(8,128)(2,1)S(1)} %slice.152), channel_id=1, source_target_pairs={{0,32},{16,48},{32,64},{48,80},{64,96},{80,112},{96,128},{112,144}... | collective-permute-start | bytes 466952 | tf_op jit(solution)/shard_map/ppermute | solution.py:45
  59.3 10.1 %collective-permute-start.11 = (bf16[608,128]{1,0:T(8,128)(2,1)S(1)}, bf16[608,128]{1,0:T(8,128)(2,1)S(1)}, u32[]{:S(2)}, u32[]{:S(2)}) collective-permute-start(bf16[608,128]{1,0:T(8,128)(2,1)S(1)} %slice.153), channel_id=1, source_target_pairs={{32,0},{48,16},{64,32},{80,48},{96,64},{112,80},{128,96},{144,112}... | collective-permute-start | bytes 466952 | tf_op jit(solution)/shard_map/ppermute | solution.py:45
  80.4 10.8 %collective-permute-start.13 = (bf16[512,256]{1,0:T(8,128)(2,1)}, bf16[512,256]{1,0:T(8,128)(2,1)S(1)}, u32[]{:S(2)}, u32[]{:S(2)}) collective-permute-start(bf16[512,256]{1,0:T(8,128)(2,1)} %shard_map.112.rest_0_), channel_id=1, source_target_pairs={{0,32},{16,48},{32,64},{48,80},{64,96},{80,112},{96,128},{112,144}... | collective-permute-start | bytes 786440 | tf_op jit(solution)/shard_map/ppermute | solution.py:45
  92.1 14.2 %collective-permute-start.14 = (bf16[512,256]{1,0:T(8,128)(2,1)S(1)}, bf16[512,256]{1,0:T(8,128)(2,1)S(1)}, u32[]{:S(2)}, u32[]{:S(2)}) collective-permute-start(bf16[512,256]{1,0:T(8,128)(2,1)S(1)} %collective-permute-done.13.rest_0_), channel_id=1, source_target_pairs={{0,32},{16,48},{32,64},{48,80},{64,96},{80,112},{96,128},{112,144}... | collective-permute-start | bytes 786440 | tf_op jit(solution)/shard_map/ppermute | solution.py:45
  96.3 17.5 %collective-permute-start.15 = (bf16[512,256]{1,0:T(8,128)(2,1)S(1)}, bf16[512,256]{1,0:T(8,128)(2,1)S(1)}, u32[]{:S(2)}, u32[]{:S(2)}) collective-permute-start(bf16[512,256]{1,0:T(8,128)(2,1)S(1)} %broadcast_select_fusion.3), channel_id=1, source_target_pairs={{0,16},{16,0},{32,48},{48,32},{64,80},{80,64},{96,112},{112,96},{1... | collective-permute-start | bytes 786440 | tf_op jit(solution)/shard_map/ppermute | solution.py:45
  113.7 18.6 %collective-permute-start.16 = (bf16[512,256]{1,0:T(8,128)(2,1)S(1)}, bf16[512,256]{1,0:T(8,128)(2,1)S(1)}, u32[]{:S(2)}, u32[]{:S(2)}) collective-permute-start(bf16[512,256]{1,0:T(8,128)(2,1)S(1)} %collective-permute-done.14.rest_0_), channel_id=1, source_target_pairs={{0,32},{16,48},{32,64},{48,80},{64,96},{80,112},{96,128},{112,144}... | collective-permute-start | bytes 786440 | tf_op jit(solution)/shard_map/ppermute | solution.py:45
  118.6 13.7 %collective-permute-start.18 = (bf16[288,256]{1,0:T(8,128)(2,1)S(1)}, bf16[288,256]{1,0:T(8,128)(2,1)S(1)}, u32[]{:S(2)}, u32[]{:S(2)}) collective-permute-start(bf16[288,256]{1,0:T(8,128)(2,1)S(1)} %collective-permute-done.12), channel_id=1, source_target_pairs={{0,16},{16,0},{32,48},{48,32},{64,80},{80,64},{96,112},{112,96},{1... | collective-permute-start | bytes 442376 | tf_op jit(solution)/shard_map/ppermute | solution.py:45
  121.9 10.5 %collective-permute-start.17 = (bf16[512,256]{1,0:T(8,128)(2,1)S(1)}, bf16[512,256]{1,0:T(8,128)(2,1)S(1)}, u32[]{:S(2)}, u32[]{:S(2)}) collective-permute-start(bf16[512,256]{1,0:T(8,128)(2,1)S(1)} %broadcast_select_fusion.2), channel_id=1, source_target_pairs={{0,16},{16,0},{32,48},{48,32},{64,80},{80,64},{96,112},{112,96},{1... | collective-permute-start | bytes 786440 | tf_op jit(solution)/shard_map/ppermute | solution.py:45
  132.3 12.2 %collective-permute-start.19 = (bf16[512,256]{1,0:T(8,128)(2,1)S(1)}, bf16[512,256]{1,0:T(8,128)(2,1)S(1)}, u32[]{:S(2)}, u32[]{:S(2)}) collective-permute-start(bf16[512,256]{1,0:T(8,128)(2,1)S(1)} %collective-permute-done.16.rest_0_), channel_id=1, source_target_pairs={{0,32},{16,48},{32,64},{48,80},{64,96},{80,112},{96,128},{112,144}... | collective-permute-start | bytes 786440 | tf_op jit(solution)/shard_map/ppermute | solution.py:45
  161.8 10.7 %collective-permute-start.23 = (bf16[2,512,256]{2,1,0:T(8,128)(2,1)S(1)}, bf16[2,512,256]{2,1,0:T(8,128)(2,1)S(1)}, u32[]{:S(2)}, u32[]{:S(2)}) collective-permute-start(bf16[2,512,256]{2,1,0:T(8,128)(2,1)S(1)} %pad_maximum_fusion.rest_0_), channel_id=1, source_target_pairs={{0,4},{1,5},{2,6},{3,7},{4,8},{5,9},{6,10},{7,11},{8,12},{9,13},{1... | collective-permute-start | bytes 1572872 | tf_op jit(solution)/shard_map/ppermute | solution.py:49
  161.9 10.6 %collective-permute-start.24 = (bf16[2,512,256]{2,1,0:T(8,128)(2,1)S(1)}, bf16[2,512,256]{2,1,0:T(8,128)(2,1)S(1)}, u32[]{:S(2)}, u32[]{:S(2)}) collective-permute-start(bf16[2,512,256]{2,1,0:T(8,128)(2,1)S(1)} %pad_maximum_fusion.rest_0_), channel_id=1, source_target_pairs={{4,0},{5,1},{6,2},{7,3},{8,4},{9,5},{10,6},{11,7},{12,8},{13,9},{1... | collective-permute-start | bytes 1572872 | tf_op jit(solution)/shard_map/ppermute | solution.py:49
  172.6 17.2 %collective-permute-start.28 = (bf16[2,512,256]{2,1,0:T(8,128)(2,1)S(1)}, bf16[2,512,256]{2,1,0:T(8,128)(2,1)S(1)}, u32[]{:S(2)}, u32[]{:S(2)}) collective-permute-start(bf16[2,512,256]{2,1,0:T(8,128)(2,1)S(1)} %collective-permute-done.23.rest_1_), channel_id=1, source_target_pairs={{0,1},{1,0},{2,3},{3,2},{4,5},{5,4},{6,7},{7,6},{8,9},{9,8},{10,11... | collective-permute-start | bytes 1572872 | tf_op jit(solution)/shard_map/ppermute | solution.py:49
  177.6 12.3 %collective-permute-start.29 = (bf16[2,512,256]{2,1,0:T(8,128)(2,1)S(1)}, bf16[2,512,256]{2,1,0:T(8,128)(2,1)}, u32[]{:S(2)}, u32[]{:S(2)}) collective-permute-start(bf16[2,512,256]{2,1,0:T(8,128)(2,1)S(1)} %collective-permute-done.24.rest_2_), channel_id=1, source_target_pairs={{0,1},{1,0},{2,3},{3,2},{4,5},{5,4},{6,7},{7,6},{8,9},{9,8},{10,11... | collective-permute-start | bytes 1572872 | tf_op jit(solution)/shard_map/ppermute | solution.py:49
  177.7 12.1 %collective-permute-start.26 = (bf16[1,512,256]{2,1,0:T(8,128)(2,1)S(1)}, bf16[1,512,256]{2,1,0:T(8,128)(2,1)}, u32[]{:S(2)}, u32[]{:S(2)}) collective-permute-start(bf16[1,512,256]{2,1,0:T(8,128)(2,1)S(1)} %slice.161), channel_id=1, source_target_pairs={{0,4},{1,5},{2,6},{3,7},{4,8},{5,9},{6,10},{7,11},{8,12},{9,13},{1... | collective-permute-start | bytes 786440 | tf_op jit(solution)/shard_map/ppermute | solution.py:49
  178.1 11.7 %collective-permute-start.27 = (bf16[1,512,256]{2,1,0:T(8,128)(2,1)S(1)}, bf16[1,512,256]{2,1,0:T(8,128)(2,1)}, u32[]{:S(2)}, u32[]{:S(2)}) collective-permute-start(bf16[1,512,256]{2,1,0:T(8,128)(2,1)S(1)} %slice.162), channel_id=1, source_target_pairs={{4,0},{5,1},{6,2},{7,3},{8,4},{9,5},{10,6},{11,7},{12,8},{13,9},{1... | collective-permute-start | bytes 786440 | tf_op jit(solution)/shard_map/ppermute | solution.py:49
  (39 other events, 588.9 us)
Sparse Core Ops, SparseCore 0:
  10.2 47.2 all-gather.6
  59.3 54.3 all-gather.8
  144.7 40.2 all-gather.10

commit v11 on v9

--- a/solution.py
+++ b/solution.py
@@ -61,13 +61,13 @@
     for k, (which, lead, slot, offset) in enumerate(pieces):
         place = index_ref[2 + ROUNDS + slot]
         source = w_refs[which] if lead is None else w_refs[which].at[lead]
-        width = source.shape[1]
+        length, width = source.shape[0] // 2, source.shape[1]
         for part in range(2):
             parity = index_ref[1] if part == 0 else 1 - index_ref[1]
             copies.append(
                 pltpu.make_async_copy(
-                    source.at[pl.ds(part * depth, depth)],
-                    w_ref.at[2 * place + parity, :, pl.ds(offset, width)],
+                    source.at[pl.ds(part * length, length)],
+                    w_ref.at[2 * place + parity, pl.ds(0, length), pl.ds(offset, width)],
                     w_sem.at[2 * k + part],
                 )
             )
@@ -80,6 +80,8 @@
         )
     for copy in copies:
         copy.start()
+    if length < depth:
+        w_ref[:, length:, :] = jnp.zeros((chunks, depth - length, 2 * HD), BF)
     for copy in copies[:-4]:
         copy.wait()
     squares = jnp.zeros((1, rows), F32)
@@ -258,7 +260,8 @@
             else:
                 total = out_ref[...] + total
                 out_ref[...] = total
-                square_ref[...] = jnp.sum(total * total, axis=0, keepdims=True)
+                squares = jnp.sum(total * total, axis=0, keepdims=True)
+                square_ref[...] = jnp.broadcast_to(squares[None], square_ref.shape)
             slot += 1
 
 
@@ -271,7 +274,7 @@
         output_kernel,
         out_shape=(
             jax.ShapeDtypeStruct((features, rows), F32),
-            jax.ShapeDtypeStruct((1, rows), F32),
+            jax.ShapeDtypeStruct((SEQ, 1, rows), F32),
         ),
         in_specs=[pl.BlockSpec(memory_space=pltpu.SMEM)] + [outside] * (len(chunks) + 1),
         out_specs=(vmem, vmem),
@@ -321,8 +324,7 @@
     ring[2] = move(ring[1], AHEAD)
     ring[-2] = move(ring[-1], BEHIND)
     ring[2], ring[-2], turned = tie(ring[2], ring[-2], turned)
-    q_own = jnp.pad(w_query, ((0, EXTRA), (0, 0)))
-    q_own, _ = tie(q_own, ring[1])
+    q_own, _ = tie(w_query, ring[1])
     q_pair = jnp.concatenate([q_own, move(q_own, ACROSS)], axis=0)
     ring[3] = move(ring[2], AHEAD)
     ring[-3] = move(ring[-2], BEHIND)
@@ -425,8 +427,7 @@
         out_all.reshape(2 * ROUNDS, features, 2 * HD),
         jnp.concatenate([index[: 2 + ROUNDS], mp_index[None].astype(jnp.int32)]),
     )
-    everywhere = jnp.broadcast_to(partial, (lax.axis_size("mp"), rows))
-    square_total = jnp.sum(lax.all_to_all(everywhere, "mp", 0, 0, tiled=True), axis=0)
+    square_total = jnp.sum(lax.all_to_all(partial, "mp", 0, 0, tiled=True), axis=(0, 1))
     post_scale = lax.rsqrt(square_total / D + EPSILON)
     post = share * post_scale[None, :] * (1.0 + post_gain.astype(F32))[:, None]
     layer_output = (tokens.T.astype(F32) + post).astype(BF).T

time: 215 us -> 213 us (level)
  starting transfers between devices: 70.2 us -> 72.5 us
  transfers between devices with their start and end apart: 35 -> 35, of which waited for: 13 -> 12; matrix products, arithmetic and copies ran while one was open for 6% -> 6% of each run, Pallas kernels for 13% -> 13%
where the time goes in v11:
time: 213 us; the launch traced here: 211 us
  starting transfers between devices  72.5 us (34%)
  waiting for transfers between devices  61 us (29%)
  Pallas kernels  33 us (15%)
  between operations  22.5 us (11%)
  other arithmetic  11.5 us (5%)
  local copies, waits for them, and re-layouts  10.8 us (5%)
    ppermute x19, starting transfers between devices, move(): return lax.ppermute(block, 'seq', perm)  43.6 us
    ppermute x19, waiting for transfers between devices, move(): return lax.ppermute(block, 'seq', perm)  35.4 us
    ppermute x10, starting transfers between devices, shift(): return lax.ppermute(block, 'mp', perm)  17.4 us
    pallas_call x5, Pallas kernels, attend(): pl.pallas_call(functools.partial(attend_kernel, tuple(distances), first,...  13.4 us
    pallas_call x2, Pallas kernels, project(): pl.pallas_call(functools.partial(project_kernel, pieces, rotated, factor)...  13.3 us
    ppermute x10, waiting for transfers between devices, shift(): return lax.ppermute(block, 'mp', perm)  9.76 us
    ppermute x1, waiting for transfers between devices, shards(): turned = lax.ppermute(w_out.T, ('seq', 'mp'), TURNS[0])  6.49 us
    pallas_call x1, Pallas kernels, output(): pl.pallas_call(output_kernel, out_shape=(jax.ShapeDtypeStruct((features,...  6.36 us
  transfers between devices with their start and end apart: 35, of which 12 were waited for; matrix products, arithmetic and copies ran while one was open for 6% of the time, Pallas kernels for 13%

profile of v11, /device:TPU:1, one launch (start us, length us, event | category | flops | bytes accessed | tf_op | source)
XLA Modules:
  0.0 211.3 jit_solution(7699280388480004115)
XLA Ops:
  12.9 3.7 %collective-permute-start = (bf16[304,256]{1,0:T(8,128)(2,1)S(1)}, bf16[304,256]{1,0:T(8,128)(2,1)S(1)}, u32[]{:S(2)}, u32[]{:S(2)}) collective-permute-start(bf16[304,256]{1,0:T(8,128)(2,1)S(1)} %pad_maximum_fusion.5), channel_id=1, source_target_pairs={{0,16},{16,0},{32,48},{48,32},{64,80},{80,64},{96,112},{112,96},{1... | collective-permute-start | bytes 466952 | tf_op jit(solution)/shard_map/ppermute | solution.py:45
  21.9 4.0 %collective-permute-start.2 = (bf16[608,256]{1,0:T(8,128)(2,1)S(1)}, bf16[608,256]{1,0:T(8,128)(2,1)S(1)}, u32[]{:S(2)}, u32[]{:S(2)}) collective-permute-start(bf16[608,256]{1,0:T(8,128)(2,1)S(1)} %pad_maximum_fusion.1.rest_0_), channel_id=1, source_target_pairs={{32,0},{48,16},{64,32},{80,48},{96,64},{112,80},{128,96},{144,112}... | collective-permute-start | bytes 933896 | tf_op jit(solution)/shard_map/ppermute | solution.py:45
  26.0 6.0 %collective-permute-done.1.rest_1_ = bf16[608,256]{1,0:T(8,128)(2,1)S(1)} collective-permute-done((bf16[608,256]{1,0:T(8,128)(2,1)S(1)}, bf16[608,256]{1,0:T(8,128)(2,1)S(1)}, u32[]{:S(2)}, u32[]{:S(2)}) %collective-permute-start.1) | collective-permute-done | bytes 311328 | tf_op jit(solution)/shard_map/ppermute | solution.py:45
  34.7 4.6 %collective-permute-start.5 = (bf16[288,256]{1,0:T(8,128)(2,1)S(1)}, bf16[288,256]{1,0:T(8,128)(2,1)S(1)}, u32[]{:S(2)}, u32[]{:S(2)}) collective-permute-start(bf16[288,256]{1,0:T(8,128)(2,1)S(1)} %bitcast.78), channel_id=1, source_target_pairs={{0,0},{1,17},{2,34},{3,51},{4,68},{5,85},{6,102},{7,119},{8,136},{... | collective-permute-start | bytes 442376 | tf_op jit(solution)/shard_map/ppermute | solution.py:323
  39.3 6.5 %collective-permute-done.5 = bf16[288,256]{1,0:T(8,128)(2,1)S(1)} collective-permute-done((bf16[288,256]{1,0:T(8,128)(2,1)S(1)}, bf16[288,256]{1,0:T(8,128)(2,1)S(1)}, u32[]{:S(2)}, u32[]{:S(2)}) %collective-permute-start.5) | collective-permute-done | bytes 147488 | tf_op jit(solution)/shard_map/ppermute | solution.py:323
  50.6 7.4 %collective-permute-done.8 = bf16[288,256]{1,0:T(8,128)(2,1)S(1)} collective-permute-done((bf16[288,256]{1,0:T(8,128)(2,1)S(1)}, bf16[288,256]{1,0:T(8,128)(2,1)S(1)}, u32[]{:S(2)}, u32[]{:S(2)}) %collective-permute-start.8) | collective-permute-done | bytes 147488 | tf_op jit(solution)/shard_map/ppermute | solution.py:45
  61.7 3.0 %collective-permute-start.11 = (bf16[288,256]{1,0:T(8,128)(2,1)S(1)}, bf16[288,256]{1,0:T(8,128)(2,1)S(1)}, u32[]{:S(2)}, u32[]{:S(2)}) collective-permute-start(bf16[288,256]{1,0:T(8,128)(2,1)S(1)} %collective-permute-done.5), channel_id=1, source_target_pairs={{0,0},{1,15},{2,14},{3,13},{4,12},{5,11},{6,10},{7,9},{8,8},{9,7},... | collective-permute-start | bytes 442376 | tf_op jit(solution)/shard_map/ppermute | solution.py:333
  65.5 4.1 %collective-permute-done.11 = bf16[288,256]{1,0:T(8,128)(2,1)S(1)} collective-permute-done((bf16[288,256]{1,0:T(8,128)(2,1)S(1)}, bf16[288,256]{1,0:T(8,128)(2,1)S(1)}, u32[]{:S(2)}, u32[]{:S(2)}) %collective-permute-start.11) | collective-permute-done | bytes 147488 | tf_op jit(solution)/shard_map/ppermute | solution.py:333
  73.7 7.0 %shard_map.112.rest_0_ = bf16[512,256]{1,0:T(8,128)(2,1)} custom-call(s32[18]{0:T(128)} %stack.105.index_ref, f32[64,512]{1,0:T(8,128)} %get-tuple-element.104.cos_ref, f32[64,512]{1,0:T(8,128)} %get-tuple-element.103.sin_ref, bf16[16,304,512]{2,1,0:T(8,128)(2,1)} %bitcast.71, bf16[608,256]{1,0:T(8,128)(2,1)} %copy-done.8, bf16[608,256]{1,0:T(8,128)(2,1)} %copy-done.16, ...), custom_call_target="tpu_custom_call" | custom-call | flops 1207959552 | bytes 8388608 | tf_op jit(solution)/shard_map/pallas_call | solution.py:125
  82.0 11.5 %collective-permute-done.12.rest_0_ = bf16[512,256]{1,0:T(8,128)(2,1)S(1)} collective-permute-done((bf16[512,256]{1,0:T(8,128)(2,1)}, bf16[512,256]{1,0:T(8,128)(2,1)S(1)}, u32[]{:S(2)}, u32[]{:S(2)}) %collective-permute-start.12) | collective-permute-done | bytes 262176 | tf_op jit(solution)/shard_map/ppermute | solution.py:45
  94.5 4.1 %collective-permute-start.13 = (bf16[512,256]{1,0:T(8,128)(2,1)S(1)}, bf16[512,256]{1,0:T(8,128)(2,1)S(1)}, u32[]{:S(2)}, u32[]{:S(2)}) collective-permute-start(bf16[512,256]{1,0:T(8,128)(2,1)S(1)} %collective-permute-done.12.rest_0_), channel_id=1, source_target_pairs={{0,32},{16,48},{32,64},{48,80},{64,96},{80,112},{96,128},{112,144}... | collective-permute-start | bytes 786440 | tf_op jit(solution)/shard_map/ppermute | solution.py:45
  100.2 7.8 %collective-permute-done.13.rest_0_ = bf16[512,256]{1,0:T(8,128)(2,1)S(1)} collective-permute-done((bf16[512,256]{1,0:T(8,128)(2,1)S(1)}, bf16[512,256]{1,0:T(8,128)(2,1)S(1)}, u32[]{:S(2)}, u32[]{:S(2)}) %collective-permute-start.13) | collective-permute-done | bytes 262176 | tf_op jit(solution)/shard_map/ppermute | solution.py:45
  108.1 4.1 %collective-permute-start.15 = (bf16[512,256]{1,0:T(8,128)(2,1)S(1)}, bf16[512,256]{1,0:T(8,128)(2,1)S(1)}, u32[]{:S(2)}, u32[]{:S(2)}) collective-permute-start(bf16[512,256]{1,0:T(8,128)(2,1)S(1)} %collective-permute-done.13.rest_0_), channel_id=1, source_target_pairs={{0,32},{16,48},{32,64},{48,80},{64,96},{80,112},{96,128},{112,144}... | collective-permute-start | bytes 786440 | tf_op jit(solution)/shard_map/ppermute | solution.py:45
  113.0 3.3 %collective-permute-start.17 = (bf16[288,256]{1,0:T(8,128)(2,1)S(1)}, bf16[288,256]{1,0:T(8,128)(2,1)S(1)}, u32[]{:S(2)}, u32[]{:S(2)}) collective-permute-start(bf16[288,256]{1,0:T(8,128)(2,1)S(1)} %collective-permute-done.11), channel_id=1, source_target_pairs={{0,16},{16,0},{32,48},{48,32},{64,80},{80,64},{96,112},{112,96},{1... | collective-permute-start | bytes 442376 | tf_op jit(solution)/shard_map/ppermute | solution.py:45
  116.6 6.2 %shard_map.113.q_ref = bf16[512,256]{1,0:T(8,128)(2,1)} custom-call(s32[18]{0:T(128)} %stack.96.index_ref, f32[64,512]{1,0:T(8,128)} %get-tuple-element.104.cos_ref, f32[64,512]{1,0:T(8,128)} %get-tuple-element.103.sin_ref, bf16[16,304,512]{2,1,0:T(8,128)(2,1)} %bitcast.72, bf16[8,576,256]{2,1,0:T(8,128)(2,1)} %bitcast.74), custom_call_target="tpu_custom_call" | custom-call | flops 1207959552 | bytes 8388608 | tf_op jit(solution)/shard_map/pallas_call | solution.py:125
  126.6 4.2 %collective-permute-start.18 = (bf16[512,256]{1,0:T(8,128)(2,1)S(1)}, bf16[512,256]{1,0:T(8,128)(2,1)S(1)}, u32[]{:S(2)}, u32[]{:S(2)}) collective-permute-start(bf16[512,256]{1,0:T(8,128)(2,1)S(1)} %collective-permute-done.15.rest_0_), channel_id=1, source_target_pairs={{0,32},{16,48},{32,64},{48,80},{64,96},{80,112},{96,128},{112,144}... | collective-permute-start | bytes 786440 | tf_op jit(solution)/shard_map/ppermute | solution.py:45
  144.4 2.9 %shard_map.117 = (f32[512,256]{1,0:T(8,128)S(1)}, f32[512,256]{1,0:T(8,128)S(1)}) custom-call(s32[512,1]{1,0:T(8,128)S(1)} %copy.27.low_ref, bf16[512,256]{1,0:T(8,128)(2,1)S(1)} %copy-done.2, bf16[512,256]{1,0:T(8,128)(2,1)S(1)} %collective-permute-done.15.rest_0_, ...), custom_call_target="tpu_custom_call", output_to_operand_aliasing={{0}: (4, {}), {1}: (5, {})} | custom-call | flops 536870912 | bytes 4194304 | tf_op jit(solution)/shard_map/pallas_call | solution.py:201
  147.3 2.9 %shard_map.118 = bf16[512,256]{1,0:T(8,128)(2,1)S(1)} custom-call(s32[512,1]{1,0:T(8,128)S(1)} %copy.27.low_ref, bf16[512,256]{1,0:T(8,128)(2,1)S(1)} %copy-done.2, bf16[512,256]{1,0:T(8,128)(2,1)S(1)} %collective-permute-done.18.rest_0_, bf16[512,256]{1,0:T(8,128)(2,1)S(1)} %collective-permute-done.20.rest_1_, f32[512,256]{1,0:T(8,128)S(1)} %get-tuple-element.83.rest_2_, ...), custom_call_target="tpu_custom_call" | custom-call | flops 536870912 | bytes 4194304 | tf_op jit(solution)/shard_map/pallas_call | solution.py:201
  150.3 5.6 %collective-permute-done.21 = bf16[1,512,256]{2,1,0:T(8,128)(2,1)S(1)} collective-permute-done((bf16[1,512,256]{2,1,0:T(8,128)(2,1)S(1)}, bf16[1,512,256]{2,1,0:T(8,128)(2,1)S(1)}, u32[]{:S(2)}, u32[]{:S(2)}) %collective-permute-start.21) | collective-permute-done | bytes 262176 | tf_op jit(solution)/shard_map/ppermute | solution.py:49
  158.7 5.1 %collective-permute-start.24 = (bf16[2,512,256]{2,1,0:T(8,128)(2,1)S(1)}, bf16[2,512,256]{2,1,0:T(8,128)(2,1)S(1)}, u32[]{:S(2)}, u32[]{:S(2)}) collective-permute-start(bf16[2,512,256]{2,1,0:T(8,128)(2,1)S(1)} %pad_maximum_fusion.rest_0_), channel_id=1, source_target_pairs={{0,1},{1,0},{2,3},{3,2},{4,5},{5,4},{6,7},{7,6},{8,9},{9,8},{10,11... | collective-permute-start | bytes 1572872 | tf_op jit(solution)/shard_map/ppermute | solution.py:49
  166.3 5.4 %collective-permute-start.27 = (bf16[2,512,256]{2,1,0:T(8,128)(2,1)S(1)}, bf16[2,512,256]{2,1,0:T(8,128)(2,1)S(1)}, u32[]{:S(2)}, u32[]{:S(2)}) collective-permute-start(bf16[2,512,256]{2,1,0:T(8,128)(2,1)S(1)} %collective-permute-done.22.rest_1_), channel_id=1, source_target_pairs={{0,1},{1,0},{2,3},{3,2},{4,5},{5,4},{6,7},{7,6},{8,9},{9,8},{10,11... | collective-permute-start | bytes 1572872 | tf_op jit(solution)/shard_map/ppermute | solution.py:49
  186.9 6.4 %shard_map.119 = (f32[288,512]{1,0:T(8,128)}, f32[16,1,512]{2,1,0:T(1,128)}) custom-call(s32[11]{0:T(128)} %concatenate.28.index_ref, bf16[2,512,256]{2,1,0:T(8,128)(2,1)} %copy-done.7, bf16[2,512,256]{2,1,0:T(8,128)(2,1)} %copy-done.10, bf16[2,512,256]{2,1,0:T(8,128)(2,1)} %copy-done.11, bf16[1,512,256]{2,1,0:T(8,128)(2,1)} %collective-permute-done.25.rest_3_, ...), custom_call_target="tpu_custom_call" | custom-call | flops 1207959552 | bytes 8388608 | tf_op jit(solution)/shard_map/pallas_call | solution.py:273
  193.3 3.7 %all-to-all-start = ((f32[16,1,512]{2,1,0:T(1,128)}), f32[16,1,512]{2,1,0:T(1,128)S(1)}, u32[]{:S(2)}, u32[]{:S(2)}) async-start(f32[16,1,512]{2,1,0:T(1,128)} %get-tuple-element.94), calls=%async_computation | async-start | bytes 65536 | tf_op jit(solution)/shard_map/all_to_all | solution.py:430
  197.7 5.1 %all-to-all-done = f32[16,1,512]{2,1,0:T(1,128)S(1)} async-done(((f32[16,1,512]{2,1,0:T(1,128)}), f32[16,1,512]{2,1,0:T(1,128)S(1)}, u32[]{:S(2)}, u32[]{:S(2)}) %all-to-all-start) | async-done | bytes 32800 | tf_op jit(solution)/shard_map/all_to_all | solution.py:430
  (156 shorter events, 64.1 us)
Async XLA Ops:
  7.2 66.4 %all-gather.7.cloned.1.call-start = ((), (), s32[]{:S(2)}) async-start(), calls=%async_computation.1 | async-start | bytes 5292032 | tf_op jit(solution)/shard_map/all_gather | solution.py:310
  10.1 98.0 %all-gather.9.cloned.1.call-start = ((), (), s32[]{:S(2)}) async-start(), calls=%async_computation.2 | async-start | bytes 2654208 | tf_op jit(solution)/shard_map/all_gather | solution.py:332
  19.2 12.7 %collective-permute-start.1 = (bf16[608,256]{1,0:T(8,128)(2,1)S(1)}, bf16[608,256]{1,0:T(8,128)(2,1)S(1)}, u32[]{:S(2)}, u32[]{:S(2)}) collective-permute-start(bf16[608,256]{1,0:T(8,128)(2,1)S(1)} %pad_maximum_fusion.1.rest_0_), channel_id=1, source_target_pairs={{0,32},{16,48},{32,64},{48,80},{64,96},{80,112},{96,128},{112,144}... | collective-permute-start | bytes 933896 | tf_op jit(solution)/shard_map/ppermute | solution.py:45
  21.9 10.1 %collective-permute-start.2 = (bf16[608,256]{1,0:T(8,128)(2,1)S(1)}, bf16[608,256]{1,0:T(8,128)(2,1)S(1)}, u32[]{:S(2)}, u32[]{:S(2)}) collective-permute-start(bf16[608,256]{1,0:T(8,128)(2,1)S(1)} %pad_maximum_fusion.1.rest_0_), channel_id=1, source_target_pairs={{32,0},{48,16},{64,32},{80,48},{96,64},{112,80},{128,96},{144,112}... | collective-permute-start | bytes 933896 | tf_op jit(solution)/shard_map/ppermute | solution.py:45
  32.0 13.8 %collective-permute-start.3 = (bf16[608,256]{1,0:T(8,128)(2,1)S(1)}, bf16[608,256]{1,0:T(8,128)(2,1)S(1)}, u32[]{:S(2)}, u32[]{:S(2)}) collective-permute-start(bf16[608,256]{1,0:T(8,128)(2,1)S(1)} %collective-permute-done.1.rest_1_), channel_id=1, source_target_pairs={{0,32},{16,48},{32,64},{48,80},{64,96},{80,112},{96,128},{112,144}... | collective-permute-start | bytes 933896 | tf_op jit(solution)/shard_map/ppermute | solution.py:45
  32.0 13.8 %collective-permute-start.4 = (bf16[608,256]{1,0:T(8,128)(2,1)S(1)}, bf16[608,256]{1,0:T(8,128)(2,1)S(1)}, u32[]{:S(2)}, u32[]{:S(2)}) collective-permute-start(bf16[608,256]{1,0:T(8,128)(2,1)S(1)} %collective-permute-done.2.rest_2_), channel_id=1, source_target_pairs={{32,0},{48,16},{64,32},{80,48},{96,64},{112,80},{128,96},{144,112}... | collective-permute-start | bytes 933896 | tf_op jit(solution)/shard_map/ppermute | solution.py:45
  34.7 11.1 %collective-permute-start.5 = (bf16[288,256]{1,0:T(8,128)(2,1)S(1)}, bf16[288,256]{1,0:T(8,128)(2,1)S(1)}, u32[]{:S(2)}, u32[]{:S(2)}) collective-permute-start(bf16[288,256]{1,0:T(8,128)(2,1)S(1)} %bitcast.78), channel_id=1, source_target_pairs={{0,0},{1,17},{2,34},{3,51},{4,68},{5,85},{6,102},{7,119},{8,136},{... | collective-permute-start | bytes 442376 | tf_op jit(solution)/shard_map/ppermute | solution.py:323
  45.8 12.9 %collective-permute-start.6 = (bf16[608,256]{1,0:T(8,128)(2,1)S(1)}, bf16[608,256]{1,0:T(8,128)(2,1)S(1)}, u32[]{:S(2)}, u32[]{:S(2)}) collective-permute-start(bf16[608,256]{1,0:T(8,128)(2,1)S(1)} %collective-permute-done.3.rest_3_), channel_id=1, source_target_pairs={{0,32},{16,48},{32,64},{48,80},{64,96},{80,112},{96,128},{112,144}... | collective-permute-start | bytes 933896 | tf_op jit(solution)/shard_map/ppermute | solution.py:45
  45.9 12.8 %collective-permute-start.7 = (bf16[608,256]{1,0:T(8,128)(2,1)S(1)}, bf16[608,256]{1,0:T(8,128)(2,1)S(1)}, u32[]{:S(2)}, u32[]{:S(2)}) collective-permute-start(bf16[608,256]{1,0:T(8,128)(2,1)S(1)} %collective-permute-done.4.rest_4_), channel_id=1, source_target_pairs={{32,0},{48,16},{64,32},{80,48},{96,64},{112,80},{128,96},{144,112}... | collective-permute-start | bytes 933896 | tf_op jit(solution)/shard_map/ppermute | solution.py:45
  58.7 128.1 %all-gather.11.cloned.1.call-start = ((), (), s32[]{:S(2)}) async-start(), calls=%async_computation.3 | async-start | bytes 2654208 | tf_op jit(solution)/shard_map/all_gather | solution.py:412
  58.8 10.8 %collective-permute-start.9 = (bf16[608,128]{1,0:T(8,128)(2,1)S(1)}, bf16[608,128]{1,0:T(8,128)(2,1)S(1)}, u32[]{:S(2)}, u32[]{:S(2)}) collective-permute-start(bf16[608,128]{1,0:T(8,128)(2,1)S(1)} %slice.144), channel_id=1, source_target_pairs={{0,32},{16,48},{32,64},{48,80},{64,96},{80,112},{96,128},{112,144}... | collective-permute-start | bytes 466952 | tf_op jit(solution)/shard_map/ppermute | solution.py:45
  58.9 10.7 %collective-permute-start.10 = (bf16[608,128]{1,0:T(8,128)(2,1)S(1)}, bf16[608,128]{1,0:T(8,128)(2,1)S(1)}, u32[]{:S(2)}, u32[]{:S(2)}) collective-permute-start(bf16[608,128]{1,0:T(8,128)(2,1)S(1)} %slice.145), channel_id=1, source_target_pairs={{32,0},{48,16},{64,32},{80,48},{96,64},{112,80},{128,96},{144,112}... | collective-permute-start | bytes 466952 | tf_op jit(solution)/shard_map/ppermute | solution.py:45
  80.7 12.8 %collective-permute-start.12 = (bf16[512,256]{1,0:T(8,128)(2,1)}, bf16[512,256]{1,0:T(8,128)(2,1)S(1)}, u32[]{:S(2)}, u32[]{:S(2)}) collective-permute-start(bf16[512,256]{1,0:T(8,128)(2,1)} %shard_map.112.rest_0_), channel_id=1, source_target_pairs={{0,32},{16,48},{32,64},{48,80},{64,96},{80,112},{96,128},{112,144}... | collective-permute-start | bytes 786440 | tf_op jit(solution)/shard_map/ppermute | solution.py:45
  94.5 13.6 %collective-permute-start.13 = (bf16[512,256]{1,0:T(8,128)(2,1)S(1)}, bf16[512,256]{1,0:T(8,128)(2,1)S(1)}, u32[]{:S(2)}, u32[]{:S(2)}) collective-permute-start(bf16[512,256]{1,0:T(8,128)(2,1)S(1)} %collective-permute-done.12.rest_0_), channel_id=1, source_target_pairs={{0,32},{16,48},{32,64},{48,80},{64,96},{80,112},{96,128},{112,144}... | collective-permute-start | bytes 786440 | tf_op jit(solution)/shard_map/ppermute | solution.py:45
  108.1 18.4 %collective-permute-start.15 = (bf16[512,256]{1,0:T(8,128)(2,1)S(1)}, bf16[512,256]{1,0:T(8,128)(2,1)S(1)}, u32[]{:S(2)}, u32[]{:S(2)}) collective-permute-start(bf16[512,256]{1,0:T(8,128)(2,1)S(1)} %collective-permute-done.13.rest_0_), channel_id=1, source_target_pairs={{0,32},{16,48},{32,64},{48,80},{64,96},{80,112},{96,128},{112,144}... | collective-permute-start | bytes 786440 | tf_op jit(solution)/shard_map/ppermute | solution.py:45
  113.0 13.5 %collective-permute-start.17 = (bf16[288,256]{1,0:T(8,128)(2,1)S(1)}, bf16[288,256]{1,0:T(8,128)(2,1)S(1)}, u32[]{:S(2)}, u32[]{:S(2)}) collective-permute-start(bf16[288,256]{1,0:T(8,128)(2,1)S(1)} %collective-permute-done.11), channel_id=1, source_target_pairs={{0,16},{16,0},{32,48},{48,32},{64,80},{80,64},{96,112},{112,96},{1... | collective-permute-start | bytes 442376 | tf_op jit(solution)/shard_map/ppermute | solution.py:45
  116.3 10.3 %collective-permute-start.16 = (bf16[512,256]{1,0:T(8,128)(2,1)S(1)}, bf16[512,256]{1,0:T(8,128)(2,1)S(1)}, u32[]{:S(2)}, u32[]{:S(2)}) collective-permute-start(bf16[512,256]{1,0:T(8,128)(2,1)S(1)} %broadcast_select_fusion.2), channel_id=1, source_target_pairs={{0,16},{16,0},{32,48},{48,32},{64,80},{80,64},{96,112},{112,96},{1... | collective-permute-start | bytes 786440 | tf_op jit(solution)/shard_map/ppermute | solution.py:45
  126.6 12.5 %collective-permute-start.18 = (bf16[512,256]{1,0:T(8,128)(2,1)S(1)}, bf16[512,256]{1,0:T(8,128)(2,1)S(1)}, u32[]{:S(2)}, u32[]{:S(2)}) collective-permute-start(bf16[512,256]{1,0:T(8,128)(2,1)S(1)} %collective-permute-done.15.rest_0_), channel_id=1, source_target_pairs={{0,32},{16,48},{32,64},{48,80},{64,96},{80,112},{96,128},{112,144}... | collective-permute-start | bytes 786440 | tf_op jit(solution)/shard_map/ppermute | solution.py:45
  156.0 10.3 %collective-permute-start.22 = (bf16[2,512,256]{2,1,0:T(8,128)(2,1)S(1)}, bf16[2,512,256]{2,1,0:T(8,128)(2,1)S(1)}, u32[]{:S(2)}, u32[]{:S(2)}) collective-permute-start(bf16[2,512,256]{2,1,0:T(8,128)(2,1)S(1)} %pad_maximum_fusion.rest_0_), channel_id=1, source_target_pairs={{0,4},{1,5},{2,6},{3,7},{4,8},{5,9},{6,10},{7,11},{8,12},{9,13},{1... | collective-permute-start | bytes 1572872 | tf_op jit(solution)/shard_map/ppermute | solution.py:49
  156.6 9.7 %collective-permute-start.23 = (bf16[2,512,256]{2,1,0:T(8,128)(2,1)S(1)}, bf16[2,512,256]{2,1,0:T(8,128)(2,1)S(1)}, u32[]{:S(2)}, u32[]{:S(2)}) collective-permute-start(bf16[2,512,256]{2,1,0:T(8,128)(2,1)S(1)} %pad_maximum_fusion.rest_0_), channel_id=1, source_target_pairs={{4,0},{5,1},{6,2},{7,3},{8,4},{9,5},{10,6},{11,7},{12,8},{13,9},{1... | collective-permute-start | bytes 1572872 | tf_op jit(solution)/shard_map/ppermute | solution.py:49
  166.3 17.7 %collective-permute-start.27 = (bf16[2,512,256]{2,1,0:T(8,128)(2,1)S(1)}, bf16[2,512,256]{2,1,0:T(8,128)(2,1)S(1)}, u32[]{:S(2)}, u32[]{:S(2)}) collective-permute-start(bf16[2,512,256]{2,1,0:T(8,128)(2,1)S(1)} %collective-permute-done.22.rest_1_), channel_id=1, source_target_pairs={{0,1},{1,0},{2,3},{3,2},{4,5},{5,4},{6,7},{7,6},{8,9},{9,8},{10,11... | collective-permute-start | bytes 1572872 | tf_op jit(solution)/shard_map/ppermute | solution.py:49
  171.7 12.3 %collective-permute-start.28 = (bf16[2,512,256]{2,1,0:T(8,128)(2,1)S(1)}, bf16[2,512,256]{2,1,0:T(8,128)(2,1)}, u32[]{:S(2)}, u32[]{:S(2)}) collective-permute-start(bf16[2,512,256]{2,1,0:T(8,128)(2,1)S(1)} %collective-permute-done.23.rest_2_), channel_id=1, source_target_pairs={{0,1},{1,0},{2,3},{3,2},{4,5},{5,4},{6,7},{7,6},{8,9},{9,8},{10,11... | collective-permute-start | bytes 1572872 | tf_op jit(solution)/shard_map/ppermute | solution.py:49
  171.9 12.1 %collective-permute-start.25 = (bf16[1,512,256]{2,1,0:T(8,128)(2,1)S(1)}, bf16[1,512,256]{2,1,0:T(8,128)(2,1)}, u32[]{:S(2)}, u32[]{:S(2)}) collective-permute-start(bf16[1,512,256]{2,1,0:T(8,128)(2,1)S(1)} %slice.153), channel_id=1, source_target_pairs={{0,4},{1,5},{2,6},{3,7},{4,8},{5,9},{6,10},{7,11},{8,12},{9,13},{1... | collective-permute-start | bytes 786440 | tf_op jit(solution)/shard_map/ppermute | solution.py:49
  172.0 12.0 %collective-permute-start.26 = (bf16[1,512,256]{2,1,0:T(8,128)(2,1)S(1)}, bf16[1,512,256]{2,1,0:T(8,128)(2,1)}, u32[]{:S(2)}, u32[]{:S(2)}) collective-permute-start(bf16[1,512,256]{2,1,0:T(8,128)(2,1)S(1)} %slice.154), channel_id=1, source_target_pairs={{4,0},{5,1},{6,2},{7,3},{8,4},{9,5},{10,6},{11,7},{12,8},{13,9},{1... | collective-permute-start | bytes 786440 | tf_op jit(solution)/shard_map/ppermute | solution.py:49
  (38 other events, 617.7 us)
Sparse Core Ops, SparseCore 0:
  10.2 46.5 all-gather.6
  59.1 45.5 all-gather.8
  139.3 39.5 all-gather.10

commit v12 on v11

--- a/solution.py
+++ b/solution.py
@@ -364,13 +364,20 @@
     offsets = jnp.zeros((rows,), jnp.int32)
     for s in range(1, SEGS):
         offsets = jnp.where(segment_ids == s, starts[s - 1], offsets)
-    within = (global_index - offsets).astype(F32)
     low = (jnp.maximum(offsets, global_index - (WINDOW - 1)) - base)[:, None]
     half = HD // 2
     freqs = jnp.exp(-math.log(10000.0) * jnp.arange(half, dtype=F32) * (2.0 / HD))
-    angles = freqs[:, None] * within[None, :]
-    cos = jnp.cos(angles)
-    sin = jnp.sin(angles)
+    angles = freqs[:, None] * global_index.astype(F32)[None, :]
+    cos_index, sin_index = tie(jnp.cos(angles), jnp.sin(angles), ring[2])[:2]
+    turns = freqs[:, None] * starts.astype(F32)[None, :]
+    cos_starts, sin_starts = jnp.cos(turns), jnp.sin(turns)
+    cos_start, sin_start = jnp.ones_like(angles), jnp.zeros_like(angles)
+    for s in range(1, SEGS):
+        here = (segment_ids == s)[None, :]
+        cos_start = jnp.where(here, cos_starts[:, s - 1 : s], cos_start)
+        sin_start = jnp.where(here, sin_starts[:, s - 1 : s], sin_start)
+    cos = cos_index * cos_start + sin_index * sin_start
+    sin = sin_index * cos_start - cos_index * sin_start
 
     kv = project(x_all, kv_weights, kv_pieces, index, cos, sin, (True, False), 1.0)
 

time: 213 us -> 213 us (level)
    sub x0 -> x2, other arithmetic: none -> 2.77 us  [the longest x1 1.94 us: shards(): low = (jnp.maximum(offsets, global_index - (WINDOW - 1)) - base)[:, None]]
where the time goes in v12:
time: 213 us; the launch traced here: 210 us
  starting transfers between devices  72.2 us (34%)
  waiting for transfers between devices  60.8 us (29%)
  Pallas kernels  33 us (15%)
  between operations  22.2 us (10%)
  other arithmetic  11.8 us (6%)
  local copies, waits for them, and re-layouts  10.6 us (5%)
    ppermute x19, starting transfers between devices, move(): return lax.ppermute(block, 'seq', perm)  43 us
    ppermute x19, waiting for transfers between devices, move(): return lax.ppermute(block, 'seq', perm)  35.4 us
    ppermute x10, starting transfers between devices, shift(): return lax.ppermute(block, 'mp', perm)  17.7 us
    pallas_call x5, Pallas kernels, attend(): pl.pallas_call(functools.partial(attend_kernel, tuple(distances), first,...  13.4 us
    pallas_call x2, Pallas kernels, project(): pl.pallas_call(functools.partial(project_kernel, pieces, rotated, factor)...  13.2 us
    ppermute x10, waiting for transfers between devices, shift(): return lax.ppermute(block, 'mp', perm)  9.44 us
    ppermute x1, waiting for transfers between devices, shards(): turned = lax.ppermute(w_out.T, ('seq', 'mp'), TURNS[0])  6.49 us
    pallas_call x1, Pallas kernels, output(): pl.pallas_call(output_kernel, out_shape=(jax.ShapeDtypeStruct((features,...  6.34 us
  transfers between devices with their start and end apart: 35, of which 12 were waited for; matrix products, arithmetic and copies ran while one was open for 6% of the time, Pallas kernels for 13%

profile of v12, /device:TPU:1, one launch (start us, length us, event | category | flops | bytes accessed | tf_op | source)
XLA Modules:
  0.0 210.5 jit_solution(3652072224815777443)
XLA Ops:
  12.8 3.7 %collective-permute-start = (bf16[304,256]{1,0:T(8,128)(2,1)S(1)}, bf16[304,256]{1,0:T(8,128)(2,1)S(1)}, u32[]{:S(2)}, u32[]{:S(2)}) collective-permute-start(bf16[304,256]{1,0:T(8,128)(2,1)S(1)} %pad_maximum_fusion.5), channel_id=1, source_target_pairs={{0,16},{16,0},{32,48},{48,32},{64,80},{80,64},{96,112},{112,96},{1... | collective-permute-start | bytes 466952 | tf_op jit(solution)/shard_map/ppermute | solution.py:45
  21.9 4.0 %collective-permute-start.2 = (bf16[608,256]{1,0:T(8,128)(2,1)S(1)}, bf16[608,256]{1,0:T(8,128)(2,1)S(1)}, u32[]{:S(2)}, u32[]{:S(2)}) collective-permute-start(bf16[608,256]{1,0:T(8,128)(2,1)S(1)} %pad_maximum_fusion.1.rest_0_), channel_id=1, source_target_pairs={{32,0},{48,16},{64,32},{80,48},{96,64},{112,80},{128,96},{144,112}... | collective-permute-start | bytes 933896 | tf_op jit(solution)/shard_map/ppermute | solution.py:45
  25.9 6.0 %collective-permute-done.1.rest_1_ = bf16[608,256]{1,0:T(8,128)(2,1)S(1)} collective-permute-done((bf16[608,256]{1,0:T(8,128)(2,1)S(1)}, bf16[608,256]{1,0:T(8,128)(2,1)S(1)}, u32[]{:S(2)}, u32[]{:S(2)}) %collective-permute-start.1) | collective-permute-done | bytes 311328 | tf_op jit(solution)/shard_map/ppermute | solution.py:45
  34.6 4.6 %collective-permute-start.5 = (bf16[288,256]{1,0:T(8,128)(2,1)S(1)}, bf16[288,256]{1,0:T(8,128)(2,1)S(1)}, u32[]{:S(2)}, u32[]{:S(2)}) collective-permute-start(bf16[288,256]{1,0:T(8,128)(2,1)S(1)} %bitcast.90), channel_id=1, source_target_pairs={{0,0},{1,17},{2,34},{3,51},{4,68},{5,85},{6,102},{7,119},{8,136},{... | collective-permute-start | bytes 442376 | tf_op jit(solution)/shard_map/ppermute | solution.py:323
  39.3 6.5 %collective-permute-done.5 = bf16[288,256]{1,0:T(8,128)(2,1)S(1)} collective-permute-done((bf16[288,256]{1,0:T(8,128)(2,1)S(1)}, bf16[288,256]{1,0:T(8,128)(2,1)S(1)}, u32[]{:S(2)}, u32[]{:S(2)}) %collective-permute-start.5) | collective-permute-done | bytes 147488 | tf_op jit(solution)/shard_map/ppermute | solution.py:323
  50.6 7.4 %collective-permute-done.8 = bf16[288,256]{1,0:T(8,128)(2,1)S(1)} collective-permute-done((bf16[288,256]{1,0:T(8,128)(2,1)S(1)}, bf16[288,256]{1,0:T(8,128)(2,1)S(1)}, u32[]{:S(2)}, u32[]{:S(2)}) %collective-permute-start.8) | collective-permute-done | bytes 147488 | tf_op jit(solution)/shard_map/ppermute | solution.py:45
  61.6 3.0 %collective-permute-start.11 = (bf16[288,256]{1,0:T(8,128)(2,1)S(1)}, bf16[288,256]{1,0:T(8,128)(2,1)S(1)}, u32[]{:S(2)}, u32[]{:S(2)}) collective-permute-start(bf16[288,256]{1,0:T(8,128)(2,1)S(1)} %collective-permute-done.5), channel_id=1, source_target_pairs={{0,0},{1,15},{2,14},{3,13},{4,12},{5,11},{6,10},{7,9},{8,8},{9,7},... | collective-permute-start | bytes 442376 | tf_op jit(solution)/shard_map/ppermute | solution.py:333
  65.4 4.2 %collective-permute-done.11 = bf16[288,256]{1,0:T(8,128)(2,1)S(1)} collective-permute-done((bf16[288,256]{1,0:T(8,128)(2,1)S(1)}, bf16[288,256]{1,0:T(8,128)(2,1)S(1)}, u32[]{:S(2)}, u32[]{:S(2)}) %collective-permute-start.11) | collective-permute-done | bytes 147488 | tf_op jit(solution)/shard_map/ppermute | solution.py:333
  73.9 7.0 %shard_map.112.rest_0_ = bf16[512,256]{1,0:T(8,128)(2,1)} custom-call(s32[18]{0:T(128)} %stack.105.index_ref, f32[64,512]{1,0:T(8,128)} %get-tuple-element.108.cos_ref, f32[64,512]{1,0:T(8,128)} %get-tuple-element.107.sin_ref, bf16[16,304,512]{2,1,0:T(8,128)(2,1)} %bitcast.83, bf16[608,256]{1,0:T(8,128)(2,1)} %copy-done.8, bf16[608,256]{1,0:T(8,128)(2,1)} %copy-done.16, ...), custom_call_target="tpu_custom_call" | custom-call | flops 1207959552 | bytes 8388608 | tf_op jit(solution)/shard_map/pallas_call | solution.py:125
  82.2 11.4 %collective-permute-done.12.rest_0_ = bf16[512,256]{1,0:T(8,128)(2,1)S(1)} collective-permute-done((bf16[512,256]{1,0:T(8,128)(2,1)}, bf16[512,256]{1,0:T(8,128)(2,1)S(1)}, u32[]{:S(2)}, u32[]{:S(2)}) %collective-permute-start.12) | collective-permute-done | bytes 262176 | tf_op jit(solution)/shard_map/ppermute | solution.py:45
  94.6 4.1 %collective-permute-start.13 = (bf16[512,256]{1,0:T(8,128)(2,1)S(1)}, bf16[512,256]{1,0:T(8,128)(2,1)S(1)}, u32[]{:S(2)}, u32[]{:S(2)}) collective-permute-start(bf16[512,256]{1,0:T(8,128)(2,1)S(1)} %collective-permute-done.12.rest_0_), channel_id=1, source_target_pairs={{0,32},{16,48},{32,64},{48,80},{64,96},{80,112},{96,128},{112,144}... | collective-permute-start | bytes 786440 | tf_op jit(solution)/shard_map/ppermute | solution.py:45
  100.2 7.9 %collective-permute-done.13.rest_0_ = bf16[512,256]{1,0:T(8,128)(2,1)S(1)} collective-permute-done((bf16[512,256]{1,0:T(8,128)(2,1)S(1)}, bf16[512,256]{1,0:T(8,128)(2,1)S(1)}, u32[]{:S(2)}, u32[]{:S(2)}) %collective-permute-start.13) | collective-permute-done | bytes 262176 | tf_op jit(solution)/shard_map/ppermute | solution.py:45
  108.2 4.1 %collective-permute-start.15 = (bf16[512,256]{1,0:T(8,128)(2,1)S(1)}, bf16[512,256]{1,0:T(8,128)(2,1)S(1)}, u32[]{:S(2)}, u32[]{:S(2)}) collective-permute-start(bf16[512,256]{1,0:T(8,128)(2,1)S(1)} %collective-permute-done.13.rest_0_), channel_id=1, source_target_pairs={{0,32},{16,48},{32,64},{48,80},{64,96},{80,112},{96,128},{112,144}... | collective-permute-start | bytes 786440 | tf_op jit(solution)/shard_map/ppermute | solution.py:45
  113.1 2.9 %collective-permute-start.17 = (bf16[288,256]{1,0:T(8,128)(2,1)S(1)}, bf16[288,256]{1,0:T(8,128)(2,1)S(1)}, u32[]{:S(2)}, u32[]{:S(2)}) collective-permute-start(bf16[288,256]{1,0:T(8,128)(2,1)S(1)} %collective-permute-done.11), channel_id=1, source_target_pairs={{0,16},{16,0},{32,48},{48,32},{64,80},{80,64},{96,112},{112,96},{1... | collective-permute-start | bytes 442376 | tf_op jit(solution)/shard_map/ppermute | solution.py:45
  116.2 6.2 %shard_map.113.q_ref = bf16[512,256]{1,0:T(8,128)(2,1)} custom-call(s32[18]{0:T(128)} %stack.96.index_ref, f32[64,512]{1,0:T(8,128)} %get-tuple-element.108.cos_ref, f32[64,512]{1,0:T(8,128)} %get-tuple-element.107.sin_ref, bf16[16,304,512]{2,1,0:T(8,128)(2,1)} %bitcast.84, bf16[8,576,256]{2,1,0:T(8,128)(2,1)} %bitcast.86), custom_call_target="tpu_custom_call" | custom-call | flops 1207959552 | bytes 8388608 | tf_op jit(solution)/shard_map/pallas_call | solution.py:125
  126.3 4.2 %collective-permute-start.18 = (bf16[512,256]{1,0:T(8,128)(2,1)S(1)}, bf16[512,256]{1,0:T(8,128)(2,1)S(1)}, u32[]{:S(2)}, u32[]{:S(2)}) collective-permute-start(bf16[512,256]{1,0:T(8,128)(2,1)S(1)} %collective-permute-done.15.rest_0_), channel_id=1, source_target_pairs={{0,32},{16,48},{32,64},{48,80},{64,96},{80,112},{96,128},{112,144}... | collective-permute-start | bytes 786440 | tf_op jit(solution)/shard_map/ppermute | solution.py:45
  144.0 2.9 %shard_map.117 = (f32[512,256]{1,0:T(8,128)S(1)}, f32[512,256]{1,0:T(8,128)S(1)}) custom-call(s32[512,1]{1,0:T(8,128)S(1)} %copy.27.low_ref, bf16[512,256]{1,0:T(8,128)(2,1)S(1)} %copy-done.2, bf16[512,256]{1,0:T(8,128)(2,1)S(1)} %collective-permute-done.15.rest_0_, ...), custom_call_target="tpu_custom_call", output_to_operand_aliasing={{0}: (4, {}), {1}: (5, {})} | custom-call | flops 536870912 | bytes 4194304 | tf_op jit(solution)/shard_map/pallas_call | solution.py:201
  146.9 2.9 %shard_map.118 = bf16[512,256]{1,0:T(8,128)(2,1)S(1)} custom-call(s32[512,1]{1,0:T(8,128)S(1)} %copy.27.low_ref, bf16[512,256]{1,0:T(8,128)(2,1)S(1)} %copy-done.2, bf16[512,256]{1,0:T(8,128)(2,1)S(1)} %collective-permute-done.18.rest_0_, bf16[512,256]{1,0:T(8,128)(2,1)S(1)} %collective-permute-done.20.rest_1_, f32[512,256]{1,0:T(8,128)S(1)} %get-tuple-element.87.rest_2_, ...), custom_call_target="tpu_custom_call" | custom-call | flops 536870912 | bytes 4194304 | tf_op jit(solution)/shard_map/pallas_call | solution.py:201
  149.9 5.6 %collective-permute-done.21 = bf16[1,512,256]{2,1,0:T(8,128)(2,1)S(1)} collective-permute-done((bf16[1,512,256]{2,1,0:T(8,128)(2,1)S(1)}, bf16[1,512,256]{2,1,0:T(8,128)(2,1)S(1)}, u32[]{:S(2)}, u32[]{:S(2)}) %collective-permute-start.21) | collective-permute-done | bytes 262176 | tf_op jit(solution)/shard_map/ppermute | solution.py:49
  158.3 5.3 %collective-permute-start.24 = (bf16[2,512,256]{2,1,0:T(8,128)(2,1)S(1)}, bf16[2,512,256]{2,1,0:T(8,128)(2,1)S(1)}, u32[]{:S(2)}, u32[]{:S(2)}) collective-permute-start(bf16[2,512,256]{2,1,0:T(8,128)(2,1)S(1)} %pad_maximum_fusion.rest_0_), channel_id=1, source_target_pairs={{0,1},{1,0},{2,3},{3,2},{4,5},{5,4},{6,7},{7,6},{8,9},{9,8},{10,11... | collective-permute-start | bytes 1572872 | tf_op jit(solution)/shard_map/ppermute | solution.py:49
  165.7 5.6 %collective-permute-start.27 = (bf16[2,512,256]{2,1,0:T(8,128)(2,1)S(1)}, bf16[2,512,256]{2,1,0:T(8,128)(2,1)S(1)}, u32[]{:S(2)}, u32[]{:S(2)}) collective-permute-start(bf16[2,512,256]{2,1,0:T(8,128)(2,1)S(1)} %collective-permute-done.22.rest_1_), channel_id=1, source_target_pairs={{0,1},{1,0},{2,3},{3,2},{4,5},{5,4},{6,7},{7,6},{8,9},{9,8},{10,11... | collective-permute-start | bytes 1572872 | tf_op jit(solution)/shard_map/ppermute | solution.py:49
  186.1 6.3 %shard_map.119 = (f32[288,512]{1,0:T(8,128)}, f32[16,1,512]{2,1,0:T(1,128)}) custom-call(s32[11]{0:T(128)} %concatenate.28.index_ref, bf16[2,512,256]{2,1,0:T(8,128)(2,1)} %copy-done.7, bf16[2,512,256]{2,1,0:T(8,128)(2,1)} %copy-done.10, bf16[2,512,256]{2,1,0:T(8,128)(2,1)} %copy-done.11, bf16[1,512,256]{2,1,0:T(8,128)(2,1)} %collective-permute-done.25.rest_3_, ...), custom_call_target="tpu_custom_call" | custom-call | flops 1207959552 | bytes 8388608 | tf_op jit(solution)/shard_map/pallas_call | solution.py:273
  192.5 3.7 %all-to-all-start = ((f32[16,1,512]{2,1,0:T(1,128)}), f32[16,1,512]{2,1,0:T(1,128)S(1)}, u32[]{:S(2)}, u32[]{:S(2)}) async-start(f32[16,1,512]{2,1,0:T(1,128)} %get-tuple-element.98), calls=%async_computation | async-start | bytes 65536 | tf_op jit(solution)/shard_map/all_to_all | solution.py:437
  196.9 5.1 %all-to-all-done = f32[16,1,512]{2,1,0:T(1,128)S(1)} async-done(((f32[16,1,512]{2,1,0:T(1,128)}), f32[16,1,512]{2,1,0:T(1,128)S(1)}, u32[]{:S(2)}, u32[]{:S(2)}) %all-to-all-start) | async-done | bytes 32800 | tf_op jit(solution)/shard_map/all_to_all | solution.py:437
  (159 shorter events, 63.7 us)
Async XLA Ops:
  7.2 66.6 %all-gather.7.cloned.1.call-start = ((), (), s32[]{:S(2)}) async-start(), calls=%async_computation.1 | async-start | bytes 5292032 | tf_op jit(solution)/shard_map/all_gather | solution.py:310
  10.1 98.1 %all-gather.9.cloned.1.call-start = ((), (), s32[]{:S(2)}) async-start(), calls=%async_computation.2 | async-start | bytes 2654208 | tf_op jit(solution)/shard_map/all_gather | solution.py:332
  19.2 12.7 %collective-permute-start.1 = (bf16[608,256]{1,0:T(8,128)(2,1)S(1)}, bf16[608,256]{1,0:T(8,128)(2,1)S(1)}, u32[]{:S(2)}, u32[]{:S(2)}) collective-permute-start(bf16[608,256]{1,0:T(8,128)(2,1)S(1)} %pad_maximum_fusion.1.rest_0_), channel_id=1, source_target_pairs={{0,32},{16,48},{32,64},{48,80},{64,96},{80,112},{96,128},{112,144}... | collective-permute-start | bytes 933896 | tf_op jit(solution)/shard_map/ppermute | solution.py:45
  21.9 10.1 %collective-permute-start.2 = (bf16[608,256]{1,0:T(8,128)(2,1)S(1)}, bf16[608,256]{1,0:T(8,128)(2,1)S(1)}, u32[]{:S(2)}, u32[]{:S(2)}) collective-permute-start(bf16[608,256]{1,0:T(8,128)(2,1)S(1)} %pad_maximum_fusion.1.rest_0_), channel_id=1, source_target_pairs={{32,0},{48,16},{64,32},{80,48},{96,64},{112,80},{128,96},{144,112}... | collective-permute-start | bytes 933896 | tf_op jit(solution)/shard_map/ppermute | solution.py:45
  32.0 13.8 %collective-permute-start.3 = (bf16[608,256]{1,0:T(8,128)(2,1)S(1)}, bf16[608,256]{1,0:T(8,128)(2,1)S(1)}, u32[]{:S(2)}, u32[]{:S(2)}) collective-permute-start(bf16[608,256]{1,0:T(8,128)(2,1)S(1)} %collective-permute-done.1.rest_1_), channel_id=1, source_target_pairs={{0,32},{16,48},{32,64},{48,80},{64,96},{80,112},{96,128},{112,144}... | collective-permute-start | bytes 933896 | tf_op jit(solution)/shard_map/ppermute | solution.py:45
  32.0 13.8 %collective-permute-start.4 = (bf16[608,256]{1,0:T(8,128)(2,1)S(1)}, bf16[608,256]{1,0:T(8,128)(2,1)S(1)}, u32[]{:S(2)}, u32[]{:S(2)}) collective-permute-start(bf16[608,256]{1,0:T(8,128)(2,1)S(1)} %collective-permute-done.2.rest_2_), channel_id=1, source_target_pairs={{32,0},{48,16},{64,32},{80,48},{96,64},{112,80},{128,96},{144,112}... | collective-permute-start | bytes 933896 | tf_op jit(solution)/shard_map/ppermute | solution.py:45
  34.6 11.1 %collective-permute-start.5 = (bf16[288,256]{1,0:T(8,128)(2,1)S(1)}, bf16[288,256]{1,0:T(8,128)(2,1)S(1)}, u32[]{:S(2)}, u32[]{:S(2)}) collective-permute-start(bf16[288,256]{1,0:T(8,128)(2,1)S(1)} %bitcast.90), channel_id=1, source_target_pairs={{0,0},{1,17},{2,34},{3,51},{4,68},{5,85},{6,102},{7,119},{8,136},{... | collective-permute-start | bytes 442376 | tf_op jit(solution)/shard_map/ppermute | solution.py:323
  45.8 12.9 %collective-permute-start.6 = (bf16[608,256]{1,0:T(8,128)(2,1)S(1)}, bf16[608,256]{1,0:T(8,128)(2,1)S(1)}, u32[]{:S(2)}, u32[]{:S(2)}) collective-permute-start(bf16[608,256]{1,0:T(8,128)(2,1)S(1)} %collective-permute-done.3.rest_3_), channel_id=1, source_target_pairs={{0,32},{16,48},{32,64},{48,80},{64,96},{80,112},{96,128},{112,144}... | collective-permute-start | bytes 933896 | tf_op jit(solution)/shard_map/ppermute | solution.py:45
  45.9 12.8 %collective-permute-start.7 = (bf16[608,256]{1,0:T(8,128)(2,1)S(1)}, bf16[608,256]{1,0:T(8,128)(2,1)S(1)}, u32[]{:S(2)}, u32[]{:S(2)}) collective-permute-start(bf16[608,256]{1,0:T(8,128)(2,1)S(1)} %collective-permute-done.4.rest_4_), channel_id=1, source_target_pairs={{32,0},{48,16},{64,32},{80,48},{96,64},{112,80},{128,96},{144,112}... | collective-permute-start | bytes 933896 | tf_op jit(solution)/shard_map/ppermute | solution.py:45
  58.7 127.4 %all-gather.11.cloned.1.call-start = ((), (), s32[]{:S(2)}) async-start(), calls=%async_computation.3 | async-start | bytes 2654208 | tf_op jit(solution)/shard_map/all_gather | solution.py:419
  58.8 10.8 %collective-permute-start.9 = (bf16[608,128]{1,0:T(8,128)(2,1)S(1)}, bf16[608,128]{1,0:T(8,128)(2,1)S(1)}, u32[]{:S(2)}, u32[]{:S(2)}) collective-permute-start(bf16[608,128]{1,0:T(8,128)(2,1)S(1)} %slice.162), channel_id=1, source_target_pairs={{0,32},{16,48},{32,64},{48,80},{64,96},{80,112},{96,128},{112,144}... | collective-permute-start | bytes 466952 | tf_op jit(solution)/shard_map/ppermute | solution.py:45
  58.9 10.7 %collective-permute-start.10 = (bf16[608,128]{1,0:T(8,128)(2,1)S(1)}, bf16[608,128]{1,0:T(8,128)(2,1)S(1)}, u32[]{:S(2)}, u32[]{:S(2)}) collective-permute-start(bf16[608,128]{1,0:T(8,128)(2,1)S(1)} %slice.163), channel_id=1, source_target_pairs={{32,0},{48,16},{64,32},{80,48},{96,64},{112,80},{128,96},{144,112}... | collective-permute-start | bytes 466952 | tf_op jit(solution)/shard_map/ppermute | solution.py:45
  80.9 12.7 %collective-permute-start.12 = (bf16[512,256]{1,0:T(8,128)(2,1)}, bf16[512,256]{1,0:T(8,128)(2,1)S(1)}, u32[]{:S(2)}, u32[]{:S(2)}) collective-permute-start(bf16[512,256]{1,0:T(8,128)(2,1)} %shard_map.112.rest_0_), channel_id=1, source_target_pairs={{0,32},{16,48},{32,64},{48,80},{64,96},{80,112},{96,128},{112,144}... | collective-permute-start | bytes 786440 | tf_op jit(solution)/shard_map/ppermute | solution.py:45
  94.6 13.5 %collective-permute-start.13 = (bf16[512,256]{1,0:T(8,128)(2,1)S(1)}, bf16[512,256]{1,0:T(8,128)(2,1)S(1)}, u32[]{:S(2)}, u32[]{:S(2)}) collective-permute-start(bf16[512,256]{1,0:T(8,128)(2,1)S(1)} %collective-permute-done.12.rest_0_), channel_id=1, source_target_pairs={{0,32},{16,48},{32,64},{48,80},{64,96},{80,112},{96,128},{112,144}... | collective-permute-start | bytes 786440 | tf_op jit(solution)/shard_map/ppermute | solution.py:45
  108.2 18.0 %collective-permute-start.15 = (bf16[512,256]{1,0:T(8,128)(2,1)S(1)}, bf16[512,256]{1,0:T(8,128)(2,1)S(1)}, u32[]{:S(2)}, u32[]{:S(2)}) collective-permute-start(bf16[512,256]{1,0:T(8,128)(2,1)S(1)} %collective-permute-done.13.rest_0_), channel_id=1, source_target_pairs={{0,32},{16,48},{32,64},{48,80},{64,96},{80,112},{96,128},{112,144}... | collective-permute-start | bytes 786440 | tf_op jit(solution)/shard_map/ppermute | solution.py:45
  113.1 13.2 %collective-permute-start.17 = (bf16[288,256]{1,0:T(8,128)(2,1)S(1)}, bf16[288,256]{1,0:T(8,128)(2,1)S(1)}, u32[]{:S(2)}, u32[]{:S(2)}) collective-permute-start(bf16[288,256]{1,0:T(8,128)(2,1)S(1)} %collective-permute-done.11), channel_id=1, source_target_pairs={{0,16},{16,0},{32,48},{48,32},{64,80},{80,64},{96,112},{112,96},{1... | collective-permute-start | bytes 442376 | tf_op jit(solution)/shard_map/ppermute | solution.py:45
  116.0 10.3 %collective-permute-start.16 = (bf16[512,256]{1,0:T(8,128)(2,1)S(1)}, bf16[512,256]{1,0:T(8,128)(2,1)S(1)}, u32[]{:S(2)}, u32[]{:S(2)}) collective-permute-start(bf16[512,256]{1,0:T(8,128)(2,1)S(1)} %broadcast_select_fusion.2), channel_id=1, source_target_pairs={{0,16},{16,0},{32,48},{48,32},{64,80},{80,64},{96,112},{112,96},{1... | collective-permute-start | bytes 786440 | tf_op jit(solution)/shard_map/ppermute | solution.py:45
  126.3 12.5 %collective-permute-start.18 = (bf16[512,256]{1,0:T(8,128)(2,1)S(1)}, bf16[512,256]{1,0:T(8,128)(2,1)S(1)}, u32[]{:S(2)}, u32[]{:S(2)}) collective-permute-start(bf16[512,256]{1,0:T(8,128)(2,1)S(1)} %collective-permute-done.15.rest_0_), channel_id=1, source_target_pairs={{0,32},{16,48},{32,64},{48,80},{64,96},{80,112},{96,128},{112,144}... | collective-permute-start | bytes 786440 | tf_op jit(solution)/shard_map/ppermute | solution.py:45
  155.6 10.1 %collective-permute-start.22 = (bf16[2,512,256]{2,1,0:T(8,128)(2,1)S(1)}, bf16[2,512,256]{2,1,0:T(8,128)(2,1)S(1)}, u32[]{:S(2)}, u32[]{:S(2)}) collective-permute-start(bf16[2,512,256]{2,1,0:T(8,128)(2,1)S(1)} %pad_maximum_fusion.rest_0_), channel_id=1, source_target_pairs={{0,4},{1,5},{2,6},{3,7},{4,8},{5,9},{6,10},{7,11},{8,12},{9,13},{1... | collective-permute-start | bytes 1572872 | tf_op jit(solution)/shard_map/ppermute | solution.py:49
  165.7 17.5 %collective-permute-start.27 = (bf16[2,512,256]{2,1,0:T(8,128)(2,1)S(1)}, bf16[2,512,256]{2,1,0:T(8,128)(2,1)S(1)}, u32[]{:S(2)}, u32[]{:S(2)}) collective-permute-start(bf16[2,512,256]{2,1,0:T(8,128)(2,1)S(1)} %collective-permute-done.22.rest_1_), channel_id=1, source_target_pairs={{0,1},{1,0},{2,3},{3,2},{4,5},{5,4},{6,7},{7,6},{8,9},{9,8},{10,11... | collective-permute-start | bytes 1572872 | tf_op jit(solution)/shard_map/ppermute | solution.py:49
  171.3 11.9 %collective-permute-start.28 = (bf16[2,512,256]{2,1,0:T(8,128)(2,1)S(1)}, bf16[2,512,256]{2,1,0:T(8,128)(2,1)}, u32[]{:S(2)}, u32[]{:S(2)}) collective-permute-start(bf16[2,512,256]{2,1,0:T(8,128)(2,1)S(1)} %collective-permute-done.23.rest_2_), channel_id=1, source_target_pairs={{0,1},{1,0},{2,3},{3,2},{4,5},{5,4},{6,7},{7,6},{8,9},{9,8},{10,11... | collective-permute-start | bytes 1572872 | tf_op jit(solution)/shard_map/ppermute | solution.py:49
  171.5 11.7 %collective-permute-start.25 = (bf16[1,512,256]{2,1,0:T(8,128)(2,1)S(1)}, bf16[1,512,256]{2,1,0:T(8,128)(2,1)}, u32[]{:S(2)}, u32[]{:S(2)}) collective-permute-start(bf16[1,512,256]{2,1,0:T(8,128)(2,1)S(1)} %slice.177), channel_id=1, source_target_pairs={{0,4},{1,5},{2,6},{3,7},{4,8},{5,9},{6,10},{7,11},{8,12},{9,13},{1... | collective-permute-start | bytes 786440 | tf_op jit(solution)/shard_map/ppermute | solution.py:49
  171.6 11.6 %collective-permute-start.26 = (bf16[1,512,256]{2,1,0:T(8,128)(2,1)S(1)}, bf16[1,512,256]{2,1,0:T(8,128)(2,1)}, u32[]{:S(2)}, u32[]{:S(2)}) collective-permute-start(bf16[1,512,256]{2,1,0:T(8,128)(2,1)S(1)} %slice.178), channel_id=1, source_target_pairs={{4,0},{5,1},{6,2},{7,3},{8,4},{9,5},{10,6},{11,7},{12,8},{13,9},{1... | collective-permute-start | bytes 786440 | tf_op jit(solution)/shard_map/ppermute | solution.py:49
  192.5 9.5 %all-to-all-start = ((f32[16,1,512]{2,1,0:T(1,128)}), f32[16,1,512]{2,1,0:T(1,128)S(1)}, u32[]{:S(2)}, u32[]{:S(2)}) async-start(f32[16,1,512]{2,1,0:T(1,128)} %get-tuple-element.98), calls=%async_computation | async-start | bytes 65536 | tf_op jit(solution)/shard_map/all_to_all | solution.py:437
  (38 other events, 617.5 us)
Sparse Core Ops, SparseCore 0:
  10.2 46.5 all-gather.6
  59.1 45.4 all-gather.8
  138.9 39.7 all-gather.10
